TPU v7x, 256 devices: a whole 4x4x8 slice. The times are simulated.
256 devices in a mesh: row: 8 (over y, z_lo), col: 32 (over x, z_hi, core).
Axes of the slice: x: 4, y: 4, z: 8 (z_hi: 4, z_lo: 2; z = z_hi * 2 + z_lo), core: 2. Of those that a mesh axis runs over, the one named last changes fastest.
Arguments:
- image_student: bfloat16 [16384, 1024], P(('row', 'col')), may hold values from -2.5 to 2.5
- text_student: bfloat16 [16384, 1024], P(('col', 'row')), may hold values from -2.5 to 2.5
- image_teacher: bfloat16 [16384, 1024], P(('row', 'col')), may hold values from -2.5 to 2.5
- text_teacher: bfloat16 [16384, 1024], P(('col', 'row')), may hold values from -2.5 to 2.5
Outputs:
- loss: float32 [], replicated
- image_grad: float32 [16384, 1024], P(('row', 'col'))
- text_grad: float32 [16384, 1024], P(('col', 'row'))
All inputs are finite; a program needn't handle non-finite values.
Results may differ from a plain program's by a relative error of at most 0.002.
Values may be sent and summed in bfloat16 or wider, within the bound.
No kernel may reach another device: no remote copies, remote signals or barrier semaphores. Data moves between devices by JAX's collectives and lax.ppermute only.
A program may use at most 128 MiB of HBM per device.

v0:
```python
import functools

import jax
import jax.numpy as jnp
from jax import lax
from jax.sharding import Mesh
from jax.sharding import PartitionSpec as P

COL = ("col_0", "col_1", "col_2")
ROW = ("row_0", "row_1")
ROW_COL = ("row_0", "row_1", "col_0", "col_1", "col_2")
COL_ROW = ("col_0", "col_1", "col_2", "row_0", "row_1")


logit_scale = 100.0


def sent_together(arrays, axis, dim, along):
    widths = [a.shape[along] for a in arrays]
    both = jnp.concatenate(arrays, axis=along)
    result = lax.all_gather(both, axis, axis=dim, tiled=True)
    return tuple(jnp.split(result, [sum(widths[:k]) for k in range(1, len(widths))], axis=along))


def gathered_once(x, axis):
    leaves = jax.tree.leaves(x)
    turns = sorted(range(len(leaves)), key=lambda k: -leaves[k].size)
    width = (1, *leaves[turns[0]].shape)[-1]
    lines = [
        jnp.pad(leaves[k].reshape(-1), (0, -leaves[k].size % width)).reshape(-1, width)
        for k in turns
    ]
    both, at, found = (lax.all_gather(jnp.concatenate(lines), axis), 0, {})
    for k, line in zip(turns, lines):
        slab = both[:, at : at + len(line)].reshape(len(both), -1)
        found[k] = slab[:, : leaves[k].size].reshape(-1, *leaves[k].shape)
        at += len(line)
    numbers = iter(range(len(leaves)))
    return jax.tree.map(lambda _: found[next(numbers)], x)


def merged_by_axis(x, axes, combine):
    for axis in axes:
        pieces = gathered_once(x, axis)
        x = jax.tree.map(lambda part: part[0], pieces)
        for k in range(1, lax.axis_size(axis)):
            x = combine(x, jax.tree.map(lambda part: part[k], pieces))
    return x


def sent_to_all(x, axis):
    copies = jnp.broadcast_to(x, (lax.axis_size(axis), *x.shape))
    return lax.all_to_all(copies, axis, split_axis=0, concat_axis=0, tiled=True)


def all_in_one(x, axis):
    leaves = jax.tree.leaves(x)
    turns = sorted(range(len(leaves)), key=lambda k: -leaves[k].size)
    width = (1, *leaves[turns[0]].shape)[-1]
    lines = [
        jnp.pad(leaves[k].reshape(-1), (0, -leaves[k].size % width)).reshape(-1, width)
        for k in turns
    ]
    both, at, found = (sent_to_all(jnp.concatenate(lines), axis), 0, {})
    for k, line in zip(turns, lines):
        slab = both[:, at : at + len(line)].reshape(len(both), -1)
        found[k] = slab[:, : leaves[k].size].reshape(-1, *leaves[k].shape)
        at += len(line)
    numbers = iter(range(len(leaves)))
    return jax.tree.map(lambda _: found[next(numbers)], x)


def folded_in_pairs(pieces, combine):
    while len(jax.tree.leaves(pieces)[0]) > 1:
        pieces = jax.vmap(combine)(
            *(jax.tree.map(lambda part: part[side::2], pieces) for side in (0, 1))
        )
    return jax.tree.map(lambda part: part[0], pieces)


def joined_all(x, axis, combine):
    pieces = all_in_one(x, axis)
    return folded_in_pairs(pieces, combine)


def one_axis_at_a_time(x, axes):
    return functools.reduce(lax.psum, axes, x)


def in_blocks(x, dim, length):
    before, after = (x.shape[:dim], x.shape[dim + 1 :])
    return jnp.moveaxis(x.reshape(*before, length, -1, *after), dim, 0)


def sent_and_summed(x, axis, dim):
    length = lax.axis_size(axis)
    blocks = lax.all_to_all(in_blocks(x, dim, length), axis, 0, 0, tiled=True)
    return jnp.sum(blocks, axis=0)


def tile_logits(left, right):
    return logit_scale * lax.dot_general(
        left, right, (((1,), (1,)), ((), ())), preferred_element_type=jnp.float32
    )


def partial_stats(student, teacher, along):
    student_high = jnp.max(student, along, keepdims=True)
    student_total = jnp.sum(jnp.exp(student - student_high), along)
    teacher_high = jnp.max(teacher, along, keepdims=True)
    weights = jnp.exp(teacher - teacher_high)
    teacher_total = jnp.sum(weights, along)
    divergence = jnp.sum(weights * (teacher - student), along)
    return (
        jnp.squeeze(student_high, along),
        student_total,
        jnp.squeeze(teacher_high, along),
        teacher_total,
        divergence,
    )


def merge_stats(first, second):
    student_high = jnp.maximum(first[0], second[0])
    teacher_high = jnp.maximum(first[2], second[2])
    early = jnp.exp(first[2] - teacher_high)
    later = jnp.exp(second[2] - teacher_high)
    student_total = first[1] * jnp.exp(first[0] - student_high) + second[1] * jnp.exp(
        second[0] - student_high
    )
    return (
        student_high,
        student_total,
        teacher_high,
        first[3] * early + second[3] * later,
        first[4] * early + second[4] * later,
    )


def finish(stats):
    student_lse = stats[0] + jnp.log(stats[1])
    teacher_lse = stats[2] + jnp.log(stats[3])
    divergence = stats[4] / stats[3] - teacher_lse + student_lse
    return (student_lse, teacher_lse, 0.5 * (student_lse + divergence))


def body(image_student, text_student, image_teacher, text_teacher):
    per_device = image_student.shape[0]
    image_slab, image_frozen = sent_together((image_student, image_teacher), COL, 0, 1)
    text_slab, text_frozen = sent_together((text_student, text_teacher), ROW, 0, 1)
    student = tile_logits(image_slab, text_slab)
    teacher = tile_logits(image_frozen, text_frozen)
    row_stats = merged_by_axis(partial_stats(student, teacher, 1), COL, merge_stats)
    column_stats = joined_all(partial_stats(student, teacher, 0), ROW, merge_stats)
    student_rows, teacher_rows, row_terms = finish(row_stats)
    student_columns, teacher_columns, column_terms = finish(column_stats)
    row_place = lax.axis_index(ROW)
    col_place = lax.axis_index(COL)
    row_index = row_place * student.shape[0] + jnp.arange(student.shape[0], dtype=jnp.int32)
    column_index = col_place * student.shape[1] + jnp.arange(student.shape[1], dtype=jnp.int32)
    identity = (row_index[:, None] == column_index[None, :]).astype(jnp.float32)
    own_rows = lax.dynamic_slice_in_dim(row_terms, col_place * per_device, per_device)
    own_columns = lax.dynamic_slice_in_dim(column_terms, row_place * per_device, per_device)
    partial_value = jnp.sum(own_rows) + jnp.sum(own_columns) - jnp.sum(student * identity)
    pair_count = per_device * lax.axis_size(ROW) * lax.axis_size(COL)
    loss = one_axis_at_a_time(partial_value, ROW_COL) / pair_count
    gradient = (
        jnp.exp(student - student_rows[:, None])
        + jnp.exp(student - student_columns[None, :])
        - 0.5
        * (jnp.exp(teacher - teacher_rows[:, None]) + jnp.exp(teacher - teacher_columns[None, :]))
        - identity
    ).astype(jnp.bfloat16)
    picked = gradient
    image_grad = lax.psum_scatter(
        logit_scale * jnp.dot(picked, text_slab, preferred_element_type=jnp.float32),
        COL,
        scatter_dimension=0,
        tiled=True,
    )
    picked = gradient
    text_grad = sent_and_summed(
        logit_scale
        * lax.dot_general(
            picked, image_slab, (((0,), (0,)), ((), ())), preferred_element_type=jnp.float32
        ),
        ROW,
        0,
    )
    return (loss, image_grad, text_grad)


def solution(mesh):
    finer = Mesh(mesh.devices.reshape(4, 2, 4, 4, 2), ("row_0", "row_1", "col_0", "col_1", "col_2"))
    placed = (P(ROW_COL, None), P(COL_ROW, None), P(ROW_COL, None), P(COL_ROW, None))
    return jax.shard_map(
        body,
        mesh=finer,
        in_specs=placed,
        out_specs=(P(), P(ROW_COL, None), P(COL_ROW, None)),
        check_vma=False,
    )
```

profile of v0, /device:TPU:8, one launch (start us, length us, event | category | flops | bytes accessed | tf_op | source)
XLA Modules:
  0.0 342.5 jit_solution(16331013128731658910)
XLA Ops:
  7.2 1.7 pad_maximum_fusion.1
  9.0 1.7 pad_maximum_fusion
  10.7 55.6 %all-gather.11.cloned.1.call-done = bf16[512,2048]{1,0:T(8,128)(2,1)} async-done(((bf16[64,2048]{1,0:T(8,128)(2,1)}), bf16[512,2048]{1,0:T(8,128)(2,1)}) %all-gather.11.cloned.1.call-update) | async-done | bytes 2097168 | tf_op jit(solution)/shard_map/all_gather | solution.py:21
  66.3 82.3 %all-gather.9.cloned.1.call-done = bf16[2048,2048]{1,0:T(8,128)(2,1)} async-done(((bf16[64,2048]{1,0:T(8,128)(2,1)}), bf16[2048,2048]{1,0:T(8,128)(2,1)}) %all-gather.9.cloned.1.call-update) | async-done | bytes 8388624 | tf_op jit(solution)/shard_map/all_gather | solution.py:21
  148.6 5.2 %fusion.103 = (f32[512]{0:T(512)S(1)}, f32[2048]{0:T(1024)S(1)}, f32[2048,512]{1,0:T(8,128)S(1)}) fusion(bf16[512,2048]{1,0:T(8,128)(2,1)} %all-gather.11.cloned.1.call-done, bf16[2048,2048]{1,0:T(8,128)(2,1)} %all-gather.9.cloned.1.call-done), kind=kOutput, calls=%fused_computation.201 | convolution fusion | flops 2150626816 | bytes 9447424 | tf_op jit(solution)/shard_map/dot_general | solution.py:102
  153.8 2.5 fusion.102
  156.3 5.4 %multiply_reduce_fusion = (f32[512]{0:T(512)S(1)}, f32[2048]{0:T(1024)S(1)}, f32[2048]{0:T(1024)S(1)}, f32[512]{0:T(512)S(1)}, f32[]{:T(128)}, /*index=5*/f32[512]{0:T(512)S(1)}, f32[2048]{0:T(1024)S(1)}) fusion(f32[2048,512]{1,0:T(8,128)S(1)} %get-tuple-element.55, f32[512]{0:T(512)S(1)} %get-tuple-element.10, f32[2048,512]{1,0:T(8,128)S(1)} %get-tuple-element.54, ...), kind=kLoop, calls=%fused_computation.8 | loop fusion | flops 16769535 | bytes 8450052 | tf_op jit(solution)/shard_map/reduce_sum | solution.py:113
  161.8 12.5 %all-gather.3 = f32[4,5,2048]{2,1,0:T(8,128)S(1)} all-gather(f32[1,5,2048]{2,1,0:T(8,128)S(1)} %bitcast.437), channel_id=2, replica_groups=mesh['row_0'=4,'row_1'=2,'col_0'=4,'col_1'=4,'col_2'=2] {'col_0'}, dimensions={0}, use_global_device_ids=true | all-gather | bytes 204800 | tf_op jit(solution)/shard_map/all_gather | solution.py:33
  174.7 14.8 %all-gather.4 = f32[4,5,2048]{2,1,0:T(8,128)S(1)} all-gather(f32[1,5,2048]{2,1,0:T(8,128)S(1)} %bitcast.438), channel_id=3, replica_groups=mesh['row_0'=4,'row_1'=2,'col_0'=4,'col_1'=4,'col_2'=2] {'col_1'}, dimensions={0}, use_global_device_ids=true | all-gather | bytes 204800 | tf_op jit(solution)/shard_map/all_gather | solution.py:33
  189.9 1.9 all-gather.5
  192.6 5.8 %all-to-all-start = ((f32[8,5,512]{2,1,0:T(8,128)}), f32[8,5,512]{2,1,0:T(8,128)S(1)}, u32[]{:S(2)}, u32[]{:S(2)}) async-start(f32[8,5,512]{2,1,0:T(8,128)} %broadcast_in_dim.2), calls=%async_computation | async-start | bytes 262144 | tf_op jit(solution)/shard_map/all_to_all | solution.py:53
  198.4 5.0 %all-to-all-done = f32[8,5,512]{2,1,0:T(8,128)S(1)} async-done(((f32[8,5,512]{2,1,0:T(8,128)}), f32[8,5,512]{2,1,0:T(8,128)S(1)}, u32[]{:S(2)}, u32[]{:S(2)}) %all-to-all-start) | async-done | bytes 81952 | tf_op jit(solution)/shard_map/all_to_all | solution.py:53
  204.2 5.6 %fusion.2 = bf16[2048,512]{1,0:T(8,128)(2,1)S(1)} fusion(f32[2048,512]{1,0:T(8,128)} %copy-done.1, f32[2048,512]{1,0:T(8,128)} %copy-done, f32[512]{0:T(512)S(1)} %bitcast.466, f32[2048]{0:T(1024)S(1)} %get-tuple-element.26, f32[512]{0:T(512)S(1)} %bitcast.459, f32[2048]{0:T(1024)S(1)} %get-tuple-element.56, s32[512]{0:T(512)S(1)} %iota_add_fusion.1, ...), kind=kLoop, calls=%fused_computation.5 | loop fusion | flops 12582912 | bytes 10516480 | tf_op jit(solution)/shard_map/convert_element_type | solution.py:173
  209.9 5.6 %convolution_multiply_fusion = f32[2048,1024]{1,0:T(8,128)} fusion(bf16[2048,512]{1,0:T(8,128)(2,1)S(1)} %fusion.2, bf16[512,2048]{1,0:T(8,128)(2,1)S(1)} %copy-done.4), kind=kOutput, calls=%fused_computation.2 | convolution fusion | flops 2149580800 | bytes 11534336 | tf_op jit(solution)/shard_map/dot_general | solution.py:176
  215.5 5.9 %fusion.17 = f32[512,1024]{1,0:T(8,128)} fusion(bf16[2048,512]{1,0:T(8,128)(2,1)S(1)} %fusion.2, bf16[2048,2048]{1,0:T(8,128)(2,1)} %all-gather.9.cloned.1.call-done), kind=kOutput, calls=%fused_computation.22 | convolution fusion | flops 2148007936 | bytes 8388608 | tf_op jit(solution)/shard_map/dot_general | solution.py:184
  221.5 5.2 %all-to-all-start.1 = ((f32[8,64,1024]{2,1,0:T(8,128)}), f32[8,64,1024]{2,1,0:T(8,128)S(1)}, u32[]{:S(2)}, u32[]{:S(2)}) async-start(f32[8,64,1024]{2,1,0:T(8,128)} %bitcast.436), calls=%async_computation.2 | async-start | bytes 4194304 | tf_op jit(solution)/shard_map/all_to_all | solution.py:97
  227.3 0.8 dynamic-slice_reduce_fusion
  230.0 22.8 %psum.35 = f32[]{:T(128)} all-reduce(f32[]{:T(128)S(6)} %sub.492), channel_id=1, replica_groups=mesh['row_0'=4,'row_1'=2,'col_0'=4,'col_1'=4,'col_2'=2] {'row_0'}, use_global_device_ids=true, to_apply=%region_13.14 | all-reduce | flops 1 | bytes 8 | tf_op jit(solution)/shard_map/psum | solution.py:87
  252.8 5.5 %psum.36 = f32[]{:T(128)} all-reduce(f32[]{:T(128)} %psum.35), channel_id=1, replica_groups=mesh['row_0'=4,'row_1'=2,'col_0'=4,'col_1'=4,'col_2'=2] {'row_1'}, use_global_device_ids=true, to_apply=%region_14.15 | all-reduce | flops 1 | bytes 8 | tf_op jit(solution)/shard_map/psum | solution.py:87
  258.4 11.2 %psum.37 = f32[]{:T(128)} all-reduce(f32[]{:T(128)} %psum.36), channel_id=1, replica_groups=mesh['row_0'=4,'row_1'=2,'col_0'=4,'col_1'=4,'col_2'=2] {'col_0'}, use_global_device_ids=true, to_apply=%region_15.16 | all-reduce | flops 1 | bytes 8 | tf_op jit(solution)/shard_map/psum | solution.py:87
  269.6 11.2 %psum.38 = f32[]{:T(128)} all-reduce(f32[]{:T(128)} %psum.37), channel_id=1, replica_groups=mesh['row_0'=4,'row_1'=2,'col_0'=4,'col_1'=4,'col_2'=2] {'col_1'}, use_global_device_ids=true, to_apply=%region_16.17 | all-reduce | flops 1 | bytes 8 | tf_op jit(solution)/shard_map/psum | solution.py:87
  280.8 3.1 psum.39
  284.5 0.8 reduce_sum.99
  285.4 49.4 %reduce-scatter.2.cloned.1.call-done = f32[64,1024]{1,0:T(8,128)} async-done(((f32[2048,1024]{1,0:T(8,128)}), f32[64,1024]{1,0:T(8,128)}) %reduce-scatter.2.cloned.1.call-update) | async-done | bytes 262160 | tf_op jit(solution)/shard_map/reduce_scatter | solution.py:175
  (65 shorter events, 3.1 us)
Async XLA Ops:
  7.2 59.1 %all-gather.11.cloned.1.call-start = ((), (), s32[]{:S(2)}) async-start(), calls=%async_computation.4 | async-start | bytes 2359296 | tf_op jit(solution)/shard_map/all_gather | solution.py:21
  8.9 139.6 %all-gather.9.cloned.1.call-start = ((), (), s32[]{:S(2)}) async-start(), calls=%async_computation.3 | async-start | bytes 8650752 | tf_op jit(solution)/shard_map/all_gather | solution.py:21
  66.3 87.5 %copy-start.3 = (bf16[512,2048]{1,0:T(8,128)(2,1)S(1)}, bf16[512,2048]{1,0:T(8,128)(2,1)}, u32[]{:S(2)}) copy-start(bf16[512,2048]{1,0:T(8,128)(2,1)} %all-gather.11.cloned.1.call-done) | copy-start | bytes 6291460
  148.6 5.2 %copy-start.2 = (bf16[2048,2048]{1,0:T(8,128)(2,1)S(1)}, bf16[2048,2048]{1,0:T(8,128)(2,1)}, u32[]{:S(2)}) copy-start(bf16[2048,2048]{1,0:T(8,128)(2,1)} %all-gather.9.cloned.1.call-done) | copy-start | bytes 25165828
  153.8 2.6 copy-start
  156.3 5.4 %copy-start.1 = (f32[2048,512]{1,0:T(8,128)}, f32[2048,512]{1,0:T(8,128)S(1)}, u32[]{:S(2)}) copy-start(f32[2048,512]{1,0:T(8,128)S(1)} %get-tuple-element.55) | copy-start | bytes 12582916
  192.6 10.9 %all-to-all-start = ((f32[8,5,512]{2,1,0:T(8,128)}), f32[8,5,512]{2,1,0:T(8,128)S(1)}, u32[]{:S(2)}, u32[]{:S(2)}) async-start(f32[8,5,512]{2,1,0:T(8,128)} %broadcast_in_dim.2), calls=%async_computation | async-start | bytes 262144 | tf_op jit(solution)/shard_map/all_to_all | solution.py:53
  198.4 136.4 %reduce-scatter.2.cloned.1.call-start = ((), (), s32[]{:S(2)}) async-start(), calls=%async_computation.5 | async-start | bytes 8650752 | tf_op jit(solution)/shard_map/reduce_scatter | solution.py:175
  204.2 5.7 %copy-start.4 = (bf16[512,2048]{1,0:T(8,128)(2,1)S(1)}, bf16[512,2048]{1,0:T(8,128)(2,1)}, u32[]{:S(2)}) copy-start(bf16[512,2048]{1,0:T(8,128)(2,1)} %all-gather.11.cloned.1.call-done) | copy-start | bytes 6291460
  221.5 63.1 %all-to-all-start.1 = ((f32[8,64,1024]{2,1,0:T(8,128)}), f32[8,64,1024]{2,1,0:T(8,128)S(1)}, u32[]{:S(2)}, u32[]{:S(2)}) async-start(f32[8,64,1024]{2,1,0:T(8,128)} %bitcast.436), calls=%async_computation.2 | async-start | bytes 4194304 | tf_op jit(solution)/shard_map/all_to_all | solution.py:97
Sparse Core Ops, SparseCore 0:
  10.4 55.8 all-gather.10
  69.4 79.1 all-gather.8
  215.6 119.1 reduce-scatter.1
where the time goes:
time: 343 us; the launch traced here: 342 us
  waiting for transfers between devices  192 us (56%)
  blocking collectives  83 us (24%)
  matrix products  19.3 us (6%)
  between operations  17.7 us (5%)
  other arithmetic  17.5 us (5%)
  starting transfers between devices  11.1 us (3%)
    all_gather x2, waiting for transfers between devices, sent_together(): result = lax.all_gather(both, axis, axis=dim, tiled=True)  138 us
    psum x5, blocking collectives, one_axis_at_a_time(): return functools.reduce(lax.psum, axes, x)  53.8 us
    reduce_scatter x1, waiting for transfers between devices, body(): lax.psum_scatter(logit_scale * jnp.dot(picked, text_slab, preferred_eleme...  49.4 us
    all_gather x3, blocking collectives, gathered_once(): both, at, found = (lax.all_gather(jnp.concatenate(lines), axis), 0, {})  29.2 us
    dot_general x2, matrix products, tile_logits(): lax.dot_general(left, right, (((1,), (1,)), ((), ())), preferred_element_...  7.72 us
  transfers between devices with their start and end apart: 5, of which 4 were waited for; matrix products, arithmetic and copies ran while one was open for 3% of the time, Pallas kernels for 0%

commit v1 on v0

v1 whole, which is shorter than its diff:
```python
import itertools
import math

import jax
import jax.numpy as jnp
from jax import lax
from jax.experimental import pallas as pl
from jax.experimental.pallas import tpu as pltpu
from jax.sharding import Mesh
from jax.sharding import PartitionSpec as P

NAMES = ("y", "zl", "x", "zh", "c")
SIZES = (4, 2, 4, 4, 2)
ROW_COL = ("y", "zl", "x", "zh", "c")
COL_ROW = ("x", "zh", "c", "y", "zl")
TEXT_GROUP = ("y", "x")
IMAGE_GROUP = ("zl", "zh", "c")

LOG2E = math.log2(math.e)
LN2 = math.log(2.0)
SCALE = 100.0
BLOCK = 64
WIDTH = 1024
SIDE = 1024
STRIP = 128
VMEM_LIMIT = 52 * 1024 * 1024


def places():
    return list(itertools.product(*(range(n) for n in SIZES)))


def index_of(place):
    at = 0
    for value, size in zip(place, SIZES):
        at = at * size + value % size
    return at


def shifted(place, axis, by):
    y, zl, x, zh, c = place
    if axis == "z":
        z = (zh * 2 + zl + by) % 8
        return (y, z % 2, x, z // 2, c)
    if axis == "x":
        return (y, zl, (x + by) % 4, zh, c)
    if axis == "y":
        return ((y + by) % 4, zl, x, zh, c)
    return (y, zl, x, zh, (c + by) % 2)


def moved(value, to):
    pairs = [(index_of(p), index_of(to(p))) for p in places()]
    return lax.ppermute(value, NAMES, pairs)


def along_u(by):
    return lambda p: shifted(p, "x" if p[4] == 0 else "y", by)


def along_v(by):
    return lambda p: shifted(p, "y" if p[4] == 0 else "x", by)


def along_z(by):
    return lambda p: shifted(p, "z", by if p[4] == 0 else -by)


def other_core(p):
    return shifted(p, "c", 1)


def gathered_text(own):
    back = moved(own, along_u(1))
    ahead = moved(own, along_u(-1))
    far = moved(back, along_u(1))
    first = jnp.concatenate([own, back], axis=0)
    second = jnp.concatenate([ahead, far], axis=0)
    first_back = moved(first, along_v(1))
    first_ahead = moved(first, along_v(-1))
    second_back = moved(second, along_v(1))
    second_ahead = moved(second, along_v(-1))
    first_far = moved(first_back, along_v(1))
    second_far = moved(second_ahead, along_v(-1))
    pieces = [
        (first, ((0, 0), (-1, 0))),
        (second, ((1, 0), (2, 0))),
        (first_back, ((0, -1), (-1, -1))),
        (first_ahead, ((0, 1), (-1, 1))),
        (second_back, ((1, -1), (2, -1))),
        (second_ahead, ((1, 1), (2, 1))),
        (first_far, ((0, 2), (-1, 2))),
        (second_far, ((1, 2), (2, 2))),
    ]
    return pieces


def gathered_images(own):
    backs, aheads = [own], [own]
    for _ in range(3):
        backs.append(moved(backs[-1], along_z(1)))
        aheads.append(moved(aheads[-1], along_z(-1)))
    far = moved(backs[3], along_z(1))
    near = jnp.concatenate([own, backs[1], aheads[1], backs[2]], axis=0)
    rest = jnp.concatenate([aheads[2], backs[3], aheads[3], far], axis=0)
    near_other = moved(near, other_core)
    rest_other = moved(rest, other_core)
    steps_near, steps_rest = (0, -1, 1, -2), (2, -3, 3, 4)
    return [
        (near, [(0, k) for k in steps_near]),
        (rest, [(0, k) for k in steps_rest]),
        (near_other, [(1, k) for k in steps_near]),
        (rest_other, [(1, k) for k in steps_rest]),
    ]


def fill(value, shape):
    return jnp.full(shape, value, jnp.float32)


def logits_kernel(counts, *refs):
    n_text, n_image = counts
    place_ref = refs[0]
    row_id_ref, col_id_ref = refs[1:3]
    text_refs = refs[3 : 3 + n_text]
    image_refs = refs[3 + n_text : 3 + n_text + n_image]
    (s_ref, t_ref, text_out, image_out, row_ref, col_ref) = refs[
        3 + n_text + n_image : 9 + n_text + n_image
    ]
    (text_frozen, image_frozen, s_high, t_high, sems) = refs[9 + n_text + n_image :]
    copies = []
    k = 0
    for group, out, frozen in (
        (text_refs, text_out, text_frozen),
        (image_refs, image_out, image_frozen),
    ):
        for ref in group:
            for b in range(ref.shape[0] // BLOCK):
                at = pl.multiple_of(place_ref[k] * BLOCK, BLOCK)
                for half, target in ((0, out), (1, frozen)):
                    copies.append(
                        pltpu.make_async_copy(
                            ref.at[pl.ds(b * BLOCK, BLOCK), pl.ds(half * WIDTH, WIDTH)],
                            target.at[pl.ds(at, BLOCK), :],
                            sems.at[2 * k + half],
                        )
                    )
                k += 1
    for copy in copies:
        copy.start()
    for copy in copies:
        copy.wait()

    lowest = -3.0e38
    s_high[...] = fill(lowest, (8, SIDE))
    t_high[...] = fill(lowest, (8, SIDE))

    @pl.loop(0, SIDE // STRIP)
    def _(i):
        rows = pl.ds(pl.multiple_of(i * STRIP, STRIP), STRIP)
        for left, right, out, high in (
            (image_out, text_out, s_ref, s_high),
            (image_frozen, text_frozen, t_ref, t_high),
        ):
            tile = (SCALE * LOG2E) * lax.dot_general(
                left[rows, :],
                right[...],
                (((1,), (1,)), ((), ())),
                preferred_element_type=jnp.float32,
            )
            out[rows, :] = tile
            high[...] = jnp.maximum(high[...], jnp.max(tile.reshape(STRIP // 8, 8, SIDE), axis=0))

    s_top = jnp.max(s_high[...], axis=0, keepdims=True)
    t_top = jnp.max(t_high[...], axis=0, keepdims=True)
    size = 16

    def strip(i, carry):
        s_sum, t_sum, d_sum, diagonal = carry
        base = pl.multiple_of(i * STRIP, STRIP)
        made = []
        for g in range(STRIP // size):
            rows = pl.ds(pl.multiple_of(base + g * size, size), size)
            s = s_ref[rows, :]
            t = t_ref[rows, :]
            gap = t - s
            s_row = jnp.max(s, axis=1, keepdims=True)
            t_row = jnp.max(t, axis=1, keepdims=True)
            s_total = jnp.sum(jnp.exp2(s - s_row), axis=1, keepdims=True)
            weights = jnp.exp2(t - t_row)
            t_total = jnp.sum(weights, axis=1, keepdims=True)
            divergence = jnp.sum(weights * gap, axis=1, keepdims=True)
            made.append(
                (
                    s_row + jnp.log2(s_total),
                    t_row + jnp.log2(t_total),
                    divergence / t_total,
                )
            )
            s_sum = s_sum + jnp.sum(jnp.exp2(s - s_top).reshape(size // 8, 8, SIDE), axis=0)
            weights = jnp.exp2(t - t_top)
            t_sum = t_sum + jnp.sum(weights.reshape(size // 8, 8, SIDE), axis=0)
            d_sum = d_sum + jnp.sum((weights * gap).reshape(size // 8, 8, SIDE), axis=0)
            same = row_id_ref[rows, :] == col_id_ref[...]
            diagonal = diagonal + jnp.sum(
                jnp.where(same, s, 0.0).reshape(size // 8, 8, SIDE), axis=0
            )
        lanes = pl.ds(base, STRIP)
        for which in range(3):
            column = jnp.concatenate([m[which] for m in made], axis=0)
            row_ref[pl.ds(which, 1), lanes] = jnp.transpose(
                jnp.broadcast_to(column, (STRIP, STRIP))
            )[0:1, :]
        return s_sum, t_sum, d_sum, diagonal

    zero = fill(0.0, (8, SIDE))
    s_sum, t_sum, d_sum, diagonal = lax.fori_loop(0, SIDE // STRIP, strip, (zero, zero, zero, zero))
    s_sum = jnp.sum(s_sum, axis=0, keepdims=True)
    t_sum = jnp.sum(t_sum, axis=0, keepdims=True)
    d_sum = jnp.sum(d_sum, axis=0, keepdims=True)
    col_ref[0:1, :] = s_top + jnp.log2(s_sum)
    col_ref[1:2, :] = t_top + jnp.log2(t_sum)
    col_ref[2:3, :] = d_sum / t_sum
    row_ref[3:4, :] = jnp.max(jnp.abs(text_out[...]).astype(jnp.float32), axis=0, keepdims=True)
    col_ref[3:4, :] = jnp.max(jnp.abs(image_out[...]).astype(jnp.float32), axis=0, keepdims=True)
    col_ref[4:5, :] = jnp.sum(diagonal, axis=0, keepdims=True)
    col_ref[5:8, :] = fill(0.0, (3, SIDE))
    row_ref[4:8, :] = fill(0.0, (4, SIDE))


def logits_and_statistics(places_in, row_id, col_id, text, images):
    f32 = jnp.float32
    anywhere = pl.BlockSpec(memory_space=pl.ANY)
    vmem = pl.BlockSpec(memory_space=pltpu.VMEM)
    smem = pl.BlockSpec(memory_space=pltpu.SMEM)

    def kernel(*refs):
        logits_kernel((len(text), len(images)), *refs)

    square = jax.ShapeDtypeStruct((SIDE, SIDE), f32)
    half = jax.ShapeDtypeStruct((SIDE, WIDTH), jnp.bfloat16)
    small = jax.ShapeDtypeStruct((8, SIDE), f32)
    return pl.pallas_call(
        kernel,
        out_shape=(square, square, half, half, small, small),
        in_specs=[smem, vmem, vmem] + [anywhere] * (len(text) + len(images)),
        out_specs=(vmem,) * 6,
        scratch_shapes=[
            pltpu.VMEM((SIDE, WIDTH), jnp.bfloat16),
            pltpu.VMEM((SIDE, WIDTH), jnp.bfloat16),
            pltpu.VMEM((8, SIDE), f32),
            pltpu.VMEM((8, SIDE), f32),
            pltpu.SemaphoreType.DMA((64,)),
        ],
        compiler_params=pltpu.CompilerParams(vmem_limit_bytes=VMEM_LIMIT),
        cost_estimate=pl.CostEstimate(
            flops=4 * SIDE * SIDE * WIDTH, bytes_accessed=20 << 20, transcendentals=4 * SIDE * SIDE
        ),
    )(places_in, row_id, col_id, *text, *images)


def gradient_kernel(s_ref, t_ref, row_ref, col_ref, row_id_ref, col_id_ref, out_ref):
    s_col = col_ref[0:1, :]
    t_col = col_ref[1:2, :] + 1.0
    size = 16

    @pl.loop(0, SIDE // STRIP)
    def _(i):
        base = pl.multiple_of(i * STRIP, STRIP)
        turned = jnp.transpose(row_ref[:, pl.ds(base, STRIP)])
        for g in range(STRIP // size):
            rows = pl.ds(pl.multiple_of(base + g * size, size), size)
            s = s_ref[rows, :]
            t = t_ref[rows, :]
            s_row = turned[g * size : (g + 1) * size, 0:1]
            t_row = turned[g * size : (g + 1) * size, 1:2] + 1.0
            value = (jnp.exp2(s - s_row) + jnp.exp2(s - s_col)) - (
                jnp.exp2(t - t_row) + jnp.exp2(t - t_col)
            )
            same = row_id_ref[rows, :] == col_id_ref[...]
            out_ref[rows, :] = jnp.where(same, value - 1.0, value).astype(jnp.bfloat16)


def gradient_of_logits(s, t, row, col, row_id, col_id):
    vmem = pl.BlockSpec(memory_space=pltpu.VMEM)
    return pl.pallas_call(
        gradient_kernel,
        out_shape=jax.ShapeDtypeStruct((SIDE, SIDE), jnp.bfloat16),
        in_specs=[vmem] * 6,
        out_specs=vmem,
        compiler_params=pltpu.CompilerParams(vmem_limit_bytes=VMEM_LIMIT),
        cost_estimate=pl.CostEstimate(
            flops=16 * SIDE * SIDE, bytes_accessed=10 << 20, transcendentals=4 * SIDE * SIDE
        ),
    )(s, t, row, col, row_id, col_id)


def sent_to_all(x, axis):
    copies = jnp.broadcast_to(x, (lax.axis_size(axis), *x.shape))
    return lax.all_to_all(copies, axis, split_axis=0, concat_axis=0, tiled=True)


def merged(pieces):
    s, t, d = pieces[:, 0], pieces[:, 1], pieces[:, 2]
    s_high, t_high = jnp.max(s, axis=0), jnp.max(t, axis=0)
    s_lse = s_high + jnp.log2(jnp.sum(jnp.exp2(s - s_high), axis=0))
    weights = jnp.exp2(t - t_high)
    total = jnp.sum(weights, axis=0)
    t_lse = t_high + jnp.log2(total)
    divergence = jnp.sum(weights * d, axis=0) / total - t_lse + s_lse
    largest = jnp.maximum(jnp.max(pieces[:, 3]), 1e-30)
    return s_lse, t_lse, jnp.sum(0.5 * LN2 * (s_lse + divergence)), largest


def summed_over(value, steps):
    for to in steps:
        value = value + moved(value, to)
    return value


def body(image_student, text_student, image_teacher, text_teacher):
    y, zl, x, zh, c = (lax.axis_index(n) for n in NAMES)
    z = zh * 2 + zl
    text_pieces = gathered_text(jnp.concatenate([text_student, text_teacher], axis=1))
    image_pieces = gathered_images(jnp.concatenate([image_student, image_teacher], axis=1))

    sign = 1 - 2 * c
    at = []
    for _, offsets in text_pieces:
        for du, dv in offsets:
            dx = jnp.where(c == 0, du, dv)
            dy = jnp.where(c == 0, dv, du)
            at.append(((y + dy) % 4) * 4 + (x + dx) % 4)
    for _, offsets in image_pieces:
        for swapped, step in offsets:
            core = c ^ swapped
            toward = sign if swapped == 0 else -sign
            at.append(core * 8 + (z + toward * step) % 8)
    where = jnp.stack(at).astype(jnp.int32)

    numbers = jnp.arange(SIDE, dtype=jnp.int32)
    slot, inner = numbers // BLOCK, numbers % BLOCK
    text_y, text_x = slot // 4, slot % 4
    col_id = (((text_x * 8 + zh * 2 + c) * 8) + text_y * 2 + zl) * BLOCK + inner
    image_c, image_z = slot // 8, slot % 8
    row_id = ((y * 2 + image_z % 2) * 32 + x * 8 + (image_z // 2) * 2 + image_c) * BLOCK + inner
    row_id, col_id = row_id[:, None], col_id[None, :]

    s, t, text_slab, image_slab, row_part, col_part = logits_and_statistics(
        where, row_id, col_id, [p for p, _ in text_pieces], [p for p, _ in image_pieces]
    )

    col_all = sent_to_all(col_part, TEXT_GROUP)
    s_col, t_col, col_terms, image_top = merged(col_all)
    diagonal = jnp.sum(col_all[:, 4]) * LN2
    row_all = sent_to_all(row_part, IMAGE_GROUP)
    s_row, t_row, row_terms, text_top = merged(row_all)

    col_value = col_terms - diagonal
    row_value = summed_over(
        jnp.full((8, 128), row_terms),
        [lambda p, k=k, a=a: flipped(p, a, k) for a in ("x", "y") for k in (1, 2)],
    )
    col_value = summed_over(
        jnp.full((8, 128), col_value),
        [other_core] + [lambda p, k=k: flipped(p, "z", k) for k in (1, 2, 4)],
    )
    loss = (row_value[0, 0] + col_value[0, 0]) / (256 * BLOCK)

    pad = jnp.zeros((6, SIDE), jnp.float32)
    gradient = gradient_of_logits(
        s,
        t,
        jnp.concatenate([s_row[None], t_row[None], pad]),
        jnp.concatenate([s_col[None], t_col[None], pad]),
        row_id,
        col_id,
    )

    text_scale = 2.0 / text_top
    image_scale = 2.0 / image_top
    half = SIDE // 2
    theirs = lax.dynamic_slice_in_dim(gradient, (1 - c) * half, half)
    mine = lax.dynamic_slice_in_dim(gradient, c * half, half)
    image_theirs = jnp.dot(theirs, text_slab, preferred_element_type=jnp.float32)
    arrived = moved((image_theirs * text_scale).astype(jnp.float16), other_core)
    text_part = (
        lax.dot_general(
            gradient, image_slab, (((0,), (0,)), ((), ())), preferred_element_type=jnp.float32
        )
        * image_scale
    ).astype(jnp.float16)
    text_blocks = lax.all_to_all(text_part.reshape(16, BLOCK, WIDTH), TEXT_GROUP, 0, 0, tiled=True)
    image_mine = (
        jnp.dot(mine, text_slab, preferred_element_type=jnp.float32) * text_scale
    ) + arrived.astype(jnp.float32)
    blocks = image_mine.astype(jnp.float16).reshape(8, BLOCK, WIDTH)

    def block(step):
        return lax.dynamic_index_in_dim(blocks, (z + sign * step) % 8, 0, keepdims=False).astype(
            jnp.float32
        )

    def narrow(v):
        return v.astype(jnp.float16)

    down = moved(narrow(block(4)), along_z(-1)).astype(jnp.float32)
    up = None
    for k in (3, 2, 1):
        first = narrow(block(-k) + down)
        second = block(k) if up is None else block(k) + up
        down = moved(first, along_z(-1)).astype(jnp.float32)
        up = moved(narrow(second), along_z(1)).astype(jnp.float32)
    image_grad = (block(0) + down + up) * (SCALE / text_scale)
    text_grad = jnp.sum(text_blocks.astype(jnp.float32), axis=0) * (SCALE / image_scale)
    return (loss, image_grad, text_grad)


def flipped(p, axis, bit):
    y, zl, x, zh, c = p
    if axis == "x":
        return (y, zl, x ^ bit, zh, c)
    if axis == "y":
        return (y ^ bit, zl, x, zh, c)
    z = (zh * 2 + zl) ^ bit
    return (y, z % 2, x, z // 2, c)


def solution(mesh):
    finer = Mesh(mesh.devices.reshape(SIZES), NAMES)
    placed = (P(ROW_COL, None), P(COL_ROW, None), P(ROW_COL, None), P(COL_ROW, None))
    return jax.shard_map(
        body,
        mesh=finer,
        in_specs=placed,
        out_specs=(P(), P(ROW_COL, None), P(COL_ROW, None)),
        check_vma=False,
    )
```

time: 343 us -> 215 us (0.63)
  waiting for transfers between devices: 192 us -> 65.7 us
  blocking collectives: 83 us -> 15.1 us
  starting transfers between devices: 11.1 us -> 63.3 us
  Pallas kernels: 0 us -> 36.6 us
  between operations: 17.7 us -> 6.1 us
  matrix products: 19.3 us -> 9.23 us
  other arithmetic: 17.5 us -> 9.08 us
  local copies, waits for them, and re-layouts: 1.53 us -> 9.42 us
    all_gather x2 -> x0, waiting for transfers between devices: 138 us -> none  [sent_together(): result = lax.all_gather(both, axis, axis=dim, tiled=True)]
    psum x5 -> x0, blocking collectives: 53.8 us -> none  [one_axis_at_a_time(): return functools.reduce(lax.psum, axes, x)]
    ppermute x0 -> x34, starting transfers between devices: none -> 50.2 us  [moved(): return lax.ppermute(value, NAMES, pairs)]
    reduce_scatter x1 -> x0, waiting for transfers between devices: 49.4 us -> none  [body(): lax.psum_scatter(logit_scale * jnp.dot(picked, text_slab, preferred_eleme...]
    ppermute x0 -> x34, waiting for transfers between devices: none -> 49.4 us  [moved(): return lax.ppermute(value, NAMES, pairs)]
    pallas_call x0 -> x2, Pallas kernels: none -> 36.6 us  [the longest x1 28.4 us: logits_and_statistics(): pl.pallas_call(kernel, out_shape=(square, square, half, half, small, smal...]
    all_gather x3 -> x0, blocking collectives: 29.2 us -> none  [gathered_once(): both, at, found = (lax.all_gather(jnp.concatenate(lines), axis), 0, {})]
    all_to_all x0 -> x1, blocking collectives: none -> 15.1 us  [sent_to_all(): return lax.all_to_all(copies, axis, split_axis=0, concat_axis=0, tiled=True)]
  transfers between devices with their start and end apart: 5 -> 36, of which waited for: 4 -> 16; matrix products, arithmetic and copies ran while one was open for 3% -> 8% of each run, Pallas kernels for 0% -> 0%
where the time goes in v1:
time: 215 us; the launch traced here: 214 us
  waiting for transfers between devices  65.7 us (31%)
  starting transfers between devices  63.3 us (29%)
  Pallas kernels  36.6 us (17%)
  blocking collectives  15.1 us (7%)
  local copies, waits for them, and re-layouts  9.42 us (4%)
  matrix products  9.23 us (4%)
  other arithmetic  9.08 us (4%)
  between operations  6.1 us (3%)
    ppermute x34, starting transfers between devices, moved(): return lax.ppermute(value, NAMES, pairs)  50.2 us
    ppermute x34, waiting for transfers between devices, moved(): return lax.ppermute(value, NAMES, pairs)  49.4 us
    pallas_call x1, Pallas kernels, logits_and_statistics(): pl.pallas_call(kernel, out_shape=(square, square, half, half, small, smal...  28.4 us
    all_to_all x1, waiting for transfers between devices, sent_to_all(): return lax.all_to_all(copies, axis, split_axis=0, concat_axis=0, tiled=True)  16.3 us
    all_to_all x1, blocking collectives, sent_to_all(): return lax.all_to_all(copies, axis, split_axis=0, concat_axis=0, tiled=True)  15.1 us
    pallas_call x1, Pallas kernels, gradient_of_logits(): pl.pallas_call(gradient_kernel, out_shape=jax.ShapeDtypeStruct((SIDE, SID...  8.22 us
    all_to_all x1, starting transfers between devices, sent_to_all(): return lax.all_to_all(copies, axis, split_axis=0, concat_axis=0, tiled=True)  7.01 us
    all_to_all x1, starting transfers between devices, body(): lax.all_to_all(text_part.reshape(16, BLOCK, WIDTH), TEXT_GROUP, 0, 0, til...  6.1 us
  transfers between devices with their start and end apart: 36, of which 16 were waited for; matrix products, arithmetic and copies ran while one was open for 8% of the time, Pallas kernels for 0%

profile of v1, /device:TPU:8, one launch (start us, length us, event | category | flops | bytes accessed | tf_op | source)
XLA Modules:
  0.0 214.5 jit_solution(13909865535827760419)
XLA Ops:
  7.9 4.0 %collective-permute-start.10 = (bf16[64,2048]{1,0:T(8,128)(2,1)S(1)}, bf16[64,2048]{1,0:T(8,128)(2,1)S(1)}, u32[]{:S(2)}, u32[]{:S(2)}) collective-permute-start(bf16[64,2048]{1,0:T(8,128)(2,1)S(1)} %constant_dynamic-update-slice_fusion.4), channel_id=1, source_target_pairs={{0,38},{1,33},{2,32},{3,35},{4,34},{5,37},{6,36},{7,39},{8,46},{9,... | collective-permute-start | bytes 786440 | tf_op jit(solution)/shard_map/ppermute | solution.py:54
  18.2 3.7 %collective-permute-start.12 = (bf16[64,2048]{1,0:T(8,128)(2,1)S(1)}, bf16[64,2048]{1,0:T(8,128)(2,1)S(1)}, u32[]{:S(2)}, u32[]{:S(2)}) collective-permute-start(bf16[64,2048]{1,0:T(8,128)(2,1)S(1)} %collective-permute-done.10), channel_id=1, source_target_pairs={{0,38},{1,33},{2,32},{3,35},{4,34},{5,37},{6,36},{7,39},{8,46},{9,... | collective-permute-start | bytes 786440 | tf_op jit(solution)/shard_map/ppermute | solution.py:54
  22.1 3.7 %collective-permute-done.12 = bf16[64,2048]{1,0:T(8,128)(2,1)S(1)} collective-permute-done((bf16[64,2048]{1,0:T(8,128)(2,1)S(1)}, bf16[64,2048]{1,0:T(8,128)(2,1)S(1)}, u32[]{:S(2)}, u32[]{:S(2)}) %collective-permute-start.12) | collective-permute-done | bytes 262176 | tf_op jit(solution)/shard_map/ppermute | solution.py:54
  27.8 2.4 %collective-permute-start.14 = (bf16[64,2048]{1,0:T(8,128)(2,1)S(1)}, bf16[64,2048]{1,0:T(8,128)(2,1)S(1)}, u32[]{:S(2)}, u32[]{:S(2)}) collective-permute-start(bf16[64,2048]{1,0:T(8,128)(2,1)S(1)} %collective-permute-done.12), channel_id=1, source_target_pairs={{0,38},{1,33},{2,32},{3,35},{4,34},{5,37},{6,36},{7,39},{8,46},{9,... | collective-permute-start | bytes 786440 | tf_op jit(solution)/shard_map/ppermute | solution.py:54
  30.2 5.9 %collective-permute-done.13 = bf16[64,2048]{1,0:T(8,128)(2,1)S(1)} collective-permute-done((bf16[64,2048]{1,0:T(8,128)(2,1)S(1)}, bf16[64,2048]{1,0:T(8,128)(2,1)S(1)}, u32[]{:S(2)}, u32[]{:S(2)}) %collective-permute-start.13) | collective-permute-done | bytes 262176 | tf_op jit(solution)/shard_map/ppermute | solution.py:54
  37.1 2.5 %collective-permute-done.14 = bf16[64,2048]{1,0:T(8,128)(2,1)S(1)} collective-permute-done((bf16[64,2048]{1,0:T(8,128)(2,1)S(1)}, bf16[64,2048]{1,0:T(8,128)(2,1)S(1)}, u32[]{:S(2)}, u32[]{:S(2)}) %collective-permute-start.14) | collective-permute-done | bytes 262176 | tf_op jit(solution)/shard_map/ppermute | solution.py:54
  41.1 2.6 %collective-permute-done.15 = bf16[64,2048]{1,0:T(8,128)(2,1)S(1)} collective-permute-done((bf16[64,2048]{1,0:T(8,128)(2,1)S(1)}, bf16[64,2048]{1,0:T(8,128)(2,1)S(1)}, u32[]{:S(2)}, u32[]{:S(2)}) %collective-permute-start.15) | collective-permute-done | bytes 262176 | tf_op jit(solution)/shard_map/ppermute | solution.py:54
  50.2 3.6 %collective-permute-done.5.refs_7_ = bf16[128,2048]{1,0:T(8,128)(2,1)} collective-permute-done((bf16[128,2048]{1,0:T(8,128)(2,1)S(1)}, bf16[128,2048]{1,0:T(8,128)(2,1)}, u32[]{:S(2)}, u32[]{:S(2)}) %collective-permute-start.5) | collective-permute-done | bytes 524320 | tf_op jit(solution)/shard_map/ppermute | solution.py:54
  53.8 5.6 %collective-permute-done.7.refs_9_ = bf16[128,2048]{1,0:T(8,128)(2,1)} collective-permute-done((bf16[128,2048]{1,0:T(8,128)(2,1)S(1)}, bf16[128,2048]{1,0:T(8,128)(2,1)}, u32[]{:S(2)}, u32[]{:S(2)}) %collective-permute-start.7) | collective-permute-done | bytes 524320 | tf_op jit(solution)/shard_map/ppermute | solution.py:54
  59.4 28.4 %shard_map.67 = (f32[1024,1024]{1,0:T(8,128)}, f32[1024,1024]{1,0:T(8,128)}, bf16[1024,1024]{1,0:T(8,128)(2,1)}, bf16[1024,1024]{1,0:T(8,128)(2,1)}, f32[8,1024]{1,0:T(8,128)S(1)}, /*index=5*/f32[8,1024]{1,0:T(8,128)S(1)}) custom-call(s32[32]{0:T(128)S(1)} %stack.131.refs_0_, s32[1024,1]{1,0:T(8,128)S(1)} %fusion.15.refs_1_.row_id_ref, ...), custom_call_target="tpu_custom_call" | custom-call | flops 4294967296 | bytes 20971520 | tf_op jit(solution)/shard_map/pallas_call | solution.py:243
  87.8 15.1 %all_to_all.15 = f32[16,8,1024]{2,1,0:T(8,128)S(1)} all-to-all(f32[16,8,1024]{2,1,0:T(8,128)S(1)} %broadcast_in_dim.12), channel_id=1, replica_groups=mesh['y'=4,'zl'=2,'x'=4,'zh'=4,'c'=2] {'y','x'}, dimensions={0} | all-to-all | bytes 1048576 | tf_op jit(solution)/shard_map/all_to_all | solution.py:300
  103.8 7.0 %all-to-all-start = ((f32[16,8,1024]{2,1,0:T(8,128)}), f32[16,8,1024]{2,1,0:T(8,128)S(1)}, u32[]{:S(2)}, u32[]{:S(2)}) async-start(f32[16,8,1024]{2,1,0:T(8,128)} %broadcast_in_dim.10), calls=%async_computation | async-start | bytes 1048576 | tf_op jit(solution)/shard_map/all_to_all | solution.py:300
  110.9 16.3 %all-to-all-done = f32[16,8,1024]{2,1,0:T(8,128)S(1)} async-done(((f32[16,8,1024]{2,1,0:T(8,128)}), f32[16,8,1024]{2,1,0:T(8,128)S(1)}, u32[]{:S(2)}, u32[]{:S(2)}) %all-to-all-start) | async-done | bytes 524320 | tf_op jit(solution)/shard_map/all_to_all | solution.py:300
  130.5 8.2 %shard_map.68 = bf16[1024,1024]{1,0:T(8,128)(2,1)} custom-call(f32[1024,1024]{1,0:T(8,128)} %get-tuple-element.11.s_ref, f32[1024,1024]{1,0:T(8,128)} %get-tuple-element.12.t_ref, f32[8,1024]{1,0:T(8,128)S(1)} %get-tuple-element.50.row_ref, f32[8,1024]{1,0:T(8,128)S(1)} %get-tuple-element.49.col_ref, s32[1024,1]{1,0:T(8,128)S(1)} %fusion.15.refs_1_.row_id_ref, ...), custom_call_target="tpu_custom_call" | custom-call | flops 16777216 | bytes 10485760 | tf_op jit(solution)/shard_map/pallas_call | solution.py:286
  138.8 2.6 %multiply_convert_fusion.1 = f16[512,1024]{1,0:T(8,128)(2,1)S(1)} fusion(bf16[1024,1024]{1,0:T(8,128)(2,1)S(1)} %copy-done.4, bf16[1024,1024]{1,0:T(8,128)(2,1)} %shard_map.68, s32[]{:T(128)S(6)} %select_n.487, f32[]{:T(128)S(6)} %div.88), kind=kOutput, calls=%fused_computation.3 | convolution fusion | flops 1074790400 | bytes 4194312 | tf_op jit(solution)/shard_map/dot_general | solution.py:385
  143.5 2.8 %fusion.1 = f32[512,1024]{1,0:T(8,128)S(1)} fusion(bf16[1024,1024]{1,0:T(8,128)(2,1)} %get-tuple-element.13, bf16[1024,1024]{1,0:T(8,128)(2,1)S(1)} %copy-done, s32[]{:T(128)S(6)} %select_n.486), kind=kOutput, calls=%fused_computation.6 | convolution fusion | flops 1073741824 | bytes 5242884 | tf_op jit(solution)/shard_map/dot_general | solution.py:395
  148.6 3.8 %multiply_convert_fusion = f16[1024,1024]{1,0:T(8,128)(2,1)} fusion(bf16[1024,1024]{1,0:T(8,128)(2,1)S(1)} %copy-done, bf16[1024,1024]{1,0:T(8,128)(2,1)S(1)} %copy-done.5, f32[]{:T(128)S(6)} %div.90), kind=kOutput, calls=%fused_computation.1 | convolution fusion | flops 2149580800 | bytes 6291460 | tf_op jit(solution)/shard_map/dot_general | solution.py:388
  152.3 6.1 %all-to-all-start.2 = ((f16[16,64,1024]{2,1,0:T(8,128)(2,1)}), f16[16,64,1024]{2,1,0:T(8,128)(2,1)S(1)}, u32[]{:S(2)}, u32[]{:S(2)}) async-start(f16[16,64,1024]{2,1,0:T(8,128)(2,1)} %bitcast.125), calls=%async_computation.2 | async-start | bytes 4194304 | tf_op jit(solution)/shard_map/all_to_all | solution.py:393
  162.1 2.8 %collective-permute-start.28 = (f16[64,1024]{1,0:T(8,128)(2,1)S(1)}, f16[64,1024]{1,0:T(8,128)(2,1)S(1)}, u32[]{:S(2)}, u32[]{:S(2)}) collective-permute-start(f16[64,1024]{1,0:T(8,128)(2,1)S(1)} %fusion.29), channel_id=1, source_target_pairs={{0,38},{1,33},{2,32},{3,35},{4,34},{5,37},{6,36},{7,39},{8,46},{9,... | collective-permute-start | bytes 393224 | tf_op jit(solution)/shard_map/ppermute | solution.py:54
  168.6 3.8 %collective-permute-start.29 = (f16[64,1024]{1,0:T(8,128)(2,1)S(1)}, f16[64,1024]{1,0:T(8,128)(2,1)S(1)}, u32[]{:S(2)}, u32[]{:S(2)}) collective-permute-start(f16[64,1024]{1,0:T(8,128)(2,1)S(1)} %fusion.30), channel_id=1, source_target_pairs={{0,38},{1,33},{2,32},{3,35},{4,34},{5,37},{6,36},{7,39},{8,46},{9,... | collective-permute-start | bytes 393224 | tf_op jit(solution)/shard_map/ppermute | solution.py:54
  172.4 15.0 %collective-permute-done.18 = f32[8,128]{1,0:T(8,128)S(1)} collective-permute-done((f32[8,128]{1,0:T(8,128)S(1)}, f32[8,128]{1,0:T(8,128)S(1)}, u32[]{:S(2)}, u32[]{:S(2)}) %collective-permute-start.18) | collective-permute-done | bytes 4128 | tf_op jit(solution)/shard_map/ppermute | solution.py:54
  197.6 2.6 %collective-permute-start.20 = (f32[8,128]{1,0:T(8,128)S(1)}, f32[8,128]{1,0:T(8,128)S(1)}, u32[]{:S(2)}, u32[]{:S(2)}) collective-permute-start(f32[8,128]{1,0:T(8,128)S(1)} %fusion.72), channel_id=1, source_target_pairs={{0,64},{1,65},{2,66},{3,67},{4,68},{5,69},{6,70},{7,71},{8,72},{9,... | collective-permute-start | bytes 12296 | tf_op jit(solution)/shard_map/ppermute | solution.py:54
  200.2 4.2 %collective-permute-start.25 = (f32[8,128]{1,0:T(8,128)S(1)}, f32[8,128]{1,0:T(8,128)S(1)}, u32[]{:S(2)}, u32[]{:S(2)}) collective-permute-start(f32[8,128]{1,0:T(8,128)S(1)} %add.907), channel_id=1, source_target_pairs={{0,4},{1,5},{2,6},{3,7},{4,0},{5,1},{6,2},{7,3},{8,12},{9,13},{10,... | collective-permute-start | bytes 12296 | tf_op jit(solution)/shard_map/ppermute | solution.py:54
  204.8 3.0 %collective-permute-done.25 = f32[8,128]{1,0:T(8,128)S(1)} collective-permute-done((f32[8,128]{1,0:T(8,128)S(1)}, f32[8,128]{1,0:T(8,128)S(1)}, u32[]{:S(2)}, u32[]{:S(2)}) %collective-permute-start.25) | collective-permute-done | bytes 4128 | tf_op jit(solution)/shard_map/ppermute | solution.py:54
  (114 shorter events, 52.9 us)
Async XLA Ops:
  2.5 11.1 %collective-permute-start.9 = (bf16[64,2048]{1,0:T(8,128)(2,1)S(1)}, bf16[64,2048]{1,0:T(8,128)(2,1)S(1)}, u32[]{:S(2)}, u32[]{:S(2)}) collective-permute-start(bf16[64,2048]{1,0:T(8,128)(2,1)S(1)} %constant_dynamic-update-slice_fusion.4), channel_id=1, source_target_pairs={{0,32},{1,39},{2,34},{3,33},{4,36},{5,35},{6,38},{7,37},{8,40},{9,... | collective-permute-start | bytes 786440 | tf_op jit(solution)/shard_map/ppermute | solution.py:54
  7.9 8.7 %collective-permute-start.10 = (bf16[64,2048]{1,0:T(8,128)(2,1)S(1)}, bf16[64,2048]{1,0:T(8,128)(2,1)S(1)}, u32[]{:S(2)}, u32[]{:S(2)}) collective-permute-start(bf16[64,2048]{1,0:T(8,128)(2,1)S(1)} %constant_dynamic-update-slice_fusion.4), channel_id=1, source_target_pairs={{0,38},{1,33},{2,32},{3,35},{4,34},{5,37},{6,36},{7,39},{8,46},{9,... | collective-permute-start | bytes 786440 | tf_op jit(solution)/shard_map/ppermute | solution.py:54
  14.0 30.4 %collective-permute-start.3 = (bf16[128,2048]{1,0:T(8,128)(2,1)S(1)}, bf16[128,2048]{1,0:T(8,128)(2,1)S(1)}, u32[]{:S(2)}, u32[]{:S(2)}) collective-permute-start(bf16[128,2048]{1,0:T(8,128)(2,1)S(1)} %pad_maximum_fusion.1.refs_3_), channel_id=1, source_target_pairs={{0,64},{1,9},{2,66},{3,11},{4,68},{5,13},{6,70},{7,15},{8,72},{9,1... | collective-permute-start | bytes 1572872 | tf_op jit(solution)/shard_map/ppermute | solution.py:54
  15.6 30.1 %collective-permute-start.4 = (bf16[128,2048]{1,0:T(8,128)(2,1)S(1)}, bf16[128,2048]{1,0:T(8,128)(2,1)S(1)}, u32[]{:S(2)}, u32[]{:S(2)}) collective-permute-start(bf16[128,2048]{1,0:T(8,128)(2,1)S(1)} %pad_maximum_fusion.1.refs_3_), channel_id=1, source_target_pairs={{0,192},{1,25},{2,194},{3,27},{4,196},{5,29},{6,198},{7,31},{8,200... | collective-permute-start | bytes 1572872 | tf_op jit(solution)/shard_map/ppermute | solution.py:54
  16.6 11.2 %collective-permute-start.2 = (bf16[64,2048]{1,0:T(8,128)(2,1)S(1)}, bf16[64,2048]{1,0:T(8,128)(2,1)S(1)}, u32[]{:S(2)}, u32[]{:S(2)}) collective-permute-start(bf16[64,2048]{1,0:T(8,128)(2,1)S(1)} %collective-permute-done), channel_id=1, source_target_pairs={{0,8},{1,65},{2,10},{3,67},{4,12},{5,69},{6,14},{7,71},{8,16},{9,7... | collective-permute-start | bytes 786440 | tf_op jit(solution)/shard_map/ppermute | solution.py:54
  22.0 37.4 %collective-permute-start.16 = (bf16[256,2048]{1,0:T(8,128)(2,1)S(1)}, bf16[256,2048]{1,0:T(8,128)(2,1)}, u32[]{:S(2)}, u32[]{:S(2)}) collective-permute-start(bf16[256,2048]{1,0:T(8,128)(2,1)S(1)} %pad_maximum_fusion.refs_11_), channel_id=1, source_target_pairs={{0,1},{1,0},{2,3},{3,2},{4,5},{5,4},{6,7},{7,6},{8,9},{9,8},{10,11... | collective-permute-start | bytes 3145736 | tf_op jit(solution)/shard_map/ppermute | solution.py:54
  25.8 10.3 %collective-permute-start.13 = (bf16[64,2048]{1,0:T(8,128)(2,1)S(1)}, bf16[64,2048]{1,0:T(8,128)(2,1)S(1)}, u32[]{:S(2)}, u32[]{:S(2)}) collective-permute-start(bf16[64,2048]{1,0:T(8,128)(2,1)S(1)} %collective-permute-done.11), channel_id=1, source_target_pairs={{0,32},{1,39},{2,34},{3,33},{4,36},{5,35},{6,38},{7,37},{8,40},{9,... | collective-permute-start | bytes 786440 | tf_op jit(solution)/shard_map/ppermute | solution.py:54
  27.8 11.9 %collective-permute-start.14 = (bf16[64,2048]{1,0:T(8,128)(2,1)S(1)}, bf16[64,2048]{1,0:T(8,128)(2,1)S(1)}, u32[]{:S(2)}, u32[]{:S(2)}) collective-permute-start(bf16[64,2048]{1,0:T(8,128)(2,1)S(1)} %collective-permute-done.12), channel_id=1, source_target_pairs={{0,38},{1,33},{2,32},{3,35},{4,34},{5,37},{6,36},{7,39},{8,46},{9,... | collective-permute-start | bytes 786440 | tf_op jit(solution)/shard_map/ppermute | solution.py:54
  39.6 9.3 %collective-permute-start.6 = (bf16[128,2048]{1,0:T(8,128)(2,1)S(1)}, bf16[128,2048]{1,0:T(8,128)(2,1)}, u32[]{:S(2)}, u32[]{:S(2)}) collective-permute-start(bf16[128,2048]{1,0:T(8,128)(2,1)S(1)} %constant_dynamic-update-slice_fusion.2.refs_4_), channel_id=1, source_target_pairs={{0,192},{1,25},{2,194},{3,27},{4,196},{5,29},{6,198},{7,31},{8,200... | collective-permute-start | bytes 1572872 | tf_op jit(solution)/shard_map/ppermute | solution.py:54
  44.4 15.0 %collective-permute-start.17 = (bf16[256,2048]{1,0:T(8,128)(2,1)}, bf16[256,2048]{1,0:T(8,128)(2,1)}, u32[]{:S(2)}, u32[]{:S(2)}) collective-permute-start(bf16[256,2048]{1,0:T(8,128)(2,1)} %constant_dynamic-update-slice_fusion.6.refs_12_), channel_id=1, source_target_pairs={{0,1},{1,0},{2,3},{3,2},{4,5},{5,4},{6,7},{7,6},{8,9},{9,8},{10,11... | collective-permute-start | bytes 3145736 | tf_op jit(solution)/shard_map/ppermute | solution.py:54
  44.4 9.4 %collective-permute-start.5 = (bf16[128,2048]{1,0:T(8,128)(2,1)S(1)}, bf16[128,2048]{1,0:T(8,128)(2,1)}, u32[]{:S(2)}, u32[]{:S(2)}) collective-permute-start(bf16[128,2048]{1,0:T(8,128)(2,1)S(1)} %constant_dynamic-update-slice_fusion.2.refs_4_), channel_id=1, source_target_pairs={{0,64},{1,9},{2,66},{3,11},{4,68},{5,13},{6,70},{7,15},{8,72},{9,1... | collective-permute-start | bytes 1572872 | tf_op jit(solution)/shard_map/ppermute | solution.py:54
  45.8 13.6 %collective-permute-start.7 = (bf16[128,2048]{1,0:T(8,128)(2,1)S(1)}, bf16[128,2048]{1,0:T(8,128)(2,1)}, u32[]{:S(2)}, u32[]{:S(2)}) collective-permute-start(bf16[128,2048]{1,0:T(8,128)(2,1)S(1)} %collective-permute-done.3.refs_5_), channel_id=1, source_target_pairs={{0,64},{1,9},{2,66},{3,11},{4,68},{5,13},{6,70},{7,15},{8,72},{9,1... | collective-permute-start | bytes 1572872 | tf_op jit(solution)/shard_map/ppermute | solution.py:54
  48.9 10.4 %collective-permute-start.8 = (bf16[128,2048]{1,0:T(8,128)(2,1)}, bf16[128,2048]{1,0:T(8,128)(2,1)}, u32[]{:S(2)}, u32[]{:S(2)}) collective-permute-start(bf16[128,2048]{1,0:T(8,128)(2,1)} %collective-permute-done.6.refs_8_), channel_id=1, source_target_pairs={{0,192},{1,25},{2,194},{3,27},{4,196},{5,29},{6,198},{7,31},{8,200... | collective-permute-start | bytes 1572872 | tf_op jit(solution)/shard_map/ppermute | solution.py:54
  103.8 23.4 %all-to-all-start = ((f32[16,8,1024]{2,1,0:T(8,128)}), f32[16,8,1024]{2,1,0:T(8,128)S(1)}, u32[]{:S(2)}, u32[]{:S(2)}) async-start(f32[16,8,1024]{2,1,0:T(8,128)} %broadcast_in_dim.10), calls=%async_computation | async-start | bytes 1048576 | tf_op jit(solution)/shard_map/all_to_all | solution.py:300
  148.2 13.8 %collective-permute-start.27 = (f16[64,1024]{1,0:T(8,128)(2,1)S(1)}, f16[64,1024]{1,0:T(8,128)(2,1)S(1)}, u32[]{:S(2)}, u32[]{:S(2)}) collective-permute-start(f16[64,1024]{1,0:T(8,128)(2,1)S(1)} %get-tuple-element.32), channel_id=1, source_target_pairs={{0,38},{1,33},{2,32},{3,35},{4,34},{5,37},{6,36},{7,39},{8,46},{9,... | collective-permute-start | bytes 393224 | tf_op jit(solution)/shard_map/ppermute | solution.py:54
  152.3 59.8 %all-to-all-start.2 = ((f16[16,64,1024]{2,1,0:T(8,128)(2,1)}), f16[16,64,1024]{2,1,0:T(8,128)(2,1)S(1)}, u32[]{:S(2)}, u32[]{:S(2)}) async-start(f16[16,64,1024]{2,1,0:T(8,128)(2,1)} %bitcast.125), calls=%async_computation.2 | async-start | bytes 4194304 | tf_op jit(solution)/shard_map/all_to_all | solution.py:393
  160.5 26.8 %collective-permute-start.18 = (f32[8,128]{1,0:T(8,128)S(1)}, f32[8,128]{1,0:T(8,128)S(1)}, u32[]{:S(2)}, u32[]{:S(2)}) collective-permute-start(f32[8,128]{1,0:T(8,128)S(1)} %broadcast_in_dim.11), channel_id=1, source_target_pairs={{0,8},{1,9},{2,10},{3,11},{4,12},{5,13},{6,14},{7,15},{8,0},{9,1},... | collective-permute-start | bytes 12296 | tf_op jit(solution)/shard_map/ppermute | solution.py:54
  164.9 26.4 %collective-permute-start.23 = (f32[8,128]{1,0:T(8,128)S(1)}, f32[8,128]{1,0:T(8,128)S(1)}, u32[]{:S(2)}, u32[]{:S(2)}) collective-permute-start(f32[8,128]{1,0:T(8,128)S(1)} %broadcast_add_fusion), channel_id=1, source_target_pairs={{0,32},{1,33},{2,34},{3,35},{4,36},{5,37},{6,38},{7,39},{8,40},{9,... | collective-permute-start | bytes 12296 | tf_op jit(solution)/shard_map/ppermute | solution.py:54
  164.9 25.0 %collective-permute-start.31 = (f16[64,1024]{1,0:T(8,128)(2,1)S(1)}, f16[64,1024]{1,0:T(8,128)(2,1)S(1)}, u32[]{:S(2)}, u32[]{:S(2)}) collective-permute-start(f16[64,1024]{1,0:T(8,128)(2,1)S(1)} %get-tuple-element.33), channel_id=1, source_target_pairs={{0,32},{1,39},{2,34},{3,33},{4,36},{5,35},{6,38},{7,37},{8,40},{9,... | collective-permute-start | bytes 393224 | tf_op jit(solution)/shard_map/ppermute | solution.py:54
  168.6 21.3 %collective-permute-start.29 = (f16[64,1024]{1,0:T(8,128)(2,1)S(1)}, f16[64,1024]{1,0:T(8,128)(2,1)S(1)}, u32[]{:S(2)}, u32[]{:S(2)}) collective-permute-start(f16[64,1024]{1,0:T(8,128)(2,1)S(1)} %fusion.30), channel_id=1, source_target_pairs={{0,38},{1,33},{2,32},{3,35},{4,34},{5,37},{6,36},{7,39},{8,46},{9,... | collective-permute-start | bytes 393224 | tf_op jit(solution)/shard_map/ppermute | solution.py:54
  188.0 9.0 %collective-permute-start.19 = (f32[8,128]{1,0:T(8,128)S(1)}, f32[8,128]{1,0:T(8,128)S(1)}, u32[]{:S(2)}, u32[]{:S(2)}) collective-permute-start(f32[8,128]{1,0:T(8,128)S(1)} %broadcast_add_fusion.1), channel_id=1, source_target_pairs={{0,16},{1,17},{2,18},{3,19},{4,20},{5,21},{6,22},{7,23},{8,24},{9,... | collective-permute-start | bytes 12296 | tf_op jit(solution)/shard_map/ppermute | solution.py:54
  191.3 8.9 %collective-permute-start.24 = (f32[8,128]{1,0:T(8,128)S(1)}, f32[8,128]{1,0:T(8,128)S(1)}, u32[]{:S(2)}, u32[]{:S(2)}) collective-permute-start(f32[8,128]{1,0:T(8,128)S(1)} %fusion.71), channel_id=1, source_target_pairs={{0,2},{1,3},{2,0},{3,1},{4,6},{5,7},{6,4},{7,5},{8,10},{9,11},{10,... | collective-permute-start | bytes 12296 | tf_op jit(solution)/shard_map/ppermute | solution.py:54
  192.7 18.7 %collective-permute-start.30 = (f16[64,1024]{1,0:T(8,128)(2,1)}, f16[64,1024]{1,0:T(8,128)(2,1)S(1)}, u32[]{:S(2)}, u32[]{:S(2)}) collective-permute-start(f16[64,1024]{1,0:T(8,128)(2,1)} %get-tuple-element.30), channel_id=1, source_target_pairs={{0,38},{1,33},{2,32},{3,35},{4,34},{5,37},{6,36},{7,39},{8,46},{9,... | collective-permute-start | bytes 393224 | tf_op jit(solution)/shard_map/ppermute | solution.py:54
  196.9 14.5 %collective-permute-start.33 = (f16[64,1024]{1,0:T(8,128)(2,1)S(1)}, f16[64,1024]{1,0:T(8,128)(2,1)S(1)}, u32[]{:S(2)}, u32[]{:S(2)}) collective-permute-start(f16[64,1024]{1,0:T(8,128)(2,1)S(1)} %fusion.28), channel_id=1, source_target_pairs={{0,32},{1,39},{2,34},{3,33},{4,36},{5,35},{6,38},{7,37},{8,40},{9,... | collective-permute-start | bytes 393224 | tf_op jit(solution)/shard_map/ppermute | solution.py:54
  (18 other events, 141.2 us)

commit v2 on v1

v2 whole, which is shorter than its diff:
```python
import functools
import itertools
import math

import jax
import jax.numpy as jnp
from jax import lax
from jax.experimental import pallas as pl
from jax.experimental.pallas import tpu as pltpu
from jax.sharding import Mesh
from jax.sharding import PartitionSpec as P

NAMES = ("y", "zl", "x", "zh", "c")
SIZES = (4, 2, 4, 4, 2)
ROW_COL = ("y", "zl", "x", "zh", "c")
COL_ROW = ("x", "zh", "c", "y", "zl")
TEXT_GROUP = ("y", "x")
IMAGE_GROUP = ("zl", "zh", "c")

LOG2E = math.log2(math.e)
LN2 = math.log(2.0)
SCALE = 100.0
BLOCK = 64
WIDTH = 1024
SIDE = 1024
STRIP = 128
CHUNK = 256
GROUP = 16
LOGITS_VMEM = 30 * 1024 * 1024
GRADIENT_VMEM = 20 * 1024 * 1024


def places():
    return list(itertools.product(*(range(n) for n in SIZES)))


def index_of(place):
    at = 0
    for value, size in zip(place, SIZES):
        at = at * size + value % size
    return at


def shifted(place, axis, by):
    y, zl, x, zh, c = place
    if axis == "z":
        z = (zh * 2 + zl + by) % 8
        return (y, z % 2, x, z // 2, c)
    if axis == "x":
        return (y, zl, (x + by) % 4, zh, c)
    if axis == "y":
        return ((y + by) % 4, zl, x, zh, c)
    return (y, zl, x, zh, (c + by) % 2)


def moved(value, to):
    pairs = [(index_of(p), index_of(to(p))) for p in places()]
    return lax.ppermute(value, NAMES, pairs)


def along_u(by):
    return lambda p: shifted(p, "x" if p[4] == 0 else "y", by)


def along_v(by):
    return lambda p: shifted(p, "y" if p[4] == 0 else "x", by)


def along_z(by):
    return lambda p: shifted(p, "z", by if p[4] == 0 else -by)


def other_core(p):
    return shifted(p, "c", 1)


def gathered_text(own):
    back = moved(own, along_u(1))
    ahead = moved(own, along_u(-1))
    far = moved(back, along_u(1))
    first = jnp.concatenate([own, back], axis=0)
    second = jnp.concatenate([ahead, far], axis=0)
    first_back = moved(first, along_v(1))
    first_ahead = moved(first, along_v(-1))
    second_back = moved(second, along_v(1))
    second_ahead = moved(second, along_v(-1))
    first_far = moved(first_back, along_v(1))
    second_far = moved(second_ahead, along_v(-1))
    pieces = [
        (first, ((0, 0), (-1, 0))),
        (second, ((1, 0), (2, 0))),
        (first_back, ((0, -1), (-1, -1))),
        (first_ahead, ((0, 1), (-1, 1))),
        (second_back, ((1, -1), (2, -1))),
        (second_ahead, ((1, 1), (2, 1))),
        (first_far, ((0, 2), (-1, 2))),
        (second_far, ((1, 2), (2, 2))),
    ]
    return pieces


def gathered_images(own):
    backs, aheads = [own], [own]
    for _ in range(3):
        backs.append(moved(backs[-1], along_z(1)))
        aheads.append(moved(aheads[-1], along_z(-1)))
    far = moved(backs[3], along_z(1))
    near = jnp.concatenate([own, backs[1], aheads[1], backs[2]], axis=0)
    rest = jnp.concatenate([aheads[2], backs[3], aheads[3], far], axis=0)
    near_other = moved(near, other_core)
    rest_other = moved(rest, other_core)
    steps_near, steps_rest = (0, -1, 1, -2), (2, -3, 3, 4)
    return [
        (near, [(0, k) for k in steps_near]),
        (rest, [(0, k) for k in steps_rest]),
        (near_other, [(1, k) for k in steps_near]),
        (rest_other, [(1, k) for k in steps_rest]),
    ]


def logits_kernel(counts, *refs):
    n_text, n_image = counts
    place_ref = refs[0]
    text_refs = refs[1 : 1 + n_text]
    image_refs = refs[1 + n_text : 1 + n_text + n_image]
    (s_ref, t_ref, text_out, image_out, row_ref, col_ref) = refs[
        1 + n_text + n_image : 7 + n_text + n_image
    ]
    (text_frozen, image_frozen, s_high, s_sum, t_high, t_sum, sems) = refs[7 + n_text + n_image :]
    copies = []
    k = 0
    for group, out, frozen in (
        (text_refs, text_out, text_frozen),
        (image_refs, image_out, image_frozen),
    ):
        for ref in group:
            for b in range(ref.shape[0] // BLOCK):
                at = pl.multiple_of(place_ref[k] * BLOCK, BLOCK)
                for half, target in ((0, out), (1, frozen)):
                    copies.append(
                        pltpu.make_async_copy(
                            ref.at[pl.ds(b * BLOCK, BLOCK), pl.ds(half * WIDTH, WIDTH)],
                            target.at[pl.ds(at, BLOCK), :],
                            sems.at[2 * k + half],
                        )
                    )
                k += 1
    for copy in copies:
        copy.start()
    for copy in copies:
        copy.wait()

    @pl.loop(0, SIDE // CHUNK)
    def _(j):
        cols = pl.ds(pl.multiple_of(j * CHUNK, CHUNK), CHUNK)
        for which, left, right, out in (
            (0, image_out, text_out, s_ref),
            (1, image_frozen, text_frozen, t_ref),
        ):
            tile = (SCALE * LOG2E) * lax.dot_general(
                left[...],
                right[cols, :],
                (((1,), (1,)), ((), ())),
                preferred_element_type=jnp.float32,
            )
            out[:, cols] = tile
            tile = tile.reshape(SIDE // 8, 8, CHUNK)
            high = jnp.max(tile, axis=0)
            total = jnp.sum(jnp.exp2(tile - high), axis=0)
            top = jnp.max(high, axis=0, keepdims=True)
            total = jnp.sum(total * jnp.exp2(high - top), axis=0, keepdims=True)
            lse = top + jnp.log2(total)
            for n in range(GROUP):
                col_ref[n, which : which + 1, cols] = lse

    @pl.loop(0, SIDE // 64)
    def _(i):
        for g in range(8):
            rows = pl.ds(pl.multiple_of(i * 64 + g * 8, 8), 8)
            for ref, high_ref, sum_ref in ((s_ref, s_high, s_sum), (t_ref, t_high, t_sum)):
                tiles = [ref[rows, pl.ds(k * 128, 128)] for k in range(SIDE // 128)]
                high = functools.reduce(jnp.maximum, tiles)
                high_ref[rows, :] = high
                sum_ref[rows, :] = functools.reduce(jnp.add, [jnp.exp2(v - high) for v in tiles])

    @pl.loop(0, SIDE // 128)
    def _(i):
        rows = pl.ds(pl.multiple_of(i * 128, 128), 128)
        for which, high_ref, sum_ref in ((0, s_high, s_sum), (1, t_high, t_sum)):
            high = jnp.transpose(high_ref[rows, :])
            total = jnp.transpose(sum_ref[rows, :])
            top = jnp.max(high, axis=0, keepdims=True)
            total = jnp.sum(total * jnp.exp2(high - top), axis=0, keepdims=True)
            lse = top + jnp.log2(total)
            for n in range(GROUP):
                row_ref[n, which : which + 1, rows] = lse

    for slab, ref in ((text_out, row_ref), (image_out, col_ref)):
        largest = jnp.max(jnp.abs(slab[...]), axis=0, keepdims=True).astype(jnp.float32)
        largest = jnp.full((2, 128), jnp.max(largest), jnp.float32)
        for n in range(GROUP):
            ref[n, :, SIDE : SIDE + 128] = largest


def logits_and_statistics(places_in, text, images):
    f32 = jnp.float32
    anywhere = pl.BlockSpec(memory_space=pl.ANY)
    vmem = pl.BlockSpec(memory_space=pltpu.VMEM)
    smem = pl.BlockSpec(memory_space=pltpu.SMEM)

    def kernel(*refs):
        logits_kernel((len(text), len(images)), *refs)

    square = jax.ShapeDtypeStruct((SIDE, SIDE), f32)
    half = jax.ShapeDtypeStruct((SIDE, WIDTH), jnp.bfloat16)
    small = jax.ShapeDtypeStruct((GROUP, 2, SIDE + 128), f32)
    return pl.pallas_call(
        kernel,
        out_shape=(square, square, half, half, small, small),
        in_specs=[smem] + [anywhere] * (len(text) + len(images)),
        out_specs=(vmem,) * 6,
        scratch_shapes=[
            pltpu.VMEM((SIDE, WIDTH), jnp.bfloat16),
            pltpu.VMEM((SIDE, WIDTH), jnp.bfloat16),
            pltpu.VMEM((SIDE, 128), f32),
            pltpu.VMEM((SIDE, 128), f32),
            pltpu.VMEM((SIDE, 128), f32),
            pltpu.VMEM((SIDE, 128), f32),
            pltpu.SemaphoreType.DMA((64,)),
        ],
        compiler_params=pltpu.CompilerParams(vmem_limit_bytes=LOGITS_VMEM),
        cost_estimate=pl.CostEstimate(
            flops=4 * SIDE * SIDE * WIDTH, bytes_accessed=20 << 20, transcendentals=4 * SIDE * SIDE
        ),
    )(places_in, *text, *images)


def gradient_kernel(
    s_ref, t_ref, row_ref, col_ref, row_id_ref, col_id_ref, out_ref, factor_ref, part_ref, lse_ref
):
    def joined(ref, which):
        values = ref[:, which, :SIDE]
        top = jnp.max(values, axis=0, keepdims=True)
        return top + jnp.log2(jnp.sum(jnp.exp2(values - top), axis=0, keepdims=True))

    s_row_all, t_row_all = joined(row_ref, 0), joined(row_ref, 1)
    s_col_all, t_col_all = joined(col_ref, 0), joined(col_ref, 1)
    shared = (s_row_all - 0.5 * t_row_all) + (s_col_all - 0.5 * t_col_all)
    lse_ref[0:1, :] = s_row_all
    lse_ref[1:2, :] = t_row_all + 1.0
    lse_ref[2:3, :] = s_col_all
    lse_ref[3:4, :] = t_col_all + 1.0
    for k, ref in ((0, row_ref), (1, col_ref)):
        scale = 2.0 / jnp.maximum(jnp.max(ref[:, 0, SIDE : SIDE + 128]), 1e-30)
        factor_ref[k : k + 1, :] = jnp.full((1, SIDE), scale, jnp.float32)
        factor_ref[k + 2 : k + 3, :] = jnp.full((1, SIDE), SCALE, jnp.float32) / jnp.full(
            (1, SIDE), scale, jnp.float32
        )
    factor_ref[4:8, :] = jnp.zeros((4, SIDE), jnp.float32)
    size = 16

    def strip(i, total):
        base = pl.multiple_of(i * STRIP, STRIP)
        turned = jnp.transpose(lse_ref[:, pl.ds(base, STRIP)])
        for g in range(STRIP // size):
            rows = pl.ds(pl.multiple_of(base + g * size, size), size)
            s_row = jnp.broadcast_to(turned[g * size : (g + 1) * size, 0:1], (size, 128))
            t_row = jnp.broadcast_to(turned[g * size : (g + 1) * size, 1:2], (size, 128))
            row_id = jnp.broadcast_to(row_id_ref[rows, :], (size, 128))
            for k in range(SIDE // 128):
                lanes = pl.ds(k * 128, 128)
                s = s_ref[rows, lanes]
                t = t_ref[rows, lanes]
                weights = jnp.exp2(t - t_row) + jnp.exp2(t - lse_ref[3:4, lanes])
                value = (jnp.exp2(s - s_row) + jnp.exp2(s - lse_ref[2:3, lanes])) - weights
                same = row_id == col_id_ref[:, lanes]
                out_ref[rows, lanes] = jnp.where(same, value - 1.0, value).astype(jnp.bfloat16)
                total = total + (weights * (t - s) - jnp.where(same, s, 0.0))
        return total

    total = lax.fori_loop(0, SIDE // STRIP, strip, jnp.zeros((size, 128), jnp.float32))
    part = LN2 * (jnp.sum(total) + jnp.sum(shared) * (1.0 / GROUP))
    part_ref[...] = jnp.full(part_ref.shape, part, jnp.float32)


def gradient_of_logits(s, t, row, col, row_id, col_id):
    vmem = pl.BlockSpec(memory_space=pltpu.VMEM)
    f32 = jnp.float32
    return pl.pallas_call(
        gradient_kernel,
        out_shape=(
            jax.ShapeDtypeStruct((SIDE, SIDE), jnp.bfloat16),
            jax.ShapeDtypeStruct((8, SIDE), f32),
            jax.ShapeDtypeStruct((GROUP, 8, 128), f32),
        ),
        in_specs=[vmem] * 6,
        out_specs=(vmem,) * 3,
        scratch_shapes=[pltpu.VMEM((8, SIDE), f32)],
        compiler_params=pltpu.CompilerParams(vmem_limit_bytes=GRADIENT_VMEM),
        cost_estimate=pl.CostEstimate(
            flops=16 * SIDE * SIDE, bytes_accessed=10 << 20, transcendentals=4 * SIDE * SIDE
        ),
    )(s, t, row, col, row_id, col_id)


def exchanged(copies, axis):
    return lax.all_to_all(copies, axis, split_axis=0, concat_axis=0, tiled=True)


def summed_over(value, steps):
    for to in steps:
        value = value + moved(value, to)
    return value


def body(image_student, text_student, image_teacher, text_teacher):
    y, zl, x, zh, c = (lax.axis_index(n) for n in NAMES)
    z = zh * 2 + zl
    text_pieces = gathered_text(jnp.concatenate([text_student, text_teacher], axis=1))
    image_pieces = gathered_images(jnp.concatenate([image_student, image_teacher], axis=1))

    sign = 1 - 2 * c
    at = []
    for _, offsets in text_pieces:
        for du, dv in offsets:
            dx = jnp.where(c == 0, du, dv)
            dy = jnp.where(c == 0, dv, du)
            at.append(((y + dy) % 4) * 4 + (x + dx) % 4)
    for _, offsets in image_pieces:
        for swapped, step in offsets:
            core = c ^ swapped
            toward = sign if swapped == 0 else -sign
            at.append(core * 8 + (z + toward * step) % 8)
    where = jnp.stack(at).astype(jnp.int32)

    numbers = jnp.arange(SIDE, dtype=jnp.int32)
    slot, inner = numbers // BLOCK, numbers % BLOCK
    text_y, text_x = slot // 4, slot % 4
    col_id = (((text_x * 8 + zh * 2 + c) * 8) + text_y * 2 + zl) * BLOCK + inner
    image_c, image_z = slot // 8, slot % 8
    row_id = ((y * 2 + image_z % 2) * 32 + x * 8 + (image_z // 2) * 2 + image_c) * BLOCK + inner
    row_id, col_id = row_id[:, None], col_id[None, :]

    s, t, text_slab, image_slab, row_part, col_part = logits_and_statistics(
        where, [p for p, _ in text_pieces], [p for p, _ in image_pieces]
    )
    col_all = exchanged(col_part, TEXT_GROUP)
    row_all = exchanged(row_part, IMAGE_GROUP)
    gradient, factors, part = gradient_of_logits(s, t, row_all, col_all, row_id, col_id)
    text_scale, image_scale = factors[0:1], factors[1:2]
    image_factor, text_factor = factors[2:3], factors[3:4]

    value = jnp.sum(exchanged(part, TEXT_GROUP), axis=0)
    value = summed_over(
        value, [other_core] + [lambda p, k=k: flipped(p, "z", k) for k in (1, 2, 4)]
    )
    loss = value[0, 0] / (256 * BLOCK)

    half = SIDE // 2
    theirs = lax.dynamic_slice_in_dim(gradient, (1 - c) * half, half)
    mine = lax.dynamic_slice_in_dim(gradient, c * half, half)
    image_theirs = jnp.dot(theirs, text_slab, preferred_element_type=jnp.float32)
    arrived = moved((image_theirs * text_scale).astype(jnp.float16), other_core)
    text_part = (
        lax.dot_general(
            gradient, image_slab, (((0,), (0,)), ((), ())), preferred_element_type=jnp.float32
        )
        * image_scale
    ).astype(jnp.float16)
    text_blocks = lax.all_to_all(text_part.reshape(16, BLOCK, WIDTH), TEXT_GROUP, 0, 0, tiled=True)
    image_mine = (
        jnp.dot(mine, text_slab, preferred_element_type=jnp.float32) * text_scale
    ) + arrived.astype(jnp.float32)
    blocks = image_mine.astype(jnp.float16).reshape(8, BLOCK, WIDTH)

    def block(step):
        return lax.dynamic_index_in_dim(blocks, (z + sign * step) % 8, 0, keepdims=False).astype(
            jnp.float32
        )

    def narrow(v):
        return v.astype(jnp.float16)

    down = moved(narrow(block(4)), along_z(-1)).astype(jnp.float32)
    up = None
    for k in (3, 2, 1):
        first = narrow(block(-k) + down)
        second = block(k) if up is None else block(k) + up
        down = moved(first, along_z(-1)).astype(jnp.float32)
        up = moved(narrow(second), along_z(1)).astype(jnp.float32)
    image_grad = (block(0) + down + up) * image_factor
    text_grad = jnp.sum(text_blocks.astype(jnp.float32), axis=0) * text_factor
    return (loss, image_grad, text_grad)


def flipped(p, axis, bit):
    y, zl, x, zh, c = p
    if axis == "x":
        return (y, zl, x ^ bit, zh, c)
    if axis == "y":
        return (y ^ bit, zl, x, zh, c)
    z = (zh * 2 + zl) ^ bit
    return (y, z % 2, x, z // 2, c)


def solution(mesh):
    finer = Mesh(mesh.devices.reshape(SIZES), NAMES)
    placed = (P(ROW_COL, None), P(COL_ROW, None), P(ROW_COL, None), P(COL_ROW, None))
    return jax.shard_map(
        body,
        mesh=finer,
        in_specs=placed,
        out_specs=(P(), P(ROW_COL, None), P(COL_ROW, None)),
        check_vma=False,
    )
```

time: 215 us -> 195 us (0.907)
  Pallas kernels: 36.6 us -> 19.8 us
  blocking collectives: 15.1 us -> 0 us
  local copies, waits for them, and re-layouts: 9.42 us -> 18.1 us
  starting transfers between devices: 63.3 us -> 67 us
  between operations: 6.1 us -> 2.64 us
  waiting for transfers between devices: 65.7 us -> 68.6 us
    all_to_all x1 -> x0, blocking collectives: 15.1 us -> none  [sent_to_all(): return lax.all_to_all(copies, axis, split_axis=0, concat_axis=0, tiled=True)]
    pallas_call x1, Pallas kernels: 28.4 us -> 14.7 us  [logits_and_statistics(): pl.pallas_call(kernel, out_shape=(square, square, half, half, small, smal...]
    all_to_all x1 -> x3, starting transfers between devices: 7.01 us -> 18.9 us  [exchanged(): return lax.all_to_all(copies, axis, split_axis=0, concat_axis=0, tiled=True)]
    unnamed x18 -> x26, local copies, waits for them, and re-layouts: 4 us -> 14.9 us
    ppermute x34 -> x30, starting transfers between devices: 50.2 us -> 40.8 us  [moved(): return lax.ppermute(value, NAMES, pairs)]
    ppermute x34 -> x30, waiting for transfers between devices: 49.4 us -> 53.4 us  [moved(): return lax.ppermute(value, NAMES, pairs)]
    pallas_call x1, Pallas kernels: 8.22 us -> 5.06 us  [gradient_of_logits(): pl.pallas_call(gradient_kernel, out_shape=(jax.ShapeDtypeStruct((SIDE, SI...]
    all_to_all x1 -> x3, waiting for transfers between devices: 16.3 us -> 15.2 us  [exchanged(): return lax.all_to_all(copies, axis, split_axis=0, concat_axis=0, tiled=True)]
  transfers between devices with their start and end apart: 36 -> 34, of which waited for: 16 -> 21; matrix products, arithmetic and copies ran while one was open for 8% -> 9% of each run, Pallas kernels for 0% -> 0%
where the time goes in v2:
time: 195 us; the launch traced here: 194 us
  waiting for transfers between devices  68.6 us (35%)
  starting transfers between devices  67 us (34%)
  Pallas kernels  19.8 us (10%)
  local copies, waits for them, and re-layouts  18.1 us (9%)
  matrix products  10.3 us (5%)
  other arithmetic  7.53 us (4%)
  between operations  2.64 us (1%)
    ppermute x30, waiting for transfers between devices, moved(): return lax.ppermute(value, NAMES, pairs)  53.4 us
    ppermute x30, starting transfers between devices, moved(): return lax.ppermute(value, NAMES, pairs)  40.8 us
    all_to_all x3, starting transfers between devices, exchanged(): return lax.all_to_all(copies, axis, split_axis=0, concat_axis=0, tiled=True)  18.9 us
    all_to_all x3, waiting for transfers between devices, exchanged(): return lax.all_to_all(copies, axis, split_axis=0, concat_axis=0, tiled=True)  15.2 us
    unnamed x26, local copies, waits for them, and re-layouts  14.9 us
    pallas_call x1, Pallas kernels, logits_and_statistics(): pl.pallas_call(kernel, out_shape=(square, square, half, half, small, smal...  14.7 us
    all_to_all x1, starting transfers between devices, body(): lax.all_to_all(text_part.reshape(16, BLOCK, WIDTH), TEXT_GROUP, 0, 0, til...  7.27 us
    dot_general x1, matrix products, body(): lax.dot_general(gradient, image_slab, (((0,), (0,)), ((), ())), preferred...  5.48 us
  transfers between devices with their start and end apart: 34, of which 21 were waited for; matrix products, arithmetic and copies ran while one was open for 9% of the time, Pallas kernels for 0%

profile of v2, /device:TPU:8, one launch (start us, length us, event | category | flops | bytes accessed | tf_op | source)
XLA Modules:
  0.0 194.0 jit_solution(8288410793162232530)
XLA Ops:
  7.9 4.0 %collective-permute-start.10 = (bf16[64,2048]{1,0:T(8,128)(2,1)S(1)}, bf16[64,2048]{1,0:T(8,128)(2,1)S(1)}, u32[]{:S(2)}, u32[]{:S(2)}) collective-permute-start(bf16[64,2048]{1,0:T(8,128)(2,1)S(1)} %constant_dynamic-update-slice_fusion.4), channel_id=1, source_target_pairs={{0,38},{1,33},{2,32},{3,35},{4,34},{5,37},{6,36},{7,39},{8,46},{9,... | collective-permute-start | bytes 786440 | tf_op jit(solution)/shard_map/ppermute | solution.py:58
  18.2 3.7 %collective-permute-start.12 = (bf16[64,2048]{1,0:T(8,128)(2,1)S(1)}, bf16[64,2048]{1,0:T(8,128)(2,1)S(1)}, u32[]{:S(2)}, u32[]{:S(2)}) collective-permute-start(bf16[64,2048]{1,0:T(8,128)(2,1)S(1)} %collective-permute-done.10), channel_id=1, source_target_pairs={{0,38},{1,33},{2,32},{3,35},{4,34},{5,37},{6,36},{7,39},{8,46},{9,... | collective-permute-start | bytes 786440 | tf_op jit(solution)/shard_map/ppermute | solution.py:58
  22.1 3.7 %collective-permute-done.12 = bf16[64,2048]{1,0:T(8,128)(2,1)S(1)} collective-permute-done((bf16[64,2048]{1,0:T(8,128)(2,1)S(1)}, bf16[64,2048]{1,0:T(8,128)(2,1)S(1)}, u32[]{:S(2)}, u32[]{:S(2)}) %collective-permute-start.12) | collective-permute-done | bytes 262176 | tf_op jit(solution)/shard_map/ppermute | solution.py:58
  29.6 6.0 %collective-permute-done.13 = bf16[64,2048]{1,0:T(8,128)(2,1)S(1)} collective-permute-done((bf16[64,2048]{1,0:T(8,128)(2,1)S(1)}, bf16[64,2048]{1,0:T(8,128)(2,1)S(1)}, u32[]{:S(2)}, u32[]{:S(2)}) %collective-permute-start.13) | collective-permute-done | bytes 262176 | tf_op jit(solution)/shard_map/ppermute | solution.py:58
  36.4 3.2 %collective-permute-done.14 = bf16[64,2048]{1,0:T(8,128)(2,1)S(1)} collective-permute-done((bf16[64,2048]{1,0:T(8,128)(2,1)S(1)}, bf16[64,2048]{1,0:T(8,128)(2,1)S(1)}, u32[]{:S(2)}, u32[]{:S(2)}) %collective-permute-start.14) | collective-permute-done | bytes 262176 | tf_op jit(solution)/shard_map/ppermute | solution.py:58
  49.7 3.0 %collective-permute-done.5.refs_5_ = bf16[128,2048]{1,0:T(8,128)(2,1)} collective-permute-done((bf16[128,2048]{1,0:T(8,128)(2,1)S(1)}, bf16[128,2048]{1,0:T(8,128)(2,1)}, u32[]{:S(2)}, u32[]{:S(2)}) %collective-permute-start.5) | collective-permute-done | bytes 524320 | tf_op jit(solution)/shard_map/ppermute | solution.py:58
  52.7 5.6 %collective-permute-done.7.refs_7_ = bf16[128,2048]{1,0:T(8,128)(2,1)} collective-permute-done((bf16[128,2048]{1,0:T(8,128)(2,1)}, bf16[128,2048]{1,0:T(8,128)(2,1)}, u32[]{:S(2)}, u32[]{:S(2)}) %collective-permute-start.7) | collective-permute-done | bytes 524320 | tf_op jit(solution)/shard_map/ppermute | solution.py:58
  59.5 14.7 %shard_map.67 = (f32[1024,1024]{1,0:T(8,128)S(1)}, f32[1024,1024]{1,0:T(8,128)S(1)}, bf16[1024,1024]{1,0:T(8,128)(2,1)S(1)}, bf16[1024,1024]{1,0:T(8,128)(2,1)S(...) custom-call(s32[32]{0:T(128)S(1)} %stack.131.refs_0_, bf16[128,2048]{1,0:T(8,128)(2,1)S(1)} %pad_maximum_fusion.1.refs_1_, ...), custom_call_target="tpu_custom_call" | custom-call | flops 4294967296 | bytes 20971520 | tf_op jit(solution)/shard_map/pallas_call | solution.py:217
  80.9 7.2 %all-to-all-start.1 = ((f32[16,2,1152]{2,1,0:T(2,128)}), f32[16,2,1152]{2,1,0:T(2,128)S(1)}, u32[]{:S(2)}, u32[]{:S(2)}) async-start(f32[16,2,1152]{2,1,0:T(2,128)} %get-tuple-element.15), calls=%async_computation.1 | async-start | bytes 294912 | tf_op jit(solution)/shard_map/all_to_all | solution.py:307
  88.1 6.4 %all-to-all-done.1.col_ref = f32[16,2,1152]{2,1,0:T(2,128)S(1)} async-done(((f32[16,2,1152]{2,1,0:T(2,128)}), f32[16,2,1152]{2,1,0:T(2,128)S(1)}, u32[]{:S(2)}, u32[]{:S(2)}) %all-to-all-start.1) | async-done | bytes 147488 | tf_op jit(solution)/shard_map/all_to_all | solution.py:307
  94.5 6.6 %all-to-all-start = ((f32[16,2,1152]{2,1,0:T(2,128)}), f32[16,2,1152]{2,1,0:T(2,128)S(1)}, u32[]{:S(2)}, u32[]{:S(2)}) async-start(f32[16,2,1152]{2,1,0:T(2,128)} %get-tuple-element.14), calls=%async_computation | async-start | bytes 294912 | tf_op jit(solution)/shard_map/all_to_all | solution.py:307
  101.5 8.8 %all-to-all-done.row_ref = f32[16,2,1152]{2,1,0:T(2,128)S(1)} async-done(((f32[16,2,1152]{2,1,0:T(2,128)}), f32[16,2,1152]{2,1,0:T(2,128)S(1)}, u32[]{:S(2)}, u32[]{:S(2)}) %all-to-all-start) | async-done | bytes 147488 | tf_op jit(solution)/shard_map/all_to_all | solution.py:307
  114.7 5.1 %shard_map.68 = (bf16[1024,1024]{1,0:T(8,128)(2,1)S(1)}, f32[8,1024]{1,0:T(8,128)S(1)}, f32[16,8,128]{2,1,0:T(8,128)}) custom-call(f32[1024,1024]{1,0:T(8,128)S(1)} %copy-done.1, f32[1024,1024]{1,0:T(8,128)S(1)} %copy-done.3, f32[16,2,1152]{2,1,0:T(2,128)S(1)} %all-to-all-done.row_ref, f32[16,2,1152]{2,1,0:T(2,128)S(1)} %all-to-all-done.1.col_ref, ...), custom_call_target="tpu_custom_call" | custom-call | flops 16777216 | bytes 10485760 | tf_op jit(solution)/shard_map/pallas_call | solution.py:289
  122.8 5.2 %all-to-all-start.2 = ((f32[16,8,128]{2,1,0:T(8,128)}), f32[16,8,128]{2,1,0:T(8,128)S(1)}, u32[]{:S(2)}, u32[]{:S(2)}) async-start(f32[16,8,128]{2,1,0:T(8,128)} %get-tuple-element.16), calls=%async_computation.2 | async-start | bytes 131072 | tf_op jit(solution)/shard_map/all_to_all | solution.py:307
  127.9 5.5 %multiply_convert_fusion = f16[1024,1024]{1,0:T(8,128)(2,1)} fusion(bf16[1024,1024]{1,0:T(8,128)(2,1)S(1)} %get-tuple-element.17, bf16[1024,1024]{1,0:T(8,128)(2,1)} %copy-done.9, f32[1024]{0:T(1024)S(1)} %bitcast.76), kind=kOutput, calls=%fused_computation.1 | convolution fusion | flops 2149580800 | bytes 6295552 | tf_op jit(solution)/shard_map/dot_general | solution.py:365
  136.0 7.3 %all-to-all-start.3 = ((f16[16,64,1024]{2,1,0:T(8,128)(2,1)}), f16[16,64,1024]{2,1,0:T(8,128)(2,1)S(1)}, u32[]{:S(2)}, u32[]{:S(2)}) async-start(f16[16,64,1024]{2,1,0:T(8,128)(2,1)} %bitcast.71), calls=%async_computation.3 | async-start | bytes 4194304 | tf_op jit(solution)/shard_map/all_to_all | solution.py:370
  146.8 4.5 %collective-permute-done.23 = f16[64,1024]{1,0:T(8,128)(2,1)S(1)} collective-permute-done((f16[64,1024]{1,0:T(8,128)(2,1)S(1)}, f16[64,1024]{1,0:T(8,128)(2,1)S(1)}, u32[]{:S(2)}, u32[]{:S(2)}) %collective-permute-start.23) | collective-permute-done | bytes 131104 | tf_op jit(solution)/shard_map/ppermute | solution.py:58
  153.4 3.5 %collective-permute-done.24 = f16[64,1024]{1,0:T(8,128)(2,1)S(1)} collective-permute-done((f16[64,1024]{1,0:T(8,128)(2,1)S(1)}, f16[64,1024]{1,0:T(8,128)(2,1)S(1)}, u32[]{:S(2)}, u32[]{:S(2)}) %collective-permute-start.24) | collective-permute-done | bytes 131104 | tf_op jit(solution)/shard_map/ppermute | solution.py:58
  157.0 3.8 %collective-permute-start.25 = (f16[64,1024]{1,0:T(8,128)(2,1)S(1)}, f16[64,1024]{1,0:T(8,128)(2,1)S(1)}, u32[]{:S(2)}, u32[]{:S(2)}) collective-permute-start(f16[64,1024]{1,0:T(8,128)(2,1)S(1)} %fusion.30), channel_id=1, source_target_pairs={{0,38},{1,33},{2,32},{3,35},{4,34},{5,37},{6,36},{7,39},{8,46},{9,... | collective-permute-start | bytes 393224 | tf_op jit(solution)/shard_map/ppermute | solution.py:58
  164.9 3.7 %collective-permute-start.26 = (f16[64,1024]{1,0:T(8,128)(2,1)}, f16[64,1024]{1,0:T(8,128)(2,1)}, u32[]{:S(2)}, u32[]{:S(2)}) collective-permute-start(f16[64,1024]{1,0:T(8,128)(2,1)} %get-tuple-element.21), channel_id=1, source_target_pairs={{0,38},{1,33},{2,32},{3,35},{4,34},{5,37},{6,36},{7,39},{8,46},{9,... | collective-permute-start | bytes 393224 | tf_op jit(solution)/shard_map/ppermute | solution.py:58
  168.6 3.2 %collective-permute-done.28 = f16[64,1024]{1,0:T(8,128)(2,1)S(1)} collective-permute-done((f16[64,1024]{1,0:T(8,128)(2,1)}, f16[64,1024]{1,0:T(8,128)(2,1)S(1)}, u32[]{:S(2)}, u32[]{:S(2)}) %collective-permute-start.28) | collective-permute-done | bytes 131104 | tf_op jit(solution)/shard_map/ppermute | solution.py:58
  173.2 3.6 %collective-permute-done.19 = f32[8,128]{1,0:T(8,128)S(1)} collective-permute-done((f32[8,128]{1,0:T(8,128)S(1)}, f32[8,128]{1,0:T(8,128)S(1)}, u32[]{:S(2)}, u32[]{:S(2)}) %collective-permute-start.19) | collective-permute-done | bytes 4128 | tf_op jit(solution)/shard_map/ppermute | solution.py:58
  178.2 3.1 %collective-permute-done.20 = f32[8,128]{1,0:T(8,128)S(1)} collective-permute-done((f32[8,128]{1,0:T(8,128)S(1)}, f32[8,128]{1,0:T(8,128)S(1)}, u32[]{:S(2)}, u32[]{:S(2)}) %collective-permute-start.20) | collective-permute-done | bytes 4128 | tf_op jit(solution)/shard_map/ppermute | solution.py:58
  184.2 4.6 %collective-permute-done.21 = f32[8,128]{1,0:T(8,128)S(1)} collective-permute-done((f32[8,128]{1,0:T(8,128)S(1)}, f32[8,128]{1,0:T(8,128)S(1)}, u32[]{:S(2)}, u32[]{:S(2)}) %collective-permute-start.21) | collective-permute-done | bytes 4128 | tf_op jit(solution)/shard_map/ppermute | solution.py:58
  (100 shorter events, 65.7 us)
Async XLA Ops:
  2.5 11.1 %collective-permute-start.9 = (bf16[64,2048]{1,0:T(8,128)(2,1)S(1)}, bf16[64,2048]{1,0:T(8,128)(2,1)S(1)}, u32[]{:S(2)}, u32[]{:S(2)}) collective-permute-start(bf16[64,2048]{1,0:T(8,128)(2,1)S(1)} %constant_dynamic-update-slice_fusion.4), channel_id=1, source_target_pairs={{0,32},{1,39},{2,34},{3,33},{4,36},{5,35},{6,38},{7,37},{8,40},{9,... | collective-permute-start | bytes 786440 | tf_op jit(solution)/shard_map/ppermute | solution.py:58
  6.3 7.7 %collective-permute-start = (bf16[64,2048]{1,0:T(8,128)(2,1)S(1)}, bf16[64,2048]{1,0:T(8,128)(2,1)S(1)}, u32[]{:S(2)}, u32[]{:S(2)}) collective-permute-start(bf16[64,2048]{1,0:T(8,128)(2,1)S(1)} %constant_dynamic-update-slice_fusion), channel_id=1, source_target_pairs={{0,8},{1,65},{2,10},{3,67},{4,12},{5,69},{6,14},{7,71},{8,16},{9,7... | collective-permute-start | bytes 786440 | tf_op jit(solution)/shard_map/ppermute | solution.py:58
  7.9 8.7 %collective-permute-start.10 = (bf16[64,2048]{1,0:T(8,128)(2,1)S(1)}, bf16[64,2048]{1,0:T(8,128)(2,1)S(1)}, u32[]{:S(2)}, u32[]{:S(2)}) collective-permute-start(bf16[64,2048]{1,0:T(8,128)(2,1)S(1)} %constant_dynamic-update-slice_fusion.4), channel_id=1, source_target_pairs={{0,38},{1,33},{2,32},{3,35},{4,34},{5,37},{6,36},{7,39},{8,46},{9,... | collective-permute-start | bytes 786440 | tf_op jit(solution)/shard_map/ppermute | solution.py:58
  13.6 8.3 %collective-permute-start.11 = (bf16[64,2048]{1,0:T(8,128)(2,1)S(1)}, bf16[64,2048]{1,0:T(8,128)(2,1)S(1)}, u32[]{:S(2)}, u32[]{:S(2)}) collective-permute-start(bf16[64,2048]{1,0:T(8,128)(2,1)S(1)} %collective-permute-done.9), channel_id=1, source_target_pairs={{0,32},{1,39},{2,34},{3,33},{4,36},{5,35},{6,38},{7,37},{8,40},{9,... | collective-permute-start | bytes 786440 | tf_op jit(solution)/shard_map/ppermute | solution.py:58
  14.0 29.3 %collective-permute-start.3 = (bf16[128,2048]{1,0:T(8,128)(2,1)S(1)}, bf16[128,2048]{1,0:T(8,128)(2,1)}, u32[]{:S(2)}, u32[]{:S(2)}) collective-permute-start(bf16[128,2048]{1,0:T(8,128)(2,1)S(1)} %pad_maximum_fusion.1.refs_1_), channel_id=1, source_target_pairs={{0,64},{1,9},{2,66},{3,11},{4,68},{5,13},{6,70},{7,15},{8,72},{9,1... | collective-permute-start | bytes 1572872 | tf_op jit(solution)/shard_map/ppermute | solution.py:58
  15.6 29.3 %collective-permute-start.4 = (bf16[128,2048]{1,0:T(8,128)(2,1)S(1)}, bf16[128,2048]{1,0:T(8,128)(2,1)S(1)}, u32[]{:S(2)}, u32[]{:S(2)}) collective-permute-start(bf16[128,2048]{1,0:T(8,128)(2,1)S(1)} %pad_maximum_fusion.1.refs_1_), channel_id=1, source_target_pairs={{0,192},{1,25},{2,194},{3,27},{4,196},{5,29},{6,198},{7,31},{8,200... | collective-permute-start | bytes 1572872 | tf_op jit(solution)/shard_map/ppermute | solution.py:58
  16.6 10.5 %collective-permute-start.2 = (bf16[64,2048]{1,0:T(8,128)(2,1)S(1)}, bf16[64,2048]{1,0:T(8,128)(2,1)S(1)}, u32[]{:S(2)}, u32[]{:S(2)}) collective-permute-start(bf16[64,2048]{1,0:T(8,128)(2,1)S(1)} %collective-permute-done), channel_id=1, source_target_pairs={{0,8},{1,65},{2,10},{3,67},{4,12},{5,69},{6,14},{7,71},{8,16},{9,7... | collective-permute-start | bytes 786440 | tf_op jit(solution)/shard_map/ppermute | solution.py:58
  22.0 36.3 %collective-permute-start.16 = (bf16[256,2048]{1,0:T(8,128)(2,1)S(1)}, bf16[256,2048]{1,0:T(8,128)(2,1)}, u32[]{:S(2)}, u32[]{:S(2)}) collective-permute-start(bf16[256,2048]{1,0:T(8,128)(2,1)S(1)} %pad_maximum_fusion.refs_9_), channel_id=1, source_target_pairs={{0,1},{1,0},{2,3},{3,2},{4,5},{5,4},{6,7},{7,6},{8,9},{9,8},{10,11... | collective-permute-start | bytes 3145736 | tf_op jit(solution)/shard_map/ppermute | solution.py:58
  25.8 9.9 %collective-permute-start.13 = (bf16[64,2048]{1,0:T(8,128)(2,1)S(1)}, bf16[64,2048]{1,0:T(8,128)(2,1)S(1)}, u32[]{:S(2)}, u32[]{:S(2)}) collective-permute-start(bf16[64,2048]{1,0:T(8,128)(2,1)S(1)} %collective-permute-done.11), channel_id=1, source_target_pairs={{0,32},{1,39},{2,34},{3,33},{4,36},{5,35},{6,38},{7,37},{8,40},{9,... | collective-permute-start | bytes 786440 | tf_op jit(solution)/shard_map/ppermute | solution.py:58
  27.1 12.6 %collective-permute-start.14 = (bf16[64,2048]{1,0:T(8,128)(2,1)S(1)}, bf16[64,2048]{1,0:T(8,128)(2,1)S(1)}, u32[]{:S(2)}, u32[]{:S(2)}) collective-permute-start(bf16[64,2048]{1,0:T(8,128)(2,1)S(1)} %collective-permute-done.12), channel_id=1, source_target_pairs={{0,38},{1,33},{2,32},{3,35},{4,34},{5,37},{6,36},{7,39},{8,46},{9,... | collective-permute-start | bytes 786440 | tf_op jit(solution)/shard_map/ppermute | solution.py:58
  35.6 7.6 %collective-permute-start.15 = (bf16[64,2048]{1,0:T(8,128)(2,1)S(1)}, bf16[64,2048]{1,0:T(8,128)(2,1)S(1)}, u32[]{:S(2)}, u32[]{:S(2)}) collective-permute-start(bf16[64,2048]{1,0:T(8,128)(2,1)S(1)} %collective-permute-done.13), channel_id=1, source_target_pairs={{0,32},{1,39},{2,34},{3,33},{4,36},{5,35},{6,38},{7,37},{8,40},{9,... | collective-permute-start | bytes 786440 | tf_op jit(solution)/shard_map/ppermute | solution.py:58
  39.6 9.3 %collective-permute-start.6 = (bf16[128,2048]{1,0:T(8,128)(2,1)S(1)}, bf16[128,2048]{1,0:T(8,128)(2,1)}, u32[]{:S(2)}, u32[]{:S(2)}) collective-permute-start(bf16[128,2048]{1,0:T(8,128)(2,1)S(1)} %constant_dynamic-update-slice_fusion.2.refs_2_), channel_id=1, source_target_pairs={{0,192},{1,25},{2,194},{3,27},{4,196},{5,29},{6,198},{7,31},{8,200... | collective-permute-start | bytes 1572872 | tf_op jit(solution)/shard_map/ppermute | solution.py:58
  43.2 15.2 %collective-permute-start.17 = (bf16[256,2048]{1,0:T(8,128)(2,1)S(1)}, bf16[256,2048]{1,0:T(8,128)(2,1)}, u32[]{:S(2)}, u32[]{:S(2)}) collective-permute-start(bf16[256,2048]{1,0:T(8,128)(2,1)S(1)} %constant_dynamic-update-slice_fusion.6.refs_10_), channel_id=1, source_target_pairs={{0,1},{1,0},{2,3},{3,2},{4,5},{5,4},{6,7},{7,6},{8,9},{9,8},{10,11... | collective-permute-start | bytes 3145736 | tf_op jit(solution)/shard_map/ppermute | solution.py:58
  43.3 9.4 %collective-permute-start.5 = (bf16[128,2048]{1,0:T(8,128)(2,1)S(1)}, bf16[128,2048]{1,0:T(8,128)(2,1)}, u32[]{:S(2)}, u32[]{:S(2)}) collective-permute-start(bf16[128,2048]{1,0:T(8,128)(2,1)S(1)} %constant_dynamic-update-slice_fusion.2.refs_2_), channel_id=1, source_target_pairs={{0,64},{1,9},{2,66},{3,11},{4,68},{5,13},{6,70},{7,15},{8,72},{9,1... | collective-permute-start | bytes 1572872 | tf_op jit(solution)/shard_map/ppermute | solution.py:58
  45.8 12.5 %collective-permute-start.7 = (bf16[128,2048]{1,0:T(8,128)(2,1)}, bf16[128,2048]{1,0:T(8,128)(2,1)}, u32[]{:S(2)}, u32[]{:S(2)}) collective-permute-start(bf16[128,2048]{1,0:T(8,128)(2,1)} %collective-permute-done.3.refs_3_), channel_id=1, source_target_pairs={{0,64},{1,9},{2,66},{3,11},{4,68},{5,13},{6,70},{7,15},{8,72},{9,1... | collective-permute-start | bytes 1572872 | tf_op jit(solution)/shard_map/ppermute | solution.py:58
  48.9 9.5 %collective-permute-start.8 = (bf16[128,2048]{1,0:T(8,128)(2,1)}, bf16[128,2048]{1,0:T(8,128)(2,1)}, u32[]{:S(2)}, u32[]{:S(2)}) collective-permute-start(bf16[128,2048]{1,0:T(8,128)(2,1)} %collective-permute-done.6.refs_6_), channel_id=1, source_target_pairs={{0,192},{1,25},{2,194},{3,27},{4,196},{5,29},{6,198},{7,31},{8,200... | collective-permute-start | bytes 1572872 | tf_op jit(solution)/shard_map/ppermute | solution.py:58
  80.9 13.6 %all-to-all-start.1 = ((f32[16,2,1152]{2,1,0:T(2,128)}), f32[16,2,1152]{2,1,0:T(2,128)S(1)}, u32[]{:S(2)}, u32[]{:S(2)}) async-start(f32[16,2,1152]{2,1,0:T(2,128)} %get-tuple-element.15), calls=%async_computation.1 | async-start | bytes 294912 | tf_op jit(solution)/shard_map/all_to_all | solution.py:307
  94.5 15.8 %all-to-all-start = ((f32[16,2,1152]{2,1,0:T(2,128)}), f32[16,2,1152]{2,1,0:T(2,128)S(1)}, u32[]{:S(2)}, u32[]{:S(2)}) async-start(f32[16,2,1152]{2,1,0:T(2,128)} %get-tuple-element.14), calls=%async_computation | async-start | bytes 294912 | tf_op jit(solution)/shard_map/all_to_all | solution.py:307
  122.1 21.2 %collective-permute-start.22 = (f16[512,1024]{1,0:T(8,128)(2,1)}, f16[512,1024]{1,0:T(8,128)(2,1)}, u32[]{:S(2)}, u32[]{:S(2)}) collective-permute-start(f16[512,1024]{1,0:T(8,128)(2,1)} %multiply_convert_fusion.1), channel_id=1, source_target_pairs={{0,1},{1,0},{2,3},{3,2},{4,5},{5,4},{6,7},{7,6},{8,9},{9,8},{10,11... | collective-permute-start | bytes 3145736 | tf_op jit(solution)/shard_map/ppermute | solution.py:58
  122.8 13.3 %all-to-all-start.2 = ((f32[16,8,128]{2,1,0:T(8,128)}), f32[16,8,128]{2,1,0:T(8,128)S(1)}, u32[]{:S(2)}, u32[]{:S(2)}) async-start(f32[16,8,128]{2,1,0:T(8,128)} %get-tuple-element.16), calls=%async_computation.2 | async-start | bytes 131072 | tf_op jit(solution)/shard_map/all_to_all | solution.py:307
  136.0 55.6 %all-to-all-start.3 = ((f16[16,64,1024]{2,1,0:T(8,128)(2,1)}), f16[16,64,1024]{2,1,0:T(8,128)(2,1)S(1)}, u32[]{:S(2)}, u32[]{:S(2)}) async-start(f16[16,64,1024]{2,1,0:T(8,128)(2,1)} %bitcast.71), calls=%async_computation.3 | async-start | bytes 4194304 | tf_op jit(solution)/shard_map/all_to_all | solution.py:370
  153.1 7.7 %collective-permute-start.27 = (f16[64,1024]{1,0:T(8,128)(2,1)}, f16[64,1024]{1,0:T(8,128)(2,1)}, u32[]{:S(2)}, u32[]{:S(2)}) collective-permute-start(f16[64,1024]{1,0:T(8,128)(2,1)} %get-tuple-element.24), channel_id=1, source_target_pairs={{0,32},{1,39},{2,34},{3,33},{4,36},{5,35},{6,38},{7,37},{8,40},{9,... | collective-permute-start | bytes 393224 | tf_op jit(solution)/shard_map/ppermute | solution.py:58
  164.9 25.0 %collective-permute-start.26 = (f16[64,1024]{1,0:T(8,128)(2,1)}, f16[64,1024]{1,0:T(8,128)(2,1)}, u32[]{:S(2)}, u32[]{:S(2)}) collective-permute-start(f16[64,1024]{1,0:T(8,128)(2,1)} %get-tuple-element.21), channel_id=1, source_target_pairs={{0,38},{1,33},{2,32},{3,35},{4,34},{5,37},{6,36},{7,39},{8,46},{9,... | collective-permute-start | bytes 393224 | tf_op jit(solution)/shard_map/ppermute | solution.py:58
  171.8 18.2 %collective-permute-start.29 = (f16[64,1024]{1,0:T(8,128)(2,1)S(1)}, f16[64,1024]{1,0:T(8,128)(2,1)S(1)}, u32[]{:S(2)}, u32[]{:S(2)}) collective-permute-start(f16[64,1024]{1,0:T(8,128)(2,1)S(1)} %fusion.28), channel_id=1, source_target_pairs={{0,32},{1,39},{2,34},{3,33},{4,36},{5,35},{6,38},{7,37},{8,40},{9,... | collective-permute-start | bytes 393224 | tf_op jit(solution)/shard_map/ppermute | solution.py:58
  (20 other events, 78.0 us)

commit v3 on v2

--- a/solution.py
+++ b/solution.py
@@ -26,8 +26,9 @@
 STRIP = 128
 CHUNK = 256
 GROUP = 16
-LOGITS_VMEM = 30 * 1024 * 1024
-GRADIENT_VMEM = 20 * 1024 * 1024
+LOGITS_VMEM = 58 * 1024 * 1024
+GRADIENT_VMEM = 56 * 1024 * 1024
+ROWS = 256
 
 
 def places():
@@ -74,19 +75,38 @@
     return shifted(p, "c", 1)
 
 
-def gathered_text(own):
-    back = moved(own, along_u(1))
-    ahead = moved(own, along_u(-1))
+def gathered(text, image):
+    tie = lax.optimization_barrier
+    back, ahead = moved(text, along_u(1)), moved(text, along_u(-1))
+    backs, aheads = [image, moved(image, along_z(1))], [image, moved(image, along_z(-1))]
+    back, ahead, backs[1], aheads[1] = tie((back, ahead, backs[1], aheads[1]))
+
+    first = jnp.concatenate([text, back], axis=0)
     far = moved(back, along_u(1))
-    first = jnp.concatenate([own, back], axis=0)
+    first_back, first_ahead = moved(first, along_v(1)), moved(first, along_v(-1))
+    backs.append(moved(backs[1], along_z(1)))
+    aheads.append(moved(aheads[1], along_z(-1)))
+    far, first_back, first_ahead, backs[2], aheads[2] = tie(
+        (far, first_back, first_ahead, backs[2], aheads[2])
+    )
+
     second = jnp.concatenate([ahead, far], axis=0)
-    first_back = moved(first, along_v(1))
-    first_ahead = moved(first, along_v(-1))
-    second_back = moved(second, along_v(1))
-    second_ahead = moved(second, along_v(-1))
+    second_back, second_ahead = moved(second, along_v(1)), moved(second, along_v(-1))
+    backs.append(moved(backs[2], along_z(1)))
+    aheads.append(moved(aheads[2], along_z(-1)))
+    near = jnp.concatenate([image, backs[1], aheads[1], backs[2]], axis=0)
+    near_other = moved(near, other_core)
+    second_back, second_ahead, backs[3], aheads[3], near_other = tie(
+        (second_back, second_ahead, backs[3], aheads[3], near_other)
+    )
+
     first_far = moved(first_back, along_v(1))
     second_far = moved(second_ahead, along_v(-1))
-    pieces = [
+    distant = moved(backs[3], along_z(1))
+    rest = jnp.concatenate([aheads[2], backs[3], aheads[3], distant], axis=0)
+    rest_other = moved(rest, other_core)
+    steps_near, steps_rest = (0, -1, 1, -2), (2, -3, 3, 4)
+    return [
         (first, ((0, 0), (-1, 0))),
         (second, ((1, 0), (2, 0))),
         (first_back, ((0, -1), (-1, -1))),
@@ -95,22 +115,7 @@
         (second_ahead, ((1, 1), (2, 1))),
         (first_far, ((0, 2), (-1, 2))),
         (second_far, ((1, 2), (2, 2))),
-    ]
-    return pieces
-
-
-def gathered_images(own):
-    backs, aheads = [own], [own]
-    for _ in range(3):
-        backs.append(moved(backs[-1], along_z(1)))
-        aheads.append(moved(aheads[-1], along_z(-1)))
-    far = moved(backs[3], along_z(1))
-    near = jnp.concatenate([own, backs[1], aheads[1], backs[2]], axis=0)
-    rest = jnp.concatenate([aheads[2], backs[3], aheads[3], far], axis=0)
-    near_other = moved(near, other_core)
-    rest_other = moved(rest, other_core)
-    steps_near, steps_rest = (0, -1, 1, -2), (2, -3, 3, 4)
-    return [
+    ], [
         (near, [(0, k) for k in steps_near]),
         (rest, [(0, k) for k in steps_rest]),
         (near_other, [(1, k) for k in steps_near]),
@@ -123,10 +128,23 @@
     place_ref = refs[0]
     text_refs = refs[1 : 1 + n_text]
     image_refs = refs[1 + n_text : 1 + n_text + n_image]
-    (s_ref, t_ref, text_out, image_out, row_ref, col_ref) = refs[
+    (s_hbm, t_hbm, text_hbm, image_hbm, row_ref, col_ref) = refs[
         1 + n_text + n_image : 7 + n_text + n_image
     ]
-    (text_frozen, image_frozen, s_high, s_sum, t_high, t_sum, sems) = refs[7 + n_text + n_image :]
+    (
+        s_ref,
+        t_ref,
+        text_out,
+        image_out,
+        text_frozen,
+        image_frozen,
+        s_high,
+        s_sum,
+        t_high,
+        t_sum,
+        sems,
+        out_sems,
+    ) = refs[7 + n_text + n_image :]
     copies = []
     k = 0
     for group, out, frozen in (
@@ -149,6 +167,12 @@
         copy.start()
     for copy in copies:
         copy.wait()
+    slabs = [
+        pltpu.make_async_copy(text_out, text_hbm, out_sems.at[2]),
+        pltpu.make_async_copy(image_out, image_hbm, out_sems.at[3]),
+    ]
+    for copy in slabs:
+        copy.start()
 
     @pl.loop(0, SIDE // CHUNK)
     def _(j):
@@ -173,6 +197,13 @@
             for n in range(GROUP):
                 col_ref[n, which : which + 1, cols] = lse
 
+    logits = [
+        pltpu.make_async_copy(s_ref, s_hbm, out_sems.at[0]),
+        pltpu.make_async_copy(t_ref, t_hbm, out_sems.at[1]),
+    ]
+    for copy in logits:
+        copy.start()
+
     @pl.loop(0, SIDE // 64)
     def _(i):
         for g in range(8):
@@ -200,6 +231,8 @@
         largest = jnp.full((2, 128), jnp.max(largest), jnp.float32)
         for n in range(GROUP):
             ref[n, :, SIDE : SIDE + 128] = largest
+    for copy in slabs + logits:
+        copy.wait()
 
 
 def logits_and_statistics(places_in, text, images):
@@ -207,6 +240,7 @@
     anywhere = pl.BlockSpec(memory_space=pl.ANY)
     vmem = pl.BlockSpec(memory_space=pltpu.VMEM)
     smem = pl.BlockSpec(memory_space=pltpu.SMEM)
+    hbm = pl.BlockSpec(memory_space=pltpu.HBM)
 
     def kernel(*refs):
         logits_kernel((len(text), len(images)), *refs)
@@ -218,8 +252,12 @@
         kernel,
         out_shape=(square, square, half, half, small, small),
         in_specs=[smem] + [anywhere] * (len(text) + len(images)),
-        out_specs=(vmem,) * 6,
+        out_specs=(hbm,) * 4 + (vmem,) * 2,
         scratch_shapes=[
+            pltpu.VMEM((SIDE, SIDE), f32),
+            pltpu.VMEM((SIDE, SIDE), f32),
+            pltpu.VMEM((SIDE, WIDTH), jnp.bfloat16),
+            pltpu.VMEM((SIDE, WIDTH), jnp.bfloat16),
             pltpu.VMEM((SIDE, WIDTH), jnp.bfloat16),
             pltpu.VMEM((SIDE, WIDTH), jnp.bfloat16),
             pltpu.VMEM((SIDE, 128), f32),
@@ -227,6 +265,7 @@
             pltpu.VMEM((SIDE, 128), f32),
             pltpu.VMEM((SIDE, 128), f32),
             pltpu.SemaphoreType.DMA((64,)),
+            pltpu.SemaphoreType.DMA((4,)),
         ],
         compiler_params=pltpu.CompilerParams(vmem_limit_bytes=LOGITS_VMEM),
         cost_estimate=pl.CostEstimate(
@@ -236,32 +275,48 @@
 
 
 def gradient_kernel(
-    s_ref, t_ref, row_ref, col_ref, row_id_ref, col_id_ref, out_ref, factor_ref, part_ref, lse_ref
+    s_ref,
+    t_ref,
+    row_ref,
+    col_ref,
+    row_id_ref,
+    col_id_ref,
+    out_ref,
+    factor_ref,
+    part_ref,
+    lse_ref,
+    total_ref,
 ):
+    step = pl.program_id(0)
+    size = 16
+
     def joined(ref, which):
         values = ref[:, which, :SIDE]
         top = jnp.max(values, axis=0, keepdims=True)
         return top + jnp.log2(jnp.sum(jnp.exp2(values - top), axis=0, keepdims=True))
 
-    s_row_all, t_row_all = joined(row_ref, 0), joined(row_ref, 1)
-    s_col_all, t_col_all = joined(col_ref, 0), joined(col_ref, 1)
-    shared = (s_row_all - 0.5 * t_row_all) + (s_col_all - 0.5 * t_col_all)
-    lse_ref[0:1, :] = s_row_all
-    lse_ref[1:2, :] = t_row_all + 1.0
-    lse_ref[2:3, :] = s_col_all
-    lse_ref[3:4, :] = t_col_all + 1.0
-    for k, ref in ((0, row_ref), (1, col_ref)):
-        scale = 2.0 / jnp.maximum(jnp.max(ref[:, 0, SIDE : SIDE + 128]), 1e-30)
-        factor_ref[k : k + 1, :] = jnp.full((1, SIDE), scale, jnp.float32)
-        factor_ref[k + 2 : k + 3, :] = jnp.full((1, SIDE), SCALE, jnp.float32) / jnp.full(
-            (1, SIDE), scale, jnp.float32
-        )
-    factor_ref[4:8, :] = jnp.zeros((4, SIDE), jnp.float32)
-    size = 16
+    @pl.when(step == 0)
+    def _():
+        s_row_all, t_row_all = joined(row_ref, 0), joined(row_ref, 1)
+        s_col_all, t_col_all = joined(col_ref, 0), joined(col_ref, 1)
+        shared = (s_row_all - 0.5 * t_row_all) + (s_col_all - 0.5 * t_col_all)
+        lse_ref[0:1, :] = s_row_all
+        lse_ref[1:2, :] = t_row_all + 1.0
+        lse_ref[2:3, :] = s_col_all
+        lse_ref[3:4, :] = t_col_all + 1.0
+        lse_ref[4:5, :] = shared
+        for k, ref in ((0, row_ref), (1, col_ref)):
+            scale = 2.0 / jnp.maximum(jnp.max(ref[:, 0, SIDE : SIDE + 128]), 1e-30)
+            scale = jnp.full((1, SIDE), scale, jnp.float32)
+            factor_ref[k : k + 1, :] = scale
+            factor_ref[k + 2 : k + 3, :] = SCALE / scale
+        factor_ref[4:8, :] = jnp.zeros((4, SIDE), jnp.float32)
+        total_ref[...] = jnp.zeros((size, 128), jnp.float32)
 
     def strip(i, total):
         base = pl.multiple_of(i * STRIP, STRIP)
-        turned = jnp.transpose(lse_ref[:, pl.ds(base, STRIP)])
+        at = pl.multiple_of(step * ROWS + base, STRIP)
+        turned = jnp.transpose(lse_ref[:, pl.ds(at, STRIP)])
         for g in range(STRIP // size):
             rows = pl.ds(pl.multiple_of(base + g * size, size), size)
             s_row = jnp.broadcast_to(turned[g * size : (g + 1) * size, 0:1], (size, 128))
@@ -278,24 +333,39 @@
                 total = total + (weights * (t - s) - jnp.where(same, s, 0.0))
         return total
 
-    total = lax.fori_loop(0, SIDE // STRIP, strip, jnp.zeros((size, 128), jnp.float32))
-    part = LN2 * (jnp.sum(total) + jnp.sum(shared) * (1.0 / GROUP))
-    part_ref[...] = jnp.full(part_ref.shape, part, jnp.float32)
+    total_ref[...] = lax.fori_loop(0, ROWS // STRIP, strip, total_ref[...])
+
+    @pl.when(step == pl.num_programs(0) - 1)
+    def _():
+        part = jnp.sum(total_ref[...]) + jnp.sum(lse_ref[4:5, :]) * (1.0 / GROUP)
+        part_ref[...] = jnp.full(part_ref.shape, LN2 * part, jnp.float32)
 
 
 def gradient_of_logits(s, t, row, col, row_id, col_id):
-    vmem = pl.BlockSpec(memory_space=pltpu.VMEM)
     f32 = jnp.float32
+    by_rows = pl.BlockSpec((ROWS, SIDE), lambda i: (i, 0))
+
+    def whole(shape):
+        return pl.BlockSpec(shape, lambda i: (0,) * len(shape))
+
     return pl.pallas_call(
         gradient_kernel,
+        grid=(SIDE // ROWS,),
         out_shape=(
             jax.ShapeDtypeStruct((SIDE, SIDE), jnp.bfloat16),
             jax.ShapeDtypeStruct((8, SIDE), f32),
-            jax.ShapeDtypeStruct((GROUP, 8, 128), f32),
+            jax.ShapeDtypeStruct((8, 128), f32),
         ),
-        in_specs=[vmem] * 6,
-        out_specs=(vmem,) * 3,
-        scratch_shapes=[pltpu.VMEM((8, SIDE), f32)],
+        in_specs=[
+            by_rows,
+            by_rows,
+            whole(row.shape),
+            whole(col.shape),
+            pl.BlockSpec((ROWS, 1), lambda i: (i, 0)),
+            whole(col_id.shape),
+        ],
+        out_specs=(by_rows, whole((8, SIDE)), whole((8, 128))),
+        scratch_shapes=[pltpu.VMEM((8, SIDE), f32), pltpu.VMEM((16, 128), f32)],
         compiler_params=pltpu.CompilerParams(vmem_limit_bytes=GRADIENT_VMEM),
         cost_estimate=pl.CostEstimate(
             flops=16 * SIDE * SIDE, bytes_accessed=10 << 20, transcendentals=4 * SIDE * SIDE
@@ -307,17 +377,13 @@
     return lax.all_to_all(copies, axis, split_axis=0, concat_axis=0, tiled=True)
 
 
-def summed_over(value, steps):
-    for to in steps:
-        value = value + moved(value, to)
-    return value
-
-
 def body(image_student, text_student, image_teacher, text_teacher):
     y, zl, x, zh, c = (lax.axis_index(n) for n in NAMES)
     z = zh * 2 + zl
-    text_pieces = gathered_text(jnp.concatenate([text_student, text_teacher], axis=1))
-    image_pieces = gathered_images(jnp.concatenate([image_student, image_teacher], axis=1))
+    text_pieces, image_pieces = gathered(
+        jnp.concatenate([text_student, text_teacher], axis=1),
+        jnp.concatenate([image_student, image_teacher], axis=1),
+    )
 
     sign = 1 - 2 * c
     at = []
@@ -350,11 +416,8 @@
     text_scale, image_scale = factors[0:1], factors[1:2]
     image_factor, text_factor = factors[2:3], factors[3:4]
 
-    value = jnp.sum(exchanged(part, TEXT_GROUP), axis=0)
-    value = summed_over(
-        value, [other_core] + [lambda p, k=k: flipped(p, "z", k) for k in (1, 2, 4)]
-    )
-    loss = value[0, 0] / (256 * BLOCK)
+    everyone = lax.all_gather(part, NAMES, axis=0, tiled=True)
+    loss = jnp.sum(everyone) * (1.0 / (256 * BLOCK * 8 * 128))
 
     half = SIDE // 2
     theirs = lax.dynamic_slice_in_dim(gradient, (1 - c) * half, half)
@@ -393,16 +456,6 @@
     return (loss, image_grad, text_grad)
 
 
-def flipped(p, axis, bit):
-    y, zl, x, zh, c = p
-    if axis == "x":
-        return (y, zl, x ^ bit, zh, c)
-    if axis == "y":
-        return (y ^ bit, zl, x, zh, c)
-    z = (zh * 2 + zl) ^ bit
-    return (y, z % 2, x, z // 2, c)
-
-
 def solution(mesh):
     finer = Mesh(mesh.devices.reshape(SIZES), NAMES)
     placed = (P(ROW_COL, None), P(COL_ROW, None), P(ROW_COL, None), P(COL_ROW, None))

time: 195 us -> 538 us (2.76)
  waiting for transfers between devices: 68.6 us -> 417 us
  starting transfers between devices: 67 us -> 49.9 us
  between operations: 2.64 us -> 16.1 us
  local copies, waits for them, and re-layouts: 18.1 us -> 7.59 us
    all_gather x0 -> x1, waiting for transfers between devices: none -> 346 us  [body(): everyone = lax.all_gather(part, NAMES, axis=0, tiled=True)]
    unnamed x26 -> x28, local copies, waits for them, and re-layouts: 14.9 us -> 3.39 us
    ppermute x30 -> x26, starting transfers between devices: 40.8 us -> 32.7 us  [moved(): return lax.ppermute(value, NAMES, pairs)]
    all_to_all x3 -> x2, starting transfers between devices: 18.9 us -> 11.8 us  [exchanged(): return lax.all_to_all(copies, axis, split_axis=0, concat_axis=0, tiled=True)]
    ppermute x30 -> x26, waiting for transfers between devices: 53.4 us -> 56.7 us  [moved(): return lax.ppermute(value, NAMES, pairs)]
    all_to_all x3 -> x2, waiting for transfers between devices: 15.2 us -> 13.9 us  [exchanged(): return lax.all_to_all(copies, axis, split_axis=0, concat_axis=0, tiled=True)]
  transfers between devices with their start and end apart: 34 -> 30, of which waited for: 21 -> 15; matrix products, arithmetic and copies ran while one was open for 9% -> 4% of each run, Pallas kernels for 0% -> 0%
where the time goes in v3:
time: 538 us; the launch traced here: 535 us
  waiting for transfers between devices  417 us (78%)
  starting transfers between devices  49.9 us (9%)
  Pallas kernels  24 us (4%)
  between operations  16.1 us (3%)
  matrix products  11.1 us (2%)
  other arithmetic  9.64 us (2%)
  local copies, waits for them, and re-layouts  7.59 us (1%)
    all_gather x1, waiting for transfers between devices, body(): everyone = lax.all_gather(part, NAMES, axis=0, tiled=True)  346 us
    ppermute x26, waiting for transfers between devices, moved(): return lax.ppermute(value, NAMES, pairs)  56.7 us
    ppermute x26, starting transfers between devices, moved(): return lax.ppermute(value, NAMES, pairs)  32.7 us
    pallas_call x1, Pallas kernels, logits_and_statistics(): pl.pallas_call(kernel, out_shape=(square, square, half, half, small, smal...  15.5 us
    all_to_all x2, waiting for transfers between devices, exchanged(): return lax.all_to_all(copies, axis, split_axis=0, concat_axis=0, tiled=True)  13.9 us
    all_to_all x2, starting transfers between devices, exchanged(): return lax.all_to_all(copies, axis, split_axis=0, concat_axis=0, tiled=True)  11.8 us
  transfers between devices with their start and end apart: 30, of which 15 were waited for; matrix products, arithmetic and copies ran while one was open for 4% of the time, Pallas kernels for 0%

profile of v3, /device:TPU:8, one launch (start us, length us, event | category | flops | bytes accessed | tf_op | source)
XLA Modules:
  0.0 535.4 jit_solution(13665149759473457028)
XLA Ops:
  16.1 4.0 collective-permute-start.3
  20.2 7.0 %collective-permute-done.2 = bf16[64,2048]{1,0:T(8,128)(2,1)S(1)} collective-permute-done((bf16[64,2048]{1,0:T(8,128)(2,1)S(1)}, bf16[64,2048]{1,0:T(8,128)(2,1)S(1)}, u32[]{:S(2)}, u32[]{:S(2)}) %collective-permute-start.2) | collective-permute-done | bytes 262176 | tf_op jit(solution)/shard_map/ppermute | solution.py:59
  29.4 3.2 collective-permute-start.8
  32.6 7.1 %collective-permute-done.4 = bf16[64,2048]{1,0:T(8,128)(2,1)S(1)} collective-permute-done((bf16[64,2048]{1,0:T(8,128)(2,1)S(1)}, bf16[64,2048]{1,0:T(8,128)(2,1)S(1)}, u32[]{:S(2)}, u32[]{:S(2)}) %collective-permute-start.4) | collective-permute-done | bytes 262176 | tf_op jit(solution)/shard_map/ppermute | solution.py:59
  42.1 3.2 collective-permute-start.12
  45.4 6.6 %collective-permute-done.11 = bf16[64,2048]{1,0:T(8,128)(2,1)S(1)} collective-permute-done((bf16[64,2048]{1,0:T(8,128)(2,1)S(1)}, bf16[64,2048]{1,0:T(8,128)(2,1)S(1)}, u32[]{:S(2)}, u32[]{:S(2)}) %collective-permute-start.11) | collective-permute-done | bytes 262176 | tf_op jit(solution)/shard_map/ppermute | solution.py:59
  52.9 7.5 %collective-permute-done.16 = bf16[64,2048]{1,0:T(8,128)(2,1)S(1)} collective-permute-done((bf16[64,2048]{1,0:T(8,128)(2,1)S(1)}, bf16[64,2048]{1,0:T(8,128)(2,1)S(1)}, u32[]{:S(2)}, u32[]{:S(2)}) %collective-permute-start.16) | collective-permute-done | bytes 262176 | tf_op jit(solution)/shard_map/ppermute | solution.py:59
  63.6 6.5 %collective-permute-done.14.refs_7_ = bf16[128,2048]{1,0:T(8,128)(2,1)} collective-permute-done((bf16[128,2048]{1,0:T(8,128)(2,1)S(1)}, bf16[128,2048]{1,0:T(8,128)(2,1)}, u32[]{:S(2)}, u32[]{:S(2)}) %collective-permute-start.14) | collective-permute-done | bytes 524320 | tf_op jit(solution)/shard_map/ppermute | solution.py:59
  72.3 15.5 %shard_map.67 = (f32[1024,1024]{1,0:T(8,128)}, f32[1024,1024]{1,0:T(8,128)}, bf16[1024,1024]{1,0:T(8,128)(2,1)}, bf16[1024,1024]{1,0:T(8,128)(2,1)}, f32[16,2,1152]{2,1,0:T(2,128)}, /*index=5*/f32[16,2,1152]{2,1,0:T(2,128)}) custom-call(s32[32]{0:T(128)} %stack.131.refs_0_, bf16[128,2048]{1,0:T(8,128)(2,1)} %copy-done.3, bf16[128,2048]{1,0:T(8,128)(2,1)} %copy-done.4, ...), custom_call_target="tpu_custom_call" | custom-call | flops 4294967296 | bytes 20971520 | tf_op jit(solution)/shard_map/pallas_call | solution.py:251
  87.7 7.8 %all-to-all-start.1 = ((f32[16,2,1152]{2,1,0:T(2,128)}), f32[16,2,1152]{2,1,0:T(2,128)S(1)}, u32[]{:S(2)}, u32[]{:S(2)}) async-start(f32[16,2,1152]{2,1,0:T(2,128)} %get-tuple-element.43), calls=%async_computation.1 | async-start | bytes 294912 | tf_op jit(solution)/shard_map/all_to_all | solution.py:377
  95.5 6.4 %all-to-all-done.1.col_ref = f32[16,2,1152]{2,1,0:T(2,128)S(1)} async-done(((f32[16,2,1152]{2,1,0:T(2,128)}), f32[16,2,1152]{2,1,0:T(2,128)S(1)}, u32[]{:S(2)}, u32[]{:S(2)}) %all-to-all-start.1) | async-done | bytes 147488 | tf_op jit(solution)/shard_map/all_to_all | solution.py:377
  101.9 4.0 all-to-all-start
  107.8 7.4 %all-to-all-done.row_ref = f32[16,2,1152]{2,1,0:T(2,128)S(1)} async-done(((f32[16,2,1152]{2,1,0:T(2,128)}), f32[16,2,1152]{2,1,0:T(2,128)S(1)}, u32[]{:S(2)}, u32[]{:S(2)}) %all-to-all-start) | async-done | bytes 147488 | tf_op jit(solution)/shard_map/all_to_all | solution.py:377
  115.9 8.5 %shard_map.68 = (bf16[1024,1024]{1,0:T(8,128)(2,1)}, f32[8,1024]{1,0:T(8,128)}, f32[8,128]{1,0:T(8,128)}) custom-call(f32[1024,1024]{1,0:T(8,128)} %get-tuple-element.40.s_ref, f32[1024,1024]{1,0:T(8,128)} %get-tuple-element.41.t_ref, f32[16,2,1152]{2,1,0:T(2,128)} %copy-done.2, f32[16,2,1152]{2,1,0:T(2,128)} %copy-done.1, s32[1024,1]{1,0:T(8,128)} %fusion.15.row_id_ref, ...), custom_call_target="tpu_custom_call" | custom-call | flops 16777216 | bytes 10485760 | tf_op jit(solution)/shard_map/pallas_call | solution.py:351
  128.8 5.3 multiply_convert_fusion
  134.1 5.3 all-to-all-start.2
  139.5 3.2 fusion.1
  145.5 4.5 collective-permute-done.19
  152.1 3.8 collective-permute-done.20
  156.0 2.9 collective-permute-start.21
  162.5 3.7 collective-permute-start.22
  166.3 2.9 collective-permute-done.24
  170.0 5.4 %collective-permute-done.25 = f16[64,1024]{1,0:T(8,128)(2,1)S(1)} collective-permute-done((f16[64,1024]{1,0:T(8,128)(2,1)S(1)}, f16[64,1024]{1,0:T(8,128)(2,1)S(1)}, u32[]{:S(2)}, u32[]{:S(2)}) %collective-permute-start.25) | collective-permute-done | bytes 131104 | tf_op jit(solution)/shard_map/ppermute | solution.py:59
  178.3 346.4 %all-gather.2.cloned.1.call-done = f32[2048,128]{1,0:T(8,128)} async-done(((f32[8,128]{1,0:T(8,128)}), f32[2048,128]{1,0:T(8,128)}) %all-gather.2.cloned.1.call-update) | async-done | bytes 1048592 | tf_op jit(solution)/shard_map/all_gather | solution.py:419
  (90 shorter events, 41.0 us)
Async XLA Ops:
  9.0 11.2 %collective-permute-start = (bf16[64,2048]{1,0:T(8,128)(2,1)S(1)}, bf16[64,2048]{1,0:T(8,128)(2,1)S(1)}, u32[]{:S(2)}, u32[]{:S(2)}) collective-permute-start(bf16[64,2048]{1,0:T(8,128)(2,1)S(1)} %constant_dynamic-update-slice_fusion), channel_id=1, source_target_pairs={{0,8},{1,65},{2,10},{3,67},{4,12},{5,69},{6,14},{7,71},{8,16},{9,7... | collective-permute-start | bytes 786440 | tf_op jit(solution)/shard_map/ppermute | solution.py:59
  10.6 9.6 %collective-permute-start.1 = (bf16[64,2048]{1,0:T(8,128)(2,1)S(1)}, bf16[64,2048]{1,0:T(8,128)(2,1)S(1)}, u32[]{:S(2)}, u32[]{:S(2)}) collective-permute-start(bf16[64,2048]{1,0:T(8,128)(2,1)S(1)} %constant_dynamic-update-slice_fusion), channel_id=1, source_target_pairs={{0,24},{1,193},{2,26},{3,195},{4,28},{5,197},{6,30},{7,199},{8,0},... | collective-permute-start | bytes 786440 | tf_op jit(solution)/shard_map/ppermute | solution.py:59
  14.1 13.0 %collective-permute-start.2 = (bf16[64,2048]{1,0:T(8,128)(2,1)S(1)}, bf16[64,2048]{1,0:T(8,128)(2,1)S(1)}, u32[]{:S(2)}, u32[]{:S(2)}) collective-permute-start(bf16[64,2048]{1,0:T(8,128)(2,1)S(1)} %constant_dynamic-update-slice_fusion.2), channel_id=1, source_target_pairs={{0,32},{1,39},{2,34},{3,33},{4,36},{5,35},{6,38},{7,37},{8,40},{9,... | collective-permute-start | bytes 786440 | tf_op jit(solution)/shard_map/ppermute | solution.py:59
  16.1 11.1 %collective-permute-start.3 = (bf16[64,2048]{1,0:T(8,128)(2,1)S(1)}, bf16[64,2048]{1,0:T(8,128)(2,1)S(1)}, u32[]{:S(2)}, u32[]{:S(2)}) collective-permute-start(bf16[64,2048]{1,0:T(8,128)(2,1)S(1)} %constant_dynamic-update-slice_fusion.2), channel_id=1, source_target_pairs={{0,38},{1,33},{2,32},{3,35},{4,34},{5,37},{6,36},{7,39},{8,46},{9,... | collective-permute-start | bytes 786440 | tf_op jit(solution)/shard_map/ppermute | solution.py:59
  27.2 12.4 %collective-permute-start.5 = (bf16[128,2048]{1,0:T(8,128)(2,1)S(1)}, bf16[128,2048]{1,0:T(8,128)(2,1)S(1)}, u32[]{:S(2)}, u32[]{:S(2)}) collective-permute-start(bf16[128,2048]{1,0:T(8,128)(2,1)S(1)} %pad_maximum_fusion.1.refs_1_), channel_id=1, source_target_pairs={{0,64},{1,9},{2,66},{3,11},{4,68},{5,13},{6,70},{7,15},{8,72},{9,1... | collective-permute-start | bytes 1572872 | tf_op jit(solution)/shard_map/ppermute | solution.py:59
  28.9 10.8 %collective-permute-start.6 = (bf16[128,2048]{1,0:T(8,128)(2,1)S(1)}, bf16[128,2048]{1,0:T(8,128)(2,1)}, u32[]{:S(2)}, u32[]{:S(2)}) collective-permute-start(bf16[128,2048]{1,0:T(8,128)(2,1)S(1)} %pad_maximum_fusion.1.refs_1_), channel_id=1, source_target_pairs={{0,192},{1,25},{2,194},{3,27},{4,196},{5,29},{6,198},{7,31},{8,200... | collective-permute-start | bytes 1572872 | tf_op jit(solution)/shard_map/ppermute | solution.py:59
  29.4 10.3 %collective-permute-start.4 = (bf16[64,2048]{1,0:T(8,128)(2,1)S(1)}, bf16[64,2048]{1,0:T(8,128)(2,1)S(1)}, u32[]{:S(2)}, u32[]{:S(2)}) collective-permute-start(bf16[64,2048]{1,0:T(8,128)(2,1)S(1)} %collective-permute-done), channel_id=1, source_target_pairs={{0,8},{1,65},{2,10},{3,67},{4,12},{5,69},{6,14},{7,71},{8,16},{9,7... | collective-permute-start | bytes 786440 | tf_op jit(solution)/shard_map/ppermute | solution.py:59
  29.4 10.3 %collective-permute-start.7 = (bf16[64,2048]{1,0:T(8,128)(2,1)S(1)}, bf16[64,2048]{1,0:T(8,128)(2,1)S(1)}, u32[]{:S(2)}, u32[]{:S(2)}) collective-permute-start(bf16[64,2048]{1,0:T(8,128)(2,1)S(1)} %collective-permute-done.2), channel_id=1, source_target_pairs={{0,32},{1,39},{2,34},{3,33},{4,36},{5,35},{6,38},{7,37},{8,40},{9,... | collective-permute-start | bytes 786440 | tf_op jit(solution)/shard_map/ppermute | solution.py:59
  29.4 10.3 %collective-permute-start.8 = (bf16[64,2048]{1,0:T(8,128)(2,1)S(1)}, bf16[64,2048]{1,0:T(8,128)(2,1)S(1)}, u32[]{:S(2)}, u32[]{:S(2)}) collective-permute-start(bf16[64,2048]{1,0:T(8,128)(2,1)S(1)} %collective-permute-done.3), channel_id=1, source_target_pairs={{0,38},{1,33},{2,32},{3,35},{4,34},{5,37},{6,36},{7,39},{8,46},{9,... | collective-permute-start | bytes 786440 | tf_op jit(solution)/shard_map/ppermute | solution.py:59
  39.8 13.0 %collective-permute-start.13 = (bf16[256,2048]{1,0:T(8,128)(2,1)S(1)}, bf16[256,2048]{1,0:T(8,128)(2,1)S(1)}, u32[]{:S(2)}, u32[]{:S(2)}) collective-permute-start(bf16[256,2048]{1,0:T(8,128)(2,1)S(1)} %pad_maximum_fusion.refs_9_), channel_id=1, source_target_pairs={{0,1},{1,0},{2,3},{3,2},{4,5},{5,4},{6,7},{7,6},{8,9},{9,8},{10,11... | collective-permute-start | bytes 3145736 | tf_op jit(solution)/shard_map/ppermute | solution.py:59
  40.0 12.0 %collective-permute-start.10 = (bf16[128,2048]{1,0:T(8,128)(2,1)S(1)}, bf16[128,2048]{1,0:T(8,128)(2,1)}, u32[]{:S(2)}, u32[]{:S(2)}) collective-permute-start(bf16[128,2048]{1,0:T(8,128)(2,1)S(1)} %constant_dynamic-update-slice_fusion.4.refs_2_), channel_id=1, source_target_pairs={{0,192},{1,25},{2,194},{3,27},{4,196},{5,29},{6,198},{7,31},{8,200... | collective-permute-start | bytes 1572872 | tf_op jit(solution)/shard_map/ppermute | solution.py:59
  41.6 10.4 %collective-permute-start.9 = (bf16[128,2048]{1,0:T(8,128)(2,1)S(1)}, bf16[128,2048]{1,0:T(8,128)(2,1)S(1)}, u32[]{:S(2)}, u32[]{:S(2)}) collective-permute-start(bf16[128,2048]{1,0:T(8,128)(2,1)S(1)} %constant_dynamic-update-slice_fusion.4.refs_2_), channel_id=1, source_target_pairs={{0,64},{1,9},{2,66},{3,11},{4,68},{5,13},{6,70},{7,15},{8,72},{9,1... | collective-permute-start | bytes 1572872 | tf_op jit(solution)/shard_map/ppermute | solution.py:59
  42.1 9.9 %collective-permute-start.11 = (bf16[64,2048]{1,0:T(8,128)(2,1)S(1)}, bf16[64,2048]{1,0:T(8,128)(2,1)S(1)}, u32[]{:S(2)}, u32[]{:S(2)}) collective-permute-start(bf16[64,2048]{1,0:T(8,128)(2,1)S(1)} %collective-permute-done.7), channel_id=1, source_target_pairs={{0,32},{1,39},{2,34},{3,33},{4,36},{5,35},{6,38},{7,37},{8,40},{9,... | collective-permute-start | bytes 786440 | tf_op jit(solution)/shard_map/ppermute | solution.py:59
  42.1 9.9 %collective-permute-start.12 = (bf16[64,2048]{1,0:T(8,128)(2,1)S(1)}, bf16[64,2048]{1,0:T(8,128)(2,1)S(1)}, u32[]{:S(2)}, u32[]{:S(2)}) collective-permute-start(bf16[64,2048]{1,0:T(8,128)(2,1)S(1)} %collective-permute-done.8), channel_id=1, source_target_pairs={{0,38},{1,33},{2,32},{3,35},{4,34},{5,37},{6,36},{7,39},{8,46},{9,... | collective-permute-start | bytes 786440 | tf_op jit(solution)/shard_map/ppermute | solution.py:59
  52.8 7.6 %collective-permute-start.16 = (bf16[64,2048]{1,0:T(8,128)(2,1)S(1)}, bf16[64,2048]{1,0:T(8,128)(2,1)S(1)}, u32[]{:S(2)}, u32[]{:S(2)}) collective-permute-start(bf16[64,2048]{1,0:T(8,128)(2,1)S(1)} %collective-permute-done.11), channel_id=1, source_target_pairs={{0,32},{1,39},{2,34},{3,33},{4,36},{5,35},{6,38},{7,37},{8,40},{9,... | collective-permute-start | bytes 786440 | tf_op jit(solution)/shard_map/ppermute | solution.py:59
  60.4 11.8 %collective-permute-start.17 = (bf16[256,2048]{1,0:T(8,128)(2,1)S(1)}, bf16[256,2048]{1,0:T(8,128)(2,1)}, u32[]{:S(2)}, u32[]{:S(2)}) collective-permute-start(bf16[256,2048]{1,0:T(8,128)(2,1)S(1)} %constant_dynamic-update-slice_fusion.6.refs_10_), channel_id=1, source_target_pairs={{0,1},{1,0},{2,3},{3,2},{4,5},{5,4},{6,7},{7,6},{8,9},{9,8},{10,11... | collective-permute-start | bytes 3145736 | tf_op jit(solution)/shard_map/ppermute | solution.py:59
  60.7 9.4 %collective-permute-start.14 = (bf16[128,2048]{1,0:T(8,128)(2,1)S(1)}, bf16[128,2048]{1,0:T(8,128)(2,1)}, u32[]{:S(2)}, u32[]{:S(2)}) collective-permute-start(bf16[128,2048]{1,0:T(8,128)(2,1)S(1)} %collective-permute-done.5.refs_3_), channel_id=1, source_target_pairs={{0,64},{1,9},{2,66},{3,11},{4,68},{5,13},{6,70},{7,15},{8,72},{9,1... | collective-permute-start | bytes 1572872 | tf_op jit(solution)/shard_map/ppermute | solution.py:59
  62.4 9.9 %collective-permute-start.15 = (bf16[128,2048]{1,0:T(8,128)(2,1)}, bf16[128,2048]{1,0:T(8,128)(2,1)}, u32[]{:S(2)}, u32[]{:S(2)}) collective-permute-start(bf16[128,2048]{1,0:T(8,128)(2,1)} %collective-permute-done.10.refs_6_), channel_id=1, source_target_pairs={{0,192},{1,25},{2,194},{3,27},{4,196},{5,29},{6,198},{7,31},{8,200... | collective-permute-start | bytes 1572872 | tf_op jit(solution)/shard_map/ppermute | solution.py:59
  87.7 14.2 %all-to-all-start.1 = ((f32[16,2,1152]{2,1,0:T(2,128)}), f32[16,2,1152]{2,1,0:T(2,128)S(1)}, u32[]{:S(2)}, u32[]{:S(2)}) async-start(f32[16,2,1152]{2,1,0:T(2,128)} %get-tuple-element.43), calls=%async_computation.1 | async-start | bytes 294912 | tf_op jit(solution)/shard_map/all_to_all | solution.py:377
  101.9 13.3 %all-to-all-start = ((f32[16,2,1152]{2,1,0:T(2,128)}), f32[16,2,1152]{2,1,0:T(2,128)S(1)}, u32[]{:S(2)}, u32[]{:S(2)}) async-start(f32[16,2,1152]{2,1,0:T(2,128)} %get-tuple-element.42), calls=%async_computation | async-start | bytes 294912 | tf_op jit(solution)/shard_map/all_to_all | solution.py:377
  128.0 14.6 %collective-permute-start.18 = (f16[512,1024]{1,0:T(8,128)(2,1)S(1)}, f16[512,1024]{1,0:T(8,128)(2,1)}, u32[]{:S(2)}, u32[]{:S(2)}) collective-permute-start(f16[512,1024]{1,0:T(8,128)(2,1)S(1)} %multiply_convert_fusion.1), channel_id=1, source_target_pairs={{0,1},{1,0},{2,3},{3,2},{4,5},{5,4},{6,7},{7,6},{8,9},{9,8},{10,11... | collective-permute-start | bytes 3145736 | tf_op jit(solution)/shard_map/ppermute | solution.py:59
  134.1 43.0 %all-to-all-start.2 = ((f16[16,64,1024]{2,1,0:T(8,128)(2,1)}), f16[16,64,1024]{2,1,0:T(8,128)(2,1)S(1)}, u32[]{:S(2)}, u32[]{:S(2)}) async-start(f16[16,64,1024]{2,1,0:T(8,128)(2,1)} %bitcast.70), calls=%async_computation.2 | async-start | bytes 4194304 | tf_op jit(solution)/shard_map/all_to_all | solution.py:433
  139.4 385.3 %all-gather.2.cloned.1.call-start = ((), (), s32[]{:S(2)}) async-start(), calls=%async_computation.3 | async-start | bytes 1052672 | tf_op jit(solution)/shard_map/all_gather | solution.py:419
  162.5 7.5 %collective-permute-start.22 = (f16[64,1024]{1,0:T(8,128)(2,1)S(1)}, f16[64,1024]{1,0:T(8,128)(2,1)}, u32[]{:S(2)}, u32[]{:S(2)}) collective-permute-start(f16[64,1024]{1,0:T(8,128)(2,1)S(1)} %get-tuple-element.49), channel_id=1, source_target_pairs={{0,38},{1,33},{2,32},{3,35},{4,34},{5,37},{6,36},{7,39},{8,46},{9,... | collective-permute-start | bytes 393224 | tf_op jit(solution)/shard_map/ppermute | solution.py:59
  (17 other events, 185.5 us)
Sparse Core Ops, SparseCore 0:
  145.6 379.0 all-gather.1

commit v4 on v3

--- a/solution.py
+++ b/solution.py
@@ -78,48 +78,42 @@
 def gathered(text, image):
     tie = lax.optimization_barrier
     back, ahead = moved(text, along_u(1)), moved(text, along_u(-1))
-    backs, aheads = [image, moved(image, along_z(1))], [image, moved(image, along_z(-1))]
-    back, ahead, backs[1], aheads[1] = tie((back, ahead, backs[1], aheads[1]))
-
-    first = jnp.concatenate([text, back], axis=0)
+    partner = moved(image, other_core)
+    back, ahead, partner = tie((back, ahead, partner))
+
     far = moved(back, along_u(1))
-    first_back, first_ahead = moved(first, along_v(1)), moved(first, along_v(-1))
-    backs.append(moved(backs[1], along_z(1)))
-    aheads.append(moved(aheads[1], along_z(-1)))
-    far, first_back, first_ahead, backs[2], aheads[2] = tie(
-        (far, first_back, first_ahead, backs[2], aheads[2])
-    )
-
-    second = jnp.concatenate([ahead, far], axis=0)
-    second_back, second_ahead = moved(second, along_v(1)), moved(second, along_v(-1))
-    backs.append(moved(backs[2], along_z(1)))
-    aheads.append(moved(aheads[2], along_z(-1)))
-    near = jnp.concatenate([image, backs[1], aheads[1], backs[2]], axis=0)
-    near_other = moved(near, other_core)
-    second_back, second_ahead, backs[3], aheads[3], near_other = tie(
-        (second_back, second_ahead, backs[3], aheads[3], near_other)
-    )
-
-    first_far = moved(first_back, along_v(1))
-    second_far = moved(second_ahead, along_v(-1))
-    distant = moved(backs[3], along_z(1))
-    rest = jnp.concatenate([aheads[2], backs[3], aheads[3], distant], axis=0)
-    rest_other = moved(rest, other_core)
-    steps_near, steps_rest = (0, -1, 1, -2), (2, -3, 3, 4)
+    chain = [jnp.concatenate([image, partner], axis=0)]
+    chain.append(moved(chain[0], along_z(1)))
+    far, text, back, ahead = tie((far, text, back, ahead))
+
+    line = jnp.concatenate([text, back, ahead, far], axis=0)
+    line_back, line_ahead = moved(line, along_v(1)), moved(line, along_v(-1))
+    chain.append(moved(chain[1], along_z(1)))
+    chain.append(moved(chain[2], along_z(1)))
+    both = jnp.concatenate([chain[1], chain[2]], axis=0)
+    both_other = moved(both, other_core)
+    line_back, line_ahead, chain[3] = tie((line_back, line_ahead, chain[3]))
+
+    first_far = moved(line_back[:128], along_v(1))
+    second_far = moved(line_ahead[128:], along_v(-1))
+    distant = moved(chain[3][:64], along_z(1))
+    third_other = moved(chain[3], other_core)
+    distant_other = moved(distant, other_core)
+    us = (0, -1, 1, 2)
     return [
-        (first, ((0, 0), (-1, 0))),
-        (second, ((1, 0), (2, 0))),
-        (first_back, ((0, -1), (-1, -1))),
-        (first_ahead, ((0, 1), (-1, 1))),
-        (second_back, ((1, -1), (2, -1))),
-        (second_ahead, ((1, 1), (2, 1))),
+        (line, [(du, 0) for du in us]),
+        (line_back, [(du, -1) for du in us]),
+        (line_ahead, [(du, 1) for du in us]),
         (first_far, ((0, 2), (-1, 2))),
         (second_far, ((1, 2), (2, 2))),
     ], [
-        (near, [(0, k) for k in steps_near]),
-        (rest, [(0, k) for k in steps_rest]),
-        (near_other, [(1, k) for k in steps_near]),
-        (rest_other, [(1, k) for k in steps_rest]),
+        (chain[0], ((0, 0), (1, 0))),
+        (both, ((0, -1), (1, -1), (0, -2), (1, -2))),
+        (both_other, ((1, 1), (0, 1), (1, 2), (0, 2))),
+        (chain[3], ((0, -3), (1, -3))),
+        (third_other, ((1, 3), (0, 3))),
+        (distant, ((0, 4),)),
+        (distant_other, ((1, 4),)),
     ]
 
 
@@ -354,7 +348,7 @@
         out_shape=(
             jax.ShapeDtypeStruct((SIDE, SIDE), jnp.bfloat16),
             jax.ShapeDtypeStruct((8, SIDE), f32),
-            jax.ShapeDtypeStruct((8, 128), f32),
+            jax.ShapeDtypeStruct((GROUP, 8, 128), f32),
         ),
         in_specs=[
             by_rows,
@@ -364,7 +358,7 @@
             pl.BlockSpec((ROWS, 1), lambda i: (i, 0)),
             whole(col_id.shape),
         ],
-        out_specs=(by_rows, whole((8, SIDE)), whole((8, 128))),
+        out_specs=(by_rows, whole((8, SIDE)), whole((GROUP, 8, 128))),
         scratch_shapes=[pltpu.VMEM((8, SIDE), f32), pltpu.VMEM((16, 128), f32)],
         compiler_params=pltpu.CompilerParams(vmem_limit_bytes=GRADIENT_VMEM),
         cost_estimate=pl.CostEstimate(
@@ -394,9 +388,7 @@
             at.append(((y + dy) % 4) * 4 + (x + dx) % 4)
     for _, offsets in image_pieces:
         for swapped, step in offsets:
-            core = c ^ swapped
-            toward = sign if swapped == 0 else -sign
-            at.append(core * 8 + (z + toward * step) % 8)
+            at.append((c ^ swapped) * 8 + (z + sign * step) % 8)
     where = jnp.stack(at).astype(jnp.int32)
 
     numbers = jnp.arange(SIDE, dtype=jnp.int32)
@@ -416,8 +408,7 @@
     text_scale, image_scale = factors[0:1], factors[1:2]
     image_factor, text_factor = factors[2:3], factors[3:4]
 
-    everyone = lax.all_gather(part, NAMES, axis=0, tiled=True)
-    loss = jnp.sum(everyone) * (1.0 / (256 * BLOCK * 8 * 128))
+    value = jnp.sum(exchanged(part, TEXT_GROUP), axis=0)
 
     half = SIDE // 2
     theirs = lax.dynamic_slice_in_dim(gradient, (1 - c) * half, half)
@@ -444,16 +435,31 @@
     def narrow(v):
         return v.astype(jnp.float16)
 
-    down = moved(narrow(block(4)), along_z(-1)).astype(jnp.float32)
+    tie = lax.optimization_barrier
+    steps = [other_core] + [lambda p, k=k: flipped(p, k) for k in (1, 2, 4)]
+    start, value = tie((narrow(block(4)), value))
+    down, other = tie((moved(start, along_z(-1)), moved(value, steps[0])))
+    value = value + other
+    down = down.astype(jnp.float32)
     up = None
     for k in (3, 2, 1):
         first = narrow(block(-k) + down)
-        second = block(k) if up is None else block(k) + up
-        down = moved(first, along_z(-1)).astype(jnp.float32)
-        up = moved(narrow(second), along_z(1)).astype(jnp.float32)
+        second = narrow(block(k) if up is None else block(k) + up)
+        down, up, other = tie(
+            (moved(first, along_z(-1)), moved(second, along_z(1)), moved(value, steps[4 - k]))
+        )
+        value = value + other
+        down, up = down.astype(jnp.float32), up.astype(jnp.float32)
+    loss = value[0, 0] / (256 * BLOCK)
     image_grad = (block(0) + down + up) * image_factor
     text_grad = jnp.sum(text_blocks.astype(jnp.float32), axis=0) * text_factor
     return (loss, image_grad, text_grad)
+
+
+def flipped(p, bit):
+    y, zl, x, zh, c = p
+    z = (zh * 2 + zl) ^ bit
+    return (y, z % 2, x, z // 2, c)
 
 
 def solution(mesh):

time: 538 us -> 181 us (0.34)
  waiting for transfers between devices: 417 us -> 70.3 us
  between operations: 16.1 us -> 2.65 us
    all_gather x1 -> x0, waiting for transfers between devices: 346 us -> none  [body(): everyone = lax.all_gather(part, NAMES, axis=0, tiled=True)]
    ppermute x26 -> x27, starting transfers between devices: 32.7 us -> 23.7 us  [moved(): return lax.ppermute(value, NAMES, pairs)]
    all_to_all x2 -> x3, starting transfers between devices: 11.8 us -> 19 us  [exchanged(): return lax.all_to_all(copies, axis, split_axis=0, concat_axis=0, tiled=True)]
    ppermute x26 -> x27, waiting for transfers between devices: 56.7 us -> 55.5 us  [moved(): return lax.ppermute(value, NAMES, pairs)]
    all_to_all x2 -> x3, waiting for transfers between devices: 13.9 us -> 14.8 us  [exchanged(): return lax.all_to_all(copies, axis, split_axis=0, concat_axis=0, tiled=True)]
  transfers between devices with their start and end apart: 30 -> 31, of which waited for: 15 -> 20; matrix products, arithmetic and copies ran while one was open for 4% -> 14% of each run, Pallas kernels for 0% -> 0%
where the time goes in v4:
time: 181 us; the launch traced here: 180 us
  waiting for transfers between devices  70.3 us (39%)
  starting transfers between devices  49 us (27%)
  Pallas kernels  24 us (13%)
  matrix products  13.5 us (7%)
  other arithmetic  10.9 us (6%)
  local copies, waits for them, and re-layouts  9.39 us (5%)
  between operations  2.65 us (1%)
    ppermute x27, waiting for transfers between devices, moved(): return lax.ppermute(value, NAMES, pairs)  55.5 us
    ppermute x27, starting transfers between devices, moved(): return lax.ppermute(value, NAMES, pairs)  23.7 us
    all_to_all x3, starting transfers between devices, exchanged(): return lax.all_to_all(copies, axis, split_axis=0, concat_axis=0, tiled=True)  19 us
    pallas_call x1, Pallas kernels, logits_and_statistics(): pl.pallas_call(kernel, out_shape=(square, square, half, half, small, smal...  15.5 us
    all_to_all x3, waiting for transfers between devices, exchanged(): return lax.all_to_all(copies, axis, split_axis=0, concat_axis=0, tiled=True)  14.8 us
    pallas_call x1, Pallas kernels, gradient_of_logits(): pl.pallas_call(gradient_kernel, grid=(SIDE // ROWS,), out_shape=(jax.Shap...  8.53 us
    all_to_all x1, starting transfers between devices, body(): lax.all_to_all(text_part.reshape(16, BLOCK, WIDTH), TEXT_GROUP, 0, 0, til...  6.28 us
    dot_general x1, matrix products, body(): lax.dot_general(gradient, image_slab, (((0,), (0,)), ((), ())), preferred...  5.33 us
  transfers between devices with their start and end apart: 31, of which 20 were waited for; matrix products, arithmetic and copies ran while one was open for 14% of the time, Pallas kernels for 0%

profile of v4, /device:TPU:8, one launch (start us, length us, event | category | flops | bytes accessed | tf_op | source)
XLA Modules:
  0.0 179.8 jit_solution(11478390206816249760)
XLA Ops:
  7.7 2.4 %collective-permute-done = bf16[64,2048]{1,0:T(8,128)(2,1)S(1)} collective-permute-done((bf16[64,2048]{1,0:T(8,128)(2,1)S(1)}, bf16[64,2048]{1,0:T(8,128)(2,1)S(1)}, u32[]{:S(2)}, u32[]{:S(2)}) %collective-permute-start) | collective-permute-done | bytes 262176 | tf_op jit(solution)/shard_map/ppermute | solution.py:59
  14.0 4.0 %collective-permute-done.3 = bf16[64,2048]{1,0:T(8,128)(2,1)S(1)} collective-permute-done((bf16[64,2048]{1,0:T(8,128)(2,1)S(1)}, bf16[64,2048]{1,0:T(8,128)(2,1)S(1)}, u32[]{:S(2)}, u32[]{:S(2)}) %collective-permute-start.3) | collective-permute-done | bytes 262176 | tf_op jit(solution)/shard_map/ppermute | solution.py:59
  18.0 7.0 %collective-permute-done.6 = bf16[128,2048]{1,0:T(8,128)(2,1)S(1)} collective-permute-done((bf16[128,2048]{1,0:T(8,128)(2,1)S(1)}, bf16[128,2048]{1,0:T(8,128)(2,1)S(1)}, u32[]{:S(2)}, u32[]{:S(2)}) %collective-permute-start.6) | collective-permute-done | bytes 524320 | tf_op jit(solution)/shard_map/ppermute | solution.py:59
  28.1 7.4 %collective-permute-done.7 = bf16[128,2048]{1,0:T(8,128)(2,1)S(1)} collective-permute-done((bf16[128,2048]{1,0:T(8,128)(2,1)S(1)}, bf16[128,2048]{1,0:T(8,128)(2,1)S(1)}, u32[]{:S(2)}, u32[]{:S(2)}) %collective-permute-start.7) | collective-permute-done | bytes 524320 | tf_op jit(solution)/shard_map/ppermute | solution.py:59
  36.3 3.7 %collective-permute-done.4.refs_2_ = bf16[256,2048]{1,0:T(8,128)(2,1)S(1)} collective-permute-done((bf16[256,2048]{1,0:T(8,128)(2,1)S(1)}, bf16[256,2048]{1,0:T(8,128)(2,1)S(1)}, u32[]{:S(2)}, u32[]{:S(2)}) %collective-permute-start.4) | collective-permute-done | bytes 1048608 | tf_op jit(solution)/shard_map/ppermute | solution.py:59
  41.6 4.4 %collective-permute-done.8.refs_9_ = bf16[128,2048]{1,0:T(8,128)(2,1)} collective-permute-done((bf16[128,2048]{1,0:T(8,128)(2,1)S(1)}, bf16[128,2048]{1,0:T(8,128)(2,1)}, u32[]{:S(2)}, u32[]{:S(2)}) %collective-permute-start.8) | collective-permute-done | bytes 524320 | tf_op jit(solution)/shard_map/ppermute | solution.py:59
  49.4 5.3 %collective-permute-done.13.refs_11_ = bf16[64,2048]{1,0:T(8,128)(2,1)S(1)} collective-permute-done((bf16[64,2048]{1,0:T(8,128)(2,1)S(1)}, bf16[64,2048]{1,0:T(8,128)(2,1)S(1)}, u32[]{:S(2)}, u32[]{:S(2)}) %collective-permute-start.13) | collective-permute-done | bytes 262176 | tf_op jit(solution)/shard_map/ppermute | solution.py:59
  58.1 15.5 %shard_map.67 = (f32[1024,1024]{1,0:T(8,128)}, f32[1024,1024]{1,0:T(8,128)}, bf16[1024,1024]{1,0:T(8,128)(2,1)}, bf16[1024,1024]{1,0:T(8,128)(2,1)}, f32[16,2,1152]{2,1,0:T(2,128)}, /*index=5*/f32[16,2,1152]{2,1,0:T(2,128)}) custom-call(s32[32]{0:T(128)} %stack.131.refs_0_, bf16[256,2048]{1,0:T(8,128)(2,1)} %copy-done.5, bf16[256,2048]{1,0:T(8,128)(2,1)} %copy-done.3, ...), custom_call_target="tpu_custom_call" | custom-call | flops 4294967296 | bytes 20971520 | tf_op jit(solution)/shard_map/pallas_call | solution.py:245
  73.6 7.5 %all-to-all-start.1 = ((f32[16,2,1152]{2,1,0:T(2,128)}), f32[16,2,1152]{2,1,0:T(2,128)S(1)}, u32[]{:S(2)}, u32[]{:S(2)}) async-start(f32[16,2,1152]{2,1,0:T(2,128)} %get-tuple-element.48), calls=%async_computation.1 | async-start | bytes 294912 | tf_op jit(solution)/shard_map/all_to_all | solution.py:371
  81.1 6.4 %all-to-all-done.1.col_ref = f32[16,2,1152]{2,1,0:T(2,128)S(1)} async-done(((f32[16,2,1152]{2,1,0:T(2,128)}), f32[16,2,1152]{2,1,0:T(2,128)S(1)}, u32[]{:S(2)}, u32[]{:S(2)}) %all-to-all-start.1) | async-done | bytes 147488 | tf_op jit(solution)/shard_map/all_to_all | solution.py:371
  87.5 6.5 %all-to-all-start = ((f32[16,2,1152]{2,1,0:T(2,128)}), f32[16,2,1152]{2,1,0:T(2,128)S(1)}, u32[]{:S(2)}, u32[]{:S(2)}) async-start(f32[16,2,1152]{2,1,0:T(2,128)} %get-tuple-element.47), calls=%async_computation | async-start | bytes 294912 | tf_op jit(solution)/shard_map/all_to_all | solution.py:371
  95.8 7.4 %all-to-all-done.row_ref = f32[16,2,1152]{2,1,0:T(2,128)S(1)} async-done(((f32[16,2,1152]{2,1,0:T(2,128)}), f32[16,2,1152]{2,1,0:T(2,128)S(1)}, u32[]{:S(2)}, u32[]{:S(2)}) %all-to-all-start) | async-done | bytes 147488 | tf_op jit(solution)/shard_map/all_to_all | solution.py:371
  103.9 8.5 %shard_map.68 = (bf16[1024,1024]{1,0:T(8,128)(2,1)}, f32[8,1024]{1,0:T(8,128)}, f32[16,8,128]{2,1,0:T(8,128)}) custom-call(f32[1024,1024]{1,0:T(8,128)} %get-tuple-element.45.s_ref, f32[1024,1024]{1,0:T(8,128)} %get-tuple-element.46.t_ref, f32[16,2,1152]{2,1,0:T(2,128)} %copy-done.1, f32[16,2,1152]{2,1,0:T(2,128)} %copy-done, s32[1024,1]{1,0:T(8,128)} %fusion.15.row_id_ref, ...), custom_call_target="tpu_custom_call" | custom-call | flops 16777216 | bytes 10485760 | tf_op jit(solution)/shard_map/pallas_call | solution.py:345
  113.4 3.6 %multiply_convert_fusion.1 = f16[512,1024]{1,0:T(8,128)(2,1)} fusion(bf16[1024,1024]{1,0:T(8,128)(2,1)S(1)} %copy-done.11, bf16[1024,1024]{1,0:T(8,128)(2,1)} %get-tuple-element.49, s32[]{:T(128)S(6)} %select_n.466, f32[1024]{0:T(1024)S(1)} %bitcast.73), kind=kOutput, calls=%fused_computation.3 | convolution fusion | flops 1074790400 | bytes 4198404 | tf_op jit(solution)/shard_map/dot_general | solution.py:416
  117.7 5.1 %all-to-all-start.2 = ((f32[16,8,128]{2,1,0:T(8,128)}), f32[16,8,128]{2,1,0:T(8,128)S(1)}, u32[]{:S(2)}, u32[]{:S(2)}) async-start(f32[16,8,128]{2,1,0:T(8,128)} %get-tuple-element.52), calls=%async_computation.2 | async-start | bytes 131072 | tf_op jit(solution)/shard_map/all_to_all | solution.py:371
  122.7 5.3 %multiply_convert_fusion = f16[1024,1024]{1,0:T(8,128)(2,1)} fusion(bf16[1024,1024]{1,0:T(8,128)(2,1)S(1)} %copy-done.9, bf16[1024,1024]{1,0:T(8,128)(2,1)} %get-tuple-element.66, f32[1024]{0:T(1024)S(1)} %bitcast.75), kind=kOutput, calls=%fused_computation.1 | convolution fusion | flops 2149580800 | bytes 6295552 | tf_op jit(solution)/shard_map/dot_general | solution.py:419
  129.1 6.3 %all-to-all-start.3 = ((f16[16,64,1024]{2,1,0:T(8,128)(2,1)}), f16[16,64,1024]{2,1,0:T(8,128)(2,1)S(1)}, u32[]{:S(2)}, u32[]{:S(2)}) async-start(f16[16,64,1024]{2,1,0:T(8,128)(2,1)} %bitcast.70), calls=%async_computation.3 | async-start | bytes 4194304 | tf_op jit(solution)/shard_map/all_to_all | solution.py:424
  135.3 4.6 %fusion.1 = f32[512,1024]{1,0:T(8,128)} fusion(bf16[1024,1024]{1,0:T(8,128)(2,1)} %get-tuple-element.50, bf16[1024,1024]{1,0:T(8,128)(2,1)} %get-tuple-element.49, s32[]{:T(128)S(6)} %select_n.465), kind=kOutput, calls=%fused_computation.5 | convolution fusion | flops 1073741824 | bytes 5242884 | tf_op jit(solution)/shard_map/dot_general | solution.py:426
  139.9 2.3 %add_convert_fusion = f16[512,1024]{1,0:T(8,128)(2,1)S(1)} fusion(f16[512,1024]{1,0:T(8,128)(2,1)} %collective-permute-done.15, f32[512,1024]{1,0:T(8,128)} %fusion.1, f32[1024]{0:T(1024)S(1)} %bitcast.74), kind=kLoop, calls=%fused_computation.2 | loop fusion | flops 2097152 | bytes 4198400 | tf_op jit(solution)/shard_map/convert_element_type | solution.py:428
  144.4 4.3 %collective-permute-done.16 = f16[64,1024]{1,0:T(8,128)(2,1)S(1)} collective-permute-done((f16[64,1024]{1,0:T(8,128)(2,1)S(1)}, f16[64,1024]{1,0:T(8,128)(2,1)S(1)}, u32[]{:S(2)}, u32[]{:S(2)}) %collective-permute-start.16) | collective-permute-done | bytes 131104 | tf_op jit(solution)/shard_map/ppermute | solution.py:59
  151.6 2.6 %collective-permute-done.20 = f32[8,128]{1,0:T(8,128)S(1)} collective-permute-done((f32[8,128]{1,0:T(8,128)S(1)}, f32[8,128]{1,0:T(8,128)S(1)}, u32[]{:S(2)}, u32[]{:S(2)}) %collective-permute-start.20) | collective-permute-done | bytes 4128 | tf_op jit(solution)/shard_map/ppermute | solution.py:59
  158.5 4.0 %collective-permute-done.23 = f32[8,128]{1,0:T(8,128)S(1)} collective-permute-done((f32[8,128]{1,0:T(8,128)S(1)}, f32[8,128]{1,0:T(8,128)S(1)}, u32[]{:S(2)}, u32[]{:S(2)}) %collective-permute-start.23) | collective-permute-done | bytes 4128 | tf_op jit(solution)/shard_map/ppermute | solution.py:59
  168.0 2.7 %collective-permute-start.26 = (f32[8,128]{1,0:T(8,128)S(1)}, f32[8,128]{1,0:T(8,128)S(1)}, u32[]{:S(2)}, u32[]{:S(2)}) collective-permute-start(f32[8,128]{1,0:T(8,128)S(1)} %add.784), channel_id=1, source_target_pairs={{0,4},{1,5},{2,6},{3,7},{4,0},{5,1},{6,2},{7,3},{8,12},{9,13},{10,... | collective-permute-start | bytes 12296 | tf_op jit(solution)/shard_map/ppermute | solution.py:59
  170.7 4.8 %collective-permute-done.26 = f32[8,128]{1,0:T(8,128)S(1)} collective-permute-done((f32[8,128]{1,0:T(8,128)S(1)}, f32[8,128]{1,0:T(8,128)S(1)}, u32[]{:S(2)}, u32[]{:S(2)}) %collective-permute-start.26) | collective-permute-done | bytes 4128 | tf_op jit(solution)/shard_map/ppermute | solution.py:59
  (99 shorter events, 45.5 us)
Async XLA Ops:
  2.5 7.7 %collective-permute-start = (bf16[64,2048]{1,0:T(8,128)(2,1)S(1)}, bf16[64,2048]{1,0:T(8,128)(2,1)S(1)}, u32[]{:S(2)}, u32[]{:S(2)}) collective-permute-start(bf16[64,2048]{1,0:T(8,128)(2,1)S(1)} %constant_dynamic-update-slice_fusion), channel_id=1, source_target_pairs={{0,8},{1,65},{2,10},{3,67},{4,12},{5,69},{6,14},{7,71},{8,16},{9,7... | collective-permute-start | bytes 786440 | tf_op jit(solution)/shard_map/ppermute | solution.py:59
  4.0 6.4 %collective-permute-start.1 = (bf16[64,2048]{1,0:T(8,128)(2,1)S(1)}, bf16[64,2048]{1,0:T(8,128)(2,1)S(1)}, u32[]{:S(2)}, u32[]{:S(2)}) collective-permute-start(bf16[64,2048]{1,0:T(8,128)(2,1)S(1)} %constant_dynamic-update-slice_fusion), channel_id=1, source_target_pairs={{0,24},{1,193},{2,26},{3,195},{4,28},{5,197},{6,30},{7,199},{8,0},... | collective-permute-start | bytes 786440 | tf_op jit(solution)/shard_map/ppermute | solution.py:59
  10.4 7.6 %collective-permute-start.3 = (bf16[64,2048]{1,0:T(8,128)(2,1)S(1)}, bf16[64,2048]{1,0:T(8,128)(2,1)S(1)}, u32[]{:S(2)}, u32[]{:S(2)}) collective-permute-start(bf16[64,2048]{1,0:T(8,128)(2,1)S(1)} %collective-permute-done), channel_id=1, source_target_pairs={{0,8},{1,65},{2,10},{3,67},{4,12},{5,69},{6,14},{7,71},{8,16},{9,7... | collective-permute-start | bytes 786440 | tf_op jit(solution)/shard_map/ppermute | solution.py:59
  12.0 13.1 %collective-permute-start.6 = (bf16[128,2048]{1,0:T(8,128)(2,1)S(1)}, bf16[128,2048]{1,0:T(8,128)(2,1)S(1)}, u32[]{:S(2)}, u32[]{:S(2)}) collective-permute-start(bf16[128,2048]{1,0:T(8,128)(2,1)S(1)} %pad_maximum_fusion.refs_6_), channel_id=1, source_target_pairs={{0,32},{1,39},{2,34},{3,33},{4,36},{5,35},{6,38},{7,37},{8,40},{9,... | collective-permute-start | bytes 1572872 | tf_op jit(solution)/shard_map/ppermute | solution.py:59
  25.1 10.4 %collective-permute-start.7 = (bf16[128,2048]{1,0:T(8,128)(2,1)S(1)}, bf16[128,2048]{1,0:T(8,128)(2,1)S(1)}, u32[]{:S(2)}, u32[]{:S(2)}) collective-permute-start(bf16[128,2048]{1,0:T(8,128)(2,1)S(1)} %collective-permute-done.6), channel_id=1, source_target_pairs={{0,32},{1,39},{2,34},{3,33},{4,36},{5,35},{6,38},{7,37},{8,40},{9,... | collective-permute-start | bytes 1572872 | tf_op jit(solution)/shard_map/ppermute | solution.py:59
  25.1 14.9 %collective-permute-start.4 = (bf16[256,2048]{1,0:T(8,128)(2,1)S(1)}, bf16[256,2048]{1,0:T(8,128)(2,1)S(1)}, u32[]{:S(2)}, u32[]{:S(2)}) collective-permute-start(bf16[256,2048]{1,0:T(8,128)(2,1)S(1)} %constant_dynamic-update-slice_fusion.4.refs_1_), channel_id=1, source_target_pairs={{0,64},{1,9},{2,66},{3,11},{4,68},{5,13},{6,70},{7,15},{8,72},{9,1... | collective-permute-start | bytes 3145736 | tf_op jit(solution)/shard_map/ppermute | solution.py:59
  26.8 14.8 %collective-permute-start.5 = (bf16[256,2048]{1,0:T(8,128)(2,1)S(1)}, bf16[256,2048]{1,0:T(8,128)(2,1)S(1)}, u32[]{:S(2)}, u32[]{:S(2)}) collective-permute-start(bf16[256,2048]{1,0:T(8,128)(2,1)S(1)} %constant_dynamic-update-slice_fusion.4.refs_1_), channel_id=1, source_target_pairs={{0,192},{1,25},{2,194},{3,27},{4,196},{5,29},{6,198},{7,31},{8,200... | collective-permute-start | bytes 3145736 | tf_op jit(solution)/shard_map/ppermute | solution.py:59
  35.4 10.5 %collective-permute-start.8 = (bf16[128,2048]{1,0:T(8,128)(2,1)S(1)}, bf16[128,2048]{1,0:T(8,128)(2,1)}, u32[]{:S(2)}, u32[]{:S(2)}) collective-permute-start(bf16[128,2048]{1,0:T(8,128)(2,1)S(1)} %collective-permute-done.7), channel_id=1, source_target_pairs={{0,32},{1,39},{2,34},{3,33},{4,36},{5,35},{6,38},{7,37},{8,40},{9,... | collective-permute-start | bytes 1572872 | tf_op jit(solution)/shard_map/ppermute | solution.py:59
  36.3 20.0 %collective-permute-start.11 = (bf16[256,2048]{1,0:T(8,128)(2,1)}, bf16[256,2048]{1,0:T(8,128)(2,1)}, u32[]{:S(2)}, u32[]{:S(2)}) collective-permute-start(bf16[256,2048]{1,0:T(8,128)(2,1)} %constant_dynamic-update-slice_fusion.8.refs_7_), channel_id=1, source_target_pairs={{0,1},{1,0},{2,3},{3,2},{4,5},{5,4},{6,7},{7,6},{8,9},{9,8},{10,11... | collective-permute-start | bytes 3145736 | tf_op jit(solution)/shard_map/ppermute | solution.py:59
  46.9 9.4 %collective-permute-start.12 = (bf16[128,2048]{1,0:T(8,128)(2,1)}, bf16[128,2048]{1,0:T(8,128)(2,1)}, u32[]{:S(2)}, u32[]{:S(2)}) collective-permute-start(bf16[128,2048]{1,0:T(8,128)(2,1)} %collective-permute-done.8.refs_9_), channel_id=1, source_target_pairs={{0,1},{1,0},{2,3},{3,2},{4,5},{5,4},{6,7},{7,6},{8,9},{9,8},{10,11... | collective-permute-start | bytes 1572872 | tf_op jit(solution)/shard_map/ppermute | solution.py:59
  47.0 7.7 %collective-permute-start.13 = (bf16[64,2048]{1,0:T(8,128)(2,1)S(1)}, bf16[64,2048]{1,0:T(8,128)(2,1)S(1)}, u32[]{:S(2)}, u32[]{:S(2)}) collective-permute-start(bf16[64,2048]{1,0:T(8,128)(2,1)S(1)} %slice.26), channel_id=1, source_target_pairs={{0,32},{1,39},{2,34},{3,33},{4,36},{5,35},{6,38},{7,37},{8,40},{9,... | collective-permute-start | bytes 786440 | tf_op jit(solution)/shard_map/ppermute | solution.py:59
  47.2 9.4 %collective-permute-start.10 = (bf16[128,2048]{1,0:T(8,128)(2,1)S(1)}, bf16[128,2048]{1,0:T(8,128)(2,1)}, u32[]{:S(2)}, u32[]{:S(2)}) collective-permute-start(bf16[128,2048]{1,0:T(8,128)(2,1)S(1)} %slice.25), channel_id=1, source_target_pairs={{0,192},{1,25},{2,194},{3,27},{4,196},{5,29},{6,198},{7,31},{8,200... | collective-permute-start | bytes 1572872 | tf_op jit(solution)/shard_map/ppermute | solution.py:59
  47.7 10.4 %collective-permute-start.9 = (bf16[128,2048]{1,0:T(8,128)(2,1)S(1)}, bf16[128,2048]{1,0:T(8,128)(2,1)}, u32[]{:S(2)}, u32[]{:S(2)}) collective-permute-start(bf16[128,2048]{1,0:T(8,128)(2,1)S(1)} %slice.24), channel_id=1, source_target_pairs={{0,64},{1,9},{2,66},{3,11},{4,68},{5,13},{6,70},{7,15},{8,72},{9,1... | collective-permute-start | bytes 1572872 | tf_op jit(solution)/shard_map/ppermute | solution.py:59
  73.6 13.9 %all-to-all-start.1 = ((f32[16,2,1152]{2,1,0:T(2,128)}), f32[16,2,1152]{2,1,0:T(2,128)S(1)}, u32[]{:S(2)}, u32[]{:S(2)}) async-start(f32[16,2,1152]{2,1,0:T(2,128)} %get-tuple-element.48), calls=%async_computation.1 | async-start | bytes 294912 | tf_op jit(solution)/shard_map/all_to_all | solution.py:371
  87.5 15.7 %all-to-all-start = ((f32[16,2,1152]{2,1,0:T(2,128)}), f32[16,2,1152]{2,1,0:T(2,128)S(1)}, u32[]{:S(2)}, u32[]{:S(2)}) async-start(f32[16,2,1152]{2,1,0:T(2,128)} %get-tuple-element.47), calls=%async_computation | async-start | bytes 294912 | tf_op jit(solution)/shard_map/all_to_all | solution.py:371
  117.0 22.9 %collective-permute-start.15 = (f16[512,1024]{1,0:T(8,128)(2,1)}, f16[512,1024]{1,0:T(8,128)(2,1)}, u32[]{:S(2)}, u32[]{:S(2)}) collective-permute-start(f16[512,1024]{1,0:T(8,128)(2,1)} %multiply_convert_fusion.1), channel_id=1, source_target_pairs={{0,1},{1,0},{2,3},{3,2},{4,5},{5,4},{6,7},{7,6},{8,9},{9,8},{10,11... | collective-permute-start | bytes 3145736 | tf_op jit(solution)/shard_map/ppermute | solution.py:59
  117.7 11.4 %all-to-all-start.2 = ((f32[16,8,128]{2,1,0:T(8,128)}), f32[16,8,128]{2,1,0:T(8,128)S(1)}, u32[]{:S(2)}, u32[]{:S(2)}) async-start(f32[16,8,128]{2,1,0:T(8,128)} %get-tuple-element.52), calls=%async_computation.2 | async-start | bytes 131072 | tf_op jit(solution)/shard_map/all_to_all | solution.py:371
  129.1 48.4 %all-to-all-start.3 = ((f16[16,64,1024]{2,1,0:T(8,128)(2,1)}), f16[16,64,1024]{2,1,0:T(8,128)(2,1)S(1)}, u32[]{:S(2)}, u32[]{:S(2)}) async-start(f16[16,64,1024]{2,1,0:T(8,128)(2,1)} %bitcast.70), calls=%async_computation.3 | async-start | bytes 4194304 | tf_op jit(solution)/shard_map/all_to_all | solution.py:424
  142.3 6.4 %collective-permute-start.16 = (f16[64,1024]{1,0:T(8,128)(2,1)S(1)}, f16[64,1024]{1,0:T(8,128)(2,1)S(1)}, u32[]{:S(2)}, u32[]{:S(2)}) collective-permute-start(f16[64,1024]{1,0:T(8,128)(2,1)S(1)} %get-tuple-element.54), channel_id=1, source_target_pairs={{0,38},{1,33},{2,32},{3,35},{4,34},{5,37},{6,36},{7,39},{8,46},{9,... | collective-permute-start | bytes 393224 | tf_op jit(solution)/shard_map/ppermute | solution.py:59
  142.8 8.8 %collective-permute-start.19 = (f16[64,1024]{1,0:T(8,128)(2,1)S(1)}, f16[64,1024]{1,0:T(8,128)(2,1)}, u32[]{:S(2)}, u32[]{:S(2)}) collective-permute-start(f16[64,1024]{1,0:T(8,128)(2,1)S(1)} %get-tuple-element.71), channel_id=1, source_target_pairs={{0,32},{1,39},{2,34},{3,33},{4,36},{5,35},{6,38},{7,37},{8,40},{9,... | collective-permute-start | bytes 393224 | tf_op jit(solution)/shard_map/ppermute | solution.py:59
  155.2 7.3 %collective-permute-start.21 = (f16[64,1024]{1,0:T(8,128)(2,1)S(1)}, f16[64,1024]{1,0:T(8,128)(2,1)S(1)}, u32[]{:S(2)}, u32[]{:S(2)}) collective-permute-start(f16[64,1024]{1,0:T(8,128)(2,1)S(1)} %get-tuple-element.70), channel_id=1, source_target_pairs={{0,38},{1,33},{2,32},{3,35},{4,34},{5,37},{6,36},{7,39},{8,46},{9,... | collective-permute-start | bytes 393224 | tf_op jit(solution)/shard_map/ppermute | solution.py:59
  165.1 10.4 %collective-permute-start.24 = (f16[64,1024]{1,0:T(8,128)(2,1)}, f16[64,1024]{1,0:T(8,128)(2,1)S(1)}, u32[]{:S(2)}, u32[]{:S(2)}) collective-permute-start(f16[64,1024]{1,0:T(8,128)(2,1)} %get-tuple-element.68), channel_id=1, source_target_pairs={{0,38},{1,33},{2,32},{3,35},{4,34},{5,37},{6,36},{7,39},{8,46},{9,... | collective-permute-start | bytes 393224 | tf_op jit(solution)/shard_map/ppermute | solution.py:59
  167.3 8.2 %collective-permute-start.25 = (f16[64,1024]{1,0:T(8,128)(2,1)S(1)}, f16[64,1024]{1,0:T(8,128)(2,1)S(1)}, u32[]{:S(2)}, u32[]{:S(2)}) collective-permute-start(f16[64,1024]{1,0:T(8,128)(2,1)S(1)} %get-tuple-element.67), channel_id=1, source_target_pairs={{0,32},{1,39},{2,34},{3,33},{4,36},{5,35},{6,38},{7,37},{8,40},{9,... | collective-permute-start | bytes 393224 | tf_op jit(solution)/shard_map/ppermute | solution.py:59
  168.0 7.5 %collective-permute-start.26 = (f32[8,128]{1,0:T(8,128)S(1)}, f32[8,128]{1,0:T(8,128)S(1)}, u32[]{:S(2)}, u32[]{:S(2)}) collective-permute-start(f32[8,128]{1,0:T(8,128)S(1)} %add.784), channel_id=1, source_target_pairs={{0,4},{1,5},{2,6},{3,7},{4,0},{5,1},{6,2},{7,3},{8,12},{9,13},{10,... | collective-permute-start | bytes 12296 | tf_op jit(solution)/shard_map/ppermute | solution.py:59
  (19 other events, 158.3 us)

commit v5 on v4

--- a/solution.py
+++ b/solution.py
@@ -75,30 +75,59 @@
     return shifted(p, "c", 1)
 
 
+def joined_halves(*halves):
+    def kernel(*refs):
+        sems = refs[6]
+        copies = [
+            pltpu.make_async_copy(
+                refs[k], refs[4 + k // 2].at[:, pl.ds(k % 2 * WIDTH, WIDTH)], sems.at[k]
+            )
+            for k in range(4)
+        ]
+        for copy in copies:
+            copy.start()
+        for copy in copies:
+            copy.wait()
+
+    anywhere = pl.BlockSpec(memory_space=pl.ANY)
+    pair = jax.ShapeDtypeStruct((BLOCK, 2 * WIDTH), jnp.bfloat16)
+    return pl.pallas_call(
+        kernel,
+        out_shape=(pair, pair),
+        in_specs=[anywhere] * 4,
+        out_specs=(anywhere,) * 2,
+        scratch_shapes=[pltpu.SemaphoreType.DMA((4,))],
+        cost_estimate=pl.CostEstimate(flops=0, bytes_accessed=1 << 20, transcendentals=0),
+    )(*halves)
+
+
 def gathered(text, image):
     tie = lax.optimization_barrier
     back, ahead = moved(text, along_u(1)), moved(text, along_u(-1))
-    partner = moved(image, other_core)
-    back, ahead, partner = tie((back, ahead, partner))
-
-    far = moved(back, along_u(1))
-    chain = [jnp.concatenate([image, partner], axis=0)]
-    chain.append(moved(chain[0], along_z(1)))
-    far, text, back, ahead = tie((far, text, back, ahead))
+    far = moved(text, along_u(2))
+    mine = [image, moved(image, along_z(1))]
+    theirs = [moved(image, other_core)]
+    back, ahead, far, mine[1], theirs[0] = tie((back, ahead, far, mine[1], theirs[0]))
 
     line = jnp.concatenate([text, back, ahead, far], axis=0)
+    line, mine[1], theirs[0] = tie((line, mine[1], theirs[0]))
     line_back, line_ahead = moved(line, along_v(1)), moved(line, along_v(-1))
-    chain.append(moved(chain[1], along_z(1)))
-    chain.append(moved(chain[2], along_z(1)))
-    both = jnp.concatenate([chain[1], chain[2]], axis=0)
-    both_other = moved(both, other_core)
-    line_back, line_ahead, chain[3] = tie((line_back, line_ahead, chain[3]))
+    mine.append(moved(mine[1], along_z(1)))
+    theirs.append(moved(theirs[0], along_z(1)))
+    mine[2], theirs[1] = tie((mine[2], theirs[1]))
+    mine.append(moved(mine[2], along_z(1)))
+    theirs.append(moved(theirs[1], along_z(1)))
+    line_back, line_ahead, mine[3], theirs[2] = tie((line_back, line_ahead, mine[3], theirs[2]))
 
     first_far = moved(line_back[:128], along_v(1))
     second_far = moved(line_ahead[128:], along_v(-1))
-    distant = moved(chain[3][:64], along_z(1))
-    third_other = moved(chain[3], other_core)
-    distant_other = moved(distant, other_core)
+    mine.append(moved(mine[3], along_z(1)))
+    theirs.append(moved(theirs[2], along_z(1)))
+    early = jnp.concatenate([mine[1], mine[2], mine[3], theirs[1], theirs[2]], axis=0)
+    early_other = moved(early, other_core)
+    mine[4], theirs[3] = tie((mine[4], theirs[3]))
+    late = jnp.concatenate([mine[4], theirs[3]], axis=0)
+    late_other = moved(late, other_core)
     us = (0, -1, 1, 2)
     return [
         (line, [(du, 0) for du in us]),
@@ -107,13 +136,12 @@
         (first_far, ((0, 2), (-1, 2))),
         (second_far, ((1, 2), (2, 2))),
     ], [
-        (chain[0], ((0, 0), (1, 0))),
-        (both, ((0, -1), (1, -1), (0, -2), (1, -2))),
-        (both_other, ((1, 1), (0, 1), (1, 2), (0, 2))),
-        (chain[3], ((0, -3), (1, -3))),
-        (third_other, ((1, 3), (0, 3))),
-        (distant, ((0, 4),)),
-        (distant_other, ((1, 4),)),
+        (image, ((0, 0),)),
+        (theirs[0], ((1, 0),)),
+        (early, ((0, -1), (0, -2), (0, -3), (1, -1), (1, -2))),
+        (early_other, ((1, 1), (1, 2), (1, 3), (0, 1), (0, 2))),
+        (late, ((0, 4), (1, -3))),
+        (late_other, ((1, 4), (0, 3))),
     ]
 
 
@@ -375,8 +403,7 @@
     y, zl, x, zh, c = (lax.axis_index(n) for n in NAMES)
     z = zh * 2 + zl
     text_pieces, image_pieces = gathered(
-        jnp.concatenate([text_student, text_teacher], axis=1),
-        jnp.concatenate([image_student, image_teacher], axis=1),
+        *joined_halves(text_student, text_teacher, image_student, image_teacher)
     )
 
     sign = 1 - 2 * c
@@ -437,19 +464,19 @@
 
     tie = lax.optimization_barrier
     steps = [other_core] + [lambda p, k=k: flipped(p, k) for k in (1, 2, 4)]
+    value, blocks = tie((value + moved(value, steps[0]), blocks))
     start, value = tie((narrow(block(4)), value))
-    down, other = tie((moved(start, along_z(-1)), moved(value, steps[0])))
-    value = value + other
-    down = down.astype(jnp.float32)
+    down = moved(start, along_z(-1)).astype(jnp.float32)
+    value = value + moved(value, steps[1])
     up = None
     for k in (3, 2, 1):
         first = narrow(block(-k) + down)
         second = narrow(block(k) if up is None else block(k) + up)
-        down, up, other = tie(
-            (moved(first, along_z(-1)), moved(second, along_z(1)), moved(value, steps[4 - k]))
-        )
-        value = value + other
-        down, up = down.astype(jnp.float32), up.astype(jnp.float32)
+        first, second, value = tie((first, second, value))
+        down = moved(first, along_z(-1)).astype(jnp.float32)
+        up = moved(second, along_z(1)).astype(jnp.float32)
+        if k > 1:
+            value = value + moved(value, steps[5 - k])
     loss = value[0, 0] / (256 * BLOCK)
     image_grad = (block(0) + down + up) * image_factor
     text_grad = jnp.sum(text_blocks.astype(jnp.float32), axis=0) * text_factor

time: 181 us -> 191 us (1.055)
  Pallas kernels: 24 us -> 41 us
  local copies, waits for them, and re-layouts: 9.39 us -> 3.08 us
  starting transfers between devices: 49 us -> 51.6 us
  waiting for transfers between devices: 70.3 us -> 67.8 us
    pallas_call x0 -> x1, Pallas kernels: none -> 17 us  [joined_halves(): pl.pallas_call(kernel, out_shape=(pair, pair), in_specs=[anywhere] * 4, o...]
    ppermute x27 -> x29, starting transfers between devices: 23.7 us -> 27.9 us  [moved(): return lax.ppermute(value, NAMES, pairs)]
    concatenate x4 -> x2, local copies, waits for them, and re-layouts: 2.72 us -> 0.04 us  [the longest x1 0.02 us: gathered(): jnp.concatenate([mine[1], mine[2], mine[3], theirs[1], theirs[2]], axis=0)]
    unnamed x30 -> x27, local copies, waits for them, and re-layouts: 3.42 us -> 0.88 us
    ppermute x27 -> x29, waiting for transfers between devices: 55.5 us -> 53 us  [moved(): return lax.ppermute(value, NAMES, pairs)]
  transfers between devices with their start and end apart: 31 -> 33, of which waited for: 20 -> 18; matrix products, arithmetic and copies ran while one was open for 14% -> 10% of each run, Pallas kernels for 0% -> 0%
where the time goes in v5:
time: 191 us
  waiting for transfers between devices  67.8 us (35%)
  starting transfers between devices  51.6 us (27%)
  Pallas kernels  41 us (21%)
  matrix products  12.1 us (6%)
  other arithmetic  11.5 us (6%)
  between operations  3.45 us (2%)
  local copies, waits for them, and re-layouts  3.08 us (2%)
    ppermute x29, waiting for transfers between devices, moved(): return lax.ppermute(value, NAMES, pairs)  53 us
    ppermute x29, starting transfers between devices, moved(): return lax.ppermute(value, NAMES, pairs)  27.9 us
    all_to_all x3, starting transfers between devices, exchanged(): return lax.all_to_all(copies, axis, split_axis=0, concat_axis=0, tiled=True)  17.5 us
    pallas_call x1, Pallas kernels, joined_halves(): pl.pallas_call(kernel, out_shape=(pair, pair), in_specs=[anywhere] * 4, o...  17 us
    pallas_call x1, Pallas kernels, logits_and_statistics(): pl.pallas_call(kernel, out_shape=(square, square, half, half, small, smal...  15.4 us
    all_to_all x3, waiting for transfers between devices, exchanged(): return lax.all_to_all(copies, axis, split_axis=0, concat_axis=0, tiled=True)  14.7 us
    pallas_call x1, Pallas kernels, gradient_of_logits(): pl.pallas_call(gradient_kernel, grid=(SIDE // ROWS,), out_shape=(jax.Shap...  8.57 us
    all_to_all x1, starting transfers between devices, body(): lax.all_to_all(text_part.reshape(16, BLOCK, WIDTH), TEXT_GROUP, 0, 0, til...  6.27 us
  transfers between devices with their start and end apart: 33, of which 18 were waited for; matrix products, arithmetic and copies ran while one was open for 10% of the time, Pallas kernels for 0%

profile of v5, /device:TPU:8, one launch (start us, length us, event | category | flops | bytes accessed | tf_op | source)
XLA Modules:
  0.0 190.6 jit_solution(3630548459534544540)
XLA Ops:
  0.6 17.0 %shard_map.67 = (bf16[64,2048]{1,0:T(8,128)(2,1)}, bf16[64,2048]{1,0:T(8,128)(2,1)}) custom-call(bf16[64,1024]{1,0:T(8,128)(2,1)} %refs_0_.1, bf16[64,1024]{1,0:T(8,128)(2,1)} %refs_1_.1, bf16[64,1024]{1,0:T(8,128)(2,1)} %refs_2_.1, bf16[64,1024]{1,0:T(8,128)(2,1)} %refs_3_.1), custom_call_target="tpu_custom_call" | custom-call | bytes 1048576 | tf_op jit(solution)/shard_map/pallas_call | solution.py:94
  29.3 3.9 %collective-permute-done.3 = bf16[64,2048]{1,0:T(8,128)(2,1)S(1)} collective-permute-done((bf16[64,2048]{1,0:T(8,128)(2,1)}, bf16[64,2048]{1,0:T(8,128)(2,1)S(1)}, u32[]{:S(2)}, u32[]{:S(2)}) %collective-permute-start.3) | collective-permute-done | bytes 262176 | tf_op jit(solution)/shard_map/ppermute | solution.py:59
  36.4 7.6 %collective-permute-done.7 = bf16[64,2048]{1,0:T(8,128)(2,1)S(1)} collective-permute-done((bf16[64,2048]{1,0:T(8,128)(2,1)S(1)}, bf16[64,2048]{1,0:T(8,128)(2,1)S(1)}, u32[]{:S(2)}, u32[]{:S(2)}) %collective-permute-start.7) | collective-permute-done | bytes 262176 | tf_op jit(solution)/shard_map/ppermute | solution.py:59
  44.0 2.8 %collective-permute-done.8 = bf16[64,2048]{1,0:T(8,128)(2,1)S(1)} collective-permute-done((bf16[64,2048]{1,0:T(8,128)(2,1)S(1)}, bf16[64,2048]{1,0:T(8,128)(2,1)S(1)}, u32[]{:S(2)}, u32[]{:S(2)}) %collective-permute-start.8) | collective-permute-done | bytes 262176 | tf_op jit(solution)/shard_map/ppermute | solution.py:59
  46.9 7.5 %collective-permute-done.10 = bf16[64,2048]{1,0:T(8,128)(2,1)S(1)} collective-permute-done((bf16[64,2048]{1,0:T(8,128)(2,1)S(1)}, bf16[64,2048]{1,0:T(8,128)(2,1)S(1)}, u32[]{:S(2)}, u32[]{:S(2)}) %collective-permute-start.10) | collective-permute-done | bytes 262176 | tf_op jit(solution)/shard_map/ppermute | solution.py:59
  54.4 2.8 %collective-permute-done.9 = bf16[64,2048]{1,0:T(8,128)(2,1)S(1)} collective-permute-done((bf16[64,2048]{1,0:T(8,128)(2,1)S(1)}, bf16[64,2048]{1,0:T(8,128)(2,1)S(1)}, u32[]{:S(2)}, u32[]{:S(2)}) %collective-permute-start.9) | collective-permute-done | bytes 262176 | tf_op jit(solution)/shard_map/ppermute | solution.py:59
  59.9 5.2 %collective-permute-done.14 = bf16[64,2048]{1,0:T(8,128)(2,1)S(1)} collective-permute-done((bf16[64,2048]{1,0:T(8,128)(2,1)S(1)}, bf16[64,2048]{1,0:T(8,128)(2,1)S(1)}, u32[]{:S(2)}, u32[]{:S(2)}) %collective-permute-start.14) | collective-permute-done | bytes 262176 | tf_op jit(solution)/shard_map/ppermute | solution.py:59
  70.4 15.4 %shard_map.68 = (f32[1024,1024]{1,0:T(8,128)}, f32[1024,1024]{1,0:T(8,128)}, bf16[1024,1024]{1,0:T(8,128)(2,1)}, bf16[1024,1024]{1,0:T(8,128)(2,1)}, f32[16,2,1152]{2,1,0:T(2,128)}, /*index=5*/f32[16,2,1152]{2,1,0:T(2,128)}) custom-call(s32[32]{0:T(128)} %stack.131.refs_0_, bf16[256,2048]{1,0:T(8,128)(2,1)} %copy-done, bf16[256,2048]{1,0:T(8,128)(2,1)} %copy-done.3, ...), custom_call_target="tpu_custom_call" | custom-call | flops 4294967296 | bytes 20971520 | tf_op jit(solution)/shard_map/pallas_call | solution.py:273
  85.9 6.1 %all-to-all-start.1 = ((f32[16,2,1152]{2,1,0:T(2,128)}), f32[16,2,1152]{2,1,0:T(2,128)S(1)}, u32[]{:S(2)}, u32[]{:S(2)}) async-start(f32[16,2,1152]{2,1,0:T(2,128)} %get-tuple-element.64), calls=%async_computation.1 | async-start | bytes 294912 | tf_op jit(solution)/shard_map/all_to_all | solution.py:399
  92.0 6.3 %all-to-all-done.1.col_ref = f32[16,2,1152]{2,1,0:T(2,128)S(1)} async-done(((f32[16,2,1152]{2,1,0:T(2,128)}), f32[16,2,1152]{2,1,0:T(2,128)S(1)}, u32[]{:S(2)}, u32[]{:S(2)}) %all-to-all-start.1) | async-done | bytes 147488 | tf_op jit(solution)/shard_map/all_to_all | solution.py:399
  98.3 6.3 %all-to-all-start = ((f32[16,2,1152]{2,1,0:T(2,128)}), f32[16,2,1152]{2,1,0:T(2,128)S(1)}, u32[]{:S(2)}, u32[]{:S(2)}) async-start(f32[16,2,1152]{2,1,0:T(2,128)} %get-tuple-element.63), calls=%async_computation | async-start | bytes 294912 | tf_op jit(solution)/shard_map/all_to_all | solution.py:399
  106.4 7.4 %all-to-all-done.row_ref = f32[16,2,1152]{2,1,0:T(2,128)S(1)} async-done(((f32[16,2,1152]{2,1,0:T(2,128)}), f32[16,2,1152]{2,1,0:T(2,128)S(1)}, u32[]{:S(2)}, u32[]{:S(2)}) %all-to-all-start) | async-done | bytes 147488 | tf_op jit(solution)/shard_map/all_to_all | solution.py:399
  114.5 8.6 %shard_map.69 = (bf16[1024,1024]{1,0:T(8,128)(2,1)}, f32[8,1024]{1,0:T(8,128)}, f32[16,8,128]{2,1,0:T(8,128)}) custom-call(f32[1024,1024]{1,0:T(8,128)} %get-tuple-element.61.s_ref, f32[1024,1024]{1,0:T(8,128)} %get-tuple-element.62.t_ref, f32[16,2,1152]{2,1,0:T(2,128)} %copy-done.2, f32[16,2,1152]{2,1,0:T(2,128)} %copy-done.1, ...), custom_call_target="tpu_custom_call" | custom-call | flops 16777216 | bytes 10485760 | tf_op jit(solution)/shard_map/pallas_call | solution.py:373
  124.0 3.6 %multiply_convert_fusion.1 = f16[512,1024]{1,0:T(8,128)(2,1)} fusion(bf16[1024,1024]{1,0:T(8,128)(2,1)S(1)} %copy-done.10, bf16[1024,1024]{1,0:T(8,128)(2,1)} %get-tuple-element.66, s32[]{:T(128)S(6)} %select_n.466, f32[1024]{0:T(1024)S(1)} %bitcast.73), kind=kOutput, calls=%fused_computation.3 | convolution fusion | flops 1074790400 | bytes 4198404 | tf_op jit(solution)/shard_map/dot_general | solution.py:443
  128.3 5.1 %all-to-all-start.2 = ((f32[16,8,128]{2,1,0:T(8,128)}), f32[16,8,128]{2,1,0:T(8,128)S(1)}, u32[]{:S(2)}, u32[]{:S(2)}) async-start(f32[16,8,128]{2,1,0:T(8,128)} %get-tuple-element.65), calls=%async_computation.2 | async-start | bytes 131072 | tf_op jit(solution)/shard_map/all_to_all | solution.py:399
  133.4 5.3 %multiply_convert_fusion = f16[1024,1024]{1,0:T(8,128)(2,1)} fusion(bf16[1024,1024]{1,0:T(8,128)(2,1)S(1)} %copy-done.7, bf16[1024,1024]{1,0:T(8,128)(2,1)} %get-tuple-element.82, f32[1024]{0:T(1024)S(1)} %bitcast.75), kind=kOutput, calls=%fused_computation.1 | convolution fusion | flops 2149580800 | bytes 6295552 | tf_op jit(solution)/shard_map/dot_general | solution.py:446
  139.7 6.3 %all-to-all-start.3 = ((f16[16,64,1024]{2,1,0:T(8,128)(2,1)}), f16[16,64,1024]{2,1,0:T(8,128)(2,1)S(1)}, u32[]{:S(2)}, u32[]{:S(2)}) async-start(f16[16,64,1024]{2,1,0:T(8,128)(2,1)} %bitcast.70), calls=%async_computation.3 | async-start | bytes 4194304 | tf_op jit(solution)/shard_map/all_to_all | solution.py:451
  146.1 3.2 %fusion.1 = f32[512,1024]{1,0:T(8,128)S(1)} fusion(bf16[1024,1024]{1,0:T(8,128)(2,1)} %get-tuple-element.67, bf16[1024,1024]{1,0:T(8,128)(2,1)} %get-tuple-element.66, s32[]{:T(128)S(6)} %select_n.465), kind=kOutput, calls=%fused_computation.6 | convolution fusion | flops 1073741824 | bytes 5242884 | tf_op jit(solution)/shard_map/dot_general | solution.py:453
  153.3 3.1 %collective-permute-done.20 = f32[8,128]{1,0:T(8,128)} collective-permute-done((f32[8,128]{1,0:T(8,128)S(1)}, f32[8,128]{1,0:T(8,128)}, u32[]{:S(2)}, u32[]{:S(2)}) %collective-permute-start.20) | collective-permute-done | bytes 4128 | tf_op jit(solution)/shard_map/ppermute | solution.py:59
  159.8 4.0 %collective-permute-done.23 = f32[8,128]{1,0:T(8,128)} collective-permute-done((f32[8,128]{1,0:T(8,128)S(1)}, f32[8,128]{1,0:T(8,128)}, u32[]{:S(2)}, u32[]{:S(2)}) %collective-permute-start.23) | collective-permute-done | bytes 4128 | tf_op jit(solution)/shard_map/ppermute | solution.py:59
  167.7 2.9 %collective-permute-start.26 = (f32[8,128]{1,0:T(8,128)S(1)}, f32[8,128]{1,0:T(8,128)}, u32[]{:S(2)}, u32[]{:S(2)}) collective-permute-start(f32[8,128]{1,0:T(8,128)S(1)} %add.785), channel_id=1, source_target_pairs={{0,4},{1,5},{2,6},{3,7},{4,0},{5,1},{6,2},{7,3},{8,12},{9,13},{10,... | collective-permute-start | bytes 12296 | tf_op jit(solution)/shard_map/ppermute | solution.py:59
  170.5 4.7 %collective-permute-done.26 = f32[8,128]{1,0:T(8,128)} collective-permute-done((f32[8,128]{1,0:T(8,128)S(1)}, f32[8,128]{1,0:T(8,128)}, u32[]{:S(2)}, u32[]{:S(2)}) %collective-permute-start.26) | collective-permute-done | bytes 4128 | tf_op jit(solution)/shard_map/ppermute | solution.py:59
  177.0 3.3 %collective-permute-start.27 = (f16[64,1024]{1,0:T(8,128)(2,1)S(1)}, f16[64,1024]{1,0:T(8,128)(2,1)S(1)}, u32[]{:S(2)}, u32[]{:S(2)}) collective-permute-start(f16[64,1024]{1,0:T(8,128)(2,1)S(1)} %get-tuple-element.80), channel_id=1, source_target_pairs={{0,38},{1,33},{2,32},{3,35},{4,34},{5,37},{6,36},{7,39},{8,46},{9,... | collective-permute-start | bytes 393224 | tf_op jit(solution)/shard_map/ppermute | solution.py:59
  182.8 3.8 %collective-permute-done.28 = f16[64,1024]{1,0:T(8,128)(2,1)} collective-permute-done((f16[64,1024]{1,0:T(8,128)(2,1)S(1)}, f16[64,1024]{1,0:T(8,128)(2,1)}, u32[]{:S(2)}, u32[]{:S(2)}) %collective-permute-start.28) | collective-permute-done | bytes 131104 | tf_op jit(solution)/shard_map/ppermute | solution.py:59
  (98 shorter events, 44.9 us)
Async XLA Ops:
  17.7 9.0 %collective-permute-start = (bf16[64,2048]{1,0:T(8,128)(2,1)}, bf16[64,2048]{1,0:T(8,128)(2,1)S(1)}, u32[]{:S(2)}, u32[]{:S(2)}) collective-permute-start(bf16[64,2048]{1,0:T(8,128)(2,1)} %get-tuple-element.43), channel_id=1, source_target_pairs={{0,8},{1,65},{2,10},{3,67},{4,12},{5,69},{6,14},{7,71},{8,16},{9,7... | collective-permute-start | bytes 786440 | tf_op jit(solution)/shard_map/ppermute | solution.py:59
  19.2 8.8 %collective-permute-start.1 = (bf16[64,2048]{1,0:T(8,128)(2,1)}, bf16[64,2048]{1,0:T(8,128)(2,1)S(1)}, u32[]{:S(2)}, u32[]{:S(2)}) collective-permute-start(bf16[64,2048]{1,0:T(8,128)(2,1)} %get-tuple-element.43), channel_id=1, source_target_pairs={{0,24},{1,193},{2,26},{3,195},{4,28},{5,197},{6,30},{7,199},{8,0},... | collective-permute-start | bytes 786440 | tf_op jit(solution)/shard_map/ppermute | solution.py:59
  21.0 8.3 %collective-permute-start.2 = (bf16[64,2048]{1,0:T(8,128)(2,1)}, bf16[64,2048]{1,0:T(8,128)(2,1)S(1)}, u32[]{:S(2)}, u32[]{:S(2)}) collective-permute-start(bf16[64,2048]{1,0:T(8,128)(2,1)} %get-tuple-element.43), channel_id=1, source_target_pairs={{0,16},{1,129},{2,18},{3,131},{4,20},{5,133},{6,22},{7,135},{8,24}... | collective-permute-start | bytes 786440 | tf_op jit(solution)/shard_map/ppermute | solution.py:59
  22.8 10.4 %collective-permute-start.3 = (bf16[64,2048]{1,0:T(8,128)(2,1)}, bf16[64,2048]{1,0:T(8,128)(2,1)S(1)}, u32[]{:S(2)}, u32[]{:S(2)}) collective-permute-start(bf16[64,2048]{1,0:T(8,128)(2,1)} %get-tuple-element.44.refs_6_), channel_id=1, source_target_pairs={{0,32},{1,39},{2,34},{3,33},{4,36},{5,35},{6,38},{7,37},{8,40},{9,... | collective-permute-start | bytes 786440 | tf_op jit(solution)/shard_map/ppermute | solution.py:59
  24.7 8.5 %collective-permute-start.4 = (bf16[64,2048]{1,0:T(8,128)(2,1)}, bf16[64,2048]{1,0:T(8,128)(2,1)S(1)}, u32[]{:S(2)}, u32[]{:S(2)}) collective-permute-start(bf16[64,2048]{1,0:T(8,128)(2,1)} %get-tuple-element.44.refs_6_), channel_id=1, source_target_pairs={{0,1},{1,0},{2,3},{3,2},{4,5},{5,4},{6,7},{7,6},{8,9},{9,8},{10,11... | collective-permute-start | bytes 786440 | tf_op jit(solution)/shard_map/ppermute | solution.py:59
  34.3 22.9 %collective-permute-start.5 = (bf16[256,2048]{1,0:T(8,128)(2,1)S(1)}, bf16[256,2048]{1,0:T(8,128)(2,1)S(1)}, u32[]{:S(2)}, u32[]{:S(2)}) collective-permute-start(bf16[256,2048]{1,0:T(8,128)(2,1)S(1)} %pad_maximum_fusion.refs_1_), channel_id=1, source_target_pairs={{0,64},{1,9},{2,66},{3,11},{4,68},{5,13},{6,70},{7,15},{8,72},{9,1... | collective-permute-start | bytes 3145736 | tf_op jit(solution)/shard_map/ppermute | solution.py:59
  36.0 21.2 %collective-permute-start.6 = (bf16[256,2048]{1,0:T(8,128)(2,1)S(1)}, bf16[256,2048]{1,0:T(8,128)(2,1)S(1)}, u32[]{:S(2)}, u32[]{:S(2)}) collective-permute-start(bf16[256,2048]{1,0:T(8,128)(2,1)S(1)} %pad_maximum_fusion.refs_1_), channel_id=1, source_target_pairs={{0,192},{1,25},{2,194},{3,27},{4,196},{5,29},{6,198},{7,31},{8,200... | collective-permute-start | bytes 3145736 | tf_op jit(solution)/shard_map/ppermute | solution.py:59
  36.4 7.6 %collective-permute-start.7 = (bf16[64,2048]{1,0:T(8,128)(2,1)S(1)}, bf16[64,2048]{1,0:T(8,128)(2,1)S(1)}, u32[]{:S(2)}, u32[]{:S(2)}) collective-permute-start(bf16[64,2048]{1,0:T(8,128)(2,1)S(1)} %collective-permute-done.3), channel_id=1, source_target_pairs={{0,32},{1,39},{2,34},{3,33},{4,36},{5,35},{6,38},{7,37},{8,40},{9,... | collective-permute-start | bytes 786440 | tf_op jit(solution)/shard_map/ppermute | solution.py:59
  36.4 10.4 %collective-permute-start.8 = (bf16[64,2048]{1,0:T(8,128)(2,1)S(1)}, bf16[64,2048]{1,0:T(8,128)(2,1)S(1)}, u32[]{:S(2)}, u32[]{:S(2)}) collective-permute-start(bf16[64,2048]{1,0:T(8,128)(2,1)S(1)} %collective-permute-done.4.refs_7_), channel_id=1, source_target_pairs={{0,32},{1,39},{2,34},{3,33},{4,36},{5,35},{6,38},{7,37},{8,40},{9,... | collective-permute-start | bytes 786440 | tf_op jit(solution)/shard_map/ppermute | solution.py:59
  46.8 7.6 %collective-permute-start.10 = (bf16[64,2048]{1,0:T(8,128)(2,1)S(1)}, bf16[64,2048]{1,0:T(8,128)(2,1)S(1)}, u32[]{:S(2)}, u32[]{:S(2)}) collective-permute-start(bf16[64,2048]{1,0:T(8,128)(2,1)S(1)} %collective-permute-done.8), channel_id=1, source_target_pairs={{0,32},{1,39},{2,34},{3,33},{4,36},{5,35},{6,38},{7,37},{8,40},{9,... | collective-permute-start | bytes 786440 | tf_op jit(solution)/shard_map/ppermute | solution.py:59
  46.8 10.4 %collective-permute-start.9 = (bf16[64,2048]{1,0:T(8,128)(2,1)S(1)}, bf16[64,2048]{1,0:T(8,128)(2,1)S(1)}, u32[]{:S(2)}, u32[]{:S(2)}) collective-permute-start(bf16[64,2048]{1,0:T(8,128)(2,1)S(1)} %collective-permute-done.7), channel_id=1, source_target_pairs={{0,32},{1,39},{2,34},{3,33},{4,36},{5,35},{6,38},{7,37},{8,40},{9,... | collective-permute-start | bytes 786440 | tf_op jit(solution)/shard_map/ppermute | solution.py:59
  57.3 13.0 %collective-permute-start.13 = (bf16[320,2048]{1,0:T(8,128)(2,1)S(1)}, bf16[320,2048]{1,0:T(8,128)(2,1)}, u32[]{:S(2)}, u32[]{:S(2)}) collective-permute-start(bf16[320,2048]{1,0:T(8,128)(2,1)S(1)} %constant_dynamic-update-slice_fusion.refs_8_), channel_id=1, source_target_pairs={{0,1},{1,0},{2,3},{3,2},{4,5},{5,4},{6,7},{7,6},{8,9},{9,8},{10,11... | collective-permute-start | bytes 3932168 | tf_op jit(solution)/shard_map/ppermute | solution.py:59
  57.4 7.7 %collective-permute-start.14 = (bf16[64,2048]{1,0:T(8,128)(2,1)S(1)}, bf16[64,2048]{1,0:T(8,128)(2,1)S(1)}, u32[]{:S(2)}, u32[]{:S(2)}) collective-permute-start(bf16[64,2048]{1,0:T(8,128)(2,1)S(1)} %collective-permute-done.9), channel_id=1, source_target_pairs={{0,32},{1,39},{2,34},{3,33},{4,36},{5,35},{6,38},{7,37},{8,40},{9,... | collective-permute-start | bytes 786440 | tf_op jit(solution)/shard_map/ppermute | solution.py:59
  57.5 10.4 %collective-permute-start.15 = (bf16[64,2048]{1,0:T(8,128)(2,1)S(1)}, bf16[64,2048]{1,0:T(8,128)(2,1)S(1)}, u32[]{:S(2)}, u32[]{:S(2)}) collective-permute-start(bf16[64,2048]{1,0:T(8,128)(2,1)S(1)} %collective-permute-done.10), channel_id=1, source_target_pairs={{0,32},{1,39},{2,34},{3,33},{4,36},{5,35},{6,38},{7,37},{8,40},{9,... | collective-permute-start | bytes 786440 | tf_op jit(solution)/shard_map/ppermute | solution.py:59
  57.7 11.9 %collective-permute-start.11 = (bf16[128,2048]{1,0:T(8,128)(2,1)S(1)}, bf16[128,2048]{1,0:T(8,128)(2,1)S(1)}, u32[]{:S(2)}, u32[]{:S(2)}) collective-permute-start(bf16[128,2048]{1,0:T(8,128)(2,1)S(1)} %slice.21), channel_id=1, source_target_pairs={{0,64},{1,9},{2,66},{3,11},{4,68},{5,13},{6,70},{7,15},{8,72},{9,1... | collective-permute-start | bytes 1572872 | tf_op jit(solution)/shard_map/ppermute | solution.py:59
  59.4 10.2 %collective-permute-start.12 = (bf16[128,2048]{1,0:T(8,128)(2,1)S(1)}, bf16[128,2048]{1,0:T(8,128)(2,1)}, u32[]{:S(2)}, u32[]{:S(2)}) collective-permute-start(bf16[128,2048]{1,0:T(8,128)(2,1)S(1)} %slice.22), channel_id=1, source_target_pairs={{0,192},{1,25},{2,194},{3,27},{4,196},{5,29},{6,198},{7,31},{8,200... | collective-permute-start | bytes 1572872 | tf_op jit(solution)/shard_map/ppermute | solution.py:59
  85.9 12.4 %all-to-all-start.1 = ((f32[16,2,1152]{2,1,0:T(2,128)}), f32[16,2,1152]{2,1,0:T(2,128)S(1)}, u32[]{:S(2)}, u32[]{:S(2)}) async-start(f32[16,2,1152]{2,1,0:T(2,128)} %get-tuple-element.64), calls=%async_computation.1 | async-start | bytes 294912 | tf_op jit(solution)/shard_map/all_to_all | solution.py:399
  98.3 15.6 %all-to-all-start = ((f32[16,2,1152]{2,1,0:T(2,128)}), f32[16,2,1152]{2,1,0:T(2,128)S(1)}, u32[]{:S(2)}, u32[]{:S(2)}) async-start(f32[16,2,1152]{2,1,0:T(2,128)} %get-tuple-element.63), calls=%async_computation | async-start | bytes 294912 | tf_op jit(solution)/shard_map/all_to_all | solution.py:399
  127.6 21.6 %collective-permute-start.18 = (f16[512,1024]{1,0:T(8,128)(2,1)}, f16[512,1024]{1,0:T(8,128)(2,1)}, u32[]{:S(2)}, u32[]{:S(2)}) collective-permute-start(f16[512,1024]{1,0:T(8,128)(2,1)} %multiply_convert_fusion.1), channel_id=1, source_target_pairs={{0,1},{1,0},{2,3},{3,2},{4,5},{5,4},{6,7},{7,6},{8,9},{9,8},{10,11... | collective-permute-start | bytes 3145736 | tf_op jit(solution)/shard_map/ppermute | solution.py:59
  128.3 11.4 %all-to-all-start.2 = ((f32[16,8,128]{2,1,0:T(8,128)}), f32[16,8,128]{2,1,0:T(8,128)S(1)}, u32[]{:S(2)}, u32[]{:S(2)}) async-start(f32[16,8,128]{2,1,0:T(8,128)} %get-tuple-element.65), calls=%async_computation.2 | async-start | bytes 131072 | tf_op jit(solution)/shard_map/all_to_all | solution.py:399
  139.7 48.5 %all-to-all-start.3 = ((f16[16,64,1024]{2,1,0:T(8,128)(2,1)}), f16[16,64,1024]{2,1,0:T(8,128)(2,1)S(1)}, u32[]{:S(2)}, u32[]{:S(2)}) async-start(f16[16,64,1024]{2,1,0:T(8,128)(2,1)} %bitcast.70), calls=%async_computation.3 | async-start | bytes 4194304 | tf_op jit(solution)/shard_map/all_to_all | solution.py:451
  165.5 10.4 %collective-permute-start.24 = (f16[64,1024]{1,0:T(8,128)(2,1)S(1)}, f16[64,1024]{1,0:T(8,128)(2,1)S(1)}, u32[]{:S(2)}, u32[]{:S(2)}) collective-permute-start(f16[64,1024]{1,0:T(8,128)(2,1)S(1)} %get-tuple-element.76), channel_id=1, source_target_pairs={{0,38},{1,33},{2,32},{3,35},{4,34},{5,37},{6,36},{7,39},{8,46},{9,... | collective-permute-start | bytes 393224 | tf_op jit(solution)/shard_map/ppermute | solution.py:59
  167.7 8.3 %collective-permute-start.25 = (f16[64,1024]{1,0:T(8,128)(2,1)S(1)}, f16[64,1024]{1,0:T(8,128)(2,1)}, u32[]{:S(2)}, u32[]{:S(2)}) collective-permute-start(f16[64,1024]{1,0:T(8,128)(2,1)S(1)} %get-tuple-element.77), channel_id=1, source_target_pairs={{0,32},{1,39},{2,34},{3,33},{4,36},{5,35},{6,38},{7,37},{8,40},{9,... | collective-permute-start | bytes 393224 | tf_op jit(solution)/shard_map/ppermute | solution.py:59
  167.7 7.6 %collective-permute-start.26 = (f32[8,128]{1,0:T(8,128)S(1)}, f32[8,128]{1,0:T(8,128)}, u32[]{:S(2)}, u32[]{:S(2)}) collective-permute-start(f32[8,128]{1,0:T(8,128)S(1)} %add.785), channel_id=1, source_target_pairs={{0,4},{1,5},{2,6},{3,7},{4,0},{5,1},{6,2},{7,3},{8,12},{9,13},{10,... | collective-permute-start | bytes 12296 | tf_op jit(solution)/shard_map/ppermute | solution.py:59
  (20 other events, 167.3 us)

commit v6 on v5

--- a/solution.py
+++ b/solution.py
@@ -77,26 +77,16 @@
 
 def joined_halves(*halves):
     def kernel(*refs):
-        sems = refs[6]
-        copies = [
-            pltpu.make_async_copy(
-                refs[k], refs[4 + k // 2].at[:, pl.ds(k % 2 * WIDTH, WIDTH)], sems.at[k]
-            )
-            for k in range(4)
-        ]
-        for copy in copies:
-            copy.start()
-        for copy in copies:
-            copy.wait()
-
-    anywhere = pl.BlockSpec(memory_space=pl.ANY)
+        for k in range(4):
+            refs[4 + k // 2][:, k % 2 * WIDTH : (k % 2 + 1) * WIDTH] = refs[k][...]
+
+    vmem = pl.BlockSpec(memory_space=pltpu.VMEM)
     pair = jax.ShapeDtypeStruct((BLOCK, 2 * WIDTH), jnp.bfloat16)
     return pl.pallas_call(
         kernel,
         out_shape=(pair, pair),
-        in_specs=[anywhere] * 4,
-        out_specs=(anywhere,) * 2,
-        scratch_shapes=[pltpu.SemaphoreType.DMA((4,))],
+        in_specs=[vmem] * 4,
+        out_specs=(vmem,) * 2,
         cost_estimate=pl.CostEstimate(flops=0, bytes_accessed=1 << 20, transcendentals=0),
     )(*halves)
 
@@ -185,24 +175,26 @@
                         )
                     )
                 k += 1
-    for copy in copies:
-        copy.start()
-    for copy in copies:
-        copy.wait()
-    slabs = [
+    for half in (0, 1):
+        for copy in copies[half::2]:
+            copy.start()
+    outward = [
         pltpu.make_async_copy(text_out, text_hbm, out_sems.at[2]),
         pltpu.make_async_copy(image_out, image_hbm, out_sems.at[3]),
+        pltpu.make_async_copy(s_ref, s_hbm, out_sems.at[0]),
+        pltpu.make_async_copy(t_ref, t_hbm, out_sems.at[1]),
     ]
-    for copy in slabs:
-        copy.start()
-
-    @pl.loop(0, SIDE // CHUNK)
-    def _(j):
-        cols = pl.ds(pl.multiple_of(j * CHUNK, CHUNK), CHUNK)
-        for which, left, right, out in (
-            (0, image_out, text_out, s_ref),
-            (1, image_frozen, text_frozen, t_ref),
-        ):
+
+    for which, left, right, out in (
+        (0, image_out, text_out, s_ref),
+        (1, image_frozen, text_frozen, t_ref),
+    ):
+        for copy in copies[which::2]:
+            copy.wait()
+
+        @pl.loop(0, SIDE // CHUNK)
+        def _(j):
+            cols = pl.ds(pl.multiple_of(j * CHUNK, CHUNK), CHUNK)
             tile = (SCALE * LOG2E) * lax.dot_general(
                 left[...],
                 right[cols, :],
@@ -219,12 +211,8 @@
             for n in range(GROUP):
                 col_ref[n, which : which + 1, cols] = lse
 
-    logits = [
-        pltpu.make_async_copy(s_ref, s_hbm, out_sems.at[0]),
-        pltpu.make_async_copy(t_ref, t_hbm, out_sems.at[1]),
-    ]
-    for copy in logits:
-        copy.start()
+        for copy in outward[:3] if which == 0 else outward[3:]:
+            copy.start()
 
     @pl.loop(0, SIDE // 64)
     def _(i):
@@ -253,7 +241,7 @@
         largest = jnp.full((2, 128), jnp.max(largest), jnp.float32)
         for n in range(GROUP):
             ref[n, :, SIDE : SIDE + 128] = largest
-    for copy in slabs + logits:
+    for copy in outward:
         copy.wait()
 
 
@@ -435,39 +423,38 @@
     text_scale, image_scale = factors[0:1], factors[1:2]
     image_factor, text_factor = factors[2:3], factors[3:4]
 
-    value = jnp.sum(exchanged(part, TEXT_GROUP), axis=0)
-
     half = SIDE // 2
     theirs = lax.dynamic_slice_in_dim(gradient, (1 - c) * half, half)
     mine = lax.dynamic_slice_in_dim(gradient, c * half, half)
     image_theirs = jnp.dot(theirs, text_slab, preferred_element_type=jnp.float32)
     arrived = moved((image_theirs * text_scale).astype(jnp.float16), other_core)
+    image_mine = (
+        jnp.dot(mine, text_slab, preferred_element_type=jnp.float32) * text_scale
+    ) + arrived.astype(jnp.float32)
+    blocks = image_mine.astype(jnp.float16).reshape(8, BLOCK, WIDTH)
+
+    def block(step):
+        return lax.dynamic_index_in_dim(blocks, (z + sign * step) % 8, 0, keepdims=False).astype(
+            jnp.float32
+        )
+
+    def narrow(v):
+        return v.astype(jnp.float16)
+
+    tie = lax.optimization_barrier
+    steps = [other_core] + [lambda p, k=k: flipped(p, k) for k in (1, 2, 4)]
+    start, gradient, part = tie((narrow(block(4)), gradient, part))
+    down = moved(start, along_z(-1))
+    value = jnp.sum(exchanged(part, TEXT_GROUP), axis=0)
     text_part = (
         lax.dot_general(
             gradient, image_slab, (((0,), (0,)), ((), ())), preferred_element_type=jnp.float32
         )
         * image_scale
     ).astype(jnp.float16)
+    down, value, text_part = tie((down, value, text_part))
     text_blocks = lax.all_to_all(text_part.reshape(16, BLOCK, WIDTH), TEXT_GROUP, 0, 0, tiled=True)
-    image_mine = (
-        jnp.dot(mine, text_slab, preferred_element_type=jnp.float32) * text_scale
-    ) + arrived.astype(jnp.float32)
-    blocks = image_mine.astype(jnp.float16).reshape(8, BLOCK, WIDTH)
-
-    def block(step):
-        return lax.dynamic_index_in_dim(blocks, (z + sign * step) % 8, 0, keepdims=False).astype(
-            jnp.float32
-        )
-
-    def narrow(v):
-        return v.astype(jnp.float16)
-
-    tie = lax.optimization_barrier
-    steps = [other_core] + [lambda p, k=k: flipped(p, k) for k in (1, 2, 4)]
-    value, blocks = tie((value + moved(value, steps[0]), blocks))
-    start, value = tie((narrow(block(4)), value))
-    down = moved(start, along_z(-1)).astype(jnp.float32)
-    value = value + moved(value, steps[1])
+    down = down.astype(jnp.float32)
     up = None
     for k in (3, 2, 1):
         first = narrow(block(-k) + down)
@@ -475,8 +462,8 @@
         first, second, value = tie((first, second, value))
         down = moved(first, along_z(-1)).astype(jnp.float32)
         up = moved(second, along_z(1)).astype(jnp.float32)
-        if k > 1:
-            value = value + moved(value, steps[5 - k])
+        value = value + moved(value, steps[3 - k])
+    value = value + moved(value, steps[3])
     loss = value[0, 0] / (256 * BLOCK)
     image_grad = (block(0) + down + up) * image_factor
     text_grad = jnp.sum(text_blocks.astype(jnp.float32), axis=0) * text_factor

time: 191 us -> 172 us (0.901)
  Pallas kernels: 41 us -> 26 us
  starting transfers between devices: 51.6 us -> 47.9 us
  other arithmetic: 11.5 us -> 9.01 us
  waiting for transfers between devices: 67.8 us -> 70.1 us
    pallas_call x1, Pallas kernels: 17 us -> 1.9 us  [joined_halves(): pl.pallas_call(kernel, out_shape=(pair, pair), in_specs=[vmem] * 4, out_s...]
    ppermute x29, starting transfers between devices: 27.9 us -> 23.7 us  [moved(): return lax.ppermute(value, NAMES, pairs)]
    ppermute x29, waiting for transfers between devices: 53 us -> 56 us  [moved(): return lax.ppermute(value, NAMES, pairs)]
  transfers between devices with their start and end apart: 33 -> 33, of which waited for: 18 -> 20; matrix products, arithmetic and copies ran while one was open for 10% -> 10% of each run, Pallas kernels for 0% -> 0%
where the time goes in v6:
time: 172 us; the launch traced here: 171 us
  waiting for transfers between devices  70.1 us (41%)
  starting transfers between devices  47.9 us (28%)
  Pallas kernels  26 us (15%)
  matrix products  11.6 us (7%)
  other arithmetic  9.01 us (5%)
  between operations  3.43 us (2%)
  local copies, waits for them, and re-layouts  3.3 us (2%)
    ppermute x29, waiting for transfers between devices, moved(): return lax.ppermute(value, NAMES, pairs)  56 us
    ppermute x29, starting transfers between devices, moved(): return lax.ppermute(value, NAMES, pairs)  23.7 us
    all_to_all x3, starting transfers between devices, exchanged(): return lax.all_to_all(copies, axis, split_axis=0, concat_axis=0, tiled=True)  17.4 us
    pallas_call x1, Pallas kernels, logits_and_statistics(): pl.pallas_call(kernel, out_shape=(square, square, half, half, small, smal...  15.5 us
    all_to_all x3, waiting for transfers between devices, exchanged(): return lax.all_to_all(copies, axis, split_axis=0, concat_axis=0, tiled=True)  14.1 us
    pallas_call x1, Pallas kernels, gradient_of_logits(): pl.pallas_call(gradient_kernel, grid=(SIDE // ROWS,), out_shape=(jax.Shap...  8.55 us
    all_to_all x1, starting transfers between devices, body(): lax.all_to_all(text_part.reshape(16, BLOCK, WIDTH), TEXT_GROUP, 0, 0, til...  6.91 us
    dot_general x1, matrix products, body(): lax.dot_general(gradient, image_slab, (((0,), (0,)), ((), ())), preferred...  5.95 us
  transfers between devices with their start and end apart: 33, of which 20 were waited for; matrix products, arithmetic and copies ran while one was open for 10% of the time, Pallas kernels for 0%

profile of v6, /device:TPU:8, one launch (start us, length us, event | category | flops | bytes accessed | tf_op | source)
XLA Modules:
  0.0 171.4 jit_solution(445117357907886993)
XLA Ops:
  9.5 1.9 %collective-permute-start.4 = (bf16[64,2048]{1,0:T(8,128)(2,1)}, bf16[64,2048]{1,0:T(8,128)(2,1)S(1)}, u32[]{:S(2)}, u32[]{:S(2)}) collective-permute-start(bf16[64,2048]{1,0:T(8,128)(2,1)} %get-tuple-element.46.refs_6_), channel_id=1, source_target_pairs={{0,1},{1,0},{2,3},{3,2},{4,5},{5,4},{6,7},{7,6},{8,9},{9,8},{10,11... | collective-permute-start | bytes 786440 | tf_op jit(solution)/shard_map/ppermute | solution.py:59
  14.1 3.9 %collective-permute-done.3 = bf16[64,2048]{1,0:T(8,128)(2,1)S(1)} collective-permute-done((bf16[64,2048]{1,0:T(8,128)(2,1)}, bf16[64,2048]{1,0:T(8,128)(2,1)S(1)}, u32[]{:S(2)}, u32[]{:S(2)}) %collective-permute-start.3) | collective-permute-done | bytes 262176 | tf_op jit(solution)/shard_map/ppermute | solution.py:59
  21.2 7.6 %collective-permute-done.7 = bf16[64,2048]{1,0:T(8,128)(2,1)S(1)} collective-permute-done((bf16[64,2048]{1,0:T(8,128)(2,1)S(1)}, bf16[64,2048]{1,0:T(8,128)(2,1)S(1)}, u32[]{:S(2)}, u32[]{:S(2)}) %collective-permute-start.7) | collective-permute-done | bytes 262176 | tf_op jit(solution)/shard_map/ppermute | solution.py:59
  28.8 2.8 %collective-permute-done.8 = bf16[64,2048]{1,0:T(8,128)(2,1)S(1)} collective-permute-done((bf16[64,2048]{1,0:T(8,128)(2,1)S(1)}, bf16[64,2048]{1,0:T(8,128)(2,1)S(1)}, u32[]{:S(2)}, u32[]{:S(2)}) %collective-permute-start.8) | collective-permute-done | bytes 262176 | tf_op jit(solution)/shard_map/ppermute | solution.py:59
  31.7 7.5 %collective-permute-done.10 = bf16[64,2048]{1,0:T(8,128)(2,1)S(1)} collective-permute-done((bf16[64,2048]{1,0:T(8,128)(2,1)S(1)}, bf16[64,2048]{1,0:T(8,128)(2,1)S(1)}, u32[]{:S(2)}, u32[]{:S(2)}) %collective-permute-start.10) | collective-permute-done | bytes 262176 | tf_op jit(solution)/shard_map/ppermute | solution.py:59
  39.2 2.8 %collective-permute-done.9 = bf16[64,2048]{1,0:T(8,128)(2,1)S(1)} collective-permute-done((bf16[64,2048]{1,0:T(8,128)(2,1)S(1)}, bf16[64,2048]{1,0:T(8,128)(2,1)S(1)}, u32[]{:S(2)}, u32[]{:S(2)}) %collective-permute-start.9) | collective-permute-done | bytes 262176 | tf_op jit(solution)/shard_map/ppermute | solution.py:59
  44.7 5.2 %collective-permute-done.14 = bf16[64,2048]{1,0:T(8,128)(2,1)S(1)} collective-permute-done((bf16[64,2048]{1,0:T(8,128)(2,1)S(1)}, bf16[64,2048]{1,0:T(8,128)(2,1)S(1)}, u32[]{:S(2)}, u32[]{:S(2)}) %collective-permute-start.14) | collective-permute-done | bytes 262176 | tf_op jit(solution)/shard_map/ppermute | solution.py:59
  49.9 2.8 %collective-permute-done.15 = bf16[64,2048]{1,0:T(8,128)(2,1)S(1)} collective-permute-done((bf16[64,2048]{1,0:T(8,128)(2,1)S(1)}, bf16[64,2048]{1,0:T(8,128)(2,1)S(1)}, u32[]{:S(2)}, u32[]{:S(2)}) %collective-permute-start.15) | collective-permute-done | bytes 262176 | tf_op jit(solution)/shard_map/ppermute | solution.py:59
  55.3 15.5 %shard_map.68 = (f32[1024,1024]{1,0:T(8,128)}, f32[1024,1024]{1,0:T(8,128)}, bf16[1024,1024]{1,0:T(8,128)(2,1)}, bf16[1024,1024]{1,0:T(8,128)(2,1)}, f32[16,2,1152]{2,1,0:T(2,128)}, /*index=5*/f32[16,2,1152]{2,1,0:T(2,128)}) custom-call(s32[32]{0:T(128)} %stack.131.refs_0_, bf16[256,2048]{1,0:T(8,128)(2,1)} %copy-done, bf16[256,2048]{1,0:T(8,128)(2,1)} %copy-done.3, ...), custom_call_target="tpu_custom_call" | custom-call | flops 4294967296 | bytes 20971520 | tf_op jit(solution)/shard_map/pallas_call | solution.py:261
  70.8 6.1 %all-to-all-start.1 = ((f32[16,2,1152]{2,1,0:T(2,128)}), f32[16,2,1152]{2,1,0:T(2,128)S(1)}, u32[]{:S(2)}, u32[]{:S(2)}) async-start(f32[16,2,1152]{2,1,0:T(2,128)} %get-tuple-element.66), calls=%async_computation.1 | async-start | bytes 294912 | tf_op jit(solution)/shard_map/all_to_all | solution.py:387
  76.9 6.3 %all-to-all-done.1.col_ref = f32[16,2,1152]{2,1,0:T(2,128)S(1)} async-done(((f32[16,2,1152]{2,1,0:T(2,128)}), f32[16,2,1152]{2,1,0:T(2,128)S(1)}, u32[]{:S(2)}, u32[]{:S(2)}) %all-to-all-start.1) | async-done | bytes 147488 | tf_op jit(solution)/shard_map/all_to_all | solution.py:387
  83.2 6.2 %all-to-all-start = ((f32[16,2,1152]{2,1,0:T(2,128)}), f32[16,2,1152]{2,1,0:T(2,128)S(1)}, u32[]{:S(2)}, u32[]{:S(2)}) async-start(f32[16,2,1152]{2,1,0:T(2,128)} %get-tuple-element.65), calls=%async_computation | async-start | bytes 294912 | tf_op jit(solution)/shard_map/all_to_all | solution.py:387
  91.3 7.4 %all-to-all-done.row_ref = f32[16,2,1152]{2,1,0:T(2,128)S(1)} async-done(((f32[16,2,1152]{2,1,0:T(2,128)}), f32[16,2,1152]{2,1,0:T(2,128)S(1)}, u32[]{:S(2)}, u32[]{:S(2)}) %all-to-all-start) | async-done | bytes 147488 | tf_op jit(solution)/shard_map/all_to_all | solution.py:387
  99.4 8.6 %shard_map.69 = (bf16[1024,1024]{1,0:T(8,128)(2,1)}, f32[8,1024]{1,0:T(8,128)}, f32[16,8,128]{2,1,0:T(8,128)}) custom-call(f32[1024,1024]{1,0:T(8,128)} %get-tuple-element.63.s_ref, f32[1024,1024]{1,0:T(8,128)} %get-tuple-element.64.t_ref, f32[16,2,1152]{2,1,0:T(2,128)} %copy-done.2, f32[16,2,1152]{2,1,0:T(2,128)} %copy-done.1, ...), custom_call_target="tpu_custom_call" | custom-call | flops 16777216 | bytes 10485760 | tf_op jit(solution)/shard_map/pallas_call | solution.py:361
  108.9 2.5 %multiply_convert_fusion.1 = f16[512,1024]{1,0:T(8,128)(2,1)S(1)} fusion(bf16[1024,1024]{1,0:T(8,128)(2,1)S(1)} %copy-done.9, bf16[1024,1024]{1,0:T(8,128)(2,1)} %get-tuple-element.73, s32[]{:T(128)S(6)} %select_n.466, f32[1024]{0:T(1024)S(1)} %bitcast.73), kind=kOutput, calls=%fused_computation.3 | convolution fusion | flops 1074790400 | bytes 4198404 | tf_op jit(solution)/shard_map/dot_general | solution.py:429
  112.1 3.2 %fusion.1 = f32[512,1024]{1,0:T(8,128)S(1)} fusion(bf16[1024,1024]{1,0:T(8,128)(2,1)} %get-tuple-element.68, bf16[1024,1024]{1,0:T(8,128)(2,1)} %get-tuple-element.73, s32[]{:T(128)S(6)} %select_n.465), kind=kOutput, calls=%fused_computation.6 | convolution fusion | flops 1073741824 | bytes 5242884 | tf_op jit(solution)/shard_map/dot_general | solution.py:432
  116.4 5.1 %all-to-all-start.2 = ((f32[16,8,128]{2,1,0:T(8,128)}), f32[16,8,128]{2,1,0:T(8,128)S(1)}, u32[]{:S(2)}, u32[]{:S(2)}) async-start(f32[16,8,128]{2,1,0:T(8,128)} %get-tuple-element.72), calls=%async_computation.2 | async-start | bytes 131072 | tf_op jit(solution)/shard_map/all_to_all | solution.py:387
  121.4 6.0 %multiply_convert_fusion = f16[1024,1024]{1,0:T(8,128)(2,1)} fusion(bf16[1024,1024]{1,0:T(8,128)(2,1)} %get-tuple-element.73, bf16[1024,1024]{1,0:T(8,128)(2,1)} %get-tuple-element.74, f32[1024]{0:T(1024)S(1)} %bitcast.75), kind=kOutput, calls=%fused_computation.1 | convolution fusion | flops 2149580800 | bytes 6295552 | tf_op jit(solution)/shard_map/dot_general | solution.py:450
  127.8 6.9 %all-to-all-start.3 = ((f16[16,64,1024]{2,1,0:T(8,128)(2,1)}), f16[16,64,1024]{2,1,0:T(8,128)(2,1)S(1)}, u32[]{:S(2)}, u32[]{:S(2)}) async-start(f16[16,64,1024]{2,1,0:T(8,128)(2,1)} %bitcast.70), calls=%async_computation.3 | async-start | bytes 4194304 | tf_op jit(solution)/shard_map/all_to_all | solution.py:456
  140.1 2.2 %collective-permute-done.20 = f16[64,1024]{1,0:T(8,128)(2,1)} collective-permute-done((f16[64,1024]{1,0:T(8,128)(2,1)S(1)}, f16[64,1024]{1,0:T(8,128)(2,1)}, u32[]{:S(2)}, u32[]{:S(2)}) %collective-permute-start.20) | collective-permute-done | bytes 131104 | tf_op jit(solution)/shard_map/ppermute | solution.py:59
  145.5 3.7 %collective-permute-done.24 = f32[8,128]{1,0:T(8,128)} collective-permute-done((f32[8,128]{1,0:T(8,128)S(1)}, f32[8,128]{1,0:T(8,128)}, u32[]{:S(2)}, u32[]{:S(2)}) %collective-permute-start.24) | collective-permute-done | bytes 4128 | tf_op jit(solution)/shard_map/ppermute | solution.py:59
  154.2 4.5 %collective-permute-done.25 = f32[8,128]{1,0:T(8,128)S(1)} collective-permute-done((f32[8,128]{1,0:T(8,128)S(1)}, f32[8,128]{1,0:T(8,128)S(1)}, u32[]{:S(2)}, u32[]{:S(2)}) %collective-permute-start.25) | collective-permute-done | bytes 4128 | tf_op jit(solution)/shard_map/ppermute | solution.py:59
  158.7 2.1 %collective-permute-start.26 = (f32[8,128]{1,0:T(8,128)S(1)}, f32[8,128]{1,0:T(8,128)S(1)}, u32[]{:S(2)}, u32[]{:S(2)}) collective-permute-start(f32[8,128]{1,0:T(8,128)S(1)} %add.788), channel_id=1, source_target_pairs={{0,4},{1,5},{2,6},{3,7},{4,0},{5,1},{6,2},{7,3},{8,12},{9,13},{10,... | collective-permute-start | bytes 12296 | tf_op jit(solution)/shard_map/ppermute | solution.py:59
  160.7 5.5 %collective-permute-done.26 = f32[8,128]{1,0:T(8,128)S(1)} collective-permute-done((f32[8,128]{1,0:T(8,128)S(1)}, f32[8,128]{1,0:T(8,128)S(1)}, u32[]{:S(2)}, u32[]{:S(2)}) %collective-permute-start.26) | collective-permute-done | bytes 4128 | tf_op jit(solution)/shard_map/ppermute | solution.py:59
  (96 shorter events, 41.8 us)
Async XLA Ops:
  2.5 8.9 %collective-permute-start = (bf16[64,2048]{1,0:T(8,128)(2,1)}, bf16[64,2048]{1,0:T(8,128)(2,1)S(1)}, u32[]{:S(2)}, u32[]{:S(2)}) collective-permute-start(bf16[64,2048]{1,0:T(8,128)(2,1)} %get-tuple-element.45), channel_id=1, source_target_pairs={{0,8},{1,65},{2,10},{3,67},{4,12},{5,69},{6,14},{7,71},{8,16},{9,7... | collective-permute-start | bytes 786440 | tf_op jit(solution)/shard_map/ppermute | solution.py:59
  4.0 8.8 %collective-permute-start.1 = (bf16[64,2048]{1,0:T(8,128)(2,1)}, bf16[64,2048]{1,0:T(8,128)(2,1)S(1)}, u32[]{:S(2)}, u32[]{:S(2)}) collective-permute-start(bf16[64,2048]{1,0:T(8,128)(2,1)} %get-tuple-element.45), channel_id=1, source_target_pairs={{0,24},{1,193},{2,26},{3,195},{4,28},{5,197},{6,30},{7,199},{8,0},... | collective-permute-start | bytes 786440 | tf_op jit(solution)/shard_map/ppermute | solution.py:59
  5.8 8.3 %collective-permute-start.2 = (bf16[64,2048]{1,0:T(8,128)(2,1)}, bf16[64,2048]{1,0:T(8,128)(2,1)S(1)}, u32[]{:S(2)}, u32[]{:S(2)}) collective-permute-start(bf16[64,2048]{1,0:T(8,128)(2,1)} %get-tuple-element.45), channel_id=1, source_target_pairs={{0,16},{1,129},{2,18},{3,131},{4,20},{5,133},{6,22},{7,135},{8,24}... | collective-permute-start | bytes 786440 | tf_op jit(solution)/shard_map/ppermute | solution.py:59
  7.6 10.4 %collective-permute-start.3 = (bf16[64,2048]{1,0:T(8,128)(2,1)}, bf16[64,2048]{1,0:T(8,128)(2,1)S(1)}, u32[]{:S(2)}, u32[]{:S(2)}) collective-permute-start(bf16[64,2048]{1,0:T(8,128)(2,1)} %get-tuple-element.46.refs_6_), channel_id=1, source_target_pairs={{0,32},{1,39},{2,34},{3,33},{4,36},{5,35},{6,38},{7,37},{8,40},{9,... | collective-permute-start | bytes 786440 | tf_op jit(solution)/shard_map/ppermute | solution.py:59
  9.5 8.5 %collective-permute-start.4 = (bf16[64,2048]{1,0:T(8,128)(2,1)}, bf16[64,2048]{1,0:T(8,128)(2,1)S(1)}, u32[]{:S(2)}, u32[]{:S(2)}) collective-permute-start(bf16[64,2048]{1,0:T(8,128)(2,1)} %get-tuple-element.46.refs_6_), channel_id=1, source_target_pairs={{0,1},{1,0},{2,3},{3,2},{4,5},{5,4},{6,7},{7,6},{8,9},{9,8},{10,11... | collective-permute-start | bytes 786440 | tf_op jit(solution)/shard_map/ppermute | solution.py:59
  19.1 22.9 %collective-permute-start.5 = (bf16[256,2048]{1,0:T(8,128)(2,1)S(1)}, bf16[256,2048]{1,0:T(8,128)(2,1)S(1)}, u32[]{:S(2)}, u32[]{:S(2)}) collective-permute-start(bf16[256,2048]{1,0:T(8,128)(2,1)S(1)} %pad_maximum_fusion.refs_1_), channel_id=1, source_target_pairs={{0,64},{1,9},{2,66},{3,11},{4,68},{5,13},{6,70},{7,15},{8,72},{9,1... | collective-permute-start | bytes 3145736 | tf_op jit(solution)/shard_map/ppermute | solution.py:59
  20.8 21.2 %collective-permute-start.6 = (bf16[256,2048]{1,0:T(8,128)(2,1)S(1)}, bf16[256,2048]{1,0:T(8,128)(2,1)S(1)}, u32[]{:S(2)}, u32[]{:S(2)}) collective-permute-start(bf16[256,2048]{1,0:T(8,128)(2,1)S(1)} %pad_maximum_fusion.refs_1_), channel_id=1, source_target_pairs={{0,192},{1,25},{2,194},{3,27},{4,196},{5,29},{6,198},{7,31},{8,200... | collective-permute-start | bytes 3145736 | tf_op jit(solution)/shard_map/ppermute | solution.py:59
  21.2 7.6 %collective-permute-start.7 = (bf16[64,2048]{1,0:T(8,128)(2,1)S(1)}, bf16[64,2048]{1,0:T(8,128)(2,1)S(1)}, u32[]{:S(2)}, u32[]{:S(2)}) collective-permute-start(bf16[64,2048]{1,0:T(8,128)(2,1)S(1)} %collective-permute-done.3), channel_id=1, source_target_pairs={{0,32},{1,39},{2,34},{3,33},{4,36},{5,35},{6,38},{7,37},{8,40},{9,... | collective-permute-start | bytes 786440 | tf_op jit(solution)/shard_map/ppermute | solution.py:59
  21.2 10.4 %collective-permute-start.8 = (bf16[64,2048]{1,0:T(8,128)(2,1)S(1)}, bf16[64,2048]{1,0:T(8,128)(2,1)S(1)}, u32[]{:S(2)}, u32[]{:S(2)}) collective-permute-start(bf16[64,2048]{1,0:T(8,128)(2,1)S(1)} %collective-permute-done.4.refs_7_), channel_id=1, source_target_pairs={{0,32},{1,39},{2,34},{3,33},{4,36},{5,35},{6,38},{7,37},{8,40},{9,... | collective-permute-start | bytes 786440 | tf_op jit(solution)/shard_map/ppermute | solution.py:59
  31.6 7.6 %collective-permute-start.10 = (bf16[64,2048]{1,0:T(8,128)(2,1)S(1)}, bf16[64,2048]{1,0:T(8,128)(2,1)S(1)}, u32[]{:S(2)}, u32[]{:S(2)}) collective-permute-start(bf16[64,2048]{1,0:T(8,128)(2,1)S(1)} %collective-permute-done.8), channel_id=1, source_target_pairs={{0,32},{1,39},{2,34},{3,33},{4,36},{5,35},{6,38},{7,37},{8,40},{9,... | collective-permute-start | bytes 786440 | tf_op jit(solution)/shard_map/ppermute | solution.py:59
  31.6 10.4 %collective-permute-start.9 = (bf16[64,2048]{1,0:T(8,128)(2,1)S(1)}, bf16[64,2048]{1,0:T(8,128)(2,1)S(1)}, u32[]{:S(2)}, u32[]{:S(2)}) collective-permute-start(bf16[64,2048]{1,0:T(8,128)(2,1)S(1)} %collective-permute-done.7), channel_id=1, source_target_pairs={{0,32},{1,39},{2,34},{3,33},{4,36},{5,35},{6,38},{7,37},{8,40},{9,... | collective-permute-start | bytes 786440 | tf_op jit(solution)/shard_map/ppermute | solution.py:59
  42.1 13.0 %collective-permute-start.13 = (bf16[320,2048]{1,0:T(8,128)(2,1)S(1)}, bf16[320,2048]{1,0:T(8,128)(2,1)}, u32[]{:S(2)}, u32[]{:S(2)}) collective-permute-start(bf16[320,2048]{1,0:T(8,128)(2,1)S(1)} %constant_dynamic-update-slice_fusion.refs_8_), channel_id=1, source_target_pairs={{0,1},{1,0},{2,3},{3,2},{4,5},{5,4},{6,7},{7,6},{8,9},{9,8},{10,11... | collective-permute-start | bytes 3932168 | tf_op jit(solution)/shard_map/ppermute | solution.py:59
  42.2 7.7 %collective-permute-start.14 = (bf16[64,2048]{1,0:T(8,128)(2,1)S(1)}, bf16[64,2048]{1,0:T(8,128)(2,1)S(1)}, u32[]{:S(2)}, u32[]{:S(2)}) collective-permute-start(bf16[64,2048]{1,0:T(8,128)(2,1)S(1)} %collective-permute-done.9), channel_id=1, source_target_pairs={{0,32},{1,39},{2,34},{3,33},{4,36},{5,35},{6,38},{7,37},{8,40},{9,... | collective-permute-start | bytes 786440 | tf_op jit(solution)/shard_map/ppermute | solution.py:59
  42.3 10.4 %collective-permute-start.15 = (bf16[64,2048]{1,0:T(8,128)(2,1)S(1)}, bf16[64,2048]{1,0:T(8,128)(2,1)S(1)}, u32[]{:S(2)}, u32[]{:S(2)}) collective-permute-start(bf16[64,2048]{1,0:T(8,128)(2,1)S(1)} %collective-permute-done.10), channel_id=1, source_target_pairs={{0,32},{1,39},{2,34},{3,33},{4,36},{5,35},{6,38},{7,37},{8,40},{9,... | collective-permute-start | bytes 786440 | tf_op jit(solution)/shard_map/ppermute | solution.py:59
  42.5 12.0 %collective-permute-start.11 = (bf16[128,2048]{1,0:T(8,128)(2,1)S(1)}, bf16[128,2048]{1,0:T(8,128)(2,1)S(1)}, u32[]{:S(2)}, u32[]{:S(2)}) collective-permute-start(bf16[128,2048]{1,0:T(8,128)(2,1)S(1)} %slice.21), channel_id=1, source_target_pairs={{0,64},{1,9},{2,66},{3,11},{4,68},{5,13},{6,70},{7,15},{8,72},{9,1... | collective-permute-start | bytes 1572872 | tf_op jit(solution)/shard_map/ppermute | solution.py:59
  44.2 10.3 %collective-permute-start.12 = (bf16[128,2048]{1,0:T(8,128)(2,1)S(1)}, bf16[128,2048]{1,0:T(8,128)(2,1)}, u32[]{:S(2)}, u32[]{:S(2)}) collective-permute-start(bf16[128,2048]{1,0:T(8,128)(2,1)S(1)} %slice.22), channel_id=1, source_target_pairs={{0,192},{1,25},{2,194},{3,27},{4,196},{5,29},{6,198},{7,31},{8,200... | collective-permute-start | bytes 1572872 | tf_op jit(solution)/shard_map/ppermute | solution.py:59
  70.8 12.4 %all-to-all-start.1 = ((f32[16,2,1152]{2,1,0:T(2,128)}), f32[16,2,1152]{2,1,0:T(2,128)S(1)}, u32[]{:S(2)}, u32[]{:S(2)}) async-start(f32[16,2,1152]{2,1,0:T(2,128)} %get-tuple-element.66), calls=%async_computation.1 | async-start | bytes 294912 | tf_op jit(solution)/shard_map/all_to_all | solution.py:387
  83.2 15.5 %all-to-all-start = ((f32[16,2,1152]{2,1,0:T(2,128)}), f32[16,2,1152]{2,1,0:T(2,128)S(1)}, u32[]{:S(2)}, u32[]{:S(2)}) async-start(f32[16,2,1152]{2,1,0:T(2,128)} %get-tuple-element.65), calls=%async_computation | async-start | bytes 294912 | tf_op jit(solution)/shard_map/all_to_all | solution.py:387
  115.8 11.9 %collective-permute-start.18 = (f16[64,1024]{1,0:T(8,128)(2,1)S(1)}, f16[64,1024]{1,0:T(8,128)(2,1)S(1)}, u32[]{:S(2)}, u32[]{:S(2)}) collective-permute-start(f16[64,1024]{1,0:T(8,128)(2,1)S(1)} %get-tuple-element.71), channel_id=1, source_target_pairs={{0,38},{1,33},{2,32},{3,35},{4,34},{5,37},{6,36},{7,39},{8,46},{9,... | collective-permute-start | bytes 393224 | tf_op jit(solution)/shard_map/ppermute | solution.py:59
  116.4 11.4 %all-to-all-start.2 = ((f32[16,8,128]{2,1,0:T(8,128)}), f32[16,8,128]{2,1,0:T(8,128)S(1)}, u32[]{:S(2)}, u32[]{:S(2)}) async-start(f32[16,8,128]{2,1,0:T(8,128)} %get-tuple-element.72), calls=%async_computation.2 | async-start | bytes 131072 | tf_op jit(solution)/shard_map/all_to_all | solution.py:387
  127.8 41.3 %all-to-all-start.3 = ((f16[16,64,1024]{2,1,0:T(8,128)(2,1)}), f16[16,64,1024]{2,1,0:T(8,128)(2,1)S(1)}, u32[]{:S(2)}, u32[]{:S(2)}) async-start(f16[16,64,1024]{2,1,0:T(8,128)(2,1)} %bitcast.70), calls=%async_computation.3 | async-start | bytes 4194304 | tf_op jit(solution)/shard_map/all_to_all | solution.py:456
  152.1 15.3 %collective-permute-start.27 = (f16[64,1024]{1,0:T(8,128)(2,1)S(1)}, f16[64,1024]{1,0:T(8,128)(2,1)S(1)}, u32[]{:S(2)}, u32[]{:S(2)}) collective-permute-start(f16[64,1024]{1,0:T(8,128)(2,1)S(1)} %get-tuple-element.84), channel_id=1, source_target_pairs={{0,38},{1,33},{2,32},{3,35},{4,34},{5,37},{6,36},{7,39},{8,46},{9,... | collective-permute-start | bytes 393224 | tf_op jit(solution)/shard_map/ppermute | solution.py:59
  153.5 13.9 %collective-permute-start.28 = (f16[64,1024]{1,0:T(8,128)(2,1)S(1)}, f16[64,1024]{1,0:T(8,128)(2,1)}, u32[]{:S(2)}, u32[]{:S(2)}) collective-permute-start(f16[64,1024]{1,0:T(8,128)(2,1)S(1)} %get-tuple-element.85), channel_id=1, source_target_pairs={{0,32},{1,39},{2,34},{3,33},{4,36},{5,35},{6,38},{7,37},{8,40},{9,... | collective-permute-start | bytes 393224 | tf_op jit(solution)/shard_map/ppermute | solution.py:59
  158.7 7.5 %collective-permute-start.26 = (f32[8,128]{1,0:T(8,128)S(1)}, f32[8,128]{1,0:T(8,128)S(1)}, u32[]{:S(2)}, u32[]{:S(2)}) collective-permute-start(f32[8,128]{1,0:T(8,128)S(1)} %add.788), channel_id=1, source_target_pairs={{0,4},{1,5},{2,6},{3,7},{4,0},{5,1},{6,2},{7,3},{8,12},{9,13},{10,... | collective-permute-start | bytes 12296 | tf_op jit(solution)/shard_map/ppermute | solution.py:59
  (19 other events, 151.0 us)

commit v7 on v6

--- a/solution.py
+++ b/solution.py
@@ -15,7 +15,6 @@
 ROW_COL = ("y", "zl", "x", "zh", "c")
 COL_ROW = ("x", "zh", "c", "y", "zl")
 TEXT_GROUP = ("y", "x")
-IMAGE_GROUP = ("zl", "zh", "c")
 
 LOG2E = math.log2(math.e)
 LN2 = math.log(2.0)
@@ -26,7 +25,7 @@
 STRIP = 128
 CHUNK = 256
 GROUP = 16
-LOGITS_VMEM = 58 * 1024 * 1024
+LOGITS_VMEM = 26 * 1024 * 1024
 GRADIENT_VMEM = 56 * 1024 * 1024
 ROWS = 256
 
@@ -233,14 +232,15 @@
             top = jnp.max(high, axis=0, keepdims=True)
             total = jnp.sum(total * jnp.exp2(high - top), axis=0, keepdims=True)
             lse = top + jnp.log2(total)
-            for n in range(GROUP):
-                row_ref[n, which : which + 1, rows] = lse
-
-    for slab, ref in ((text_out, row_ref), (image_out, col_ref)):
-        largest = jnp.max(jnp.abs(slab[...]), axis=0, keepdims=True).astype(jnp.float32)
-        largest = jnp.full((2, 128), jnp.max(largest), jnp.float32)
-        for n in range(GROUP):
-            ref[n, :, SIDE : SIDE + 128] = largest
+            row_ref[which : which + 1, rows] = lse
+
+    largest = [
+        jnp.full((2, 128), jnp.max(jnp.max(jnp.abs(slab[...]), axis=0).astype(jnp.float32)))
+        for slab in (text_out, image_out)
+    ]
+    row_ref[:, SIDE : SIDE + 128] = largest[0]
+    for n in range(GROUP):
+        col_ref[n, :, SIDE : SIDE + 128] = largest[1]
     for copy in outward:
         copy.wait()
 
@@ -255,12 +255,13 @@
     def kernel(*refs):
         logits_kernel((len(text), len(images)), *refs)
 
-    square = jax.ShapeDtypeStruct((SIDE, SIDE), f32)
-    half = jax.ShapeDtypeStruct((SIDE, WIDTH), jnp.bfloat16)
+    square = pltpu.HBM((SIDE, SIDE), f32)
+    half = pltpu.HBM((SIDE, WIDTH), jnp.bfloat16)
+    one = jax.ShapeDtypeStruct((2, SIDE + 128), f32)
     small = jax.ShapeDtypeStruct((GROUP, 2, SIDE + 128), f32)
     return pl.pallas_call(
         kernel,
-        out_shape=(square, square, half, half, small, small),
+        out_shape=(square, square, half, half, one, small),
         in_specs=[smem] + [anywhere] * (len(text) + len(images)),
         out_specs=(hbm,) * 4 + (vmem,) * 2,
         scratch_shapes=[
@@ -307,7 +308,7 @@
 
     @pl.when(step == 0)
     def _():
-        s_row_all, t_row_all = joined(row_ref, 0), joined(row_ref, 1)
+        s_row_all, t_row_all = row_ref[0:1, :SIDE], row_ref[1:2, :SIDE]
         s_col_all, t_col_all = joined(col_ref, 0), joined(col_ref, 1)
         shared = (s_row_all - 0.5 * t_row_all) + (s_col_all - 0.5 * t_col_all)
         lse_ref[0:1, :] = s_row_all
@@ -315,8 +316,9 @@
         lse_ref[2:3, :] = s_col_all
         lse_ref[3:4, :] = t_col_all + 1.0
         lse_ref[4:5, :] = shared
-        for k, ref in ((0, row_ref), (1, col_ref)):
-            scale = 2.0 / jnp.maximum(jnp.max(ref[:, 0, SIDE : SIDE + 128]), 1e-30)
+        tops = (jnp.max(row_ref[:, SIDE:]), jnp.max(col_ref[:, 0, SIDE:]))
+        for k, top in enumerate(tops):
+            scale = 2.0 / jnp.maximum(top, 1e-30)
             scale = jnp.full((1, SIDE), scale, jnp.float32)
             factor_ref[k : k + 1, :] = scale
             factor_ref[k + 2 : k + 3, :] = SCALE / scale
@@ -383,6 +385,12 @@
     )(s, t, row, col, row_id, col_id)
 
 
+def merged(one, other):
+    high, low = jnp.maximum(one, other), jnp.minimum(one, other)
+    sums = lax.broadcasted_iota(jnp.int32, one.shape, 1) < SIDE
+    return jnp.where(sums, high + jnp.log2(1.0 + jnp.exp2(low - high)), high)
+
+
 def exchanged(copies, axis):
     return lax.all_to_all(copies, axis, split_axis=0, concat_axis=0, tiled=True)
 
@@ -417,11 +425,28 @@
     s, t, text_slab, image_slab, row_part, col_part = logits_and_statistics(
         where, [p for p, _ in text_pieces], [p for p, _ in image_pieces]
     )
+    pairs = [other_core] + [lambda p, k=k: flipped(p, k) for k in (1, 2, 4)]
     col_all = exchanged(col_part, TEXT_GROUP)
-    row_all = exchanged(row_part, IMAGE_GROUP)
+    row_all = row_part
+    for to in pairs[:2]:
+        row_all = merged(row_all, moved(row_all, to))
+    row_all, col_all = lax.optimization_barrier((row_all, col_all))
+    for to in pairs[2:]:
+        row_all = merged(row_all, moved(row_all, to))
     gradient, factors, part = gradient_of_logits(s, t, row_all, col_all, row_id, col_id)
     text_scale, image_scale = factors[0:1], factors[1:2]
     image_factor, text_factor = factors[2:3], factors[3:4]
+
+    tie = lax.optimization_barrier
+    value = jnp.sum(exchanged(part, TEXT_GROUP), axis=0)
+    text_part = (
+        lax.dot_general(
+            gradient, image_slab, (((0,), (0,)), ((), ())), preferred_element_type=jnp.float32
+        )
+        * image_scale
+    ).astype(jnp.float16)
+    text_part, gradient, value = tie((text_part, gradient, value))
+    text_blocks = lax.all_to_all(text_part.reshape(16, BLOCK, WIDTH), TEXT_GROUP, 0, 0, tiled=True)
 
     half = SIDE // 2
     theirs = lax.dynamic_slice_in_dim(gradient, (1 - c) * half, half)
@@ -441,19 +466,9 @@
     def narrow(v):
         return v.astype(jnp.float16)
 
-    tie = lax.optimization_barrier
-    steps = [other_core] + [lambda p, k=k: flipped(p, k) for k in (1, 2, 4)]
-    start, gradient, part = tie((narrow(block(4)), gradient, part))
-    down = moved(start, along_z(-1))
-    value = jnp.sum(exchanged(part, TEXT_GROUP), axis=0)
-    text_part = (
-        lax.dot_general(
-            gradient, image_slab, (((0,), (0,)), ((), ())), preferred_element_type=jnp.float32
-        )
-        * image_scale
-    ).astype(jnp.float16)
-    down, value, text_part = tie((down, value, text_part))
-    text_blocks = lax.all_to_all(text_part.reshape(16, BLOCK, WIDTH), TEXT_GROUP, 0, 0, tiled=True)
+    blocks, value = tie((blocks, value + moved(value, pairs[0])))
+    down = moved(narrow(block(4)), along_z(-1))
+    value = value + moved(value, pairs[1])
     down = down.astype(jnp.float32)
     up = None
     for k in (3, 2, 1):
@@ -462,8 +477,8 @@
         first, second, value = tie((first, second, value))
         down = moved(first, along_z(-1)).astype(jnp.float32)
         up = moved(second, along_z(1)).astype(jnp.float32)
-        value = value + moved(value, steps[3 - k])
-    value = value + moved(value, steps[3])
+        if k > 1:
+            value = value + moved(value, pairs[5 - k])
     loss = value[0, 0] / (256 * BLOCK)
     image_grad = (block(0) + down + up) * image_factor
     text_grad = jnp.sum(text_blocks.astype(jnp.float32), axis=0) * text_factor

time: 172 us -> 181 us (1.052)
  starting transfers between devices: 47.9 us -> 56.9 us
  waiting for transfers between devices: 70.1 us -> 61.7 us
  local copies, waits for them, and re-layouts: 3.3 us -> 9.35 us
  other arithmetic: 9.01 us -> 12.3 us
    ppermute x29 -> x33, starting transfers between devices: 23.7 us -> 37.6 us  [moved(): return lax.ppermute(value, NAMES, pairs)]
    all_to_all x3 -> x2, waiting for transfers between devices: 14.1 us -> 6.47 us  [exchanged(): return lax.all_to_all(copies, axis, split_axis=0, concat_axis=0, tiled=True)]
    all_to_all x3 -> x2, starting transfers between devices: 17.4 us -> 12.2 us  [exchanged(): return lax.all_to_all(copies, axis, split_axis=0, concat_axis=0, tiled=True)]
    unnamed x25 -> x15, local copies, waits for them, and re-layouts: 0.99 us -> 4.6 us
    ppermute x29 -> x33, waiting for transfers between devices: 56 us -> 55.2 us  [moved(): return lax.ppermute(value, NAMES, pairs)]
  transfers between devices with their start and end apart: 33 -> 36, of which waited for: 20 -> 22; matrix products, arithmetic and copies ran while one was open for 10% -> 13% of each run, Pallas kernels for 0% -> 0%
where the time goes in v7:
time: 181 us; the launch traced here: 180 us
  waiting for transfers between devices  61.7 us (34%)
  starting transfers between devices  56.9 us (31%)
  Pallas kernels  25.2 us (14%)
  other arithmetic  12.3 us (7%)
  matrix products  12.1 us (7%)
  local copies, waits for them, and re-layouts  9.35 us (5%)
  between operations  2.91 us (2%)
    ppermute x33, waiting for transfers between devices, moved(): return lax.ppermute(value, NAMES, pairs)  55.2 us
    ppermute x33, starting transfers between devices, moved(): return lax.ppermute(value, NAMES, pairs)  37.6 us
    pallas_call x1, Pallas kernels, logits_and_statistics(): pl.pallas_call(kernel, out_shape=(square, square, half, half, one, small)...  15.1 us
    all_to_all x2, starting transfers between devices, exchanged(): return lax.all_to_all(copies, axis, split_axis=0, concat_axis=0, tiled=True)  12.2 us
    pallas_call x1, Pallas kernels, gradient_of_logits(): pl.pallas_call(gradient_kernel, grid=(SIDE // ROWS,), out_shape=(jax.Shap...  8.14 us
    all_to_all x1, starting transfers between devices, body(): lax.all_to_all(text_part.reshape(16, BLOCK, WIDTH), TEXT_GROUP, 0, 0, til...  7.08 us
    all_to_all x2, waiting for transfers between devices, exchanged(): return lax.all_to_all(copies, axis, split_axis=0, concat_axis=0, tiled=True)  6.47 us
    dot_general x1, matrix products, body(): lax.dot_general(gradient, image_slab, (((0,), (0,)), ((), ())), preferred...  6.11 us
  transfers between devices with their start and end apart: 36, of which 22 were waited for; matrix products, arithmetic and copies ran while one was open for 13% of the time, Pallas kernels for 0%

profile of v7, /device:TPU:8, one launch (start us, length us, event | category | flops | bytes accessed | tf_op | source)
XLA Modules:
  0.0 180.4 jit_solution(16212834458435550673)
XLA Ops:
  14.1 3.9 %collective-permute-done.3 = bf16[64,2048]{1,0:T(8,128)(2,1)S(1)} collective-permute-done((bf16[64,2048]{1,0:T(8,128)(2,1)}, bf16[64,2048]{1,0:T(8,128)(2,1)S(1)}, u32[]{:S(2)}, u32[]{:S(2)}) %collective-permute-start.3) | collective-permute-done | bytes 262176 | tf_op jit(solution)/shard_map/ppermute | solution.py:58
  21.3 7.6 %collective-permute-done.7 = bf16[64,2048]{1,0:T(8,128)(2,1)S(1)} collective-permute-done((bf16[64,2048]{1,0:T(8,128)(2,1)S(1)}, bf16[64,2048]{1,0:T(8,128)(2,1)S(1)}, u32[]{:S(2)}, u32[]{:S(2)}) %collective-permute-start.7) | collective-permute-done | bytes 262176 | tf_op jit(solution)/shard_map/ppermute | solution.py:58
  28.8 2.8 %collective-permute-done.8 = bf16[64,2048]{1,0:T(8,128)(2,1)S(1)} collective-permute-done((bf16[64,2048]{1,0:T(8,128)(2,1)S(1)}, bf16[64,2048]{1,0:T(8,128)(2,1)S(1)}, u32[]{:S(2)}, u32[]{:S(2)}) %collective-permute-start.8) | collective-permute-done | bytes 262176 | tf_op jit(solution)/shard_map/ppermute | solution.py:58
  33.1 6.1 %collective-permute-done.10 = bf16[64,2048]{1,0:T(8,128)(2,1)S(1)} collective-permute-done((bf16[64,2048]{1,0:T(8,128)(2,1)S(1)}, bf16[64,2048]{1,0:T(8,128)(2,1)S(1)}, u32[]{:S(2)}, u32[]{:S(2)}) %collective-permute-start.10) | collective-permute-done | bytes 262176 | tf_op jit(solution)/shard_map/ppermute | solution.py:58
  39.2 2.8 %collective-permute-done.9 = bf16[64,2048]{1,0:T(8,128)(2,1)S(1)} collective-permute-done((bf16[64,2048]{1,0:T(8,128)(2,1)S(1)}, bf16[64,2048]{1,0:T(8,128)(2,1)S(1)}, u32[]{:S(2)}, u32[]{:S(2)}) %collective-permute-start.9) | collective-permute-done | bytes 262176 | tf_op jit(solution)/shard_map/ppermute | solution.py:58
  48.1 3.7 %collective-permute-done.14 = bf16[64,2048]{1,0:T(8,128)(2,1)S(1)} collective-permute-done((bf16[64,2048]{1,0:T(8,128)(2,1)S(1)}, bf16[64,2048]{1,0:T(8,128)(2,1)S(1)}, u32[]{:S(2)}, u32[]{:S(2)}) %collective-permute-start.14) | collective-permute-done | bytes 262176 | tf_op jit(solution)/shard_map/ppermute | solution.py:58
  51.8 2.8 %collective-permute-done.15 = bf16[64,2048]{1,0:T(8,128)(2,1)S(1)} collective-permute-done((bf16[64,2048]{1,0:T(8,128)(2,1)S(1)}, bf16[64,2048]{1,0:T(8,128)(2,1)S(1)}, u32[]{:S(2)}, u32[]{:S(2)}) %collective-permute-start.15) | collective-permute-done | bytes 262176 | tf_op jit(solution)/shard_map/ppermute | solution.py:58
  59.3 15.1 %shard_map.68 = (f32[1024,1024]{1,0:T(8,128)}, f32[1024,1024]{1,0:T(8,128)}, bf16[1024,1024]{1,0:T(8,128)(2,1)}, bf16[1024,1024]{1,0:T(8,128)(2,1)}, f32[2,1152]{1,0:T(2,128)S(1)}, /*index=5*/f32[16,2,1152]{2,1,0:T(2,128)}) custom-call(s32[32]{0:T(128)S(1)} %stack.131.refs_0_, bf16[256,2048]{1,0:T(8,128)(2,1)S(1)} %pad_maximum_fusion.refs_1_, ...), custom_call_target="tpu_custom_call" | custom-call | flops 4294967296 | bytes 20971520 | tf_op jit(solution)/shard_map/pallas_call | solution.py:262
  77.0 7.0 %all-to-all-start = ((f32[16,2,1152]{2,1,0:T(2,128)}), f32[16,2,1152]{2,1,0:T(2,128)S(1)}, u32[]{:S(2)}, u32[]{:S(2)}) async-start(f32[16,2,1152]{2,1,0:T(2,128)} %get-tuple-element.67), calls=%async_computation | async-start | bytes 294912 | tf_op jit(solution)/shard_map/all_to_all | solution.py:395
  84.1 6.3 %all-to-all-done.col_ref = f32[16,2,1152]{2,1,0:T(2,128)S(1)} async-done(((f32[16,2,1152]{2,1,0:T(2,128)}), f32[16,2,1152]{2,1,0:T(2,128)S(1)}, u32[]{:S(2)}, u32[]{:S(2)}) %all-to-all-start) | async-done | bytes 147488 | tf_op jit(solution)/shard_map/all_to_all | solution.py:395
  90.3 3.2 %collective-permute-start.19 = (f32[2,1152]{1,0:T(2,128)S(1)}, f32[2,1152]{1,0:T(2,128)S(1)}, u32[]{:S(2)}, u32[]{:S(2)}) collective-permute-start(f32[2,1152]{1,0:T(2,128)S(1)} %add_select_fusion.7), channel_id=1, source_target_pairs={{0,2},{1,3},{2,0},{3,1},{4,6},{5,7},{6,4},{7,5},{8,10},{9,11},{10,... | collective-permute-start | bytes 27656 | tf_op jit(solution)/shard_map/ppermute | solution.py:58
  95.2 2.6 %collective-permute-start.20 = (f32[2,1152]{1,0:T(2,128)S(1)}, f32[2,1152]{1,0:T(2,128)S(1)}, u32[]{:S(2)}, u32[]{:S(2)}) collective-permute-start(f32[2,1152]{1,0:T(2,128)S(1)} %add_select_fusion.6), channel_id=1, source_target_pairs={{0,4},{1,5},{2,6},{3,7},{4,0},{5,1},{6,2},{7,3},{8,12},{9,13},{10,... | collective-permute-start | bytes 27656 | tf_op jit(solution)/shard_map/ppermute | solution.py:58
  98.4 4.5 %collective-permute-done.20 = f32[2,1152]{1,0:T(2,128)S(1)} collective-permute-done((f32[2,1152]{1,0:T(2,128)S(1)}, f32[2,1152]{1,0:T(2,128)S(1)}, u32[]{:S(2)}, u32[]{:S(2)}) %collective-permute-start.20) | collective-permute-done | bytes 9248 | tf_op jit(solution)/shard_map/ppermute | solution.py:58
  103.5 8.1 %shard_map.69 = (bf16[1024,1024]{1,0:T(8,128)(2,1)}, f32[8,1024]{1,0:T(8,128)}, f32[16,8,128]{2,1,0:T(8,128)}) custom-call(f32[1024,1024]{1,0:T(8,128)} %get-tuple-element.64.s_ref, f32[1024,1024]{1,0:T(8,128)} %get-tuple-element.65.t_ref, f32[2,1152]{1,0:T(2,128)} %add_select_fusion.5.row_ref, f32[16,2,1152]{2,1,0:T(2,128)} %copy-done.3, ...), custom_call_target="tpu_custom_call" | custom-call | flops 16777216 | bytes 10485760 | tf_op jit(solution)/shard_map/pallas_call | solution.py:363
  112.6 5.2 %all-to-all-start.1 = ((f32[16,8,128]{2,1,0:T(8,128)}), f32[16,8,128]{2,1,0:T(8,128)S(1)}, u32[]{:S(2)}, u32[]{:S(2)}) async-start(f32[16,8,128]{2,1,0:T(8,128)} %get-tuple-element.73), calls=%async_computation.1 | async-start | bytes 131072 | tf_op jit(solution)/shard_map/all_to_all | solution.py:395
  117.8 6.1 %multiply_convert_fusion = f16[1024,1024]{1,0:T(8,128)(2,1)} fusion(bf16[1024,1024]{1,0:T(8,128)(2,1)} %get-tuple-element.74, bf16[1024,1024]{1,0:T(8,128)(2,1)} %get-tuple-element.71, f32[1024]{0:T(1024)S(1)} %bitcast.75), kind=kOutput, calls=%fused_computation.1 | convolution fusion | flops 2149580800 | bytes 6295552 | tf_op jit(solution)/shard_map/dot_general | solution.py:443
  124.1 2.8 %multiply_convert_fusion.1 = f16[512,1024]{1,0:T(8,128)(2,1)S(1)} fusion(bf16[1024,1024]{1,0:T(8,128)(2,1)} %get-tuple-element.75, bf16[1024,1024]{1,0:T(8,128)(2,1)S(1)} %copy-done.4, s32[]{:T(128)S(6)} %select_n.483, f32[1024]{0:T(1024)S(1)} %bitcast.73), kind=kOutput, calls=%fused_computation.3 | convolution fusion | flops 1074790400 | bytes 4198404 | tf_op jit(solution)/shard_map/dot_general | solution.py:454
  127.1 7.1 %all-to-all-start.2 = ((f16[16,64,1024]{2,1,0:T(8,128)(2,1)}), f16[16,64,1024]{2,1,0:T(8,128)(2,1)S(1)}, u32[]{:S(2)}, u32[]{:S(2)}) async-start(f16[16,64,1024]{2,1,0:T(8,128)(2,1)} %bitcast.70), calls=%async_computation.2 | async-start | bytes 4194304 | tf_op jit(solution)/shard_map/all_to_all | solution.py:449
  134.2 3.2 %fusion.1 = f32[512,1024]{1,0:T(8,128)S(1)} fusion(bf16[1024,1024]{1,0:T(8,128)(2,1)} %get-tuple-element.75, bf16[1024,1024]{1,0:T(8,128)(2,1)} %get-tuple-element.74, s32[]{:T(128)S(6)} %select_n.482), kind=kOutput, calls=%fused_computation.6 | convolution fusion | flops 1073741824 | bytes 5242884 | tf_op jit(solution)/shard_map/dot_general | solution.py:457
  141.6 3.7 %collective-permute-done.24 = f32[8,128]{1,0:T(8,128)} collective-permute-done((f32[8,128]{1,0:T(8,128)S(1)}, f32[8,128]{1,0:T(8,128)}, u32[]{:S(2)}, u32[]{:S(2)}) %collective-permute-start.24) | collective-permute-done | bytes 4128 | tf_op jit(solution)/shard_map/ppermute | solution.py:58
  157.5 4.6 %collective-permute-start.30 = (f32[8,128]{1,0:T(8,128)S(1)}, f32[8,128]{1,0:T(8,128)}, u32[]{:S(2)}, u32[]{:S(2)}) collective-permute-start(f32[8,128]{1,0:T(8,128)S(1)} %add.817), channel_id=1, source_target_pairs={{0,4},{1,5},{2,6},{3,7},{4,0},{5,1},{6,2},{7,3},{8,12},{9,13},{10,... | collective-permute-start | bytes 12296 | tf_op jit(solution)/shard_map/ppermute | solution.py:58
  162.1 3.1 %collective-permute-done.30 = f32[8,128]{1,0:T(8,128)} collective-permute-done((f32[8,128]{1,0:T(8,128)S(1)}, f32[8,128]{1,0:T(8,128)}, u32[]{:S(2)}, u32[]{:S(2)}) %collective-permute-start.30) | collective-permute-done | bytes 4128 | tf_op jit(solution)/shard_map/ppermute | solution.py:58
  166.8 3.3 %collective-permute-start.31 = (f16[64,1024]{1,0:T(8,128)(2,1)S(1)}, f16[64,1024]{1,0:T(8,128)(2,1)S(1)}, u32[]{:S(2)}, u32[]{:S(2)}) collective-permute-start(f16[64,1024]{1,0:T(8,128)(2,1)S(1)} %get-tuple-element.86), channel_id=1, source_target_pairs={{0,38},{1,33},{2,32},{3,35},{4,34},{5,37},{6,36},{7,39},{8,46},{9,... | collective-permute-start | bytes 393224 | tf_op jit(solution)/shard_map/ppermute | solution.py:58
  172.6 3.8 %collective-permute-done.32 = f16[64,1024]{1,0:T(8,128)(2,1)} collective-permute-done((f16[64,1024]{1,0:T(8,128)(2,1)S(1)}, f16[64,1024]{1,0:T(8,128)(2,1)}, u32[]{:S(2)}, u32[]{:S(2)}) %collective-permute-start.32) | collective-permute-done | bytes 131104 | tf_op jit(solution)/shard_map/ppermute | solution.py:58
  (97 shorter events, 58.2 us)
Async XLA Ops:
  2.5 8.9 %collective-permute-start = (bf16[64,2048]{1,0:T(8,128)(2,1)}, bf16[64,2048]{1,0:T(8,128)(2,1)S(1)}, u32[]{:S(2)}, u32[]{:S(2)}) collective-permute-start(bf16[64,2048]{1,0:T(8,128)(2,1)} %get-tuple-element.46), channel_id=1, source_target_pairs={{0,8},{1,65},{2,10},{3,67},{4,12},{5,69},{6,14},{7,71},{8,16},{9,7... | collective-permute-start | bytes 786440 | tf_op jit(solution)/shard_map/ppermute | solution.py:58
  4.0 8.8 %collective-permute-start.1 = (bf16[64,2048]{1,0:T(8,128)(2,1)}, bf16[64,2048]{1,0:T(8,128)(2,1)S(1)}, u32[]{:S(2)}, u32[]{:S(2)}) collective-permute-start(bf16[64,2048]{1,0:T(8,128)(2,1)} %get-tuple-element.46), channel_id=1, source_target_pairs={{0,24},{1,193},{2,26},{3,195},{4,28},{5,197},{6,30},{7,199},{8,0},... | collective-permute-start | bytes 786440 | tf_op jit(solution)/shard_map/ppermute | solution.py:58
  5.8 8.3 %collective-permute-start.2 = (bf16[64,2048]{1,0:T(8,128)(2,1)}, bf16[64,2048]{1,0:T(8,128)(2,1)S(1)}, u32[]{:S(2)}, u32[]{:S(2)}) collective-permute-start(bf16[64,2048]{1,0:T(8,128)(2,1)} %get-tuple-element.46), channel_id=1, source_target_pairs={{0,16},{1,129},{2,18},{3,131},{4,20},{5,133},{6,22},{7,135},{8,24}... | collective-permute-start | bytes 786440 | tf_op jit(solution)/shard_map/ppermute | solution.py:58
  7.6 10.4 %collective-permute-start.3 = (bf16[64,2048]{1,0:T(8,128)(2,1)}, bf16[64,2048]{1,0:T(8,128)(2,1)S(1)}, u32[]{:S(2)}, u32[]{:S(2)}) collective-permute-start(bf16[64,2048]{1,0:T(8,128)(2,1)} %get-tuple-element.47.refs_6_), channel_id=1, source_target_pairs={{0,32},{1,39},{2,34},{3,33},{4,36},{5,35},{6,38},{7,37},{8,40},{9,... | collective-permute-start | bytes 786440 | tf_op jit(solution)/shard_map/ppermute | solution.py:58
  9.5 8.5 %collective-permute-start.4 = (bf16[64,2048]{1,0:T(8,128)(2,1)}, bf16[64,2048]{1,0:T(8,128)(2,1)S(1)}, u32[]{:S(2)}, u32[]{:S(2)}) collective-permute-start(bf16[64,2048]{1,0:T(8,128)(2,1)} %get-tuple-element.47.refs_6_), channel_id=1, source_target_pairs={{0,1},{1,0},{2,3},{3,2},{4,5},{5,4},{6,7},{7,6},{8,9},{9,8},{10,11... | collective-permute-start | bytes 786440 | tf_op jit(solution)/shard_map/ppermute | solution.py:58
  19.2 22.9 %collective-permute-start.5 = (bf16[256,2048]{1,0:T(8,128)(2,1)S(1)}, bf16[256,2048]{1,0:T(8,128)(2,1)S(1)}, u32[]{:S(2)}, u32[]{:S(2)}) collective-permute-start(bf16[256,2048]{1,0:T(8,128)(2,1)S(1)} %pad_maximum_fusion.refs_1_), channel_id=1, source_target_pairs={{0,64},{1,9},{2,66},{3,11},{4,68},{5,13},{6,70},{7,15},{8,72},{9,1... | collective-permute-start | bytes 3145736 | tf_op jit(solution)/shard_map/ppermute | solution.py:58
  20.8 21.2 %collective-permute-start.6 = (bf16[256,2048]{1,0:T(8,128)(2,1)S(1)}, bf16[256,2048]{1,0:T(8,128)(2,1)S(1)}, u32[]{:S(2)}, u32[]{:S(2)}) collective-permute-start(bf16[256,2048]{1,0:T(8,128)(2,1)S(1)} %pad_maximum_fusion.refs_1_), channel_id=1, source_target_pairs={{0,192},{1,25},{2,194},{3,27},{4,196},{5,29},{6,198},{7,31},{8,200... | collective-permute-start | bytes 3145736 | tf_op jit(solution)/shard_map/ppermute | solution.py:58
  21.3 7.6 %collective-permute-start.7 = (bf16[64,2048]{1,0:T(8,128)(2,1)S(1)}, bf16[64,2048]{1,0:T(8,128)(2,1)S(1)}, u32[]{:S(2)}, u32[]{:S(2)}) collective-permute-start(bf16[64,2048]{1,0:T(8,128)(2,1)S(1)} %collective-permute-done.3), channel_id=1, source_target_pairs={{0,32},{1,39},{2,34},{3,33},{4,36},{5,35},{6,38},{7,37},{8,40},{9,... | collective-permute-start | bytes 786440 | tf_op jit(solution)/shard_map/ppermute | solution.py:58
  21.3 10.4 %collective-permute-start.8 = (bf16[64,2048]{1,0:T(8,128)(2,1)S(1)}, bf16[64,2048]{1,0:T(8,128)(2,1)S(1)}, u32[]{:S(2)}, u32[]{:S(2)}) collective-permute-start(bf16[64,2048]{1,0:T(8,128)(2,1)S(1)} %collective-permute-done.4.refs_7_), channel_id=1, source_target_pairs={{0,32},{1,39},{2,34},{3,33},{4,36},{5,35},{6,38},{7,37},{8,40},{9,... | collective-permute-start | bytes 786440 | tf_op jit(solution)/shard_map/ppermute | solution.py:58
  31.7 10.4 %collective-permute-start.9 = (bf16[64,2048]{1,0:T(8,128)(2,1)S(1)}, bf16[64,2048]{1,0:T(8,128)(2,1)S(1)}, u32[]{:S(2)}, u32[]{:S(2)}) collective-permute-start(bf16[64,2048]{1,0:T(8,128)(2,1)S(1)} %collective-permute-done.7), channel_id=1, source_target_pairs={{0,32},{1,39},{2,34},{3,33},{4,36},{5,35},{6,38},{7,37},{8,40},{9,... | collective-permute-start | bytes 786440 | tf_op jit(solution)/shard_map/ppermute | solution.py:58
  44.2 14.1 %collective-permute-start.13 = (bf16[320,2048]{1,0:T(8,128)(2,1)}, bf16[320,2048]{1,0:T(8,128)(2,1)}, u32[]{:S(2)}, u32[]{:S(2)}) collective-permute-start(bf16[320,2048]{1,0:T(8,128)(2,1)} %constant_dynamic-update-slice_fusion.refs_8_), channel_id=1, source_target_pairs={{0,1},{1,0},{2,3},{3,2},{4,5},{5,4},{6,7},{7,6},{8,9},{9,8},{10,11... | collective-permute-start | bytes 3932168 | tf_op jit(solution)/shard_map/ppermute | solution.py:58
  44.2 7.6 %collective-permute-start.14 = (bf16[64,2048]{1,0:T(8,128)(2,1)S(1)}, bf16[64,2048]{1,0:T(8,128)(2,1)S(1)}, u32[]{:S(2)}, u32[]{:S(2)}) collective-permute-start(bf16[64,2048]{1,0:T(8,128)(2,1)S(1)} %collective-permute-done.9), channel_id=1, source_target_pairs={{0,32},{1,39},{2,34},{3,33},{4,36},{5,35},{6,38},{7,37},{8,40},{9,... | collective-permute-start | bytes 786440 | tf_op jit(solution)/shard_map/ppermute | solution.py:58
  44.2 10.4 %collective-permute-start.15 = (bf16[64,2048]{1,0:T(8,128)(2,1)S(1)}, bf16[64,2048]{1,0:T(8,128)(2,1)S(1)}, u32[]{:S(2)}, u32[]{:S(2)}) collective-permute-start(bf16[64,2048]{1,0:T(8,128)(2,1)S(1)} %collective-permute-done.10), channel_id=1, source_target_pairs={{0,32},{1,39},{2,34},{3,33},{4,36},{5,35},{6,38},{7,37},{8,40},{9,... | collective-permute-start | bytes 786440 | tf_op jit(solution)/shard_map/ppermute | solution.py:58
  45.2 11.3 %collective-permute-start.11 = (bf16[128,2048]{1,0:T(8,128)(2,1)}, bf16[128,2048]{1,0:T(8,128)(2,1)}, u32[]{:S(2)}, u32[]{:S(2)}) collective-permute-start(bf16[128,2048]{1,0:T(8,128)(2,1)} %slice.21), channel_id=1, source_target_pairs={{0,64},{1,9},{2,66},{3,11},{4,68},{5,13},{6,70},{7,15},{8,72},{9,1... | collective-permute-start | bytes 1572872 | tf_op jit(solution)/shard_map/ppermute | solution.py:58
  47.6 9.5 %collective-permute-start.12 = (bf16[128,2048]{1,0:T(8,128)(2,1)}, bf16[128,2048]{1,0:T(8,128)(2,1)}, u32[]{:S(2)}, u32[]{:S(2)}) collective-permute-start(bf16[128,2048]{1,0:T(8,128)(2,1)} %slice.22), channel_id=1, source_target_pairs={{0,192},{1,25},{2,194},{3,27},{4,196},{5,29},{6,198},{7,31},{8,200... | collective-permute-start | bytes 1572872 | tf_op jit(solution)/shard_map/ppermute | solution.py:58
  75.7 8.3 %collective-permute-start.18 = (f32[2,1152]{1,0:T(2,128)S(1)}, f32[2,1152]{1,0:T(2,128)S(1)}, u32[]{:S(2)}, u32[]{:S(2)}) collective-permute-start(f32[2,1152]{1,0:T(2,128)S(1)} %add_select_fusion.8), channel_id=1, source_target_pairs={{0,32},{1,33},{2,34},{3,35},{4,36},{5,37},{6,38},{7,39},{8,40},{9,... | collective-permute-start | bytes 27656 | tf_op jit(solution)/shard_map/ppermute | solution.py:58
  77.0 13.3 %all-to-all-start = ((f32[16,2,1152]{2,1,0:T(2,128)}), f32[16,2,1152]{2,1,0:T(2,128)S(1)}, u32[]{:S(2)}, u32[]{:S(2)}) async-start(f32[16,2,1152]{2,1,0:T(2,128)} %get-tuple-element.67), calls=%async_computation | async-start | bytes 294912 | tf_op jit(solution)/shard_map/all_to_all | solution.py:395
  95.2 7.7 %collective-permute-start.20 = (f32[2,1152]{1,0:T(2,128)S(1)}, f32[2,1152]{1,0:T(2,128)S(1)}, u32[]{:S(2)}, u32[]{:S(2)}) collective-permute-start(f32[2,1152]{1,0:T(2,128)S(1)} %add_select_fusion.6), channel_id=1, source_target_pairs={{0,4},{1,5},{2,6},{3,7},{4,0},{5,1},{6,2},{7,3},{8,12},{9,13},{10,... | collective-permute-start | bytes 27656 | tf_op jit(solution)/shard_map/ppermute | solution.py:58
  112.6 11.5 %all-to-all-start.1 = ((f32[16,8,128]{2,1,0:T(8,128)}), f32[16,8,128]{2,1,0:T(8,128)S(1)}, u32[]{:S(2)}, u32[]{:S(2)}) async-start(f32[16,8,128]{2,1,0:T(8,128)} %get-tuple-element.73), calls=%async_computation.1 | async-start | bytes 131072 | tf_op jit(solution)/shard_map/all_to_all | solution.py:395
  127.0 10.4 %collective-permute-start.21 = (f16[512,1024]{1,0:T(8,128)(2,1)S(1)}, f16[512,1024]{1,0:T(8,128)(2,1)}, u32[]{:S(2)}, u32[]{:S(2)}) collective-permute-start(f16[512,1024]{1,0:T(8,128)(2,1)S(1)} %multiply_convert_fusion.1), channel_id=1, source_target_pairs={{0,1},{1,0},{2,3},{3,2},{4,5},{5,4},{6,7},{7,6},{8,9},{9,8},{10,11... | collective-permute-start | bytes 3145736 | tf_op jit(solution)/shard_map/ppermute | solution.py:58
  127.1 51.0 %all-to-all-start.2 = ((f16[16,64,1024]{2,1,0:T(8,128)(2,1)}), f16[16,64,1024]{2,1,0:T(8,128)(2,1)S(1)}, u32[]{:S(2)}, u32[]{:S(2)}) async-start(f16[16,64,1024]{2,1,0:T(8,128)(2,1)} %bitcast.70), calls=%async_computation.2 | async-start | bytes 4194304 | tf_op jit(solution)/shard_map/all_to_all | solution.py:449
  155.2 10.7 %collective-permute-start.28 = (f16[64,1024]{1,0:T(8,128)(2,1)S(1)}, f16[64,1024]{1,0:T(8,128)(2,1)S(1)}, u32[]{:S(2)}, u32[]{:S(2)}) collective-permute-start(f16[64,1024]{1,0:T(8,128)(2,1)S(1)} %get-tuple-element.82), channel_id=1, source_target_pairs={{0,38},{1,33},{2,32},{3,35},{4,34},{5,37},{6,36},{7,39},{8,46},{9,... | collective-permute-start | bytes 393224 | tf_op jit(solution)/shard_map/ppermute | solution.py:58
  157.5 8.3 %collective-permute-start.29 = (f16[64,1024]{1,0:T(8,128)(2,1)S(1)}, f16[64,1024]{1,0:T(8,128)(2,1)}, u32[]{:S(2)}, u32[]{:S(2)}) collective-permute-start(f16[64,1024]{1,0:T(8,128)(2,1)S(1)} %get-tuple-element.83), channel_id=1, source_target_pairs={{0,32},{1,39},{2,34},{3,33},{4,36},{5,35},{6,38},{7,37},{8,40},{9,... | collective-permute-start | bytes 393224 | tf_op jit(solution)/shard_map/ppermute | solution.py:58
  157.5 7.7 %collective-permute-start.30 = (f32[8,128]{1,0:T(8,128)S(1)}, f32[8,128]{1,0:T(8,128)}, u32[]{:S(2)}, u32[]{:S(2)}) collective-permute-start(f32[8,128]{1,0:T(8,128)S(1)} %add.817), channel_id=1, source_target_pairs={{0,4},{1,5},{2,6},{3,7},{4,0},{5,1},{6,2},{7,3},{8,12},{9,13},{10,... | collective-permute-start | bytes 12296 | tf_op jit(solution)/shard_map/ppermute | solution.py:58
  (17 other events, 120.2 us)

commit v8 on v6

--- a/solution.py
+++ b/solution.py
@@ -27,7 +27,7 @@
 CHUNK = 256
 GROUP = 16
 LOGITS_VMEM = 58 * 1024 * 1024
-GRADIENT_VMEM = 56 * 1024 * 1024
+GRADIENT_VMEM = 20 * 1024 * 1024
 ROWS = 256
 
 
@@ -255,7 +255,7 @@
     def kernel(*refs):
         logits_kernel((len(text), len(images)), *refs)
 
-    square = jax.ShapeDtypeStruct((SIDE, SIDE), f32)
+    square = pltpu.HBM((SIDE, SIDE), f32)
     half = jax.ShapeDtypeStruct((SIDE, WIDTH), jnp.bfloat16)
     small = jax.ShapeDtypeStruct((GROUP, 2, SIDE + 128), f32)
     return pl.pallas_call(
@@ -380,7 +380,7 @@
         cost_estimate=pl.CostEstimate(
             flops=16 * SIDE * SIDE, bytes_accessed=10 << 20, transcendentals=4 * SIDE * SIDE
         ),
-    )(s, t, row, col, row_id, col_id)
+    )(*(pltpu.with_memory_space_constraint(v, pltpu.HBM) for v in (s, t)), row, col, row_id, col_id)
 
 
 def exchanged(copies, axis):
@@ -423,6 +423,17 @@
     text_scale, image_scale = factors[0:1], factors[1:2]
     image_factor, text_factor = factors[2:3], factors[3:4]
 
+    tie = lax.optimization_barrier
+    value = jnp.sum(exchanged(part, TEXT_GROUP), axis=0)
+    text_part = (
+        lax.dot_general(
+            gradient, image_slab, (((0,), (0,)), ((), ())), preferred_element_type=jnp.float32
+        )
+        * image_scale
+    ).astype(jnp.float16)
+    text_part, gradient, value = tie((text_part, gradient, value))
+    text_blocks = lax.all_to_all(text_part.reshape(16, BLOCK, WIDTH), TEXT_GROUP, 0, 0, tiled=True)
+
     half = SIDE // 2
     theirs = lax.dynamic_slice_in_dim(gradient, (1 - c) * half, half)
     mine = lax.dynamic_slice_in_dim(gradient, c * half, half)
@@ -441,39 +452,19 @@
     def narrow(v):
         return v.astype(jnp.float16)
 
-    tie = lax.optimization_barrier
-    steps = [other_core] + [lambda p, k=k: flipped(p, k) for k in (1, 2, 4)]
-    start, gradient, part = tie((narrow(block(4)), gradient, part))
-    down = moved(start, along_z(-1))
-    value = jnp.sum(exchanged(part, TEXT_GROUP), axis=0)
-    text_part = (
-        lax.dot_general(
-            gradient, image_slab, (((0,), (0,)), ((), ())), preferred_element_type=jnp.float32
-        )
-        * image_scale
-    ).astype(jnp.float16)
-    down, value, text_part = tie((down, value, text_part))
-    text_blocks = lax.all_to_all(text_part.reshape(16, BLOCK, WIDTH), TEXT_GROUP, 0, 0, tiled=True)
-    down = down.astype(jnp.float32)
+    down = moved(narrow(block(4)), along_z(-1)).astype(jnp.float32)
+    copies = jnp.broadcast_to(value, (GROUP, 8, 128))
+    value = jnp.sum(exchanged(copies, IMAGE_GROUP), axis=0)
     up = None
     for k in (3, 2, 1):
         first = narrow(block(-k) + down)
         second = narrow(block(k) if up is None else block(k) + up)
-        first, second, value = tie((first, second, value))
         down = moved(first, along_z(-1)).astype(jnp.float32)
         up = moved(second, along_z(1)).astype(jnp.float32)
-        value = value + moved(value, steps[3 - k])
-    value = value + moved(value, steps[3])
     loss = value[0, 0] / (256 * BLOCK)
     image_grad = (block(0) + down + up) * image_factor
     text_grad = jnp.sum(text_blocks.astype(jnp.float32), axis=0) * text_factor
     return (loss, image_grad, text_grad)
-
-
-def flipped(p, bit):
-    y, zl, x, zh, c = p
-    z = (zh * 2 + zl) ^ bit
-    return (y, z % 2, x, z // 2, c)
 
 
 def solution(mesh):

time: 172 us -> 181 us (1.052)
  local copies, waits for them, and re-layouts: 3.3 us -> 7.16 us
  starting transfers between devices: 47.9 us -> 51.1 us
  waiting for transfers between devices: 70.1 us -> 73 us
    all_to_all x3 -> x4, waiting for transfers between devices: 14.1 us -> 19.9 us  [exchanged(): return lax.all_to_all(copies, axis, split_axis=0, concat_axis=0, tiled=True)]
    all_to_all x3 -> x4, starting transfers between devices: 17.4 us -> 21.3 us  [exchanged(): return lax.all_to_all(copies, axis, split_axis=0, concat_axis=0, tiled=True)]
    ppermute x29 -> x25, waiting for transfers between devices: 56 us -> 53.1 us  [moved(): return lax.ppermute(value, NAMES, pairs)]
    unnamed x25 -> x17, local copies, waits for them, and re-layouts: 0.99 us -> 3.76 us
    convert_element_type x1, other arithmetic: 0.43 us -> 2.29 us  [body(): blocks = image_mine.astype(jnp.float16).reshape(8, BLOCK, WIDTH)]
    ppermute x29 -> x25, starting transfers between devices: 23.7 us -> 23.2 us  [moved(): return lax.ppermute(value, NAMES, pairs)]
  transfers between devices with their start and end apart: 33 -> 30, of which waited for: 20 -> 19; matrix products, arithmetic and copies ran while one was open for 10% -> 11% of each run, Pallas kernels for 0% -> 0%
where the time goes in v8:
time: 181 us; the launch traced here: 180 us
  waiting for transfers between devices  73 us (40%)
  starting transfers between devices  51.1 us (28%)
  Pallas kernels  24.9 us (14%)
  matrix products  12.4 us (7%)
  other arithmetic  8.51 us (5%)
  local copies, waits for them, and re-layouts  7.16 us (4%)
  between operations  3.38 us (2%)
    ppermute x25, waiting for transfers between devices, moved(): return lax.ppermute(value, NAMES, pairs)  53.1 us
    ppermute x25, starting transfers between devices, moved(): return lax.ppermute(value, NAMES, pairs)  23.2 us
    all_to_all x4, starting transfers between devices, exchanged(): return lax.all_to_all(copies, axis, split_axis=0, concat_axis=0, tiled=True)  21.3 us
    all_to_all x4, waiting for transfers between devices, exchanged(): return lax.all_to_all(copies, axis, split_axis=0, concat_axis=0, tiled=True)  19.9 us
    pallas_call x1, Pallas kernels, logits_and_statistics(): pl.pallas_call(kernel, out_shape=(square, square, half, half, small, smal...  15.5 us
    pallas_call x1, Pallas kernels, gradient_of_logits(): pl.pallas_call(gradient_kernel, grid=(SIDE // ROWS,), out_shape=(jax.Shap...  7.54 us
    all_to_all x1, starting transfers between devices, body(): lax.all_to_all(text_part.reshape(16, BLOCK, WIDTH), TEXT_GROUP, 0, 0, til...  6.62 us
    dot_general x1, matrix products, body(): lax.dot_general(gradient, image_slab, (((0,), (0,)), ((), ())), preferred...  5.35 us
  transfers between devices with their start and end apart: 30, of which 19 were waited for; matrix products, arithmetic and copies ran while one was open for 11% of the time, Pallas kernels for 0%

profile of v8, /device:TPU:8, one launch (start us, length us, event | category | flops | bytes accessed | tf_op | source)
XLA Modules:
  0.0 180.5 jit_solution(11038087162965718828)
XLA Ops:
  14.1 3.9 %collective-permute-done.3 = bf16[64,2048]{1,0:T(8,128)(2,1)S(1)} collective-permute-done((bf16[64,2048]{1,0:T(8,128)(2,1)}, bf16[64,2048]{1,0:T(8,128)(2,1)S(1)}, u32[]{:S(2)}, u32[]{:S(2)}) %collective-permute-start.3) | collective-permute-done | bytes 262176 | tf_op jit(solution)/shard_map/ppermute | solution.py:59
  21.3 7.6 %collective-permute-done.7 = bf16[64,2048]{1,0:T(8,128)(2,1)S(1)} collective-permute-done((bf16[64,2048]{1,0:T(8,128)(2,1)S(1)}, bf16[64,2048]{1,0:T(8,128)(2,1)S(1)}, u32[]{:S(2)}, u32[]{:S(2)}) %collective-permute-start.7) | collective-permute-done | bytes 262176 | tf_op jit(solution)/shard_map/ppermute | solution.py:59
  28.9 2.8 %collective-permute-done.8 = bf16[64,2048]{1,0:T(8,128)(2,1)S(1)} collective-permute-done((bf16[64,2048]{1,0:T(8,128)(2,1)S(1)}, bf16[64,2048]{1,0:T(8,128)(2,1)S(1)}, u32[]{:S(2)}, u32[]{:S(2)}) %collective-permute-start.8) | collective-permute-done | bytes 262176 | tf_op jit(solution)/shard_map/ppermute | solution.py:59
  33.1 6.1 %collective-permute-done.10 = bf16[64,2048]{1,0:T(8,128)(2,1)S(1)} collective-permute-done((bf16[64,2048]{1,0:T(8,128)(2,1)S(1)}, bf16[64,2048]{1,0:T(8,128)(2,1)S(1)}, u32[]{:S(2)}, u32[]{:S(2)}) %collective-permute-start.10) | collective-permute-done | bytes 262176 | tf_op jit(solution)/shard_map/ppermute | solution.py:59
  46.6 5.3 %collective-permute-done.14 = bf16[64,2048]{1,0:T(8,128)(2,1)S(1)} collective-permute-done((bf16[64,2048]{1,0:T(8,128)(2,1)S(1)}, bf16[64,2048]{1,0:T(8,128)(2,1)S(1)}, u32[]{:S(2)}, u32[]{:S(2)}) %collective-permute-start.14) | collective-permute-done | bytes 262176 | tf_op jit(solution)/shard_map/ppermute | solution.py:59
  57.8 15.5 %shard_map.68 = (f32[1024,1024]{1,0:T(8,128)}, f32[1024,1024]{1,0:T(8,128)}, bf16[1024,1024]{1,0:T(8,128)(2,1)}, bf16[1024,1024]{1,0:T(8,128)(2,1)}, f32[16,2,1152]{2,1,0:T(2,128)}, /*index=5*/f32[16,2,1152]{2,1,0:T(2,128)}) custom-call(s32[32]{0:T(128)} %stack.131.refs_0_, bf16[256,2048]{1,0:T(8,128)(2,1)} %copy-done, bf16[256,2048]{1,0:T(8,128)(2,1)} %copy-done.1, ...), custom_call_target="tpu_custom_call" | custom-call | flops 4294967296 | bytes 20971520 | tf_op jit(solution)/shard_map/pallas_call | solution.py:261
  73.3 6.1 %all-to-all-start.1 = ((f32[16,2,1152]{2,1,0:T(2,128)}), f32[16,2,1152]{2,1,0:T(2,128)S(1)}, u32[]{:S(2)}, u32[]{:S(2)}) async-start(f32[16,2,1152]{2,1,0:T(2,128)} %get-tuple-element.54), calls=%async_computation.1 | async-start | bytes 294912 | tf_op jit(solution)/shard_map/all_to_all | solution.py:387
  79.4 6.3 %all-to-all-done.1.col_ref = f32[16,2,1152]{2,1,0:T(2,128)S(1)} async-done(((f32[16,2,1152]{2,1,0:T(2,128)}), f32[16,2,1152]{2,1,0:T(2,128)S(1)}, u32[]{:S(2)}, u32[]{:S(2)}) %all-to-all-start.1) | async-done | bytes 147488 | tf_op jit(solution)/shard_map/all_to_all | solution.py:387
  85.7 6.6 %all-to-all-start = ((f32[16,2,1152]{2,1,0:T(2,128)}), f32[16,2,1152]{2,1,0:T(2,128)S(1)}, u32[]{:S(2)}, u32[]{:S(2)}) async-start(f32[16,2,1152]{2,1,0:T(2,128)} %get-tuple-element.53), calls=%async_computation | async-start | bytes 294912 | tf_op jit(solution)/shard_map/all_to_all | solution.py:387
  92.7 8.8 %all-to-all-done.row_ref = f32[16,2,1152]{2,1,0:T(2,128)S(1)} async-done(((f32[16,2,1152]{2,1,0:T(2,128)}), f32[16,2,1152]{2,1,0:T(2,128)S(1)}, u32[]{:S(2)}, u32[]{:S(2)}) %all-to-all-start) | async-done | bytes 147488 | tf_op jit(solution)/shard_map/all_to_all | solution.py:387
  101.5 7.5 %shard_map.69 = (bf16[1024,1024]{1,0:T(8,128)(2,1)S(1)}, f32[8,1024]{1,0:T(8,128)S(1)}, f32[16,8,128]{2,1,0:T(8,128)}) custom-call(f32[1024,1024]{1,0:T(8,128)} %get-tuple-element.51.s_ref, f32[1024,1024]{1,0:T(8,128)} %get-tuple-element.52.t_ref, f32[16,2,1152]{2,1,0:T(2,128)S(1)} %all-to-all-done.row_ref, f32[16,2,1152]{2,1,0:T(2,128)S(1)} %all-to-all-done.1.col_ref, ...), custom_call_target="tpu_custom_call" | custom-call | flops 16777216 | bytes 10485760 | tf_op jit(solution)/shard_map/pallas_call | solution.py:361
  109.1 5.1 %all-to-all-start.2 = ((f32[16,8,128]{2,1,0:T(8,128)}), f32[16,8,128]{2,1,0:T(8,128)S(1)}, u32[]{:S(2)}, u32[]{:S(2)}) async-start(f32[16,8,128]{2,1,0:T(8,128)} %get-tuple-element.58), calls=%async_computation.2 | async-start | bytes 131072 | tf_op jit(solution)/shard_map/all_to_all | solution.py:387
  114.1 5.4 %multiply_convert_fusion = f16[1024,1024]{1,0:T(8,128)(2,1)} fusion(bf16[1024,1024]{1,0:T(8,128)(2,1)S(1)} %get-tuple-element.60, bf16[1024,1024]{1,0:T(8,128)(2,1)} %get-tuple-element.56, f32[1024]{0:T(1024)S(1)} %bitcast.76), kind=kOutput, calls=%fused_computation.1 | convolution fusion | flops 2149580800 | bytes 6295552 | tf_op jit(solution)/shard_map/dot_general | solution.py:429
  120.5 2.8 %multiply_convert_fusion.1 = f16[512,1024]{1,0:T(8,128)(2,1)S(1)} fusion(bf16[1024,1024]{1,0:T(8,128)(2,1)} %get-tuple-element.61, bf16[1024,1024]{1,0:T(8,128)(2,1)S(1)} %get-tuple-element.60, s32[]{:T(128)S(6)} %select_n.466, f32[1024]{0:T(1024)S(1)} %bitcast.74), kind=kOutput, calls=%fused_computation.3 | convolution fusion | flops 1074790400 | bytes 4198404 | tf_op jit(solution)/shard_map/dot_general | solution.py:440
  124.1 3.5 %all-to-all-start.3 = ((f32[16,8,128]{2,1,0:T(8,128)}), f32[16,8,128]{2,1,0:T(8,128)S(1)}, u32[]{:S(2)}, u32[]{:S(2)}) async-start(f32[16,8,128]{2,1,0:T(8,128)} %broadcast_in_dim.2), calls=%async_computation.3 | async-start | bytes 131072 | tf_op jit(solution)/shard_map/all_to_all | solution.py:387
  127.7 4.2 %fusion.1 = f32[512,1024]{1,0:T(8,128)} fusion(bf16[1024,1024]{1,0:T(8,128)(2,1)} %get-tuple-element.61, bf16[1024,1024]{1,0:T(8,128)(2,1)S(1)} %get-tuple-element.60, s32[]{:T(128)S(6)} %select_n.465), kind=kOutput, calls=%fused_computation.6 | convolution fusion | flops 1073741824 | bytes 5242884 | tf_op jit(solution)/shard_map/dot_general | solution.py:443
  131.8 3.7 %all-to-all-done.3 = f32[16,8,128]{2,1,0:T(8,128)S(1)} async-done(((f32[16,8,128]{2,1,0:T(8,128)}), f32[16,8,128]{2,1,0:T(8,128)S(1)}, u32[]{:S(2)}, u32[]{:S(2)}) %all-to-all-start.3) | async-done | bytes 65568 | tf_op jit(solution)/shard_map/all_to_all | solution.py:387
  135.5 6.6 %all-to-all-start.4 = ((f16[16,64,1024]{2,1,0:T(8,128)(2,1)}), f16[16,64,1024]{2,1,0:T(8,128)(2,1)S(1)}, u32[]{:S(2)}, u32[]{:S(2)}) async-start(f16[16,64,1024]{2,1,0:T(8,128)(2,1)} %bitcast.71), calls=%async_computation.4 | async-start | bytes 4194304 | tf_op jit(solution)/shard_map/all_to_all | solution.py:435
  145.6 4.5 %collective-permute-done.18 = f16[64,1024]{1,0:T(8,128)(2,1)S(1)} collective-permute-done((f16[64,1024]{1,0:T(8,128)(2,1)S(1)}, f16[64,1024]{1,0:T(8,128)(2,1)S(1)}, u32[]{:S(2)}, u32[]{:S(2)}) %collective-permute-start.18) | collective-permute-done | bytes 131104 | tf_op jit(solution)/shard_map/ppermute | solution.py:59
  152.5 3.7 %collective-permute-done.19 = f16[64,1024]{1,0:T(8,128)(2,1)S(1)} collective-permute-done((f16[64,1024]{1,0:T(8,128)(2,1)S(1)}, f16[64,1024]{1,0:T(8,128)(2,1)S(1)}, u32[]{:S(2)}, u32[]{:S(2)}) %collective-permute-start.19) | collective-permute-done | bytes 131104 | tf_op jit(solution)/shard_map/ppermute | solution.py:59
  156.3 3.1 %collective-permute-start.20 = (f16[64,1024]{1,0:T(8,128)(2,1)S(1)}, f16[64,1024]{1,0:T(8,128)(2,1)S(1)}, u32[]{:S(2)}, u32[]{:S(2)}) collective-permute-start(f16[64,1024]{1,0:T(8,128)(2,1)S(1)} %fusion.30), channel_id=1, source_target_pairs={{0,38},{1,33},{2,32},{3,35},{4,34},{5,37},{6,36},{7,39},{8,46},{9,... | collective-permute-start | bytes 393224 | tf_op jit(solution)/shard_map/ppermute | solution.py:59
  163.6 3.7 %collective-permute-start.21 = (f16[64,1024]{1,0:T(8,128)(2,1)}, f16[64,1024]{1,0:T(8,128)(2,1)}, u32[]{:S(2)}, u32[]{:S(2)}) collective-permute-start(f16[64,1024]{1,0:T(8,128)(2,1)} %get-tuple-element.63), channel_id=1, source_target_pairs={{0,38},{1,33},{2,32},{3,35},{4,34},{5,37},{6,36},{7,39},{8,46},{9,... | collective-permute-start | bytes 393224 | tf_op jit(solution)/shard_map/ppermute | solution.py:59
  167.2 2.9 %collective-permute-done.23 = f16[64,1024]{1,0:T(8,128)(2,1)S(1)} collective-permute-done((f16[64,1024]{1,0:T(8,128)(2,1)S(1)}, f16[64,1024]{1,0:T(8,128)(2,1)S(1)}, u32[]{:S(2)}, u32[]{:S(2)}) %collective-permute-start.23) | collective-permute-done | bytes 131104 | tf_op jit(solution)/shard_map/ppermute | solution.py:59
  171.5 5.0 %collective-permute-done.24 = f16[64,1024]{1,0:T(8,128)(2,1)S(1)} collective-permute-done((f16[64,1024]{1,0:T(8,128)(2,1)S(1)}, f16[64,1024]{1,0:T(8,128)(2,1)S(1)}, u32[]{:S(2)}, u32[]{:S(2)}) %collective-permute-start.24) | collective-permute-done | bytes 131104 | tf_op jit(solution)/shard_map/ppermute | solution.py:59
  (81 shorter events, 46.4 us)
Async XLA Ops:
  2.5 8.9 %collective-permute-start = (bf16[64,2048]{1,0:T(8,128)(2,1)}, bf16[64,2048]{1,0:T(8,128)(2,1)S(1)}, u32[]{:S(2)}, u32[]{:S(2)}) collective-permute-start(bf16[64,2048]{1,0:T(8,128)(2,1)} %get-tuple-element.33), channel_id=1, source_target_pairs={{0,8},{1,65},{2,10},{3,67},{4,12},{5,69},{6,14},{7,71},{8,16},{9,7... | collective-permute-start | bytes 786440 | tf_op jit(solution)/shard_map/ppermute | solution.py:59
  4.0 8.8 %collective-permute-start.1 = (bf16[64,2048]{1,0:T(8,128)(2,1)}, bf16[64,2048]{1,0:T(8,128)(2,1)S(1)}, u32[]{:S(2)}, u32[]{:S(2)}) collective-permute-start(bf16[64,2048]{1,0:T(8,128)(2,1)} %get-tuple-element.33), channel_id=1, source_target_pairs={{0,24},{1,193},{2,26},{3,195},{4,28},{5,197},{6,30},{7,199},{8,0},... | collective-permute-start | bytes 786440 | tf_op jit(solution)/shard_map/ppermute | solution.py:59
  5.8 8.3 %collective-permute-start.2 = (bf16[64,2048]{1,0:T(8,128)(2,1)}, bf16[64,2048]{1,0:T(8,128)(2,1)S(1)}, u32[]{:S(2)}, u32[]{:S(2)}) collective-permute-start(bf16[64,2048]{1,0:T(8,128)(2,1)} %get-tuple-element.33), channel_id=1, source_target_pairs={{0,16},{1,129},{2,18},{3,131},{4,20},{5,133},{6,22},{7,135},{8,24}... | collective-permute-start | bytes 786440 | tf_op jit(solution)/shard_map/ppermute | solution.py:59
  7.6 10.4 %collective-permute-start.3 = (bf16[64,2048]{1,0:T(8,128)(2,1)}, bf16[64,2048]{1,0:T(8,128)(2,1)S(1)}, u32[]{:S(2)}, u32[]{:S(2)}) collective-permute-start(bf16[64,2048]{1,0:T(8,128)(2,1)} %get-tuple-element.34.refs_6_), channel_id=1, source_target_pairs={{0,32},{1,39},{2,34},{3,33},{4,36},{5,35},{6,38},{7,37},{8,40},{9,... | collective-permute-start | bytes 786440 | tf_op jit(solution)/shard_map/ppermute | solution.py:59
  9.5 8.5 %collective-permute-start.4 = (bf16[64,2048]{1,0:T(8,128)(2,1)}, bf16[64,2048]{1,0:T(8,128)(2,1)S(1)}, u32[]{:S(2)}, u32[]{:S(2)}) collective-permute-start(bf16[64,2048]{1,0:T(8,128)(2,1)} %get-tuple-element.34.refs_6_), channel_id=1, source_target_pairs={{0,1},{1,0},{2,3},{3,2},{4,5},{5,4},{6,7},{7,6},{8,9},{9,8},{10,11... | collective-permute-start | bytes 786440 | tf_op jit(solution)/shard_map/ppermute | solution.py:59
  19.2 22.9 %collective-permute-start.5 = (bf16[256,2048]{1,0:T(8,128)(2,1)S(1)}, bf16[256,2048]{1,0:T(8,128)(2,1)S(1)}, u32[]{:S(2)}, u32[]{:S(2)}) collective-permute-start(bf16[256,2048]{1,0:T(8,128)(2,1)S(1)} %pad_maximum_fusion.refs_1_), channel_id=1, source_target_pairs={{0,64},{1,9},{2,66},{3,11},{4,68},{5,13},{6,70},{7,15},{8,72},{9,1... | collective-permute-start | bytes 3145736 | tf_op jit(solution)/shard_map/ppermute | solution.py:59
  20.8 21.2 %collective-permute-start.6 = (bf16[256,2048]{1,0:T(8,128)(2,1)S(1)}, bf16[256,2048]{1,0:T(8,128)(2,1)S(1)}, u32[]{:S(2)}, u32[]{:S(2)}) collective-permute-start(bf16[256,2048]{1,0:T(8,128)(2,1)S(1)} %pad_maximum_fusion.refs_1_), channel_id=1, source_target_pairs={{0,192},{1,25},{2,194},{3,27},{4,196},{5,29},{6,198},{7,31},{8,200... | collective-permute-start | bytes 3145736 | tf_op jit(solution)/shard_map/ppermute | solution.py:59
  21.3 7.6 %collective-permute-start.7 = (bf16[64,2048]{1,0:T(8,128)(2,1)S(1)}, bf16[64,2048]{1,0:T(8,128)(2,1)S(1)}, u32[]{:S(2)}, u32[]{:S(2)}) collective-permute-start(bf16[64,2048]{1,0:T(8,128)(2,1)S(1)} %collective-permute-done.3), channel_id=1, source_target_pairs={{0,32},{1,39},{2,34},{3,33},{4,36},{5,35},{6,38},{7,37},{8,40},{9,... | collective-permute-start | bytes 786440 | tf_op jit(solution)/shard_map/ppermute | solution.py:59
  21.3 10.4 %collective-permute-start.8 = (bf16[64,2048]{1,0:T(8,128)(2,1)S(1)}, bf16[64,2048]{1,0:T(8,128)(2,1)S(1)}, u32[]{:S(2)}, u32[]{:S(2)}) collective-permute-start(bf16[64,2048]{1,0:T(8,128)(2,1)S(1)} %collective-permute-done.4.refs_7_), channel_id=1, source_target_pairs={{0,32},{1,39},{2,34},{3,33},{4,36},{5,35},{6,38},{7,37},{8,40},{9,... | collective-permute-start | bytes 786440 | tf_op jit(solution)/shard_map/ppermute | solution.py:59
  31.7 7.6 %collective-permute-start.10 = (bf16[64,2048]{1,0:T(8,128)(2,1)S(1)}, bf16[64,2048]{1,0:T(8,128)(2,1)S(1)}, u32[]{:S(2)}, u32[]{:S(2)}) collective-permute-start(bf16[64,2048]{1,0:T(8,128)(2,1)S(1)} %collective-permute-done.8), channel_id=1, source_target_pairs={{0,32},{1,39},{2,34},{3,33},{4,36},{5,35},{6,38},{7,37},{8,40},{9,... | collective-permute-start | bytes 786440 | tf_op jit(solution)/shard_map/ppermute | solution.py:59
  31.7 10.4 %collective-permute-start.9 = (bf16[64,2048]{1,0:T(8,128)(2,1)S(1)}, bf16[64,2048]{1,0:T(8,128)(2,1)S(1)}, u32[]{:S(2)}, u32[]{:S(2)}) collective-permute-start(bf16[64,2048]{1,0:T(8,128)(2,1)S(1)} %collective-permute-done.7), channel_id=1, source_target_pairs={{0,32},{1,39},{2,34},{3,33},{4,36},{5,35},{6,38},{7,37},{8,40},{9,... | collective-permute-start | bytes 786440 | tf_op jit(solution)/shard_map/ppermute | solution.py:59
  44.3 12.7 %collective-permute-start.13 = (bf16[320,2048]{1,0:T(8,128)(2,1)}, bf16[320,2048]{1,0:T(8,128)(2,1)}, u32[]{:S(2)}, u32[]{:S(2)}) collective-permute-start(bf16[320,2048]{1,0:T(8,128)(2,1)} %constant_dynamic-update-slice_fusion.refs_8_), channel_id=1, source_target_pairs={{0,1},{1,0},{2,3},{3,2},{4,5},{5,4},{6,7},{7,6},{8,9},{9,8},{10,11... | collective-permute-start | bytes 3932168 | tf_op jit(solution)/shard_map/ppermute | solution.py:59
  44.3 7.6 %collective-permute-start.14 = (bf16[64,2048]{1,0:T(8,128)(2,1)S(1)}, bf16[64,2048]{1,0:T(8,128)(2,1)S(1)}, u32[]{:S(2)}, u32[]{:S(2)}) collective-permute-start(bf16[64,2048]{1,0:T(8,128)(2,1)S(1)} %collective-permute-done.9), channel_id=1, source_target_pairs={{0,32},{1,39},{2,34},{3,33},{4,36},{5,35},{6,38},{7,37},{8,40},{9,... | collective-permute-start | bytes 786440 | tf_op jit(solution)/shard_map/ppermute | solution.py:59
  44.3 10.4 %collective-permute-start.15 = (bf16[64,2048]{1,0:T(8,128)(2,1)S(1)}, bf16[64,2048]{1,0:T(8,128)(2,1)S(1)}, u32[]{:S(2)}, u32[]{:S(2)}) collective-permute-start(bf16[64,2048]{1,0:T(8,128)(2,1)S(1)} %collective-permute-done.10), channel_id=1, source_target_pairs={{0,32},{1,39},{2,34},{3,33},{4,36},{5,35},{6,38},{7,37},{8,40},{9,... | collective-permute-start | bytes 786440 | tf_op jit(solution)/shard_map/ppermute | solution.py:59
  44.4 12.1 %collective-permute-start.11 = (bf16[128,2048]{1,0:T(8,128)(2,1)S(1)}, bf16[128,2048]{1,0:T(8,128)(2,1)}, u32[]{:S(2)}, u32[]{:S(2)}) collective-permute-start(bf16[128,2048]{1,0:T(8,128)(2,1)S(1)} %slice.21), channel_id=1, source_target_pairs={{0,64},{1,9},{2,66},{3,11},{4,68},{5,13},{6,70},{7,15},{8,72},{9,1... | collective-permute-start | bytes 1572872 | tf_op jit(solution)/shard_map/ppermute | solution.py:59
  46.1 10.4 %collective-permute-start.12 = (bf16[128,2048]{1,0:T(8,128)(2,1)S(1)}, bf16[128,2048]{1,0:T(8,128)(2,1)}, u32[]{:S(2)}, u32[]{:S(2)}) collective-permute-start(bf16[128,2048]{1,0:T(8,128)(2,1)S(1)} %slice.22), channel_id=1, source_target_pairs={{0,192},{1,25},{2,194},{3,27},{4,196},{5,29},{6,198},{7,31},{8,200... | collective-permute-start | bytes 1572872 | tf_op jit(solution)/shard_map/ppermute | solution.py:59
  73.3 12.4 %all-to-all-start.1 = ((f32[16,2,1152]{2,1,0:T(2,128)}), f32[16,2,1152]{2,1,0:T(2,128)S(1)}, u32[]{:S(2)}, u32[]{:S(2)}) async-start(f32[16,2,1152]{2,1,0:T(2,128)} %get-tuple-element.54), calls=%async_computation.1 | async-start | bytes 294912 | tf_op jit(solution)/shard_map/all_to_all | solution.py:387
  85.7 15.8 %all-to-all-start = ((f32[16,2,1152]{2,1,0:T(2,128)}), f32[16,2,1152]{2,1,0:T(2,128)S(1)}, u32[]{:S(2)}, u32[]{:S(2)}) async-start(f32[16,2,1152]{2,1,0:T(2,128)} %get-tuple-element.53), calls=%async_computation | async-start | bytes 294912 | tf_op jit(solution)/shard_map/all_to_all | solution.py:387
  109.1 11.4 %all-to-all-start.2 = ((f32[16,8,128]{2,1,0:T(8,128)}), f32[16,8,128]{2,1,0:T(8,128)S(1)}, u32[]{:S(2)}, u32[]{:S(2)}) async-start(f32[16,8,128]{2,1,0:T(8,128)} %get-tuple-element.58), calls=%async_computation.2 | async-start | bytes 131072 | tf_op jit(solution)/shard_map/all_to_all | solution.py:387
  123.4 18.8 %collective-permute-start.17 = (f16[512,1024]{1,0:T(8,128)(2,1)S(1)}, f16[512,1024]{1,0:T(8,128)(2,1)}, u32[]{:S(2)}, u32[]{:S(2)}) collective-permute-start(f16[512,1024]{1,0:T(8,128)(2,1)S(1)} %multiply_convert_fusion.1), channel_id=1, source_target_pairs={{0,1},{1,0},{2,3},{3,2},{4,5},{5,4},{6,7},{7,6},{8,9},{9,8},{10,11... | collective-permute-start | bytes 3145736 | tf_op jit(solution)/shard_map/ppermute | solution.py:59
  124.1 11.4 %all-to-all-start.3 = ((f32[16,8,128]{2,1,0:T(8,128)}), f32[16,8,128]{2,1,0:T(8,128)S(1)}, u32[]{:S(2)}, u32[]{:S(2)}) async-start(f32[16,8,128]{2,1,0:T(8,128)} %broadcast_in_dim.2), calls=%async_computation.3 | async-start | bytes 131072 | tf_op jit(solution)/shard_map/all_to_all | solution.py:387
  135.5 42.6 %all-to-all-start.4 = ((f16[16,64,1024]{2,1,0:T(8,128)(2,1)}), f16[16,64,1024]{2,1,0:T(8,128)(2,1)S(1)}, u32[]{:S(2)}, u32[]{:S(2)}) async-start(f16[16,64,1024]{2,1,0:T(8,128)(2,1)} %bitcast.71), calls=%async_computation.4 | async-start | bytes 4194304 | tf_op jit(solution)/shard_map/all_to_all | solution.py:435
  152.2 7.2 %collective-permute-start.22 = (f16[64,1024]{1,0:T(8,128)(2,1)}, f16[64,1024]{1,0:T(8,128)(2,1)}, u32[]{:S(2)}, u32[]{:S(2)}) collective-permute-start(f16[64,1024]{1,0:T(8,128)(2,1)} %get-tuple-element.66), channel_id=1, source_target_pairs={{0,32},{1,39},{2,34},{3,33},{4,36},{5,35},{6,38},{7,37},{8,40},{9,... | collective-permute-start | bytes 393224 | tf_op jit(solution)/shard_map/ppermute | solution.py:59
  163.6 7.9 %collective-permute-start.21 = (f16[64,1024]{1,0:T(8,128)(2,1)}, f16[64,1024]{1,0:T(8,128)(2,1)}, u32[]{:S(2)}, u32[]{:S(2)}) collective-permute-start(f16[64,1024]{1,0:T(8,128)(2,1)} %get-tuple-element.63), channel_id=1, source_target_pairs={{0,38},{1,33},{2,32},{3,35},{4,34},{5,37},{6,36},{7,39},{8,46},{9,... | collective-permute-start | bytes 393224 | tf_op jit(solution)/shard_map/ppermute | solution.py:59
  (12 other events, 112.5 us)

commit v9 on v6

--- a/solution.py
+++ b/solution.py
@@ -27,7 +27,7 @@
 CHUNK = 256
 GROUP = 16
 LOGITS_VMEM = 58 * 1024 * 1024
-GRADIENT_VMEM = 56 * 1024 * 1024
+GRADIENT_VMEM = 20 * 1024 * 1024
 ROWS = 256
 
 
@@ -255,7 +255,7 @@
     def kernel(*refs):
         logits_kernel((len(text), len(images)), *refs)
 
-    square = jax.ShapeDtypeStruct((SIDE, SIDE), f32)
+    square = pltpu.HBM((SIDE, SIDE), f32)
     half = jax.ShapeDtypeStruct((SIDE, WIDTH), jnp.bfloat16)
     small = jax.ShapeDtypeStruct((GROUP, 2, SIDE + 128), f32)
     return pl.pallas_call(
@@ -380,7 +380,13 @@
         cost_estimate=pl.CostEstimate(
             flops=16 * SIDE * SIDE, bytes_accessed=10 << 20, transcendentals=4 * SIDE * SIDE
         ),
-    )(s, t, row, col, row_id, col_id)
+    )(
+        *(pltpu.with_memory_space_constraint(v, pltpu.HBM) for v in (s, t)),
+        row,
+        col,
+        row_id,
+        col_id,
+    )
 
 
 def exchanged(copies, axis):
@@ -442,7 +448,7 @@
         return v.astype(jnp.float16)
 
     tie = lax.optimization_barrier
-    steps = [other_core] + [lambda p, k=k: flipped(p, k) for k in (1, 2, 4)]
+    steps = [lambda p, k=k: flipped(p, k) for k in (4, 2, 1)] + [other_core]
     start, gradient, part = tie((narrow(block(4)), gradient, part))
     down = moved(start, along_z(-1))
     value = jnp.sum(exchanged(part, TEXT_GROUP), axis=0)
@@ -455,14 +461,17 @@
     down, value, text_part = tie((down, value, text_part))
     text_blocks = lax.all_to_all(text_part.reshape(16, BLOCK, WIDTH), TEXT_GROUP, 0, 0, tiled=True)
     down = down.astype(jnp.float32)
+    value = value + moved(value, steps[0])
     up = None
     for k in (3, 2, 1):
         first = narrow(block(-k) + down)
         second = narrow(block(k) if up is None else block(k) + up)
-        first, second, value = tie((first, second, value))
+        if k < 3:
+            first, second, value = tie((first, second, value))
         down = moved(first, along_z(-1)).astype(jnp.float32)
         up = moved(second, along_z(1)).astype(jnp.float32)
-        value = value + moved(value, steps[3 - k])
+        if k < 3:
+            value = value + moved(value, steps[3 - k])
     value = value + moved(value, steps[3])
     loss = value[0, 0] / (256 * BLOCK)
     image_grad = (block(0) + down + up) * image_factor

time: 172 us -> 171 us (level)
  starting transfers between devices: 47.9 us -> 51.3 us
  waiting for transfers between devices: 70.1 us -> 67.9 us
    ppermute x29, waiting for transfers between devices: 56 us -> 51.8 us  [moved(): return lax.ppermute(value, NAMES, pairs)]
    ppermute x29, starting transfers between devices: 23.7 us -> 27.5 us  [moved(): return lax.ppermute(value, NAMES, pairs)]
    all_to_all x3, waiting for transfers between devices: 14.1 us -> 16.1 us  [exchanged(): return lax.all_to_all(copies, axis, split_axis=0, concat_axis=0, tiled=True)]
  transfers between devices with their start and end apart: 33 -> 33, of which waited for: 20 -> 19; matrix products, arithmetic and copies ran while one was open for 10% -> 9% of each run, Pallas kernels for 0% -> 0%
where the time goes in v9:
time: 171 us; the launch traced here: 169 us
  waiting for transfers between devices  67.9 us (40%)
  starting transfers between devices  51.3 us (30%)
  Pallas kernels  25.1 us (15%)
  matrix products  10.4 us (6%)
  other arithmetic  8.22 us (5%)
  between operations  3.45 us (2%)
  local copies, waits for them, and re-layouts  2.67 us (2%)
    ppermute x29, waiting for transfers between devices, moved(): return lax.ppermute(value, NAMES, pairs)  51.8 us
    ppermute x29, starting transfers between devices, moved(): return lax.ppermute(value, NAMES, pairs)  27.5 us
    all_to_all x3, starting transfers between devices, exchanged(): return lax.all_to_all(copies, axis, split_axis=0, concat_axis=0, tiled=True)  17.4 us
    all_to_all x3, waiting for transfers between devices, exchanged(): return lax.all_to_all(copies, axis, split_axis=0, concat_axis=0, tiled=True)  16.1 us
    pallas_call x1, Pallas kernels, logits_and_statistics(): pl.pallas_call(kernel, out_shape=(square, square, half, half, small, smal...  15.5 us
    pallas_call x1, Pallas kernels, gradient_of_logits(): pl.pallas_call(gradient_kernel, grid=(SIDE // ROWS,), out_shape=(jax.Shap...  7.69 us
    all_to_all x1, starting transfers between devices, body(): lax.all_to_all(text_part.reshape(16, BLOCK, WIDTH), TEXT_GROUP, 0, 0, til...  6.41 us
    dot_general x1, matrix products, body(): lax.dot_general(gradient, image_slab, (((0,), (0,)), ((), ())), preferred...  5.32 us
  transfers between devices with their start and end apart: 33, of which 19 were waited for; matrix products, arithmetic and copies ran while one was open for 9% of the time, Pallas kernels for 0%

profile of v9, /device:TPU:8, one launch (start us, length us, event | category | flops | bytes accessed | tf_op | source)
XLA Modules:
  0.0 169.1 jit_solution(10306311114933612748)
XLA Ops:
  14.1 3.9 %collective-permute-done.3 = bf16[64,2048]{1,0:T(8,128)(2,1)S(1)} collective-permute-done((bf16[64,2048]{1,0:T(8,128)(2,1)}, bf16[64,2048]{1,0:T(8,128)(2,1)S(1)}, u32[]{:S(2)}, u32[]{:S(2)}) %collective-permute-start.3) | collective-permute-done | bytes 262176 | tf_op jit(solution)/shard_map/ppermute | solution.py:59
  21.2 7.6 %collective-permute-done.7 = bf16[64,2048]{1,0:T(8,128)(2,1)S(1)} collective-permute-done((bf16[64,2048]{1,0:T(8,128)(2,1)S(1)}, bf16[64,2048]{1,0:T(8,128)(2,1)S(1)}, u32[]{:S(2)}, u32[]{:S(2)}) %collective-permute-start.7) | collective-permute-done | bytes 262176 | tf_op jit(solution)/shard_map/ppermute | solution.py:59
  28.8 2.8 %collective-permute-done.8 = bf16[64,2048]{1,0:T(8,128)(2,1)S(1)} collective-permute-done((bf16[64,2048]{1,0:T(8,128)(2,1)S(1)}, bf16[64,2048]{1,0:T(8,128)(2,1)S(1)}, u32[]{:S(2)}, u32[]{:S(2)}) %collective-permute-start.8) | collective-permute-done | bytes 262176 | tf_op jit(solution)/shard_map/ppermute | solution.py:59
  31.7 7.5 %collective-permute-done.10 = bf16[64,2048]{1,0:T(8,128)(2,1)S(1)} collective-permute-done((bf16[64,2048]{1,0:T(8,128)(2,1)S(1)}, bf16[64,2048]{1,0:T(8,128)(2,1)S(1)}, u32[]{:S(2)}, u32[]{:S(2)}) %collective-permute-start.10) | collective-permute-done | bytes 262176 | tf_op jit(solution)/shard_map/ppermute | solution.py:59
  39.2 2.8 %collective-permute-done.9 = bf16[64,2048]{1,0:T(8,128)(2,1)S(1)} collective-permute-done((bf16[64,2048]{1,0:T(8,128)(2,1)S(1)}, bf16[64,2048]{1,0:T(8,128)(2,1)S(1)}, u32[]{:S(2)}, u32[]{:S(2)}) %collective-permute-start.9) | collective-permute-done | bytes 262176 | tf_op jit(solution)/shard_map/ppermute | solution.py:59
  44.7 5.2 %collective-permute-done.14 = bf16[64,2048]{1,0:T(8,128)(2,1)S(1)} collective-permute-done((bf16[64,2048]{1,0:T(8,128)(2,1)S(1)}, bf16[64,2048]{1,0:T(8,128)(2,1)S(1)}, u32[]{:S(2)}, u32[]{:S(2)}) %collective-permute-start.14) | collective-permute-done | bytes 262176 | tf_op jit(solution)/shard_map/ppermute | solution.py:59
  49.9 2.8 %collective-permute-done.15 = bf16[64,2048]{1,0:T(8,128)(2,1)S(1)} collective-permute-done((bf16[64,2048]{1,0:T(8,128)(2,1)S(1)}, bf16[64,2048]{1,0:T(8,128)(2,1)S(1)}, u32[]{:S(2)}, u32[]{:S(2)}) %collective-permute-start.15) | collective-permute-done | bytes 262176 | tf_op jit(solution)/shard_map/ppermute | solution.py:59
  55.3 15.5 %shard_map.68 = (f32[1024,1024]{1,0:T(8,128)}, f32[1024,1024]{1,0:T(8,128)}, bf16[1024,1024]{1,0:T(8,128)(2,1)}, bf16[1024,1024]{1,0:T(8,128)(2,1)}, f32[16,2,1152]{2,1,0:T(2,128)}, /*index=5*/f32[16,2,1152]{2,1,0:T(2,128)}) custom-call(s32[32]{0:T(128)} %stack.131.refs_0_, bf16[256,2048]{1,0:T(8,128)(2,1)} %copy-done.2, bf16[256,2048]{1,0:T(8,128)(2,1)} %copy-done.3, ...), custom_call_target="tpu_custom_call" | custom-call | flops 4294967296 | bytes 20971520 | tf_op jit(solution)/shard_map/pallas_call | solution.py:261
  70.8 6.1 %all-to-all-start.1 = ((f32[16,2,1152]{2,1,0:T(2,128)}), f32[16,2,1152]{2,1,0:T(2,128)S(1)}, u32[]{:S(2)}, u32[]{:S(2)}) async-start(f32[16,2,1152]{2,1,0:T(2,128)} %get-tuple-element.63), calls=%async_computation.1 | async-start | bytes 294912 | tf_op jit(solution)/shard_map/all_to_all | solution.py:393
  76.9 6.3 %all-to-all-done.1.col_ref = f32[16,2,1152]{2,1,0:T(2,128)S(1)} async-done(((f32[16,2,1152]{2,1,0:T(2,128)}), f32[16,2,1152]{2,1,0:T(2,128)S(1)}, u32[]{:S(2)}, u32[]{:S(2)}) %all-to-all-start.1) | async-done | bytes 147488 | tf_op jit(solution)/shard_map/all_to_all | solution.py:393
  83.2 6.2 %all-to-all-start = ((f32[16,2,1152]{2,1,0:T(2,128)}), f32[16,2,1152]{2,1,0:T(2,128)S(1)}, u32[]{:S(2)}, u32[]{:S(2)}) async-start(f32[16,2,1152]{2,1,0:T(2,128)} %get-tuple-element.62), calls=%async_computation | async-start | bytes 294912 | tf_op jit(solution)/shard_map/all_to_all | solution.py:393
  89.9 8.8 %all-to-all-done.row_ref = f32[16,2,1152]{2,1,0:T(2,128)S(1)} async-done(((f32[16,2,1152]{2,1,0:T(2,128)}), f32[16,2,1152]{2,1,0:T(2,128)S(1)}, u32[]{:S(2)}, u32[]{:S(2)}) %all-to-all-start) | async-done | bytes 147488 | tf_op jit(solution)/shard_map/all_to_all | solution.py:393
  98.7 7.7 %shard_map.69 = (bf16[1024,1024]{1,0:T(8,128)(2,1)S(1)}, f32[8,1024]{1,0:T(8,128)S(1)}, f32[16,8,128]{2,1,0:T(8,128)}) custom-call(f32[1024,1024]{1,0:T(8,128)} %get-tuple-element.60.s_ref, f32[1024,1024]{1,0:T(8,128)} %get-tuple-element.61.t_ref, f32[16,2,1152]{2,1,0:T(2,128)S(1)} %all-to-all-done.row_ref, f32[16,2,1152]{2,1,0:T(2,128)S(1)} %all-to-all-done.1.col_ref, ...), custom_call_target="tpu_custom_call" | custom-call | flops 16777216 | bytes 10485760 | tf_op jit(solution)/shard_map/pallas_call | solution.py:361
  106.4 2.3 %multiply_convert_fusion.1 = f16[512,1024]{1,0:T(8,128)(2,1)} fusion(bf16[1024,1024]{1,0:T(8,128)(2,1)S(1)} %copy-done.9, bf16[1024,1024]{1,0:T(8,128)(2,1)S(1)} %get-tuple-element.70, s32[]{:T(128)S(6)} %select_n.466, f32[1024]{0:T(1024)S(1)} %bitcast.73), kind=kOutput, calls=%fused_computation.3 | convolution fusion | flops 1074790400 | bytes 4198404 | tf_op jit(solution)/shard_map/dot_general | solution.py:435
  109.4 2.8 %fusion.1 = f32[512,1024]{1,0:T(8,128)S(1)} fusion(bf16[1024,1024]{1,0:T(8,128)(2,1)} %get-tuple-element.65, bf16[1024,1024]{1,0:T(8,128)(2,1)S(1)} %get-tuple-element.70, s32[]{:T(128)S(6)} %select_n.465), kind=kOutput, calls=%fused_computation.6 | convolution fusion | flops 1073741824 | bytes 5242884 | tf_op jit(solution)/shard_map/dot_general | solution.py:438
  114.2 5.1 %all-to-all-start.2 = ((f32[16,8,128]{2,1,0:T(8,128)}), f32[16,8,128]{2,1,0:T(8,128)S(1)}, u32[]{:S(2)}, u32[]{:S(2)}) async-start(f32[16,8,128]{2,1,0:T(8,128)} %get-tuple-element.69), calls=%async_computation.2 | async-start | bytes 131072 | tf_op jit(solution)/shard_map/all_to_all | solution.py:393
  119.3 5.3 %multiply_convert_fusion = f16[1024,1024]{1,0:T(8,128)(2,1)} fusion(bf16[1024,1024]{1,0:T(8,128)(2,1)S(1)} %get-tuple-element.70, bf16[1024,1024]{1,0:T(8,128)(2,1)} %get-tuple-element.71, f32[1024]{0:T(1024)S(1)} %bitcast.75), kind=kOutput, calls=%fused_computation.1 | convolution fusion | flops 2149580800 | bytes 6295552 | tf_op jit(solution)/shard_map/dot_general | solution.py:456
  125.7 6.4 %all-to-all-start.3 = ((f16[16,64,1024]{2,1,0:T(8,128)(2,1)}), f16[16,64,1024]{2,1,0:T(8,128)(2,1)S(1)}, u32[]{:S(2)}, u32[]{:S(2)}) async-start(f16[16,64,1024]{2,1,0:T(8,128)(2,1)} %bitcast.70), calls=%async_computation.3 | async-start | bytes 4194304 | tf_op jit(solution)/shard_map/all_to_all | solution.py:462
  133.6 4.7 %collective-permute-done.20 = f16[64,1024]{1,0:T(8,128)(2,1)} collective-permute-done((f16[64,1024]{1,0:T(8,128)(2,1)S(1)}, f16[64,1024]{1,0:T(8,128)(2,1)}, u32[]{:S(2)}, u32[]{:S(2)}) %collective-permute-start.20) | collective-permute-done | bytes 131104 | tf_op jit(solution)/shard_map/ppermute | solution.py:59
  139.4 3.0 %collective-permute-start.21 = (f32[8,128]{1,0:T(8,128)S(1)}, f32[8,128]{1,0:T(8,128)}, u32[]{:S(2)}, u32[]{:S(2)}) collective-permute-start(f32[8,128]{1,0:T(8,128)S(1)} %reduce_sum.18), channel_id=1, source_target_pairs={{0,4},{1,5},{2,6},{3,7},{4,0},{5,1},{6,2},{7,3},{8,12},{9,13},{10,... | collective-permute-start | bytes 12296 | tf_op jit(solution)/shard_map/ppermute | solution.py:59
  142.5 4.7 %collective-permute-done.21 = f32[8,128]{1,0:T(8,128)} collective-permute-done((f32[8,128]{1,0:T(8,128)S(1)}, f32[8,128]{1,0:T(8,128)}, u32[]{:S(2)}, u32[]{:S(2)}) %collective-permute-start.21) | collective-permute-done | bytes 4128 | tf_op jit(solution)/shard_map/ppermute | solution.py:59
  151.8 2.8 %collective-permute-done.24 = f32[8,128]{1,0:T(8,128)} collective-permute-done((f32[8,128]{1,0:T(8,128)S(1)}, f32[8,128]{1,0:T(8,128)}, u32[]{:S(2)}, u32[]{:S(2)}) %collective-permute-start.24) | collective-permute-done | bytes 4128 | tf_op jit(solution)/shard_map/ppermute | solution.py:59
  156.3 2.6 %collective-permute-start.27 = (f16[64,1024]{1,0:T(8,128)(2,1)S(1)}, f16[64,1024]{1,0:T(8,128)(2,1)S(1)}, u32[]{:S(2)}, u32[]{:S(2)}) collective-permute-start(f16[64,1024]{1,0:T(8,128)(2,1)S(1)} %get-tuple-element.78), channel_id=1, source_target_pairs={{0,38},{1,33},{2,32},{3,35},{4,34},{5,37},{6,36},{7,39},{8,46},{9,... | collective-permute-start | bytes 393224 | tf_op jit(solution)/shard_map/ppermute | solution.py:59
  160.3 2.1 %collective-permute-done.25 = f32[8,128]{1,0:T(8,128)S(1)} collective-permute-done((f32[8,128]{1,0:T(8,128)S(1)}, f32[8,128]{1,0:T(8,128)S(1)}, u32[]{:S(2)}, u32[]{:S(2)}) %collective-permute-start.25) | collective-permute-done | bytes 4128 | tf_op jit(solution)/shard_map/ppermute | solution.py:59
  (96 shorter events, 40.6 us)
Async XLA Ops:
  2.5 8.9 %collective-permute-start = (bf16[64,2048]{1,0:T(8,128)(2,1)}, bf16[64,2048]{1,0:T(8,128)(2,1)S(1)}, u32[]{:S(2)}, u32[]{:S(2)}) collective-permute-start(bf16[64,2048]{1,0:T(8,128)(2,1)} %get-tuple-element.42), channel_id=1, source_target_pairs={{0,8},{1,65},{2,10},{3,67},{4,12},{5,69},{6,14},{7,71},{8,16},{9,7... | collective-permute-start | bytes 786440 | tf_op jit(solution)/shard_map/ppermute | solution.py:59
  4.0 8.8 %collective-permute-start.1 = (bf16[64,2048]{1,0:T(8,128)(2,1)}, bf16[64,2048]{1,0:T(8,128)(2,1)S(1)}, u32[]{:S(2)}, u32[]{:S(2)}) collective-permute-start(bf16[64,2048]{1,0:T(8,128)(2,1)} %get-tuple-element.42), channel_id=1, source_target_pairs={{0,24},{1,193},{2,26},{3,195},{4,28},{5,197},{6,30},{7,199},{8,0},... | collective-permute-start | bytes 786440 | tf_op jit(solution)/shard_map/ppermute | solution.py:59
  5.8 8.3 %collective-permute-start.2 = (bf16[64,2048]{1,0:T(8,128)(2,1)}, bf16[64,2048]{1,0:T(8,128)(2,1)S(1)}, u32[]{:S(2)}, u32[]{:S(2)}) collective-permute-start(bf16[64,2048]{1,0:T(8,128)(2,1)} %get-tuple-element.42), channel_id=1, source_target_pairs={{0,16},{1,129},{2,18},{3,131},{4,20},{5,133},{6,22},{7,135},{8,24}... | collective-permute-start | bytes 786440 | tf_op jit(solution)/shard_map/ppermute | solution.py:59
  7.6 10.4 %collective-permute-start.3 = (bf16[64,2048]{1,0:T(8,128)(2,1)}, bf16[64,2048]{1,0:T(8,128)(2,1)S(1)}, u32[]{:S(2)}, u32[]{:S(2)}) collective-permute-start(bf16[64,2048]{1,0:T(8,128)(2,1)} %get-tuple-element.43.refs_6_), channel_id=1, source_target_pairs={{0,32},{1,39},{2,34},{3,33},{4,36},{5,35},{6,38},{7,37},{8,40},{9,... | collective-permute-start | bytes 786440 | tf_op jit(solution)/shard_map/ppermute | solution.py:59
  9.5 8.5 %collective-permute-start.4 = (bf16[64,2048]{1,0:T(8,128)(2,1)}, bf16[64,2048]{1,0:T(8,128)(2,1)S(1)}, u32[]{:S(2)}, u32[]{:S(2)}) collective-permute-start(bf16[64,2048]{1,0:T(8,128)(2,1)} %get-tuple-element.43.refs_6_), channel_id=1, source_target_pairs={{0,1},{1,0},{2,3},{3,2},{4,5},{5,4},{6,7},{7,6},{8,9},{9,8},{10,11... | collective-permute-start | bytes 786440 | tf_op jit(solution)/shard_map/ppermute | solution.py:59
  19.1 22.9 %collective-permute-start.5 = (bf16[256,2048]{1,0:T(8,128)(2,1)S(1)}, bf16[256,2048]{1,0:T(8,128)(2,1)S(1)}, u32[]{:S(2)}, u32[]{:S(2)}) collective-permute-start(bf16[256,2048]{1,0:T(8,128)(2,1)S(1)} %pad_maximum_fusion.refs_1_), channel_id=1, source_target_pairs={{0,64},{1,9},{2,66},{3,11},{4,68},{5,13},{6,70},{7,15},{8,72},{9,1... | collective-permute-start | bytes 3145736 | tf_op jit(solution)/shard_map/ppermute | solution.py:59
  20.8 21.2 %collective-permute-start.6 = (bf16[256,2048]{1,0:T(8,128)(2,1)S(1)}, bf16[256,2048]{1,0:T(8,128)(2,1)S(1)}, u32[]{:S(2)}, u32[]{:S(2)}) collective-permute-start(bf16[256,2048]{1,0:T(8,128)(2,1)S(1)} %pad_maximum_fusion.refs_1_), channel_id=1, source_target_pairs={{0,192},{1,25},{2,194},{3,27},{4,196},{5,29},{6,198},{7,31},{8,200... | collective-permute-start | bytes 3145736 | tf_op jit(solution)/shard_map/ppermute | solution.py:59
  21.2 7.6 %collective-permute-start.7 = (bf16[64,2048]{1,0:T(8,128)(2,1)S(1)}, bf16[64,2048]{1,0:T(8,128)(2,1)S(1)}, u32[]{:S(2)}, u32[]{:S(2)}) collective-permute-start(bf16[64,2048]{1,0:T(8,128)(2,1)S(1)} %collective-permute-done.3), channel_id=1, source_target_pairs={{0,32},{1,39},{2,34},{3,33},{4,36},{5,35},{6,38},{7,37},{8,40},{9,... | collective-permute-start | bytes 786440 | tf_op jit(solution)/shard_map/ppermute | solution.py:59
  21.2 10.4 %collective-permute-start.8 = (bf16[64,2048]{1,0:T(8,128)(2,1)S(1)}, bf16[64,2048]{1,0:T(8,128)(2,1)S(1)}, u32[]{:S(2)}, u32[]{:S(2)}) collective-permute-start(bf16[64,2048]{1,0:T(8,128)(2,1)S(1)} %collective-permute-done.4.refs_7_), channel_id=1, source_target_pairs={{0,32},{1,39},{2,34},{3,33},{4,36},{5,35},{6,38},{7,37},{8,40},{9,... | collective-permute-start | bytes 786440 | tf_op jit(solution)/shard_map/ppermute | solution.py:59
  31.6 7.6 %collective-permute-start.10 = (bf16[64,2048]{1,0:T(8,128)(2,1)S(1)}, bf16[64,2048]{1,0:T(8,128)(2,1)S(1)}, u32[]{:S(2)}, u32[]{:S(2)}) collective-permute-start(bf16[64,2048]{1,0:T(8,128)(2,1)S(1)} %collective-permute-done.8), channel_id=1, source_target_pairs={{0,32},{1,39},{2,34},{3,33},{4,36},{5,35},{6,38},{7,37},{8,40},{9,... | collective-permute-start | bytes 786440 | tf_op jit(solution)/shard_map/ppermute | solution.py:59
  31.6 10.4 %collective-permute-start.9 = (bf16[64,2048]{1,0:T(8,128)(2,1)S(1)}, bf16[64,2048]{1,0:T(8,128)(2,1)S(1)}, u32[]{:S(2)}, u32[]{:S(2)}) collective-permute-start(bf16[64,2048]{1,0:T(8,128)(2,1)S(1)} %collective-permute-done.7), channel_id=1, source_target_pairs={{0,32},{1,39},{2,34},{3,33},{4,36},{5,35},{6,38},{7,37},{8,40},{9,... | collective-permute-start | bytes 786440 | tf_op jit(solution)/shard_map/ppermute | solution.py:59
  42.1 13.0 %collective-permute-start.13 = (bf16[320,2048]{1,0:T(8,128)(2,1)S(1)}, bf16[320,2048]{1,0:T(8,128)(2,1)}, u32[]{:S(2)}, u32[]{:S(2)}) collective-permute-start(bf16[320,2048]{1,0:T(8,128)(2,1)S(1)} %constant_dynamic-update-slice_fusion.refs_8_), channel_id=1, source_target_pairs={{0,1},{1,0},{2,3},{3,2},{4,5},{5,4},{6,7},{7,6},{8,9},{9,8},{10,11... | collective-permute-start | bytes 3932168 | tf_op jit(solution)/shard_map/ppermute | solution.py:59
  42.2 7.7 %collective-permute-start.14 = (bf16[64,2048]{1,0:T(8,128)(2,1)S(1)}, bf16[64,2048]{1,0:T(8,128)(2,1)S(1)}, u32[]{:S(2)}, u32[]{:S(2)}) collective-permute-start(bf16[64,2048]{1,0:T(8,128)(2,1)S(1)} %collective-permute-done.9), channel_id=1, source_target_pairs={{0,32},{1,39},{2,34},{3,33},{4,36},{5,35},{6,38},{7,37},{8,40},{9,... | collective-permute-start | bytes 786440 | tf_op jit(solution)/shard_map/ppermute | solution.py:59
  42.3 10.4 %collective-permute-start.15 = (bf16[64,2048]{1,0:T(8,128)(2,1)S(1)}, bf16[64,2048]{1,0:T(8,128)(2,1)S(1)}, u32[]{:S(2)}, u32[]{:S(2)}) collective-permute-start(bf16[64,2048]{1,0:T(8,128)(2,1)S(1)} %collective-permute-done.10), channel_id=1, source_target_pairs={{0,32},{1,39},{2,34},{3,33},{4,36},{5,35},{6,38},{7,37},{8,40},{9,... | collective-permute-start | bytes 786440 | tf_op jit(solution)/shard_map/ppermute | solution.py:59
  42.5 12.0 %collective-permute-start.11 = (bf16[128,2048]{1,0:T(8,128)(2,1)S(1)}, bf16[128,2048]{1,0:T(8,128)(2,1)S(1)}, u32[]{:S(2)}, u32[]{:S(2)}) collective-permute-start(bf16[128,2048]{1,0:T(8,128)(2,1)S(1)} %slice.21), channel_id=1, source_target_pairs={{0,64},{1,9},{2,66},{3,11},{4,68},{5,13},{6,70},{7,15},{8,72},{9,1... | collective-permute-start | bytes 1572872 | tf_op jit(solution)/shard_map/ppermute | solution.py:59
  44.2 10.3 %collective-permute-start.12 = (bf16[128,2048]{1,0:T(8,128)(2,1)S(1)}, bf16[128,2048]{1,0:T(8,128)(2,1)}, u32[]{:S(2)}, u32[]{:S(2)}) collective-permute-start(bf16[128,2048]{1,0:T(8,128)(2,1)S(1)} %slice.22), channel_id=1, source_target_pairs={{0,192},{1,25},{2,194},{3,27},{4,196},{5,29},{6,198},{7,31},{8,200... | collective-permute-start | bytes 1572872 | tf_op jit(solution)/shard_map/ppermute | solution.py:59
  70.8 12.4 %all-to-all-start.1 = ((f32[16,2,1152]{2,1,0:T(2,128)}), f32[16,2,1152]{2,1,0:T(2,128)S(1)}, u32[]{:S(2)}, u32[]{:S(2)}) async-start(f32[16,2,1152]{2,1,0:T(2,128)} %get-tuple-element.63), calls=%async_computation.1 | async-start | bytes 294912 | tf_op jit(solution)/shard_map/all_to_all | solution.py:393
  83.2 15.5 %all-to-all-start = ((f32[16,2,1152]{2,1,0:T(2,128)}), f32[16,2,1152]{2,1,0:T(2,128)S(1)}, u32[]{:S(2)}, u32[]{:S(2)}) async-start(f32[16,2,1152]{2,1,0:T(2,128)} %get-tuple-element.62), calls=%async_computation | async-start | bytes 294912 | tf_op jit(solution)/shard_map/all_to_all | solution.py:393
  113.7 12.0 %collective-permute-start.18 = (f16[64,1024]{1,0:T(8,128)(2,1)S(1)}, f16[64,1024]{1,0:T(8,128)(2,1)S(1)}, u32[]{:S(2)}, u32[]{:S(2)}) collective-permute-start(f16[64,1024]{1,0:T(8,128)(2,1)S(1)} %get-tuple-element.68), channel_id=1, source_target_pairs={{0,38},{1,33},{2,32},{3,35},{4,34},{5,37},{6,36},{7,39},{8,46},{9,... | collective-permute-start | bytes 393224 | tf_op jit(solution)/shard_map/ppermute | solution.py:59
  114.2 11.4 %all-to-all-start.2 = ((f32[16,8,128]{2,1,0:T(8,128)}), f32[16,8,128]{2,1,0:T(8,128)S(1)}, u32[]{:S(2)}, u32[]{:S(2)}) async-start(f32[16,8,128]{2,1,0:T(8,128)} %get-tuple-element.69), calls=%async_computation.2 | async-start | bytes 131072 | tf_op jit(solution)/shard_map/all_to_all | solution.py:393
  125.7 41.1 %all-to-all-start.3 = ((f16[16,64,1024]{2,1,0:T(8,128)(2,1)}), f16[16,64,1024]{2,1,0:T(8,128)(2,1)S(1)}, u32[]{:S(2)}, u32[]{:S(2)}) async-start(f16[16,64,1024]{2,1,0:T(8,128)(2,1)} %bitcast.70), calls=%async_computation.3 | async-start | bytes 4194304 | tf_op jit(solution)/shard_map/all_to_all | solution.py:462
  139.3 8.5 %collective-permute-start.19 = (f16[64,1024]{1,0:T(8,128)(2,1)S(1)}, f16[64,1024]{1,0:T(8,128)(2,1)S(1)}, u32[]{:S(2)}, u32[]{:S(2)}) collective-permute-start(f16[64,1024]{1,0:T(8,128)(2,1)S(1)} %get-tuple-element.84), channel_id=1, source_target_pairs={{0,38},{1,33},{2,32},{3,35},{4,34},{5,37},{6,36},{7,39},{8,46},{9,... | collective-permute-start | bytes 393224 | tf_op jit(solution)/shard_map/ppermute | solution.py:59
  139.4 7.7 %collective-permute-start.21 = (f32[8,128]{1,0:T(8,128)S(1)}, f32[8,128]{1,0:T(8,128)}, u32[]{:S(2)}, u32[]{:S(2)}) collective-permute-start(f32[8,128]{1,0:T(8,128)S(1)} %reduce_sum.18), channel_id=1, source_target_pairs={{0,4},{1,5},{2,6},{3,7},{4,0},{5,1},{6,2},{7,3},{8,12},{9,13},{10,... | collective-permute-start | bytes 12296 | tf_op jit(solution)/shard_map/ppermute | solution.py:59
  156.3 8.5 %collective-permute-start.27 = (f16[64,1024]{1,0:T(8,128)(2,1)S(1)}, f16[64,1024]{1,0:T(8,128)(2,1)S(1)}, u32[]{:S(2)}, u32[]{:S(2)}) collective-permute-start(f16[64,1024]{1,0:T(8,128)(2,1)S(1)} %get-tuple-element.78), channel_id=1, source_target_pairs={{0,38},{1,33},{2,32},{3,35},{4,34},{5,37},{6,36},{7,39},{8,46},{9,... | collective-permute-start | bytes 393224 | tf_op jit(solution)/shard_map/ppermute | solution.py:59
  (19 other events, 149.2 us)

commit v10 on v9

--- a/solution.py
+++ b/solution.py
@@ -449,30 +449,28 @@
 
     tie = lax.optimization_barrier
     steps = [lambda p, k=k: flipped(p, k) for k in (4, 2, 1)] + [other_core]
-    start, gradient, part = tie((narrow(block(4)), gradient, part))
-    down = moved(start, along_z(-1))
+    start, part = tie((narrow(block(4)), part))
+    down = moved(start, along_z(-1)).astype(jnp.float32)
     value = jnp.sum(exchanged(part, TEXT_GROUP), axis=0)
+
+    first, second, gradient = tie((narrow(block(-3) + down), narrow(block(3)), gradient))
+    down = moved(first, along_z(-1)).astype(jnp.float32)
+    up = moved(second, along_z(1)).astype(jnp.float32)
     text_part = (
         lax.dot_general(
             gradient, image_slab, (((0,), (0,)), ((), ())), preferred_element_type=jnp.float32
         )
         * image_scale
     ).astype(jnp.float16)
-    down, value, text_part = tie((down, value, text_part))
+    first, second, text_part = tie((narrow(block(-2) + down), narrow(block(2) + up), text_part))
+    down = moved(first, along_z(-1)).astype(jnp.float32)
+    up = moved(second, along_z(1)).astype(jnp.float32)
     text_blocks = lax.all_to_all(text_part.reshape(16, BLOCK, WIDTH), TEXT_GROUP, 0, 0, tiled=True)
-    down = down.astype(jnp.float32)
-    value = value + moved(value, steps[0])
-    up = None
-    for k in (3, 2, 1):
-        first = narrow(block(-k) + down)
-        second = narrow(block(k) if up is None else block(k) + up)
-        if k < 3:
-            first, second, value = tie((first, second, value))
-        down = moved(first, along_z(-1)).astype(jnp.float32)
-        up = moved(second, along_z(1)).astype(jnp.float32)
-        if k < 3:
-            value = value + moved(value, steps[3 - k])
-    value = value + moved(value, steps[3])
+    first, second, value = tie((narrow(block(-1) + down), narrow(block(1) + up), value))
+    down = moved(first, along_z(-1)).astype(jnp.float32)
+    up = moved(second, along_z(1)).astype(jnp.float32)
+    for to in steps:
+        value = value + moved(value, to)
     loss = value[0, 0] / (256 * BLOCK)
     image_grad = (block(0) + down + up) * image_factor
     text_grad = jnp.sum(text_blocks.astype(jnp.float32), axis=0) * text_factor

time: 171 us -> 170 us (level)
  waiting for transfers between devices: 67.9 us -> 71.3 us
  starting transfers between devices: 51.3 us -> 49.2 us
    ppermute x29, waiting for transfers between devices: 51.8 us -> 55.8 us  [moved(): return lax.ppermute(value, NAMES, pairs)]
    ppermute x29, starting transfers between devices: 27.5 us -> 24.7 us  [moved(): return lax.ppermute(value, NAMES, pairs)]
  transfers between devices with their start and end apart: 33 -> 33, of which waited for: 19 -> 20; matrix products, arithmetic and copies ran while one was open for 9% -> 8% of each run, Pallas kernels for 0% -> 0%
where the time goes in v10:
time: 170 us; the launch traced here: 168 us
  waiting for transfers between devices  71.3 us (42%)
  starting transfers between devices  49.2 us (29%)
  Pallas kernels  25.1 us (15%)
  matrix products  9.42 us (6%)
  other arithmetic  7.25 us (4%)
  between operations  3.44 us (2%)
  local copies, waits for them, and re-layouts  2.37 us (1%)
    ppermute x29, waiting for transfers between devices, moved(): return lax.ppermute(value, NAMES, pairs)  55.8 us
    ppermute x29, starting transfers between devices, moved(): return lax.ppermute(value, NAMES, pairs)  24.7 us
    all_to_all x3, starting transfers between devices, exchanged(): return lax.all_to_all(copies, axis, split_axis=0, concat_axis=0, tiled=True)  17.4 us
    pallas_call x1, Pallas kernels, logits_and_statistics(): pl.pallas_call(kernel, out_shape=(square, square, half, half, small, smal...  15.5 us
    all_to_all x3, waiting for transfers between devices, exchanged(): return lax.all_to_all(copies, axis, split_axis=0, concat_axis=0, tiled=True)  15.1 us
    pallas_call x1, Pallas kernels, gradient_of_logits(): pl.pallas_call(gradient_kernel, grid=(SIDE // ROWS,), out_shape=(jax.Shap...  7.69 us
    all_to_all x1, starting transfers between devices, body(): lax.all_to_all(text_part.reshape(16, BLOCK, WIDTH), TEXT_GROUP, 0, 0, til...  7.16 us
    dot_general x1, matrix products, body(): lax.dot_general(gradient, image_slab, (((0,), (0,)), ((), ())), preferred...  5.33 us
  transfers between devices with their start and end apart: 33, of which 20 were waited for; matrix products, arithmetic and copies ran while one was open for 8% of the time, Pallas kernels for 0%

profile of v10, /device:TPU:8, one launch (start us, length us, event | category | flops | bytes accessed | tf_op | source)
XLA Modules:
  0.0 168.1 jit_solution(12085282940177051249)
XLA Ops:
  14.1 3.9 %collective-permute-done.3 = bf16[64,2048]{1,0:T(8,128)(2,1)S(1)} collective-permute-done((bf16[64,2048]{1,0:T(8,128)(2,1)}, bf16[64,2048]{1,0:T(8,128)(2,1)S(1)}, u32[]{:S(2)}, u32[]{:S(2)}) %collective-permute-start.3) | collective-permute-done | bytes 262176 | tf_op jit(solution)/shard_map/ppermute | solution.py:59
  21.2 7.6 %collective-permute-done.7 = bf16[64,2048]{1,0:T(8,128)(2,1)S(1)} collective-permute-done((bf16[64,2048]{1,0:T(8,128)(2,1)S(1)}, bf16[64,2048]{1,0:T(8,128)(2,1)S(1)}, u32[]{:S(2)}, u32[]{:S(2)}) %collective-permute-start.7) | collective-permute-done | bytes 262176 | tf_op jit(solution)/shard_map/ppermute | solution.py:59
  28.8 2.8 %collective-permute-done.8 = bf16[64,2048]{1,0:T(8,128)(2,1)S(1)} collective-permute-done((bf16[64,2048]{1,0:T(8,128)(2,1)S(1)}, bf16[64,2048]{1,0:T(8,128)(2,1)S(1)}, u32[]{:S(2)}, u32[]{:S(2)}) %collective-permute-start.8) | collective-permute-done | bytes 262176 | tf_op jit(solution)/shard_map/ppermute | solution.py:59
  31.7 7.5 %collective-permute-done.10 = bf16[64,2048]{1,0:T(8,128)(2,1)S(1)} collective-permute-done((bf16[64,2048]{1,0:T(8,128)(2,1)S(1)}, bf16[64,2048]{1,0:T(8,128)(2,1)S(1)}, u32[]{:S(2)}, u32[]{:S(2)}) %collective-permute-start.10) | collective-permute-done | bytes 262176 | tf_op jit(solution)/shard_map/ppermute | solution.py:59
  39.2 2.8 %collective-permute-done.9 = bf16[64,2048]{1,0:T(8,128)(2,1)S(1)} collective-permute-done((bf16[64,2048]{1,0:T(8,128)(2,1)S(1)}, bf16[64,2048]{1,0:T(8,128)(2,1)S(1)}, u32[]{:S(2)}, u32[]{:S(2)}) %collective-permute-start.9) | collective-permute-done | bytes 262176 | tf_op jit(solution)/shard_map/ppermute | solution.py:59
  44.7 5.2 %collective-permute-done.14 = bf16[64,2048]{1,0:T(8,128)(2,1)S(1)} collective-permute-done((bf16[64,2048]{1,0:T(8,128)(2,1)S(1)}, bf16[64,2048]{1,0:T(8,128)(2,1)S(1)}, u32[]{:S(2)}, u32[]{:S(2)}) %collective-permute-start.14) | collective-permute-done | bytes 262176 | tf_op jit(solution)/shard_map/ppermute | solution.py:59
  49.9 2.8 %collective-permute-done.15 = bf16[64,2048]{1,0:T(8,128)(2,1)S(1)} collective-permute-done((bf16[64,2048]{1,0:T(8,128)(2,1)S(1)}, bf16[64,2048]{1,0:T(8,128)(2,1)S(1)}, u32[]{:S(2)}, u32[]{:S(2)}) %collective-permute-start.15) | collective-permute-done | bytes 262176 | tf_op jit(solution)/shard_map/ppermute | solution.py:59
  55.3 15.5 %shard_map.68 = (f32[1024,1024]{1,0:T(8,128)}, f32[1024,1024]{1,0:T(8,128)}, bf16[1024,1024]{1,0:T(8,128)(2,1)}, bf16[1024,1024]{1,0:T(8,128)(2,1)}, f32[16,2,1152]{2,1,0:T(2,128)}, /*index=5*/f32[16,2,1152]{2,1,0:T(2,128)}) custom-call(s32[32]{0:T(128)} %stack.131.refs_0_, bf16[256,2048]{1,0:T(8,128)(2,1)} %copy-done, bf16[256,2048]{1,0:T(8,128)(2,1)} %copy-done.1, ...), custom_call_target="tpu_custom_call" | custom-call | flops 4294967296 | bytes 20971520 | tf_op jit(solution)/shard_map/pallas_call | solution.py:261
  70.8 6.1 %all-to-all-start.1 = ((f32[16,2,1152]{2,1,0:T(2,128)}), f32[16,2,1152]{2,1,0:T(2,128)S(1)}, u32[]{:S(2)}, u32[]{:S(2)}) async-start(f32[16,2,1152]{2,1,0:T(2,128)} %get-tuple-element.62), calls=%async_computation.1 | async-start | bytes 294912 | tf_op jit(solution)/shard_map/all_to_all | solution.py:393
  76.9 6.3 %all-to-all-done.1.col_ref = f32[16,2,1152]{2,1,0:T(2,128)S(1)} async-done(((f32[16,2,1152]{2,1,0:T(2,128)}), f32[16,2,1152]{2,1,0:T(2,128)S(1)}, u32[]{:S(2)}, u32[]{:S(2)}) %all-to-all-start.1) | async-done | bytes 147488 | tf_op jit(solution)/shard_map/all_to_all | solution.py:393
  83.3 6.2 %all-to-all-start = ((f32[16,2,1152]{2,1,0:T(2,128)}), f32[16,2,1152]{2,1,0:T(2,128)S(1)}, u32[]{:S(2)}, u32[]{:S(2)}) async-start(f32[16,2,1152]{2,1,0:T(2,128)} %get-tuple-element.61), calls=%async_computation | async-start | bytes 294912 | tf_op jit(solution)/shard_map/all_to_all | solution.py:393
  89.9 8.8 %all-to-all-done.row_ref = f32[16,2,1152]{2,1,0:T(2,128)S(1)} async-done(((f32[16,2,1152]{2,1,0:T(2,128)}), f32[16,2,1152]{2,1,0:T(2,128)S(1)}, u32[]{:S(2)}, u32[]{:S(2)}) %all-to-all-start) | async-done | bytes 147488 | tf_op jit(solution)/shard_map/all_to_all | solution.py:393
  98.7 7.7 %shard_map.69 = (bf16[1024,1024]{1,0:T(8,128)(2,1)S(1)}, f32[8,1024]{1,0:T(8,128)S(1)}, f32[16,8,128]{2,1,0:T(8,128)}) custom-call(f32[1024,1024]{1,0:T(8,128)} %get-tuple-element.59.s_ref, f32[1024,1024]{1,0:T(8,128)} %get-tuple-element.60.t_ref, f32[16,2,1152]{2,1,0:T(2,128)S(1)} %all-to-all-done.row_ref, f32[16,2,1152]{2,1,0:T(2,128)S(1)} %all-to-all-done.1.col_ref, ...), custom_call_target="tpu_custom_call" | custom-call | flops 16777216 | bytes 10485760 | tf_op jit(solution)/shard_map/pallas_call | solution.py:361
  108.4 2.8 %fusion.1 = f32[512,1024]{1,0:T(8,128)S(1)} fusion(bf16[1024,1024]{1,0:T(8,128)(2,1)} %get-tuple-element.64, bf16[1024,1024]{1,0:T(8,128)(2,1)S(1)} %get-tuple-element.70, s32[]{:T(128)S(6)} %select_n.465), kind=kOutput, calls=%fused_computation.6 | convolution fusion | flops 1073741824 | bytes 5242884 | tf_op jit(solution)/shard_map/dot_general | solution.py:438
  114.1 5.1 %all-to-all-start.2 = ((f32[16,8,128]{2,1,0:T(8,128)}), f32[16,8,128]{2,1,0:T(8,128)S(1)}, u32[]{:S(2)}, u32[]{:S(2)}) async-start(f32[16,8,128]{2,1,0:T(8,128)} %get-tuple-element.74), calls=%async_computation.2 | async-start | bytes 131072 | tf_op jit(solution)/shard_map/all_to_all | solution.py:393
  121.4 5.3 %multiply_convert_fusion = f16[1024,1024]{1,0:T(8,128)(2,1)} fusion(bf16[1024,1024]{1,0:T(8,128)(2,1)S(1)} %get-tuple-element.70, bf16[1024,1024]{1,0:T(8,128)(2,1)} %get-tuple-element.71, f32[1024]{0:T(1024)S(1)} %bitcast.75), kind=kOutput, calls=%fused_computation.1 | convolution fusion | flops 2149580800 | bytes 6295552 | tf_op jit(solution)/shard_map/dot_general | solution.py:460
  126.9 7.2 %all-to-all-start.3 = ((f16[16,64,1024]{2,1,0:T(8,128)(2,1)}), f16[16,64,1024]{2,1,0:T(8,128)(2,1)S(1)}, u32[]{:S(2)}, u32[]{:S(2)}) async-start(f16[16,64,1024]{2,1,0:T(8,128)(2,1)} %bitcast.70), calls=%async_computation.3 | async-start | bytes 4194304 | tf_op jit(solution)/shard_map/all_to_all | solution.py:468
  134.1 2.2 %collective-permute-start.21 = (f16[64,1024]{1,0:T(8,128)(2,1)S(1)}, f16[64,1024]{1,0:T(8,128)(2,1)}, u32[]{:S(2)}, u32[]{:S(2)}) collective-permute-start(f16[64,1024]{1,0:T(8,128)(2,1)S(1)} %get-tuple-element.72), channel_id=1, source_target_pairs={{0,38},{1,33},{2,32},{3,35},{4,34},{5,37},{6,36},{7,39},{8,46},{9,... | collective-permute-start | bytes 393224 | tf_op jit(solution)/shard_map/ppermute | solution.py:59
  136.3 3.4 %collective-permute-done.21 = f16[64,1024]{1,0:T(8,128)(2,1)} collective-permute-done((f16[64,1024]{1,0:T(8,128)(2,1)S(1)}, f16[64,1024]{1,0:T(8,128)(2,1)}, u32[]{:S(2)}, u32[]{:S(2)}) %collective-permute-start.21) | collective-permute-done | bytes 131104 | tf_op jit(solution)/shard_map/ppermute | solution.py:59
  139.7 2.9 %collective-permute-done.22 = f16[64,1024]{1,0:T(8,128)(2,1)} collective-permute-done((f16[64,1024]{1,0:T(8,128)(2,1)S(1)}, f16[64,1024]{1,0:T(8,128)(2,1)}, u32[]{:S(2)}, u32[]{:S(2)}) %collective-permute-start.22) | collective-permute-done | bytes 131104 | tf_op jit(solution)/shard_map/ppermute | solution.py:59
  145.7 3.3 %collective-permute-start.23 = (f32[8,128]{1,0:T(8,128)S(1)}, f32[8,128]{1,0:T(8,128)S(1)}, u32[]{:S(2)}, u32[]{:S(2)}) collective-permute-start(f32[8,128]{1,0:T(8,128)S(1)} %reduce_sum.18), channel_id=1, source_target_pairs={{0,4},{1,5},{2,6},{3,7},{4,0},{5,1},{6,2},{7,3},{8,12},{9,13},{10,... | collective-permute-start | bytes 12296 | tf_op jit(solution)/shard_map/ppermute | solution.py:59
  149.0 4.3 %collective-permute-done.23 = f32[8,128]{1,0:T(8,128)S(1)} collective-permute-done((f32[8,128]{1,0:T(8,128)S(1)}, f32[8,128]{1,0:T(8,128)S(1)}, u32[]{:S(2)}, u32[]{:S(2)}) %collective-permute-start.23) | collective-permute-done | bytes 4128 | tf_op jit(solution)/shard_map/ppermute | solution.py:59
  153.2 4.5 %collective-permute-done.24 = f32[8,128]{1,0:T(8,128)S(1)} collective-permute-done((f32[8,128]{1,0:T(8,128)S(1)}, f32[8,128]{1,0:T(8,128)S(1)}, u32[]{:S(2)}, u32[]{:S(2)}) %collective-permute-start.24) | collective-permute-done | bytes 4128 | tf_op jit(solution)/shard_map/ppermute | solution.py:59
  157.8 3.6 %collective-permute-done.25 = f32[8,128]{1,0:T(8,128)S(1)} collective-permute-done((f32[8,128]{1,0:T(8,128)S(1)}, f32[8,128]{1,0:T(8,128)S(1)}, u32[]{:S(2)}, u32[]{:S(2)}) %collective-permute-start.25) | collective-permute-done | bytes 4128 | tf_op jit(solution)/shard_map/ppermute | solution.py:59
  (92 shorter events, 36.9 us)
Async XLA Ops:
  2.5 8.9 %collective-permute-start = (bf16[64,2048]{1,0:T(8,128)(2,1)}, bf16[64,2048]{1,0:T(8,128)(2,1)S(1)}, u32[]{:S(2)}, u32[]{:S(2)}) collective-permute-start(bf16[64,2048]{1,0:T(8,128)(2,1)} %get-tuple-element.41), channel_id=1, source_target_pairs={{0,8},{1,65},{2,10},{3,67},{4,12},{5,69},{6,14},{7,71},{8,16},{9,7... | collective-permute-start | bytes 786440 | tf_op jit(solution)/shard_map/ppermute | solution.py:59
  4.0 8.8 %collective-permute-start.1 = (bf16[64,2048]{1,0:T(8,128)(2,1)}, bf16[64,2048]{1,0:T(8,128)(2,1)S(1)}, u32[]{:S(2)}, u32[]{:S(2)}) collective-permute-start(bf16[64,2048]{1,0:T(8,128)(2,1)} %get-tuple-element.41), channel_id=1, source_target_pairs={{0,24},{1,193},{2,26},{3,195},{4,28},{5,197},{6,30},{7,199},{8,0},... | collective-permute-start | bytes 786440 | tf_op jit(solution)/shard_map/ppermute | solution.py:59
  5.8 8.3 %collective-permute-start.2 = (bf16[64,2048]{1,0:T(8,128)(2,1)}, bf16[64,2048]{1,0:T(8,128)(2,1)S(1)}, u32[]{:S(2)}, u32[]{:S(2)}) collective-permute-start(bf16[64,2048]{1,0:T(8,128)(2,1)} %get-tuple-element.41), channel_id=1, source_target_pairs={{0,16},{1,129},{2,18},{3,131},{4,20},{5,133},{6,22},{7,135},{8,24}... | collective-permute-start | bytes 786440 | tf_op jit(solution)/shard_map/ppermute | solution.py:59
  7.6 10.4 %collective-permute-start.3 = (bf16[64,2048]{1,0:T(8,128)(2,1)}, bf16[64,2048]{1,0:T(8,128)(2,1)S(1)}, u32[]{:S(2)}, u32[]{:S(2)}) collective-permute-start(bf16[64,2048]{1,0:T(8,128)(2,1)} %get-tuple-element.42.refs_6_), channel_id=1, source_target_pairs={{0,32},{1,39},{2,34},{3,33},{4,36},{5,35},{6,38},{7,37},{8,40},{9,... | collective-permute-start | bytes 786440 | tf_op jit(solution)/shard_map/ppermute | solution.py:59
  9.5 8.5 %collective-permute-start.4 = (bf16[64,2048]{1,0:T(8,128)(2,1)}, bf16[64,2048]{1,0:T(8,128)(2,1)S(1)}, u32[]{:S(2)}, u32[]{:S(2)}) collective-permute-start(bf16[64,2048]{1,0:T(8,128)(2,1)} %get-tuple-element.42.refs_6_), channel_id=1, source_target_pairs={{0,1},{1,0},{2,3},{3,2},{4,5},{5,4},{6,7},{7,6},{8,9},{9,8},{10,11... | collective-permute-start | bytes 786440 | tf_op jit(solution)/shard_map/ppermute | solution.py:59
  19.1 22.9 %collective-permute-start.5 = (bf16[256,2048]{1,0:T(8,128)(2,1)S(1)}, bf16[256,2048]{1,0:T(8,128)(2,1)S(1)}, u32[]{:S(2)}, u32[]{:S(2)}) collective-permute-start(bf16[256,2048]{1,0:T(8,128)(2,1)S(1)} %pad_maximum_fusion.refs_1_), channel_id=1, source_target_pairs={{0,64},{1,9},{2,66},{3,11},{4,68},{5,13},{6,70},{7,15},{8,72},{9,1... | collective-permute-start | bytes 3145736 | tf_op jit(solution)/shard_map/ppermute | solution.py:59
  20.8 21.2 %collective-permute-start.6 = (bf16[256,2048]{1,0:T(8,128)(2,1)S(1)}, bf16[256,2048]{1,0:T(8,128)(2,1)S(1)}, u32[]{:S(2)}, u32[]{:S(2)}) collective-permute-start(bf16[256,2048]{1,0:T(8,128)(2,1)S(1)} %pad_maximum_fusion.refs_1_), channel_id=1, source_target_pairs={{0,192},{1,25},{2,194},{3,27},{4,196},{5,29},{6,198},{7,31},{8,200... | collective-permute-start | bytes 3145736 | tf_op jit(solution)/shard_map/ppermute | solution.py:59
  21.2 7.6 %collective-permute-start.7 = (bf16[64,2048]{1,0:T(8,128)(2,1)S(1)}, bf16[64,2048]{1,0:T(8,128)(2,1)S(1)}, u32[]{:S(2)}, u32[]{:S(2)}) collective-permute-start(bf16[64,2048]{1,0:T(8,128)(2,1)S(1)} %collective-permute-done.3), channel_id=1, source_target_pairs={{0,32},{1,39},{2,34},{3,33},{4,36},{5,35},{6,38},{7,37},{8,40},{9,... | collective-permute-start | bytes 786440 | tf_op jit(solution)/shard_map/ppermute | solution.py:59
  21.2 10.4 %collective-permute-start.8 = (bf16[64,2048]{1,0:T(8,128)(2,1)S(1)}, bf16[64,2048]{1,0:T(8,128)(2,1)S(1)}, u32[]{:S(2)}, u32[]{:S(2)}) collective-permute-start(bf16[64,2048]{1,0:T(8,128)(2,1)S(1)} %collective-permute-done.4.refs_7_), channel_id=1, source_target_pairs={{0,32},{1,39},{2,34},{3,33},{4,36},{5,35},{6,38},{7,37},{8,40},{9,... | collective-permute-start | bytes 786440 | tf_op jit(solution)/shard_map/ppermute | solution.py:59
  31.6 7.6 %collective-permute-start.10 = (bf16[64,2048]{1,0:T(8,128)(2,1)S(1)}, bf16[64,2048]{1,0:T(8,128)(2,1)S(1)}, u32[]{:S(2)}, u32[]{:S(2)}) collective-permute-start(bf16[64,2048]{1,0:T(8,128)(2,1)S(1)} %collective-permute-done.8), channel_id=1, source_target_pairs={{0,32},{1,39},{2,34},{3,33},{4,36},{5,35},{6,38},{7,37},{8,40},{9,... | collective-permute-start | bytes 786440 | tf_op jit(solution)/shard_map/ppermute | solution.py:59
  31.6 10.4 %collective-permute-start.9 = (bf16[64,2048]{1,0:T(8,128)(2,1)S(1)}, bf16[64,2048]{1,0:T(8,128)(2,1)S(1)}, u32[]{:S(2)}, u32[]{:S(2)}) collective-permute-start(bf16[64,2048]{1,0:T(8,128)(2,1)S(1)} %collective-permute-done.7), channel_id=1, source_target_pairs={{0,32},{1,39},{2,34},{3,33},{4,36},{5,35},{6,38},{7,37},{8,40},{9,... | collective-permute-start | bytes 786440 | tf_op jit(solution)/shard_map/ppermute | solution.py:59
  42.1 13.0 %collective-permute-start.13 = (bf16[320,2048]{1,0:T(8,128)(2,1)S(1)}, bf16[320,2048]{1,0:T(8,128)(2,1)}, u32[]{:S(2)}, u32[]{:S(2)}) collective-permute-start(bf16[320,2048]{1,0:T(8,128)(2,1)S(1)} %constant_dynamic-update-slice_fusion.refs_8_), channel_id=1, source_target_pairs={{0,1},{1,0},{2,3},{3,2},{4,5},{5,4},{6,7},{7,6},{8,9},{9,8},{10,11... | collective-permute-start | bytes 3932168 | tf_op jit(solution)/shard_map/ppermute | solution.py:59
  42.2 7.7 %collective-permute-start.14 = (bf16[64,2048]{1,0:T(8,128)(2,1)S(1)}, bf16[64,2048]{1,0:T(8,128)(2,1)S(1)}, u32[]{:S(2)}, u32[]{:S(2)}) collective-permute-start(bf16[64,2048]{1,0:T(8,128)(2,1)S(1)} %collective-permute-done.9), channel_id=1, source_target_pairs={{0,32},{1,39},{2,34},{3,33},{4,36},{5,35},{6,38},{7,37},{8,40},{9,... | collective-permute-start | bytes 786440 | tf_op jit(solution)/shard_map/ppermute | solution.py:59
  42.3 10.4 %collective-permute-start.15 = (bf16[64,2048]{1,0:T(8,128)(2,1)S(1)}, bf16[64,2048]{1,0:T(8,128)(2,1)S(1)}, u32[]{:S(2)}, u32[]{:S(2)}) collective-permute-start(bf16[64,2048]{1,0:T(8,128)(2,1)S(1)} %collective-permute-done.10), channel_id=1, source_target_pairs={{0,32},{1,39},{2,34},{3,33},{4,36},{5,35},{6,38},{7,37},{8,40},{9,... | collective-permute-start | bytes 786440 | tf_op jit(solution)/shard_map/ppermute | solution.py:59
  42.5 12.0 %collective-permute-start.11 = (bf16[128,2048]{1,0:T(8,128)(2,1)S(1)}, bf16[128,2048]{1,0:T(8,128)(2,1)S(1)}, u32[]{:S(2)}, u32[]{:S(2)}) collective-permute-start(bf16[128,2048]{1,0:T(8,128)(2,1)S(1)} %slice.21), channel_id=1, source_target_pairs={{0,64},{1,9},{2,66},{3,11},{4,68},{5,13},{6,70},{7,15},{8,72},{9,1... | collective-permute-start | bytes 1572872 | tf_op jit(solution)/shard_map/ppermute | solution.py:59
  44.2 10.3 %collective-permute-start.12 = (bf16[128,2048]{1,0:T(8,128)(2,1)S(1)}, bf16[128,2048]{1,0:T(8,128)(2,1)}, u32[]{:S(2)}, u32[]{:S(2)}) collective-permute-start(bf16[128,2048]{1,0:T(8,128)(2,1)S(1)} %slice.22), channel_id=1, source_target_pairs={{0,192},{1,25},{2,194},{3,27},{4,196},{5,29},{6,198},{7,31},{8,200... | collective-permute-start | bytes 1572872 | tf_op jit(solution)/shard_map/ppermute | solution.py:59
  70.8 12.4 %all-to-all-start.1 = ((f32[16,2,1152]{2,1,0:T(2,128)}), f32[16,2,1152]{2,1,0:T(2,128)S(1)}, u32[]{:S(2)}, u32[]{:S(2)}) async-start(f32[16,2,1152]{2,1,0:T(2,128)} %get-tuple-element.62), calls=%async_computation.1 | async-start | bytes 294912 | tf_op jit(solution)/shard_map/all_to_all | solution.py:393
  83.3 15.4 %all-to-all-start = ((f32[16,2,1152]{2,1,0:T(2,128)}), f32[16,2,1152]{2,1,0:T(2,128)S(1)}, u32[]{:S(2)}, u32[]{:S(2)}) async-start(f32[16,2,1152]{2,1,0:T(2,128)} %get-tuple-element.61), calls=%async_computation | async-start | bytes 294912 | tf_op jit(solution)/shard_map/all_to_all | solution.py:393
  114.1 12.8 %all-to-all-start.2 = ((f32[16,8,128]{2,1,0:T(8,128)}), f32[16,8,128]{2,1,0:T(8,128)S(1)}, u32[]{:S(2)}, u32[]{:S(2)}) async-start(f32[16,8,128]{2,1,0:T(8,128)} %get-tuple-element.74), calls=%async_computation.2 | async-start | bytes 131072 | tf_op jit(solution)/shard_map/all_to_all | solution.py:393
  119.3 7.4 %collective-permute-start.19 = (f16[64,1024]{1,0:T(8,128)(2,1)S(1)}, f16[64,1024]{1,0:T(8,128)(2,1)S(1)}, u32[]{:S(2)}, u32[]{:S(2)}) collective-permute-start(f16[64,1024]{1,0:T(8,128)(2,1)S(1)} %fusion.31), channel_id=1, source_target_pairs={{0,38},{1,33},{2,32},{3,35},{4,34},{5,37},{6,36},{7,39},{8,46},{9,... | collective-permute-start | bytes 393224 | tf_op jit(solution)/shard_map/ppermute | solution.py:59
  126.9 38.8 %all-to-all-start.3 = ((f16[16,64,1024]{2,1,0:T(8,128)(2,1)}), f16[16,64,1024]{2,1,0:T(8,128)(2,1)S(1)}, u32[]{:S(2)}, u32[]{:S(2)}) async-start(f16[16,64,1024]{2,1,0:T(8,128)(2,1)} %bitcast.70), calls=%async_computation.3 | async-start | bytes 4194304 | tf_op jit(solution)/shard_map/all_to_all | solution.py:468
  143.6 20.1 %collective-permute-start.27 = (f16[64,1024]{1,0:T(8,128)(2,1)S(1)}, f16[64,1024]{1,0:T(8,128)(2,1)S(1)}, u32[]{:S(2)}, u32[]{:S(2)}) collective-permute-start(f16[64,1024]{1,0:T(8,128)(2,1)S(1)} %get-tuple-element.76), channel_id=1, source_target_pairs={{0,38},{1,33},{2,32},{3,35},{4,34},{5,37},{6,36},{7,39},{8,46},{9,... | collective-permute-start | bytes 393224 | tf_op jit(solution)/shard_map/ppermute | solution.py:59
  144.6 19.1 %collective-permute-start.28 = (f16[64,1024]{1,0:T(8,128)(2,1)S(1)}, f16[64,1024]{1,0:T(8,128)(2,1)}, u32[]{:S(2)}, u32[]{:S(2)}) collective-permute-start(f16[64,1024]{1,0:T(8,128)(2,1)S(1)} %get-tuple-element.77), channel_id=1, source_target_pairs={{0,32},{1,39},{2,34},{3,33},{4,36},{5,35},{6,38},{7,37},{8,40},{9,... | collective-permute-start | bytes 393224 | tf_op jit(solution)/shard_map/ppermute | solution.py:59
  145.7 7.5 %collective-permute-start.23 = (f32[8,128]{1,0:T(8,128)S(1)}, f32[8,128]{1,0:T(8,128)S(1)}, u32[]{:S(2)}, u32[]{:S(2)}) collective-permute-start(f32[8,128]{1,0:T(8,128)S(1)} %reduce_sum.18), channel_id=1, source_target_pairs={{0,4},{1,5},{2,6},{3,7},{4,0},{5,1},{6,2},{7,3},{8,12},{9,13},{10,... | collective-permute-start | bytes 12296 | tf_op jit(solution)/shard_map/ppermute | solution.py:59
  (17 other events, 131.7 us)

commit v11 on v10

--- a/solution.py
+++ b/solution.py
@@ -466,14 +466,15 @@
     down = moved(first, along_z(-1)).astype(jnp.float32)
     up = moved(second, along_z(1)).astype(jnp.float32)
     text_blocks = lax.all_to_all(text_part.reshape(16, BLOCK, WIDTH), TEXT_GROUP, 0, 0, tiled=True)
+    value = value + moved(value, steps[0])
     first, second, value = tie((narrow(block(-1) + down), narrow(block(1) + up), value))
     down = moved(first, along_z(-1)).astype(jnp.float32)
     up = moved(second, along_z(1)).astype(jnp.float32)
-    for to in steps:
+    for to in steps[1:]:
         value = value + moved(value, to)
     loss = value[0, 0] / (256 * BLOCK)
     image_grad = (block(0) + down + up) * image_factor
-    text_grad = jnp.sum(text_blocks.astype(jnp.float32), axis=0) * text_factor
+    text_grad = jnp.sum(text_blocks.astype(jnp.float32) * text_factor, axis=0)
     return (loss, image_grad, text_grad)
 
 

time: 170 us -> 170 us (level)
  waiting for transfers between devices: 71.3 us -> 67.3 us
  starting transfers between devices: 49.2 us -> 53.1 us
    ppermute x29, waiting for transfers between devices: 55.8 us -> 46.9 us  [moved(): return lax.ppermute(value, NAMES, pairs)]
    all_to_all x1, waiting for transfers between devices: 0.35 us -> 5.3 us  [body(): lax.all_to_all(text_part.reshape(16, BLOCK, WIDTH), TEXT_GROUP, 0, 0, til...]
    ppermute x29, starting transfers between devices: 24.7 us -> 28.6 us  [moved(): return lax.ppermute(value, NAMES, pairs)]
  transfers between devices with their start and end apart: 33 -> 33, of which waited for: 20 -> 18; matrix products, arithmetic and copies ran while one was open for 8% -> 8% of each run, Pallas kernels for 0% -> 0%
where the time goes in v11:
time: 170 us; the launch traced here: 168 us
  waiting for transfers between devices  67.3 us (40%)
  starting transfers between devices  53.1 us (31%)
  Pallas kernels  25.1 us (15%)
  matrix products  9.42 us (6%)
  other arithmetic  7.3 us (4%)
  between operations  3.44 us (2%)
  local copies, waits for them, and re-layouts  2.37 us (1%)
    ppermute x29, waiting for transfers between devices, moved(): return lax.ppermute(value, NAMES, pairs)  46.9 us
    ppermute x29, starting transfers between devices, moved(): return lax.ppermute(value, NAMES, pairs)  28.6 us
    all_to_all x3, starting transfers between devices, exchanged(): return lax.all_to_all(copies, axis, split_axis=0, concat_axis=0, tiled=True)  17.4 us
    pallas_call x1, Pallas kernels, logits_and_statistics(): pl.pallas_call(kernel, out_shape=(square, square, half, half, small, smal...  15.5 us
    all_to_all x3, waiting for transfers between devices, exchanged(): return lax.all_to_all(copies, axis, split_axis=0, concat_axis=0, tiled=True)  15.1 us
    pallas_call x1, Pallas kernels, gradient_of_logits(): pl.pallas_call(gradient_kernel, grid=(SIDE // ROWS,), out_shape=(jax.Shap...  7.69 us
    all_to_all x1, starting transfers between devices, body(): lax.all_to_all(text_part.reshape(16, BLOCK, WIDTH), TEXT_GROUP, 0, 0, til...  7.16 us
    dot_general x1, matrix products, body(): lax.dot_general(gradient, image_slab, (((0,), (0,)), ((), ())), preferred...  5.33 us
  transfers between devices with their start and end apart: 33, of which 18 were waited for; matrix products, arithmetic and copies ran while one was open for 8% of the time, Pallas kernels for 0%

profile of v11, /device:TPU:8, one launch (start us, length us, event | category | flops | bytes accessed | tf_op | source)
XLA Modules:
  0.0 168.1 jit_solution(8776192586449303491)
XLA Ops:
  14.1 3.9 %collective-permute-done.3 = bf16[64,2048]{1,0:T(8,128)(2,1)S(1)} collective-permute-done((bf16[64,2048]{1,0:T(8,128)(2,1)}, bf16[64,2048]{1,0:T(8,128)(2,1)S(1)}, u32[]{:S(2)}, u32[]{:S(2)}) %collective-permute-start.3) | collective-permute-done | bytes 262176 | tf_op jit(solution)/shard_map/ppermute | solution.py:59
  21.2 7.6 %collective-permute-done.7 = bf16[64,2048]{1,0:T(8,128)(2,1)S(1)} collective-permute-done((bf16[64,2048]{1,0:T(8,128)(2,1)S(1)}, bf16[64,2048]{1,0:T(8,128)(2,1)S(1)}, u32[]{:S(2)}, u32[]{:S(2)}) %collective-permute-start.7) | collective-permute-done | bytes 262176 | tf_op jit(solution)/shard_map/ppermute | solution.py:59
  28.8 2.8 %collective-permute-done.8 = bf16[64,2048]{1,0:T(8,128)(2,1)S(1)} collective-permute-done((bf16[64,2048]{1,0:T(8,128)(2,1)S(1)}, bf16[64,2048]{1,0:T(8,128)(2,1)S(1)}, u32[]{:S(2)}, u32[]{:S(2)}) %collective-permute-start.8) | collective-permute-done | bytes 262176 | tf_op jit(solution)/shard_map/ppermute | solution.py:59
  31.7 7.5 %collective-permute-done.10 = bf16[64,2048]{1,0:T(8,128)(2,1)S(1)} collective-permute-done((bf16[64,2048]{1,0:T(8,128)(2,1)S(1)}, bf16[64,2048]{1,0:T(8,128)(2,1)S(1)}, u32[]{:S(2)}, u32[]{:S(2)}) %collective-permute-start.10) | collective-permute-done | bytes 262176 | tf_op jit(solution)/shard_map/ppermute | solution.py:59
  39.2 2.8 %collective-permute-done.9 = bf16[64,2048]{1,0:T(8,128)(2,1)S(1)} collective-permute-done((bf16[64,2048]{1,0:T(8,128)(2,1)S(1)}, bf16[64,2048]{1,0:T(8,128)(2,1)S(1)}, u32[]{:S(2)}, u32[]{:S(2)}) %collective-permute-start.9) | collective-permute-done | bytes 262176 | tf_op jit(solution)/shard_map/ppermute | solution.py:59
  44.7 5.2 %collective-permute-done.14 = bf16[64,2048]{1,0:T(8,128)(2,1)S(1)} collective-permute-done((bf16[64,2048]{1,0:T(8,128)(2,1)S(1)}, bf16[64,2048]{1,0:T(8,128)(2,1)S(1)}, u32[]{:S(2)}, u32[]{:S(2)}) %collective-permute-start.14) | collective-permute-done | bytes 262176 | tf_op jit(solution)/shard_map/ppermute | solution.py:59
  49.9 2.8 %collective-permute-done.15 = bf16[64,2048]{1,0:T(8,128)(2,1)S(1)} collective-permute-done((bf16[64,2048]{1,0:T(8,128)(2,1)S(1)}, bf16[64,2048]{1,0:T(8,128)(2,1)S(1)}, u32[]{:S(2)}, u32[]{:S(2)}) %collective-permute-start.15) | collective-permute-done | bytes 262176 | tf_op jit(solution)/shard_map/ppermute | solution.py:59
  55.3 15.5 %shard_map.68 = (f32[1024,1024]{1,0:T(8,128)}, f32[1024,1024]{1,0:T(8,128)}, bf16[1024,1024]{1,0:T(8,128)(2,1)}, bf16[1024,1024]{1,0:T(8,128)(2,1)}, f32[16,2,1152]{2,1,0:T(2,128)}, /*index=5*/f32[16,2,1152]{2,1,0:T(2,128)}) custom-call(s32[32]{0:T(128)} %stack.131.refs_0_, bf16[256,2048]{1,0:T(8,128)(2,1)} %copy-done, bf16[256,2048]{1,0:T(8,128)(2,1)} %copy-done.1, ...), custom_call_target="tpu_custom_call" | custom-call | flops 4294967296 | bytes 20971520 | tf_op jit(solution)/shard_map/pallas_call | solution.py:261
  70.8 6.1 %all-to-all-start.1 = ((f32[16,2,1152]{2,1,0:T(2,128)}), f32[16,2,1152]{2,1,0:T(2,128)S(1)}, u32[]{:S(2)}, u32[]{:S(2)}) async-start(f32[16,2,1152]{2,1,0:T(2,128)} %get-tuple-element.62), calls=%async_computation.1 | async-start | bytes 294912 | tf_op jit(solution)/shard_map/all_to_all | solution.py:393
  76.9 6.3 %all-to-all-done.1.col_ref = f32[16,2,1152]{2,1,0:T(2,128)S(1)} async-done(((f32[16,2,1152]{2,1,0:T(2,128)}), f32[16,2,1152]{2,1,0:T(2,128)S(1)}, u32[]{:S(2)}, u32[]{:S(2)}) %all-to-all-start.1) | async-done | bytes 147488 | tf_op jit(solution)/shard_map/all_to_all | solution.py:393
  83.3 6.2 %all-to-all-start = ((f32[16,2,1152]{2,1,0:T(2,128)}), f32[16,2,1152]{2,1,0:T(2,128)S(1)}, u32[]{:S(2)}, u32[]{:S(2)}) async-start(f32[16,2,1152]{2,1,0:T(2,128)} %get-tuple-element.61), calls=%async_computation | async-start | bytes 294912 | tf_op jit(solution)/shard_map/all_to_all | solution.py:393
  89.9 8.8 %all-to-all-done.row_ref = f32[16,2,1152]{2,1,0:T(2,128)S(1)} async-done(((f32[16,2,1152]{2,1,0:T(2,128)}), f32[16,2,1152]{2,1,0:T(2,128)S(1)}, u32[]{:S(2)}, u32[]{:S(2)}) %all-to-all-start) | async-done | bytes 147488 | tf_op jit(solution)/shard_map/all_to_all | solution.py:393
  98.7 7.7 %shard_map.69 = (bf16[1024,1024]{1,0:T(8,128)(2,1)S(1)}, f32[8,1024]{1,0:T(8,128)S(1)}, f32[16,8,128]{2,1,0:T(8,128)}) custom-call(f32[1024,1024]{1,0:T(8,128)} %get-tuple-element.59.s_ref, f32[1024,1024]{1,0:T(8,128)} %get-tuple-element.60.t_ref, f32[16,2,1152]{2,1,0:T(2,128)S(1)} %all-to-all-done.row_ref, f32[16,2,1152]{2,1,0:T(2,128)S(1)} %all-to-all-done.1.col_ref, ...), custom_call_target="tpu_custom_call" | custom-call | flops 16777216 | bytes 10485760 | tf_op jit(solution)/shard_map/pallas_call | solution.py:361
  108.4 2.8 %fusion.1 = f32[512,1024]{1,0:T(8,128)S(1)} fusion(bf16[1024,1024]{1,0:T(8,128)(2,1)} %get-tuple-element.64, bf16[1024,1024]{1,0:T(8,128)(2,1)S(1)} %get-tuple-element.70, s32[]{:T(128)S(6)} %select_n.465), kind=kOutput, calls=%fused_computation.6 | convolution fusion | flops 1073741824 | bytes 5242884 | tf_op jit(solution)/shard_map/dot_general | solution.py:438
  114.1 5.1 %all-to-all-start.2 = ((f32[16,8,128]{2,1,0:T(8,128)}), f32[16,8,128]{2,1,0:T(8,128)S(1)}, u32[]{:S(2)}, u32[]{:S(2)}) async-start(f32[16,8,128]{2,1,0:T(8,128)} %get-tuple-element.74), calls=%async_computation.2 | async-start | bytes 131072 | tf_op jit(solution)/shard_map/all_to_all | solution.py:393
  121.4 5.3 %multiply_convert_fusion = f16[1024,1024]{1,0:T(8,128)(2,1)} fusion(bf16[1024,1024]{1,0:T(8,128)(2,1)S(1)} %get-tuple-element.70, bf16[1024,1024]{1,0:T(8,128)(2,1)} %get-tuple-element.71, f32[1024]{0:T(1024)S(1)} %bitcast.75), kind=kOutput, calls=%fused_computation.1 | convolution fusion | flops 2149580800 | bytes 6295552 | tf_op jit(solution)/shard_map/dot_general | solution.py:460
  126.9 7.2 %all-to-all-start.3 = ((f16[16,64,1024]{2,1,0:T(8,128)(2,1)}), f16[16,64,1024]{2,1,0:T(8,128)(2,1)S(1)}, u32[]{:S(2)}, u32[]{:S(2)}) async-start(f16[16,64,1024]{2,1,0:T(8,128)(2,1)} %bitcast.70), calls=%async_computation.3 | async-start | bytes 4194304 | tf_op jit(solution)/shard_map/all_to_all | solution.py:468
  134.1 2.2 %collective-permute-start.21 = (f16[64,1024]{1,0:T(8,128)(2,1)S(1)}, f16[64,1024]{1,0:T(8,128)(2,1)}, u32[]{:S(2)}, u32[]{:S(2)}) collective-permute-start(f16[64,1024]{1,0:T(8,128)(2,1)S(1)} %get-tuple-element.72), channel_id=1, source_target_pairs={{0,38},{1,33},{2,32},{3,35},{4,34},{5,37},{6,36},{7,39},{8,46},{9,... | collective-permute-start | bytes 393224 | tf_op jit(solution)/shard_map/ppermute | solution.py:59
  136.3 3.3 %collective-permute-start.23 = (f32[8,128]{1,0:T(8,128)S(1)}, f32[8,128]{1,0:T(8,128)S(1)}, u32[]{:S(2)}, u32[]{:S(2)}) collective-permute-start(f32[8,128]{1,0:T(8,128)S(1)} %reduce_sum.18), channel_id=1, source_target_pairs={{0,4},{1,5},{2,6},{3,7},{4,0},{5,1},{6,2},{7,3},{8,12},{9,13},{10,... | collective-permute-start | bytes 12296 | tf_op jit(solution)/shard_map/ppermute | solution.py:59
  139.6 4.3 %collective-permute-done.23 = f32[8,128]{1,0:T(8,128)S(1)} collective-permute-done((f32[8,128]{1,0:T(8,128)S(1)}, f32[8,128]{1,0:T(8,128)S(1)}, u32[]{:S(2)}, u32[]{:S(2)}) %collective-permute-start.23) | collective-permute-done | bytes 4128 | tf_op jit(solution)/shard_map/ppermute | solution.py:59
  145.0 3.3 %collective-permute-start.27 = (f16[64,1024]{1,0:T(8,128)(2,1)S(1)}, f16[64,1024]{1,0:T(8,128)(2,1)S(1)}, u32[]{:S(2)}, u32[]{:S(2)}) collective-permute-start(f16[64,1024]{1,0:T(8,128)(2,1)S(1)} %get-tuple-element.76), channel_id=1, source_target_pairs={{0,38},{1,33},{2,32},{3,35},{4,34},{5,37},{6,36},{7,39},{8,46},{9,... | collective-permute-start | bytes 393224 | tf_op jit(solution)/shard_map/ppermute | solution.py:59
  149.5 3.3 %collective-permute-done.24 = f32[8,128]{1,0:T(8,128)S(1)} collective-permute-done((f32[8,128]{1,0:T(8,128)S(1)}, f32[8,128]{1,0:T(8,128)S(1)}, u32[]{:S(2)}, u32[]{:S(2)}) %collective-permute-start.24) | collective-permute-done | bytes 4128 | tf_op jit(solution)/shard_map/ppermute | solution.py:59
  154.3 2.1 %collective-permute-done.25 = f32[8,128]{1,0:T(8,128)S(1)} collective-permute-done((f32[8,128]{1,0:T(8,128)S(1)}, f32[8,128]{1,0:T(8,128)S(1)}, u32[]{:S(2)}, u32[]{:S(2)}) %collective-permute-start.25) | collective-permute-done | bytes 4128 | tf_op jit(solution)/shard_map/ppermute | solution.py:59
  160.4 5.3 %all-to-all-done.3 = f16[16,64,1024]{2,1,0:T(8,128)(2,1)S(1)} async-done(((f16[16,64,1024]{2,1,0:T(8,128)(2,1)}), f16[16,64,1024]{2,1,0:T(8,128)(2,1)S(1)}, u32[]{:S(2)}, u32[]{:S(2)}) %all-to-all-start.3) | async-done | bytes 2097184 | tf_op jit(solution)/shard_map/all_to_all | solution.py:468
  (91 shorter events, 37.2 us)
Async XLA Ops:
  2.5 8.9 %collective-permute-start = (bf16[64,2048]{1,0:T(8,128)(2,1)}, bf16[64,2048]{1,0:T(8,128)(2,1)S(1)}, u32[]{:S(2)}, u32[]{:S(2)}) collective-permute-start(bf16[64,2048]{1,0:T(8,128)(2,1)} %get-tuple-element.41), channel_id=1, source_target_pairs={{0,8},{1,65},{2,10},{3,67},{4,12},{5,69},{6,14},{7,71},{8,16},{9,7... | collective-permute-start | bytes 786440 | tf_op jit(solution)/shard_map/ppermute | solution.py:59
  4.0 8.8 %collective-permute-start.1 = (bf16[64,2048]{1,0:T(8,128)(2,1)}, bf16[64,2048]{1,0:T(8,128)(2,1)S(1)}, u32[]{:S(2)}, u32[]{:S(2)}) collective-permute-start(bf16[64,2048]{1,0:T(8,128)(2,1)} %get-tuple-element.41), channel_id=1, source_target_pairs={{0,24},{1,193},{2,26},{3,195},{4,28},{5,197},{6,30},{7,199},{8,0},... | collective-permute-start | bytes 786440 | tf_op jit(solution)/shard_map/ppermute | solution.py:59
  5.8 8.3 %collective-permute-start.2 = (bf16[64,2048]{1,0:T(8,128)(2,1)}, bf16[64,2048]{1,0:T(8,128)(2,1)S(1)}, u32[]{:S(2)}, u32[]{:S(2)}) collective-permute-start(bf16[64,2048]{1,0:T(8,128)(2,1)} %get-tuple-element.41), channel_id=1, source_target_pairs={{0,16},{1,129},{2,18},{3,131},{4,20},{5,133},{6,22},{7,135},{8,24}... | collective-permute-start | bytes 786440 | tf_op jit(solution)/shard_map/ppermute | solution.py:59
  7.6 10.4 %collective-permute-start.3 = (bf16[64,2048]{1,0:T(8,128)(2,1)}, bf16[64,2048]{1,0:T(8,128)(2,1)S(1)}, u32[]{:S(2)}, u32[]{:S(2)}) collective-permute-start(bf16[64,2048]{1,0:T(8,128)(2,1)} %get-tuple-element.42.refs_6_), channel_id=1, source_target_pairs={{0,32},{1,39},{2,34},{3,33},{4,36},{5,35},{6,38},{7,37},{8,40},{9,... | collective-permute-start | bytes 786440 | tf_op jit(solution)/shard_map/ppermute | solution.py:59
  9.5 8.5 %collective-permute-start.4 = (bf16[64,2048]{1,0:T(8,128)(2,1)}, bf16[64,2048]{1,0:T(8,128)(2,1)S(1)}, u32[]{:S(2)}, u32[]{:S(2)}) collective-permute-start(bf16[64,2048]{1,0:T(8,128)(2,1)} %get-tuple-element.42.refs_6_), channel_id=1, source_target_pairs={{0,1},{1,0},{2,3},{3,2},{4,5},{5,4},{6,7},{7,6},{8,9},{9,8},{10,11... | collective-permute-start | bytes 786440 | tf_op jit(solution)/shard_map/ppermute | solution.py:59
  19.1 22.9 %collective-permute-start.5 = (bf16[256,2048]{1,0:T(8,128)(2,1)S(1)}, bf16[256,2048]{1,0:T(8,128)(2,1)S(1)}, u32[]{:S(2)}, u32[]{:S(2)}) collective-permute-start(bf16[256,2048]{1,0:T(8,128)(2,1)S(1)} %pad_maximum_fusion.refs_1_), channel_id=1, source_target_pairs={{0,64},{1,9},{2,66},{3,11},{4,68},{5,13},{6,70},{7,15},{8,72},{9,1... | collective-permute-start | bytes 3145736 | tf_op jit(solution)/shard_map/ppermute | solution.py:59
  20.8 21.2 %collective-permute-start.6 = (bf16[256,2048]{1,0:T(8,128)(2,1)S(1)}, bf16[256,2048]{1,0:T(8,128)(2,1)S(1)}, u32[]{:S(2)}, u32[]{:S(2)}) collective-permute-start(bf16[256,2048]{1,0:T(8,128)(2,1)S(1)} %pad_maximum_fusion.refs_1_), channel_id=1, source_target_pairs={{0,192},{1,25},{2,194},{3,27},{4,196},{5,29},{6,198},{7,31},{8,200... | collective-permute-start | bytes 3145736 | tf_op jit(solution)/shard_map/ppermute | solution.py:59
  21.2 7.6 %collective-permute-start.7 = (bf16[64,2048]{1,0:T(8,128)(2,1)S(1)}, bf16[64,2048]{1,0:T(8,128)(2,1)S(1)}, u32[]{:S(2)}, u32[]{:S(2)}) collective-permute-start(bf16[64,2048]{1,0:T(8,128)(2,1)S(1)} %collective-permute-done.3), channel_id=1, source_target_pairs={{0,32},{1,39},{2,34},{3,33},{4,36},{5,35},{6,38},{7,37},{8,40},{9,... | collective-permute-start | bytes 786440 | tf_op jit(solution)/shard_map/ppermute | solution.py:59
  21.2 10.4 %collective-permute-start.8 = (bf16[64,2048]{1,0:T(8,128)(2,1)S(1)}, bf16[64,2048]{1,0:T(8,128)(2,1)S(1)}, u32[]{:S(2)}, u32[]{:S(2)}) collective-permute-start(bf16[64,2048]{1,0:T(8,128)(2,1)S(1)} %collective-permute-done.4.refs_7_), channel_id=1, source_target_pairs={{0,32},{1,39},{2,34},{3,33},{4,36},{5,35},{6,38},{7,37},{8,40},{9,... | collective-permute-start | bytes 786440 | tf_op jit(solution)/shard_map/ppermute | solution.py:59
  31.6 10.4 %collective-permute-start.9 = (bf16[64,2048]{1,0:T(8,128)(2,1)S(1)}, bf16[64,2048]{1,0:T(8,128)(2,1)S(1)}, u32[]{:S(2)}, u32[]{:S(2)}) collective-permute-start(bf16[64,2048]{1,0:T(8,128)(2,1)S(1)} %collective-permute-done.7), channel_id=1, source_target_pairs={{0,32},{1,39},{2,34},{3,33},{4,36},{5,35},{6,38},{7,37},{8,40},{9,... | collective-permute-start | bytes 786440 | tf_op jit(solution)/shard_map/ppermute | solution.py:59
  42.1 13.0 %collective-permute-start.13 = (bf16[320,2048]{1,0:T(8,128)(2,1)S(1)}, bf16[320,2048]{1,0:T(8,128)(2,1)}, u32[]{:S(2)}, u32[]{:S(2)}) collective-permute-start(bf16[320,2048]{1,0:T(8,128)(2,1)S(1)} %constant_dynamic-update-slice_fusion.refs_8_), channel_id=1, source_target_pairs={{0,1},{1,0},{2,3},{3,2},{4,5},{5,4},{6,7},{7,6},{8,9},{9,8},{10,11... | collective-permute-start | bytes 3932168 | tf_op jit(solution)/shard_map/ppermute | solution.py:59
  42.2 7.7 %collective-permute-start.14 = (bf16[64,2048]{1,0:T(8,128)(2,1)S(1)}, bf16[64,2048]{1,0:T(8,128)(2,1)S(1)}, u32[]{:S(2)}, u32[]{:S(2)}) collective-permute-start(bf16[64,2048]{1,0:T(8,128)(2,1)S(1)} %collective-permute-done.9), channel_id=1, source_target_pairs={{0,32},{1,39},{2,34},{3,33},{4,36},{5,35},{6,38},{7,37},{8,40},{9,... | collective-permute-start | bytes 786440 | tf_op jit(solution)/shard_map/ppermute | solution.py:59
  42.3 10.4 %collective-permute-start.15 = (bf16[64,2048]{1,0:T(8,128)(2,1)S(1)}, bf16[64,2048]{1,0:T(8,128)(2,1)S(1)}, u32[]{:S(2)}, u32[]{:S(2)}) collective-permute-start(bf16[64,2048]{1,0:T(8,128)(2,1)S(1)} %collective-permute-done.10), channel_id=1, source_target_pairs={{0,32},{1,39},{2,34},{3,33},{4,36},{5,35},{6,38},{7,37},{8,40},{9,... | collective-permute-start | bytes 786440 | tf_op jit(solution)/shard_map/ppermute | solution.py:59
  42.5 12.0 %collective-permute-start.11 = (bf16[128,2048]{1,0:T(8,128)(2,1)S(1)}, bf16[128,2048]{1,0:T(8,128)(2,1)S(1)}, u32[]{:S(2)}, u32[]{:S(2)}) collective-permute-start(bf16[128,2048]{1,0:T(8,128)(2,1)S(1)} %slice.21), channel_id=1, source_target_pairs={{0,64},{1,9},{2,66},{3,11},{4,68},{5,13},{6,70},{7,15},{8,72},{9,1... | collective-permute-start | bytes 1572872 | tf_op jit(solution)/shard_map/ppermute | solution.py:59
  44.2 10.3 %collective-permute-start.12 = (bf16[128,2048]{1,0:T(8,128)(2,1)S(1)}, bf16[128,2048]{1,0:T(8,128)(2,1)}, u32[]{:S(2)}, u32[]{:S(2)}) collective-permute-start(bf16[128,2048]{1,0:T(8,128)(2,1)S(1)} %slice.22), channel_id=1, source_target_pairs={{0,192},{1,25},{2,194},{3,27},{4,196},{5,29},{6,198},{7,31},{8,200... | collective-permute-start | bytes 1572872 | tf_op jit(solution)/shard_map/ppermute | solution.py:59
  70.8 12.4 %all-to-all-start.1 = ((f32[16,2,1152]{2,1,0:T(2,128)}), f32[16,2,1152]{2,1,0:T(2,128)S(1)}, u32[]{:S(2)}, u32[]{:S(2)}) async-start(f32[16,2,1152]{2,1,0:T(2,128)} %get-tuple-element.62), calls=%async_computation.1 | async-start | bytes 294912 | tf_op jit(solution)/shard_map/all_to_all | solution.py:393
  83.3 15.4 %all-to-all-start = ((f32[16,2,1152]{2,1,0:T(2,128)}), f32[16,2,1152]{2,1,0:T(2,128)S(1)}, u32[]{:S(2)}, u32[]{:S(2)}) async-start(f32[16,2,1152]{2,1,0:T(2,128)} %get-tuple-element.61), calls=%async_computation | async-start | bytes 294912 | tf_op jit(solution)/shard_map/all_to_all | solution.py:393
  114.1 12.8 %all-to-all-start.2 = ((f32[16,8,128]{2,1,0:T(8,128)}), f32[16,8,128]{2,1,0:T(8,128)S(1)}, u32[]{:S(2)}, u32[]{:S(2)}) async-start(f32[16,8,128]{2,1,0:T(8,128)} %get-tuple-element.74), calls=%async_computation.2 | async-start | bytes 131072 | tf_op jit(solution)/shard_map/all_to_all | solution.py:393
  126.9 38.8 %all-to-all-start.3 = ((f16[16,64,1024]{2,1,0:T(8,128)(2,1)}), f16[16,64,1024]{2,1,0:T(8,128)(2,1)S(1)}, u32[]{:S(2)}, u32[]{:S(2)}) async-start(f16[16,64,1024]{2,1,0:T(8,128)(2,1)} %bitcast.70), calls=%async_computation.3 | async-start | bytes 4194304 | tf_op jit(solution)/shard_map/all_to_all | solution.py:468
  134.1 9.8 %collective-permute-start.21 = (f16[64,1024]{1,0:T(8,128)(2,1)S(1)}, f16[64,1024]{1,0:T(8,128)(2,1)}, u32[]{:S(2)}, u32[]{:S(2)}) collective-permute-start(f16[64,1024]{1,0:T(8,128)(2,1)S(1)} %get-tuple-element.72), channel_id=1, source_target_pairs={{0,38},{1,33},{2,32},{3,35},{4,34},{5,37},{6,36},{7,39},{8,46},{9,... | collective-permute-start | bytes 393224 | tf_op jit(solution)/shard_map/ppermute | solution.py:59
  136.3 7.6 %collective-permute-start.22 = (f16[64,1024]{1,0:T(8,128)(2,1)S(1)}, f16[64,1024]{1,0:T(8,128)(2,1)}, u32[]{:S(2)}, u32[]{:S(2)}) collective-permute-start(f16[64,1024]{1,0:T(8,128)(2,1)S(1)} %get-tuple-element.73), channel_id=1, source_target_pairs={{0,32},{1,39},{2,34},{3,33},{4,36},{5,35},{6,38},{7,37},{8,40},{9,... | collective-permute-start | bytes 393224 | tf_op jit(solution)/shard_map/ppermute | solution.py:59
  136.3 7.6 %collective-permute-start.23 = (f32[8,128]{1,0:T(8,128)S(1)}, f32[8,128]{1,0:T(8,128)S(1)}, u32[]{:S(2)}, u32[]{:S(2)}) collective-permute-start(f32[8,128]{1,0:T(8,128)S(1)} %reduce_sum.18), channel_id=1, source_target_pairs={{0,4},{1,5},{2,6},{3,7},{4,0},{5,1},{6,2},{7,3},{8,12},{9,13},{10,... | collective-permute-start | bytes 12296 | tf_op jit(solution)/shard_map/ppermute | solution.py:59
  145.0 13.8 %collective-permute-start.27 = (f16[64,1024]{1,0:T(8,128)(2,1)S(1)}, f16[64,1024]{1,0:T(8,128)(2,1)S(1)}, u32[]{:S(2)}, u32[]{:S(2)}) collective-permute-start(f16[64,1024]{1,0:T(8,128)(2,1)S(1)} %get-tuple-element.76), channel_id=1, source_target_pairs={{0,38},{1,33},{2,32},{3,35},{4,34},{5,37},{6,36},{7,39},{8,46},{9,... | collective-permute-start | bytes 393224 | tf_op jit(solution)/shard_map/ppermute | solution.py:59
  148.3 10.5 %collective-permute-start.28 = (f16[64,1024]{1,0:T(8,128)(2,1)S(1)}, f16[64,1024]{1,0:T(8,128)(2,1)}, u32[]{:S(2)}, u32[]{:S(2)}) collective-permute-start(f16[64,1024]{1,0:T(8,128)(2,1)S(1)} %get-tuple-element.77), channel_id=1, source_target_pairs={{0,32},{1,39},{2,34},{3,33},{4,36},{5,35},{6,38},{7,37},{8,40},{9,... | collective-permute-start | bytes 393224 | tf_op jit(solution)/shard_map/ppermute | solution.py:59
  (17 other events, 134.9 us)

commit v12 on v11

--- a/solution.py
+++ b/solution.py
@@ -292,6 +292,7 @@
     row_id_ref,
     col_id_ref,
     out_ref,
+    turned_ref,
     factor_ref,
     part_ref,
     lse_ref,
@@ -341,6 +342,11 @@
                 same = row_id == col_id_ref[:, lanes]
                 out_ref[rows, lanes] = jnp.where(same, value - 1.0, value).astype(jnp.bfloat16)
                 total = total + (weights * (t - s) - jnp.where(same, s, 0.0))
+        for k in range(SIDE // 128):
+            tile = out_ref[pl.ds(base, STRIP), pl.ds(k * 128, 128)].astype(jnp.float32)
+            turned_ref[pl.ds(k * 128, 128), pl.ds(base, STRIP)] = jnp.transpose(tile).astype(
+                jnp.bfloat16
+            )
         return total
 
     total_ref[...] = lax.fori_loop(0, ROWS // STRIP, strip, total_ref[...])
@@ -362,6 +368,7 @@
         gradient_kernel,
         grid=(SIDE // ROWS,),
         out_shape=(
+            jax.ShapeDtypeStruct((SIDE, SIDE), jnp.bfloat16),
             jax.ShapeDtypeStruct((SIDE, SIDE), jnp.bfloat16),
             jax.ShapeDtypeStruct((8, SIDE), f32),
             jax.ShapeDtypeStruct((GROUP, 8, 128), f32),
@@ -374,7 +381,7 @@
             pl.BlockSpec((ROWS, 1), lambda i: (i, 0)),
             whole(col_id.shape),
         ],
-        out_specs=(by_rows, whole((8, SIDE)), whole((GROUP, 8, 128))),
+        out_specs=(by_rows, pl.BlockSpec((SIDE, ROWS), lambda i: (0, i)), whole((8, SIDE)), whole((GROUP, 8, 128))),
         scratch_shapes=[pltpu.VMEM((8, SIDE), f32), pltpu.VMEM((16, 128), f32)],
         compiler_params=pltpu.CompilerParams(vmem_limit_bytes=GRADIENT_VMEM),
         cost_estimate=pl.CostEstimate(
@@ -425,15 +432,19 @@
     )
     col_all = exchanged(col_part, TEXT_GROUP)
     row_all = exchanged(row_part, IMAGE_GROUP)
-    gradient, factors, part = gradient_of_logits(s, t, row_all, col_all, row_id, col_id)
+    gradient, turned, factors, part = gradient_of_logits(s, t, row_all, col_all, row_id, col_id)
     text_scale, image_scale = factors[0:1], factors[1:2]
     image_factor, text_factor = factors[2:3], factors[3:4]
 
+    tie = lax.optimization_barrier
+    steps = [lambda p, k=k: flipped(p, k) for k in (4, 2, 1)] + [other_core]
     half = SIDE // 2
     theirs = lax.dynamic_slice_in_dim(gradient, (1 - c) * half, half)
     mine = lax.dynamic_slice_in_dim(gradient, c * half, half)
     image_theirs = jnp.dot(theirs, text_slab, preferred_element_type=jnp.float32)
-    arrived = moved((image_theirs * text_scale).astype(jnp.float16), other_core)
+    image_theirs, part = tie(((image_theirs * text_scale).astype(jnp.float16), part))
+    arrived = moved(image_theirs, other_core)
+    value = jnp.sum(exchanged(part, TEXT_GROUP), axis=0)
     image_mine = (
         jnp.dot(mine, text_slab, preferred_element_type=jnp.float32) * text_scale
     ) + arrived.astype(jnp.float32)
@@ -447,26 +458,20 @@
     def narrow(v):
         return v.astype(jnp.float16)
 
-    tie = lax.optimization_barrier
-    steps = [lambda p, k=k: flipped(p, k) for k in (4, 2, 1)] + [other_core]
-    start, part = tie((narrow(block(4)), part))
+    start, turned = tie((narrow(block(4)), turned))
     down = moved(start, along_z(-1)).astype(jnp.float32)
-    value = jnp.sum(exchanged(part, TEXT_GROUP), axis=0)
-
-    first, second, gradient = tie((narrow(block(-3) + down), narrow(block(3)), gradient))
+    text_part = (
+        jnp.dot(turned, image_slab, preferred_element_type=jnp.float32) * image_scale
+    ).astype(jnp.float16)
+    down, text_part = tie((down, text_part))
+    text_blocks = lax.all_to_all(text_part.reshape(16, BLOCK, WIDTH), TEXT_GROUP, 0, 0, tiled=True)
+    first, second = tie((narrow(block(-3) + down), narrow(block(3))))
     down = moved(first, along_z(-1)).astype(jnp.float32)
     up = moved(second, along_z(1)).astype(jnp.float32)
-    text_part = (
-        lax.dot_general(
-            gradient, image_slab, (((0,), (0,)), ((), ())), preferred_element_type=jnp.float32
-        )
-        * image_scale
-    ).astype(jnp.float16)
-    first, second, text_part = tie((narrow(block(-2) + down), narrow(block(2) + up), text_part))
+    value = value + moved(value, steps[0])
+    first, second = tie((narrow(block(-2) + down), narrow(block(2) + up)))
     down = moved(first, along_z(-1)).astype(jnp.float32)
     up = moved(second, along_z(1)).astype(jnp.float32)
-    text_blocks = lax.all_to_all(text_part.reshape(16, BLOCK, WIDTH), TEXT_GROUP, 0, 0, tiled=True)
-    value = value + moved(value, steps[0])
     first, second, value = tie((narrow(block(-1) + down), narrow(block(1) + up), value))
     down = moved(first, along_z(-1)).astype(jnp.float32)
     up = moved(second, along_z(1)).astype(jnp.float32)

time: 170 us -> 171 us (level)
  waiting for transfers between devices: 67.3 us -> 71.8 us
  starting transfers between devices: 53.1 us -> 49 us
    ppermute x29, waiting for transfers between devices: 46.9 us -> 56.7 us  [moved(): return lax.ppermute(value, NAMES, pairs)]
    all_to_all x1, waiting for transfers between devices: 5.3 us -> 0.01 us  [body(): lax.all_to_all(text_part.reshape(16, BLOCK, WIDTH), TEXT_GROUP, 0, 0, til...]
    ppermute x29, starting transfers between devices: 28.6 us -> 24.3 us  [moved(): return lax.ppermute(value, NAMES, pairs)]
    convert_element_type x3, other arithmetic: 1.2 us -> 3.39 us  [narrow(): return v.astype(jnp.float16)]
  transfers between devices with their start and end apart: 33 -> 33, of which waited for: 18 -> 19; matrix products, arithmetic and copies ran while one was open for 8% -> 9% of each run, Pallas kernels for 0% -> 0%
where the time goes in v12:
time: 171 us; the launch traced here: 170 us
  waiting for transfers between devices  71.8 us (42%)
  starting transfers between devices  49 us (29%)
  Pallas kernels  26.1 us (15%)
  matrix products  8.57 us (5%)
  other arithmetic  7.85 us (5%)
  between operations  3.44 us (2%)
  local copies, waits for them, and re-layouts  2.87 us (2%)
    ppermute x29, waiting for transfers between devices, moved(): return lax.ppermute(value, NAMES, pairs)  56.7 us
    ppermute x29, starting transfers between devices, moved(): return lax.ppermute(value, NAMES, pairs)  24.3 us
    all_to_all x3, starting transfers between devices, exchanged(): return lax.all_to_all(copies, axis, split_axis=0, concat_axis=0, tiled=True)  17.5 us
    pallas_call x1, Pallas kernels, logits_and_statistics(): pl.pallas_call(kernel, out_shape=(square, square, half, half, small, smal...  15.5 us
    all_to_all x3, waiting for transfers between devices, exchanged(): return lax.all_to_all(copies, axis, split_axis=0, concat_axis=0, tiled=True)  15.1 us
    pallas_call x1, Pallas kernels, gradient_of_logits(): pl.pallas_call(gradient_kernel, grid=(SIDE // ROWS,), out_shape=(jax.Shap...  8.69 us
    all_to_all x1, starting transfers between devices, body(): lax.all_to_all(text_part.reshape(16, BLOCK, WIDTH), TEXT_GROUP, 0, 0, til...  7.28 us
    dot_general x1, matrix products, body(): jnp.dot(turned, image_slab, preferred_element_type=jnp.float32)  3.69 us
  transfers between devices with their start and end apart: 33, of which 19 were waited for; matrix products, arithmetic and copies ran while one was open for 9% of the time, Pallas kernels for 0%

profile of v12, /device:TPU:8, one launch (start us, length us, event | category | flops | bytes accessed | tf_op | source)
XLA Modules:
  0.0 169.7 jit_solution(7644738649426718114)
XLA Ops:
  14.1 3.9 %collective-permute-done.3 = bf16[64,2048]{1,0:T(8,128)(2,1)S(1)} collective-permute-done((bf16[64,2048]{1,0:T(8,128)(2,1)}, bf16[64,2048]{1,0:T(8,128)(2,1)S(1)}, u32[]{:S(2)}, u32[]{:S(2)}) %collective-permute-start.3) | collective-permute-done | bytes 262176 | tf_op jit(solution)/shard_map/ppermute | solution.py:59
  21.2 7.6 %collective-permute-done.7 = bf16[64,2048]{1,0:T(8,128)(2,1)S(1)} collective-permute-done((bf16[64,2048]{1,0:T(8,128)(2,1)S(1)}, bf16[64,2048]{1,0:T(8,128)(2,1)S(1)}, u32[]{:S(2)}, u32[]{:S(2)}) %collective-permute-start.7) | collective-permute-done | bytes 262176 | tf_op jit(solution)/shard_map/ppermute | solution.py:59
  28.8 2.8 %collective-permute-done.8 = bf16[64,2048]{1,0:T(8,128)(2,1)S(1)} collective-permute-done((bf16[64,2048]{1,0:T(8,128)(2,1)S(1)}, bf16[64,2048]{1,0:T(8,128)(2,1)S(1)}, u32[]{:S(2)}, u32[]{:S(2)}) %collective-permute-start.8) | collective-permute-done | bytes 262176 | tf_op jit(solution)/shard_map/ppermute | solution.py:59
  31.7 7.5 %collective-permute-done.10 = bf16[64,2048]{1,0:T(8,128)(2,1)S(1)} collective-permute-done((bf16[64,2048]{1,0:T(8,128)(2,1)S(1)}, bf16[64,2048]{1,0:T(8,128)(2,1)S(1)}, u32[]{:S(2)}, u32[]{:S(2)}) %collective-permute-start.10) | collective-permute-done | bytes 262176 | tf_op jit(solution)/shard_map/ppermute | solution.py:59
  39.2 2.8 %collective-permute-done.9 = bf16[64,2048]{1,0:T(8,128)(2,1)S(1)} collective-permute-done((bf16[64,2048]{1,0:T(8,128)(2,1)S(1)}, bf16[64,2048]{1,0:T(8,128)(2,1)S(1)}, u32[]{:S(2)}, u32[]{:S(2)}) %collective-permute-start.9) | collective-permute-done | bytes 262176 | tf_op jit(solution)/shard_map/ppermute | solution.py:59
  44.7 5.2 %collective-permute-done.14 = bf16[64,2048]{1,0:T(8,128)(2,1)S(1)} collective-permute-done((bf16[64,2048]{1,0:T(8,128)(2,1)S(1)}, bf16[64,2048]{1,0:T(8,128)(2,1)S(1)}, u32[]{:S(2)}, u32[]{:S(2)}) %collective-permute-start.14) | collective-permute-done | bytes 262176 | tf_op jit(solution)/shard_map/ppermute | solution.py:59
  49.9 2.8 %collective-permute-done.15 = bf16[64,2048]{1,0:T(8,128)(2,1)S(1)} collective-permute-done((bf16[64,2048]{1,0:T(8,128)(2,1)S(1)}, bf16[64,2048]{1,0:T(8,128)(2,1)S(1)}, u32[]{:S(2)}, u32[]{:S(2)}) %collective-permute-start.15) | collective-permute-done | bytes 262176 | tf_op jit(solution)/shard_map/ppermute | solution.py:59
  55.2 15.5 %shard_map.68 = (f32[1024,1024]{1,0:T(8,128)}, f32[1024,1024]{1,0:T(8,128)}, bf16[1024,1024]{1,0:T(8,128)(2,1)}, bf16[1024,1024]{1,0:T(8,128)(2,1)}, f32[16,2,1152]{2,1,0:T(2,128)}, /*index=5*/f32[16,2,1152]{2,1,0:T(2,128)}) custom-call(s32[32]{0:T(128)} %stack.131.refs_0_, bf16[256,2048]{1,0:T(8,128)(2,1)} %copy-done.1, bf16[256,2048]{1,0:T(8,128)(2,1)} %copy-done.2, ...), custom_call_target="tpu_custom_call" | custom-call | flops 4294967296 | bytes 20971520 | tf_op jit(solution)/shard_map/pallas_call | solution.py:261
  70.7 6.1 %all-to-all-start.1 = ((f32[16,2,1152]{2,1,0:T(2,128)}), f32[16,2,1152]{2,1,0:T(2,128)S(1)}, u32[]{:S(2)}, u32[]{:S(2)}) async-start(f32[16,2,1152]{2,1,0:T(2,128)} %get-tuple-element.65), calls=%async_computation.1 | async-start | bytes 294912 | tf_op jit(solution)/shard_map/all_to_all | solution.py:400
  76.8 6.3 %all-to-all-done.1.col_ref = f32[16,2,1152]{2,1,0:T(2,128)S(1)} async-done(((f32[16,2,1152]{2,1,0:T(2,128)}), f32[16,2,1152]{2,1,0:T(2,128)S(1)}, u32[]{:S(2)}, u32[]{:S(2)}) %all-to-all-start.1) | async-done | bytes 147488 | tf_op jit(solution)/shard_map/all_to_all | solution.py:400
  83.1 6.3 %all-to-all-start = ((f32[16,2,1152]{2,1,0:T(2,128)}), f32[16,2,1152]{2,1,0:T(2,128)S(1)}, u32[]{:S(2)}, u32[]{:S(2)}) async-start(f32[16,2,1152]{2,1,0:T(2,128)} %get-tuple-element.64), calls=%async_computation | async-start | bytes 294912 | tf_op jit(solution)/shard_map/all_to_all | solution.py:400
  89.9 8.8 %all-to-all-done.row_ref = f32[16,2,1152]{2,1,0:T(2,128)S(1)} async-done(((f32[16,2,1152]{2,1,0:T(2,128)}), f32[16,2,1152]{2,1,0:T(2,128)S(1)}, u32[]{:S(2)}, u32[]{:S(2)}) %all-to-all-start) | async-done | bytes 147488 | tf_op jit(solution)/shard_map/all_to_all | solution.py:400
  98.7 8.7 %shard_map.69 = (bf16[1024,1024]{1,0:T(8,128)(2,1)S(1)}, bf16[1024,1024]{1,0:T(8,128)(2,1)S(1)}, f32[8,1024]{1,0:T(8,128)S(1)}, f32[16,8,128]{2,1,0:T(8,128)}) custom-call(f32[1024,1024]{1,0:T(8,128)} %get-tuple-element.62.s_ref, f32[1024,1024]{1,0:T(8,128)} %get-tuple-element.63.t_ref, f32[16,2,1152]{2,1,0:T(2,128)S(1)} %all-to-all-done.row_ref, ...), custom_call_target="tpu_custom_call" | custom-call | flops 16777216 | bytes 10485760 | tf_op jit(solution)/shard_map/pallas_call | solution.py:367
  109.5 5.1 %all-to-all-start.2 = ((f32[16,8,128]{2,1,0:T(8,128)}), f32[16,8,128]{2,1,0:T(8,128)S(1)}, u32[]{:S(2)}, u32[]{:S(2)}) async-start(f32[16,8,128]{2,1,0:T(8,128)} %get-tuple-element.80), calls=%async_computation.2 | async-start | bytes 131072 | tf_op jit(solution)/shard_map/all_to_all | solution.py:400
  114.5 3.6 %add_convert_fusion = f16[512,1024]{1,0:T(8,128)(2,1)S(1)} fusion(f16[512,1024]{1,0:T(8,128)(2,1)} %collective-permute-done.17, bf16[1024,1024]{1,0:T(8,128)(2,1)} %get-tuple-element.67, f32[1024]{0:T(1024)S(1)} %bitcast.75, bf16[1024,1024]{1,0:T(8,128)(2,1)} %copy-done, s32[]{:T(128)S(6)} %select_n.465), kind=kOutput, calls=%fused_computation.2 | convolution fusion | flops 1075838976 | bytes 5246980 | tf_op jit(solution)/shard_map/dot_general | solution.py:449
  119.4 3.7 %multiply_convert_fusion = f16[1024,1024]{1,0:T(8,128)(2,1)} fusion(bf16[1024,1024]{1,0:T(8,128)(2,1)S(1)} %get-tuple-element.73, bf16[1024,1024]{1,0:T(8,128)(2,1)S(1)} %copy-done.10, f32[1024]{0:T(1024)S(1)} %bitcast.73), kind=kOutput, calls=%fused_computation.1 | convolution fusion | flops 2149580800 | bytes 6295552 | tf_op jit(solution)/shard_map/dot_general | solution.py:464
  123.9 7.3 %all-to-all-start.3 = ((f16[16,64,1024]{2,1,0:T(8,128)(2,1)}), f16[16,64,1024]{2,1,0:T(8,128)(2,1)S(1)}, u32[]{:S(2)}, u32[]{:S(2)}) async-start(f16[16,64,1024]{2,1,0:T(8,128)(2,1)} %bitcast.65), calls=%async_computation.3 | async-start | bytes 4194304 | tf_op jit(solution)/shard_map/all_to_all | solution.py:467
  133.9 3.4 %collective-permute-done.19 = f16[64,1024]{1,0:T(8,128)(2,1)S(1)} collective-permute-done((f16[64,1024]{1,0:T(8,128)(2,1)}, f16[64,1024]{1,0:T(8,128)(2,1)S(1)}, u32[]{:S(2)}, u32[]{:S(2)}) %collective-permute-start.19) | collective-permute-done | bytes 131104 | tf_op jit(solution)/shard_map/ppermute | solution.py:59
  137.3 2.7 %collective-permute-done.20 = f16[64,1024]{1,0:T(8,128)(2,1)} collective-permute-done((f16[64,1024]{1,0:T(8,128)(2,1)}, f16[64,1024]{1,0:T(8,128)(2,1)}, u32[]{:S(2)}, u32[]{:S(2)}) %collective-permute-start.20) | collective-permute-done | bytes 131104 | tf_op jit(solution)/shard_map/ppermute | solution.py:59
  143.7 3.0 %collective-permute-start.23 = (f32[8,128]{1,0:T(8,128)S(1)}, f32[8,128]{1,0:T(8,128)S(1)}, u32[]{:S(2)}, u32[]{:S(2)}) collective-permute-start(f32[8,128]{1,0:T(8,128)S(1)} %reduce_sum.18), channel_id=1, source_target_pairs={{0,4},{1,5},{2,6},{3,7},{4,0},{5,1},{6,2},{7,3},{8,12},{9,13},{10,... | collective-permute-start | bytes 12296 | tf_op jit(solution)/shard_map/ppermute | solution.py:59
  146.7 4.6 %collective-permute-done.23 = f32[8,128]{1,0:T(8,128)S(1)} collective-permute-done((f32[8,128]{1,0:T(8,128)S(1)}, f32[8,128]{1,0:T(8,128)S(1)}, u32[]{:S(2)}, u32[]{:S(2)}) %collective-permute-start.23) | collective-permute-done | bytes 4128 | tf_op jit(solution)/shard_map/ppermute | solution.py:59
  153.0 2.2 %collective-permute-start.27 = (f16[64,1024]{1,0:T(8,128)(2,1)S(1)}, f16[64,1024]{1,0:T(8,128)(2,1)S(1)}, u32[]{:S(2)}, u32[]{:S(2)}) collective-permute-start(f16[64,1024]{1,0:T(8,128)(2,1)S(1)} %get-tuple-element.82), channel_id=1, source_target_pairs={{0,38},{1,33},{2,32},{3,35},{4,34},{5,37},{6,36},{7,39},{8,46},{9,... | collective-permute-start | bytes 393224 | tf_op jit(solution)/shard_map/ppermute | solution.py:59
  155.2 4.5 %collective-permute-done.24 = f32[8,128]{1,0:T(8,128)S(1)} collective-permute-done((f32[8,128]{1,0:T(8,128)S(1)}, f32[8,128]{1,0:T(8,128)S(1)}, u32[]{:S(2)}, u32[]{:S(2)}) %collective-permute-start.24) | collective-permute-done | bytes 4128 | tf_op jit(solution)/shard_map/ppermute | solution.py:59
  159.9 3.4 %collective-permute-done.25 = f32[8,128]{1,0:T(8,128)S(1)} collective-permute-done((f32[8,128]{1,0:T(8,128)S(1)}, f32[8,128]{1,0:T(8,128)S(1)}, u32[]{:S(2)}, u32[]{:S(2)}) %collective-permute-start.25) | collective-permute-done | bytes 4128 | tf_op jit(solution)/shard_map/ppermute | solution.py:59
  (97 shorter events, 38.4 us)
Async XLA Ops:
  2.5 8.9 %collective-permute-start = (bf16[64,2048]{1,0:T(8,128)(2,1)}, bf16[64,2048]{1,0:T(8,128)(2,1)S(1)}, u32[]{:S(2)}, u32[]{:S(2)}) collective-permute-start(bf16[64,2048]{1,0:T(8,128)(2,1)} %get-tuple-element.44), channel_id=1, source_target_pairs={{0,8},{1,65},{2,10},{3,67},{4,12},{5,69},{6,14},{7,71},{8,16},{9,7... | collective-permute-start | bytes 786440 | tf_op jit(solution)/shard_map/ppermute | solution.py:59
  4.0 8.8 %collective-permute-start.1 = (bf16[64,2048]{1,0:T(8,128)(2,1)}, bf16[64,2048]{1,0:T(8,128)(2,1)S(1)}, u32[]{:S(2)}, u32[]{:S(2)}) collective-permute-start(bf16[64,2048]{1,0:T(8,128)(2,1)} %get-tuple-element.44), channel_id=1, source_target_pairs={{0,24},{1,193},{2,26},{3,195},{4,28},{5,197},{6,30},{7,199},{8,0},... | collective-permute-start | bytes 786440 | tf_op jit(solution)/shard_map/ppermute | solution.py:59
  5.8 8.3 %collective-permute-start.2 = (bf16[64,2048]{1,0:T(8,128)(2,1)}, bf16[64,2048]{1,0:T(8,128)(2,1)S(1)}, u32[]{:S(2)}, u32[]{:S(2)}) collective-permute-start(bf16[64,2048]{1,0:T(8,128)(2,1)} %get-tuple-element.44), channel_id=1, source_target_pairs={{0,16},{1,129},{2,18},{3,131},{4,20},{5,133},{6,22},{7,135},{8,24}... | collective-permute-start | bytes 786440 | tf_op jit(solution)/shard_map/ppermute | solution.py:59
  7.6 10.4 %collective-permute-start.3 = (bf16[64,2048]{1,0:T(8,128)(2,1)}, bf16[64,2048]{1,0:T(8,128)(2,1)S(1)}, u32[]{:S(2)}, u32[]{:S(2)}) collective-permute-start(bf16[64,2048]{1,0:T(8,128)(2,1)} %get-tuple-element.45.refs_6_), channel_id=1, source_target_pairs={{0,32},{1,39},{2,34},{3,33},{4,36},{5,35},{6,38},{7,37},{8,40},{9,... | collective-permute-start | bytes 786440 | tf_op jit(solution)/shard_map/ppermute | solution.py:59
  9.5 8.5 %collective-permute-start.4 = (bf16[64,2048]{1,0:T(8,128)(2,1)}, bf16[64,2048]{1,0:T(8,128)(2,1)S(1)}, u32[]{:S(2)}, u32[]{:S(2)}) collective-permute-start(bf16[64,2048]{1,0:T(8,128)(2,1)} %get-tuple-element.45.refs_6_), channel_id=1, source_target_pairs={{0,1},{1,0},{2,3},{3,2},{4,5},{5,4},{6,7},{7,6},{8,9},{9,8},{10,11... | collective-permute-start | bytes 786440 | tf_op jit(solution)/shard_map/ppermute | solution.py:59
  19.1 22.9 %collective-permute-start.5 = (bf16[256,2048]{1,0:T(8,128)(2,1)S(1)}, bf16[256,2048]{1,0:T(8,128)(2,1)S(1)}, u32[]{:S(2)}, u32[]{:S(2)}) collective-permute-start(bf16[256,2048]{1,0:T(8,128)(2,1)S(1)} %pad_maximum_fusion.refs_1_), channel_id=1, source_target_pairs={{0,64},{1,9},{2,66},{3,11},{4,68},{5,13},{6,70},{7,15},{8,72},{9,1... | collective-permute-start | bytes 3145736 | tf_op jit(solution)/shard_map/ppermute | solution.py:59
  20.8 21.2 %collective-permute-start.6 = (bf16[256,2048]{1,0:T(8,128)(2,1)S(1)}, bf16[256,2048]{1,0:T(8,128)(2,1)S(1)}, u32[]{:S(2)}, u32[]{:S(2)}) collective-permute-start(bf16[256,2048]{1,0:T(8,128)(2,1)S(1)} %pad_maximum_fusion.refs_1_), channel_id=1, source_target_pairs={{0,192},{1,25},{2,194},{3,27},{4,196},{5,29},{6,198},{7,31},{8,200... | collective-permute-start | bytes 3145736 | tf_op jit(solution)/shard_map/ppermute | solution.py:59
  21.2 7.6 %collective-permute-start.7 = (bf16[64,2048]{1,0:T(8,128)(2,1)S(1)}, bf16[64,2048]{1,0:T(8,128)(2,1)S(1)}, u32[]{:S(2)}, u32[]{:S(2)}) collective-permute-start(bf16[64,2048]{1,0:T(8,128)(2,1)S(1)} %collective-permute-done.3), channel_id=1, source_target_pairs={{0,32},{1,39},{2,34},{3,33},{4,36},{5,35},{6,38},{7,37},{8,40},{9,... | collective-permute-start | bytes 786440 | tf_op jit(solution)/shard_map/ppermute | solution.py:59
  21.2 10.4 %collective-permute-start.8 = (bf16[64,2048]{1,0:T(8,128)(2,1)S(1)}, bf16[64,2048]{1,0:T(8,128)(2,1)S(1)}, u32[]{:S(2)}, u32[]{:S(2)}) collective-permute-start(bf16[64,2048]{1,0:T(8,128)(2,1)S(1)} %collective-permute-done.4.refs_7_), channel_id=1, source_target_pairs={{0,32},{1,39},{2,34},{3,33},{4,36},{5,35},{6,38},{7,37},{8,40},{9,... | collective-permute-start | bytes 786440 | tf_op jit(solution)/shard_map/ppermute | solution.py:59
  31.6 10.4 %collective-permute-start.9 = (bf16[64,2048]{1,0:T(8,128)(2,1)S(1)}, bf16[64,2048]{1,0:T(8,128)(2,1)S(1)}, u32[]{:S(2)}, u32[]{:S(2)}) collective-permute-start(bf16[64,2048]{1,0:T(8,128)(2,1)S(1)} %collective-permute-done.7), channel_id=1, source_target_pairs={{0,32},{1,39},{2,34},{3,33},{4,36},{5,35},{6,38},{7,37},{8,40},{9,... | collective-permute-start | bytes 786440 | tf_op jit(solution)/shard_map/ppermute | solution.py:59
  42.1 13.0 %collective-permute-start.13 = (bf16[320,2048]{1,0:T(8,128)(2,1)S(1)}, bf16[320,2048]{1,0:T(8,128)(2,1)}, u32[]{:S(2)}, u32[]{:S(2)}) collective-permute-start(bf16[320,2048]{1,0:T(8,128)(2,1)S(1)} %constant_dynamic-update-slice_fusion.refs_8_), channel_id=1, source_target_pairs={{0,1},{1,0},{2,3},{3,2},{4,5},{5,4},{6,7},{7,6},{8,9},{9,8},{10,11... | collective-permute-start | bytes 3932168 | tf_op jit(solution)/shard_map/ppermute | solution.py:59
  42.2 7.7 %collective-permute-start.14 = (bf16[64,2048]{1,0:T(8,128)(2,1)S(1)}, bf16[64,2048]{1,0:T(8,128)(2,1)S(1)}, u32[]{:S(2)}, u32[]{:S(2)}) collective-permute-start(bf16[64,2048]{1,0:T(8,128)(2,1)S(1)} %collective-permute-done.9), channel_id=1, source_target_pairs={{0,32},{1,39},{2,34},{3,33},{4,36},{5,35},{6,38},{7,37},{8,40},{9,... | collective-permute-start | bytes 786440 | tf_op jit(solution)/shard_map/ppermute | solution.py:59
  42.3 10.4 %collective-permute-start.15 = (bf16[64,2048]{1,0:T(8,128)(2,1)S(1)}, bf16[64,2048]{1,0:T(8,128)(2,1)S(1)}, u32[]{:S(2)}, u32[]{:S(2)}) collective-permute-start(bf16[64,2048]{1,0:T(8,128)(2,1)S(1)} %collective-permute-done.10), channel_id=1, source_target_pairs={{0,32},{1,39},{2,34},{3,33},{4,36},{5,35},{6,38},{7,37},{8,40},{9,... | collective-permute-start | bytes 786440 | tf_op jit(solution)/shard_map/ppermute | solution.py:59
  42.5 11.9 %collective-permute-start.11 = (bf16[128,2048]{1,0:T(8,128)(2,1)S(1)}, bf16[128,2048]{1,0:T(8,128)(2,1)S(1)}, u32[]{:S(2)}, u32[]{:S(2)}) collective-permute-start(bf16[128,2048]{1,0:T(8,128)(2,1)S(1)} %slice.21), channel_id=1, source_target_pairs={{0,64},{1,9},{2,66},{3,11},{4,68},{5,13},{6,70},{7,15},{8,72},{9,1... | collective-permute-start | bytes 1572872 | tf_op jit(solution)/shard_map/ppermute | solution.py:59
  44.2 10.2 %collective-permute-start.12 = (bf16[128,2048]{1,0:T(8,128)(2,1)S(1)}, bf16[128,2048]{1,0:T(8,128)(2,1)}, u32[]{:S(2)}, u32[]{:S(2)}) collective-permute-start(bf16[128,2048]{1,0:T(8,128)(2,1)S(1)} %slice.22), channel_id=1, source_target_pairs={{0,192},{1,25},{2,194},{3,27},{4,196},{5,29},{6,198},{7,31},{8,200... | collective-permute-start | bytes 1572872 | tf_op jit(solution)/shard_map/ppermute | solution.py:59
  70.7 12.4 %all-to-all-start.1 = ((f32[16,2,1152]{2,1,0:T(2,128)}), f32[16,2,1152]{2,1,0:T(2,128)S(1)}, u32[]{:S(2)}, u32[]{:S(2)}) async-start(f32[16,2,1152]{2,1,0:T(2,128)} %get-tuple-element.65), calls=%async_computation.1 | async-start | bytes 294912 | tf_op jit(solution)/shard_map/all_to_all | solution.py:400
  83.1 15.6 %all-to-all-start = ((f32[16,2,1152]{2,1,0:T(2,128)}), f32[16,2,1152]{2,1,0:T(2,128)S(1)}, u32[]{:S(2)}, u32[]{:S(2)}) async-start(f32[16,2,1152]{2,1,0:T(2,128)} %get-tuple-element.64), calls=%async_computation | async-start | bytes 294912 | tf_op jit(solution)/shard_map/all_to_all | solution.py:400
  109.5 14.4 %all-to-all-start.2 = ((f32[16,8,128]{2,1,0:T(8,128)}), f32[16,8,128]{2,1,0:T(8,128)S(1)}, u32[]{:S(2)}, u32[]{:S(2)}) async-start(f32[16,8,128]{2,1,0:T(8,128)} %get-tuple-element.80), calls=%async_computation.2 | async-start | bytes 131072 | tf_op jit(solution)/shard_map/all_to_all | solution.py:400
  123.9 43.5 %all-to-all-start.3 = ((f16[16,64,1024]{2,1,0:T(8,128)(2,1)}), f16[16,64,1024]{2,1,0:T(8,128)(2,1)S(1)}, u32[]{:S(2)}, u32[]{:S(2)}) async-start(f16[16,64,1024]{2,1,0:T(8,128)(2,1)} %bitcast.65), calls=%async_computation.3 | async-start | bytes 4194304 | tf_op jit(solution)/shard_map/all_to_all | solution.py:467
  141.7 9.7 %collective-permute-start.21 = (f16[64,1024]{1,0:T(8,128)(2,1)}, f16[64,1024]{1,0:T(8,128)(2,1)S(1)}, u32[]{:S(2)}, u32[]{:S(2)}) collective-permute-start(f16[64,1024]{1,0:T(8,128)(2,1)} %get-tuple-element.78), channel_id=1, source_target_pairs={{0,38},{1,33},{2,32},{3,35},{4,34},{5,37},{6,36},{7,39},{8,46},{9,... | collective-permute-start | bytes 393224 | tf_op jit(solution)/shard_map/ppermute | solution.py:59
  142.5 9.4 %collective-permute-start.22 = (f16[64,1024]{1,0:T(8,128)(2,1)S(1)}, f16[64,1024]{1,0:T(8,128)(2,1)}, u32[]{:S(2)}, u32[]{:S(2)}) collective-permute-start(f16[64,1024]{1,0:T(8,128)(2,1)S(1)} %get-tuple-element.79), channel_id=1, source_target_pairs={{0,32},{1,39},{2,34},{3,33},{4,36},{5,35},{6,38},{7,37},{8,40},{9,... | collective-permute-start | bytes 393224 | tf_op jit(solution)/shard_map/ppermute | solution.py:59
  143.7 7.6 %collective-permute-start.23 = (f32[8,128]{1,0:T(8,128)S(1)}, f32[8,128]{1,0:T(8,128)S(1)}, u32[]{:S(2)}, u32[]{:S(2)}) collective-permute-start(f32[8,128]{1,0:T(8,128)S(1)} %reduce_sum.18), channel_id=1, source_target_pairs={{0,4},{1,5},{2,6},{3,7},{4,0},{5,1},{6,2},{7,3},{8,12},{9,13},{10,... | collective-permute-start | bytes 12296 | tf_op jit(solution)/shard_map/ppermute | solution.py:59
  153.0 12.6 %collective-permute-start.27 = (f16[64,1024]{1,0:T(8,128)(2,1)S(1)}, f16[64,1024]{1,0:T(8,128)(2,1)S(1)}, u32[]{:S(2)}, u32[]{:S(2)}) collective-permute-start(f16[64,1024]{1,0:T(8,128)(2,1)S(1)} %get-tuple-element.82), channel_id=1, source_target_pairs={{0,38},{1,33},{2,32},{3,35},{4,34},{5,37},{6,36},{7,39},{8,46},{9,... | collective-permute-start | bytes 393224 | tf_op jit(solution)/shard_map/ppermute | solution.py:59
  155.2 10.5 %collective-permute-start.28 = (f16[64,1024]{1,0:T(8,128)(2,1)S(1)}, f16[64,1024]{1,0:T(8,128)(2,1)}, u32[]{:S(2)}, u32[]{:S(2)}) collective-permute-start(f16[64,1024]{1,0:T(8,128)(2,1)S(1)} %get-tuple-element.83), channel_id=1, source_target_pairs={{0,32},{1,39},{2,34},{3,33},{4,36},{5,35},{6,38},{7,37},{8,40},{9,... | collective-permute-start | bytes 393224 | tf_op jit(solution)/shard_map/ppermute | solution.py:59
  (20 other events, 142.7 us)

commit v13 on v12

--- a/solution.py
+++ b/solution.py
@@ -469,13 +469,14 @@
     down = moved(first, along_z(-1)).astype(jnp.float32)
     up = moved(second, along_z(1)).astype(jnp.float32)
     value = value + moved(value, steps[0])
-    first, second = tie((narrow(block(-2) + down), narrow(block(2) + up)))
+    first, second, value = tie((narrow(block(-2) + down), narrow(block(2) + up), value))
     down = moved(first, along_z(-1)).astype(jnp.float32)
     up = moved(second, along_z(1)).astype(jnp.float32)
+    value = value + moved(value, steps[1])
     first, second, value = tie((narrow(block(-1) + down), narrow(block(1) + up), value))
     down = moved(first, along_z(-1)).astype(jnp.float32)
     up = moved(second, along_z(1)).astype(jnp.float32)
-    for to in steps[1:]:
+    for to in steps[2:]:
         value = value + moved(value, to)
     loss = value[0, 0] / (256 * BLOCK)
     image_grad = (block(0) + down + up) * image_factor

time: 171 us -> 167 us (0.977)
  waiting for transfers between devices: 71.8 us -> 66.9 us
    ppermute x29, waiting for transfers between devices: 56.7 us -> 51.8 us  [moved(): return lax.ppermute(value, NAMES, pairs)]
where the time goes in v13:
time: 167 us; the launch traced here: 166 us
  waiting for transfers between devices  66.9 us (40%)
  starting transfers between devices  50.2 us (30%)
  Pallas kernels  26.1 us (16%)
  matrix products  8.57 us (5%)
  other arithmetic  7.85 us (5%)
  between operations  3.43 us (2%)
  local copies, waits for them, and re-layouts  2.87 us (2%)
    ppermute x29, waiting for transfers between devices, moved(): return lax.ppermute(value, NAMES, pairs)  51.8 us
    ppermute x29, starting transfers between devices, moved(): return lax.ppermute(value, NAMES, pairs)  25.4 us
    all_to_all x3, starting transfers between devices, exchanged(): return lax.all_to_all(copies, axis, split_axis=0, concat_axis=0, tiled=True)  17.5 us
    pallas_call x1, Pallas kernels, logits_and_statistics(): pl.pallas_call(kernel, out_shape=(square, square, half, half, small, smal...  15.5 us
    all_to_all x3, waiting for transfers between devices, exchanged(): return lax.all_to_all(copies, axis, split_axis=0, concat_axis=0, tiled=True)  15.1 us
    pallas_call x1, Pallas kernels, gradient_of_logits(): pl.pallas_call(gradient_kernel, grid=(SIDE // ROWS,), out_shape=(jax.Shap...  8.69 us
    all_to_all x1, starting transfers between devices, body(): lax.all_to_all(text_part.reshape(16, BLOCK, WIDTH), TEXT_GROUP, 0, 0, til...  7.28 us
    dot_general x1, matrix products, body(): jnp.dot(turned, image_slab, preferred_element_type=jnp.float32)  3.69 us
  transfers between devices with their start and end apart: 33, of which 19 were waited for; matrix products, arithmetic and copies ran while one was open for 9% of the time, Pallas kernels for 0%

profile of v13, /device:TPU:8, one launch (start us, length us, event | category | flops | bytes accessed | tf_op | source)
XLA Modules:
  0.0 165.9 jit_solution(2846459596080569563)
XLA Ops:
  9.5 1.9 %collective-permute-start.4 = (bf16[64,2048]{1,0:T(8,128)(2,1)}, bf16[64,2048]{1,0:T(8,128)(2,1)S(1)}, u32[]{:S(2)}, u32[]{:S(2)}) collective-permute-start(bf16[64,2048]{1,0:T(8,128)(2,1)} %get-tuple-element.46.refs_6_), channel_id=1, source_target_pairs={{0,1},{1,0},{2,3},{3,2},{4,5},{5,4},{6,7},{7,6},{8,9},{9,8},{10,11... | collective-permute-start | bytes 786440 | tf_op jit(solution)/shard_map/ppermute | solution.py:59
  14.1 3.9 %collective-permute-done.3 = bf16[64,2048]{1,0:T(8,128)(2,1)S(1)} collective-permute-done((bf16[64,2048]{1,0:T(8,128)(2,1)}, bf16[64,2048]{1,0:T(8,128)(2,1)S(1)}, u32[]{:S(2)}, u32[]{:S(2)}) %collective-permute-start.3) | collective-permute-done | bytes 262176 | tf_op jit(solution)/shard_map/ppermute | solution.py:59
  21.2 7.6 %collective-permute-done.7 = bf16[64,2048]{1,0:T(8,128)(2,1)S(1)} collective-permute-done((bf16[64,2048]{1,0:T(8,128)(2,1)S(1)}, bf16[64,2048]{1,0:T(8,128)(2,1)S(1)}, u32[]{:S(2)}, u32[]{:S(2)}) %collective-permute-start.7) | collective-permute-done | bytes 262176 | tf_op jit(solution)/shard_map/ppermute | solution.py:59
  28.8 2.8 %collective-permute-done.8 = bf16[64,2048]{1,0:T(8,128)(2,1)S(1)} collective-permute-done((bf16[64,2048]{1,0:T(8,128)(2,1)S(1)}, bf16[64,2048]{1,0:T(8,128)(2,1)S(1)}, u32[]{:S(2)}, u32[]{:S(2)}) %collective-permute-start.8) | collective-permute-done | bytes 262176 | tf_op jit(solution)/shard_map/ppermute | solution.py:59
  31.7 7.5 %collective-permute-done.10 = bf16[64,2048]{1,0:T(8,128)(2,1)S(1)} collective-permute-done((bf16[64,2048]{1,0:T(8,128)(2,1)S(1)}, bf16[64,2048]{1,0:T(8,128)(2,1)S(1)}, u32[]{:S(2)}, u32[]{:S(2)}) %collective-permute-start.10) | collective-permute-done | bytes 262176 | tf_op jit(solution)/shard_map/ppermute | solution.py:59
  39.2 2.8 %collective-permute-done.9 = bf16[64,2048]{1,0:T(8,128)(2,1)S(1)} collective-permute-done((bf16[64,2048]{1,0:T(8,128)(2,1)S(1)}, bf16[64,2048]{1,0:T(8,128)(2,1)S(1)}, u32[]{:S(2)}, u32[]{:S(2)}) %collective-permute-start.9) | collective-permute-done | bytes 262176 | tf_op jit(solution)/shard_map/ppermute | solution.py:59
  44.7 5.2 %collective-permute-done.14 = bf16[64,2048]{1,0:T(8,128)(2,1)S(1)} collective-permute-done((bf16[64,2048]{1,0:T(8,128)(2,1)S(1)}, bf16[64,2048]{1,0:T(8,128)(2,1)S(1)}, u32[]{:S(2)}, u32[]{:S(2)}) %collective-permute-start.14) | collective-permute-done | bytes 262176 | tf_op jit(solution)/shard_map/ppermute | solution.py:59
  49.9 2.8 %collective-permute-done.15 = bf16[64,2048]{1,0:T(8,128)(2,1)S(1)} collective-permute-done((bf16[64,2048]{1,0:T(8,128)(2,1)S(1)}, bf16[64,2048]{1,0:T(8,128)(2,1)S(1)}, u32[]{:S(2)}, u32[]{:S(2)}) %collective-permute-start.15) | collective-permute-done | bytes 262176 | tf_op jit(solution)/shard_map/ppermute | solution.py:59
  55.2 15.5 %shard_map.68 = (f32[1024,1024]{1,0:T(8,128)}, f32[1024,1024]{1,0:T(8,128)}, bf16[1024,1024]{1,0:T(8,128)(2,1)}, bf16[1024,1024]{1,0:T(8,128)(2,1)}, f32[16,2,1152]{2,1,0:T(2,128)}, /*index=5*/f32[16,2,1152]{2,1,0:T(2,128)}) custom-call(s32[32]{0:T(128)} %stack.131.refs_0_, bf16[256,2048]{1,0:T(8,128)(2,1)} %copy-done.1, bf16[256,2048]{1,0:T(8,128)(2,1)} %copy-done.2, ...), custom_call_target="tpu_custom_call" | custom-call | flops 4294967296 | bytes 20971520 | tf_op jit(solution)/shard_map/pallas_call | solution.py:261
  70.7 6.1 %all-to-all-start.1 = ((f32[16,2,1152]{2,1,0:T(2,128)}), f32[16,2,1152]{2,1,0:T(2,128)S(1)}, u32[]{:S(2)}, u32[]{:S(2)}) async-start(f32[16,2,1152]{2,1,0:T(2,128)} %get-tuple-element.66), calls=%async_computation.1 | async-start | bytes 294912 | tf_op jit(solution)/shard_map/all_to_all | solution.py:400
  76.8 6.3 %all-to-all-done.1.col_ref = f32[16,2,1152]{2,1,0:T(2,128)S(1)} async-done(((f32[16,2,1152]{2,1,0:T(2,128)}), f32[16,2,1152]{2,1,0:T(2,128)S(1)}, u32[]{:S(2)}, u32[]{:S(2)}) %all-to-all-start.1) | async-done | bytes 147488 | tf_op jit(solution)/shard_map/all_to_all | solution.py:400
  83.1 6.3 %all-to-all-start = ((f32[16,2,1152]{2,1,0:T(2,128)}), f32[16,2,1152]{2,1,0:T(2,128)S(1)}, u32[]{:S(2)}, u32[]{:S(2)}) async-start(f32[16,2,1152]{2,1,0:T(2,128)} %get-tuple-element.65), calls=%async_computation | async-start | bytes 294912 | tf_op jit(solution)/shard_map/all_to_all | solution.py:400
  89.9 8.8 %all-to-all-done.row_ref = f32[16,2,1152]{2,1,0:T(2,128)S(1)} async-done(((f32[16,2,1152]{2,1,0:T(2,128)}), f32[16,2,1152]{2,1,0:T(2,128)S(1)}, u32[]{:S(2)}, u32[]{:S(2)}) %all-to-all-start) | async-done | bytes 147488 | tf_op jit(solution)/shard_map/all_to_all | solution.py:400
  98.7 8.7 %shard_map.69 = (bf16[1024,1024]{1,0:T(8,128)(2,1)S(1)}, bf16[1024,1024]{1,0:T(8,128)(2,1)S(1)}, f32[8,1024]{1,0:T(8,128)S(1)}, f32[16,8,128]{2,1,0:T(8,128)}) custom-call(f32[1024,1024]{1,0:T(8,128)} %get-tuple-element.63.s_ref, f32[1024,1024]{1,0:T(8,128)} %get-tuple-element.64.t_ref, f32[16,2,1152]{2,1,0:T(2,128)S(1)} %all-to-all-done.row_ref, ...), custom_call_target="tpu_custom_call" | custom-call | flops 16777216 | bytes 10485760 | tf_op jit(solution)/shard_map/pallas_call | solution.py:367
  109.5 5.1 %all-to-all-start.2 = ((f32[16,8,128]{2,1,0:T(8,128)}), f32[16,8,128]{2,1,0:T(8,128)S(1)}, u32[]{:S(2)}, u32[]{:S(2)}) async-start(f32[16,8,128]{2,1,0:T(8,128)} %get-tuple-element.79), calls=%async_computation.2 | async-start | bytes 131072 | tf_op jit(solution)/shard_map/all_to_all | solution.py:400
  114.5 3.6 %add_convert_fusion = f16[512,1024]{1,0:T(8,128)(2,1)S(1)} fusion(f16[512,1024]{1,0:T(8,128)(2,1)} %collective-permute-done.17, bf16[1024,1024]{1,0:T(8,128)(2,1)} %get-tuple-element.68, f32[1024]{0:T(1024)S(1)} %bitcast.75, bf16[1024,1024]{1,0:T(8,128)(2,1)} %copy-done, s32[]{:T(128)S(6)} %select_n.465), kind=kOutput, calls=%fused_computation.2 | convolution fusion | flops 1075838976 | bytes 5246980 | tf_op jit(solution)/shard_map/dot_general | solution.py:449
  119.4 3.7 %multiply_convert_fusion = f16[1024,1024]{1,0:T(8,128)(2,1)} fusion(bf16[1024,1024]{1,0:T(8,128)(2,1)S(1)} %get-tuple-element.74, bf16[1024,1024]{1,0:T(8,128)(2,1)S(1)} %copy-done.10, f32[1024]{0:T(1024)S(1)} %bitcast.73), kind=kOutput, calls=%fused_computation.1 | convolution fusion | flops 2149580800 | bytes 6295552 | tf_op jit(solution)/shard_map/dot_general | solution.py:464
  123.9 7.3 %all-to-all-start.3 = ((f16[16,64,1024]{2,1,0:T(8,128)(2,1)}), f16[16,64,1024]{2,1,0:T(8,128)(2,1)S(1)}, u32[]{:S(2)}, u32[]{:S(2)}) async-start(f16[16,64,1024]{2,1,0:T(8,128)(2,1)} %bitcast.65), calls=%async_computation.3 | async-start | bytes 4194304 | tf_op jit(solution)/shard_map/all_to_all | solution.py:467
  133.9 2.6 %collective-permute-start.21 = (f32[8,128]{1,0:T(8,128)S(1)}, f32[8,128]{1,0:T(8,128)S(1)}, u32[]{:S(2)}, u32[]{:S(2)}) collective-permute-start(f32[8,128]{1,0:T(8,128)S(1)} %reduce_sum.18), channel_id=1, source_target_pairs={{0,4},{1,5},{2,6},{3,7},{4,0},{5,1},{6,2},{7,3},{8,12},{9,13},{10,... | collective-permute-start | bytes 12296 | tf_op jit(solution)/shard_map/ppermute | solution.py:59
  136.5 5.0 %collective-permute-done.21 = f32[8,128]{1,0:T(8,128)S(1)} collective-permute-done((f32[8,128]{1,0:T(8,128)S(1)}, f32[8,128]{1,0:T(8,128)S(1)}, u32[]{:S(2)}, u32[]{:S(2)}) %collective-permute-start.21) | collective-permute-done | bytes 4128 | tf_op jit(solution)/shard_map/ppermute | solution.py:59
  143.2 2.9 %collective-permute-start.22 = (f16[64,1024]{1,0:T(8,128)(2,1)}, f16[64,1024]{1,0:T(8,128)(2,1)S(1)}, u32[]{:S(2)}, u32[]{:S(2)}) collective-permute-start(f16[64,1024]{1,0:T(8,128)(2,1)} %get-tuple-element.80), channel_id=1, source_target_pairs={{0,38},{1,33},{2,32},{3,35},{4,34},{5,37},{6,36},{7,39},{8,46},{9,... | collective-permute-start | bytes 393224 | tf_op jit(solution)/shard_map/ppermute | solution.py:59
  146.8 3.8 %collective-permute-done.24 = f32[8,128]{1,0:T(8,128)S(1)} collective-permute-done((f32[8,128]{1,0:T(8,128)S(1)}, f32[8,128]{1,0:T(8,128)S(1)}, u32[]{:S(2)}, u32[]{:S(2)}) %collective-permute-start.24) | collective-permute-done | bytes 4128 | tf_op jit(solution)/shard_map/ppermute | solution.py:59
  153.4 2.2 %collective-permute-start.27 = (f16[64,1024]{1,0:T(8,128)(2,1)S(1)}, f16[64,1024]{1,0:T(8,128)(2,1)S(1)}, u32[]{:S(2)}, u32[]{:S(2)}) collective-permute-start(f16[64,1024]{1,0:T(8,128)(2,1)S(1)} %get-tuple-element.84), channel_id=1, source_target_pairs={{0,38},{1,33},{2,32},{3,35},{4,34},{5,37},{6,36},{7,39},{8,46},{9,... | collective-permute-start | bytes 393224 | tf_op jit(solution)/shard_map/ppermute | solution.py:59
  155.6 3.6 %collective-permute-done.25 = f32[8,128]{1,0:T(8,128)S(1)} collective-permute-done((f32[8,128]{1,0:T(8,128)S(1)}, f32[8,128]{1,0:T(8,128)S(1)}, u32[]{:S(2)}, u32[]{:S(2)}) %collective-permute-start.25) | collective-permute-done | bytes 4128 | tf_op jit(solution)/shard_map/ppermute | solution.py:59
  (97 shorter events, 36.5 us)
Async XLA Ops:
  2.5 8.9 %collective-permute-start = (bf16[64,2048]{1,0:T(8,128)(2,1)}, bf16[64,2048]{1,0:T(8,128)(2,1)S(1)}, u32[]{:S(2)}, u32[]{:S(2)}) collective-permute-start(bf16[64,2048]{1,0:T(8,128)(2,1)} %get-tuple-element.45), channel_id=1, source_target_pairs={{0,8},{1,65},{2,10},{3,67},{4,12},{5,69},{6,14},{7,71},{8,16},{9,7... | collective-permute-start | bytes 786440 | tf_op jit(solution)/shard_map/ppermute | solution.py:59
  4.0 8.8 %collective-permute-start.1 = (bf16[64,2048]{1,0:T(8,128)(2,1)}, bf16[64,2048]{1,0:T(8,128)(2,1)S(1)}, u32[]{:S(2)}, u32[]{:S(2)}) collective-permute-start(bf16[64,2048]{1,0:T(8,128)(2,1)} %get-tuple-element.45), channel_id=1, source_target_pairs={{0,24},{1,193},{2,26},{3,195},{4,28},{5,197},{6,30},{7,199},{8,0},... | collective-permute-start | bytes 786440 | tf_op jit(solution)/shard_map/ppermute | solution.py:59
  5.8 8.3 %collective-permute-start.2 = (bf16[64,2048]{1,0:T(8,128)(2,1)}, bf16[64,2048]{1,0:T(8,128)(2,1)S(1)}, u32[]{:S(2)}, u32[]{:S(2)}) collective-permute-start(bf16[64,2048]{1,0:T(8,128)(2,1)} %get-tuple-element.45), channel_id=1, source_target_pairs={{0,16},{1,129},{2,18},{3,131},{4,20},{5,133},{6,22},{7,135},{8,24}... | collective-permute-start | bytes 786440 | tf_op jit(solution)/shard_map/ppermute | solution.py:59
  7.6 10.4 %collective-permute-start.3 = (bf16[64,2048]{1,0:T(8,128)(2,1)}, bf16[64,2048]{1,0:T(8,128)(2,1)S(1)}, u32[]{:S(2)}, u32[]{:S(2)}) collective-permute-start(bf16[64,2048]{1,0:T(8,128)(2,1)} %get-tuple-element.46.refs_6_), channel_id=1, source_target_pairs={{0,32},{1,39},{2,34},{3,33},{4,36},{5,35},{6,38},{7,37},{8,40},{9,... | collective-permute-start | bytes 786440 | tf_op jit(solution)/shard_map/ppermute | solution.py:59
  9.5 8.5 %collective-permute-start.4 = (bf16[64,2048]{1,0:T(8,128)(2,1)}, bf16[64,2048]{1,0:T(8,128)(2,1)S(1)}, u32[]{:S(2)}, u32[]{:S(2)}) collective-permute-start(bf16[64,2048]{1,0:T(8,128)(2,1)} %get-tuple-element.46.refs_6_), channel_id=1, source_target_pairs={{0,1},{1,0},{2,3},{3,2},{4,5},{5,4},{6,7},{7,6},{8,9},{9,8},{10,11... | collective-permute-start | bytes 786440 | tf_op jit(solution)/shard_map/ppermute | solution.py:59
  19.1 22.9 %collective-permute-start.5 = (bf16[256,2048]{1,0:T(8,128)(2,1)S(1)}, bf16[256,2048]{1,0:T(8,128)(2,1)S(1)}, u32[]{:S(2)}, u32[]{:S(2)}) collective-permute-start(bf16[256,2048]{1,0:T(8,128)(2,1)S(1)} %pad_maximum_fusion.refs_1_), channel_id=1, source_target_pairs={{0,64},{1,9},{2,66},{3,11},{4,68},{5,13},{6,70},{7,15},{8,72},{9,1... | collective-permute-start | bytes 3145736 | tf_op jit(solution)/shard_map/ppermute | solution.py:59
  20.8 21.2 %collective-permute-start.6 = (bf16[256,2048]{1,0:T(8,128)(2,1)S(1)}, bf16[256,2048]{1,0:T(8,128)(2,1)S(1)}, u32[]{:S(2)}, u32[]{:S(2)}) collective-permute-start(bf16[256,2048]{1,0:T(8,128)(2,1)S(1)} %pad_maximum_fusion.refs_1_), channel_id=1, source_target_pairs={{0,192},{1,25},{2,194},{3,27},{4,196},{5,29},{6,198},{7,31},{8,200... | collective-permute-start | bytes 3145736 | tf_op jit(solution)/shard_map/ppermute | solution.py:59
  21.2 7.6 %collective-permute-start.7 = (bf16[64,2048]{1,0:T(8,128)(2,1)S(1)}, bf16[64,2048]{1,0:T(8,128)(2,1)S(1)}, u32[]{:S(2)}, u32[]{:S(2)}) collective-permute-start(bf16[64,2048]{1,0:T(8,128)(2,1)S(1)} %collective-permute-done.3), channel_id=1, source_target_pairs={{0,32},{1,39},{2,34},{3,33},{4,36},{5,35},{6,38},{7,37},{8,40},{9,... | collective-permute-start | bytes 786440 | tf_op jit(solution)/shard_map/ppermute | solution.py:59
  21.2 10.4 %collective-permute-start.8 = (bf16[64,2048]{1,0:T(8,128)(2,1)S(1)}, bf16[64,2048]{1,0:T(8,128)(2,1)S(1)}, u32[]{:S(2)}, u32[]{:S(2)}) collective-permute-start(bf16[64,2048]{1,0:T(8,128)(2,1)S(1)} %collective-permute-done.4.refs_7_), channel_id=1, source_target_pairs={{0,32},{1,39},{2,34},{3,33},{4,36},{5,35},{6,38},{7,37},{8,40},{9,... | collective-permute-start | bytes 786440 | tf_op jit(solution)/shard_map/ppermute | solution.py:59
  31.6 7.6 %collective-permute-start.10 = (bf16[64,2048]{1,0:T(8,128)(2,1)S(1)}, bf16[64,2048]{1,0:T(8,128)(2,1)S(1)}, u32[]{:S(2)}, u32[]{:S(2)}) collective-permute-start(bf16[64,2048]{1,0:T(8,128)(2,1)S(1)} %collective-permute-done.8), channel_id=1, source_target_pairs={{0,32},{1,39},{2,34},{3,33},{4,36},{5,35},{6,38},{7,37},{8,40},{9,... | collective-permute-start | bytes 786440 | tf_op jit(solution)/shard_map/ppermute | solution.py:59
  31.6 10.4 %collective-permute-start.9 = (bf16[64,2048]{1,0:T(8,128)(2,1)S(1)}, bf16[64,2048]{1,0:T(8,128)(2,1)S(1)}, u32[]{:S(2)}, u32[]{:S(2)}) collective-permute-start(bf16[64,2048]{1,0:T(8,128)(2,1)S(1)} %collective-permute-done.7), channel_id=1, source_target_pairs={{0,32},{1,39},{2,34},{3,33},{4,36},{5,35},{6,38},{7,37},{8,40},{9,... | collective-permute-start | bytes 786440 | tf_op jit(solution)/shard_map/ppermute | solution.py:59
  42.1 13.0 %collective-permute-start.13 = (bf16[320,2048]{1,0:T(8,128)(2,1)S(1)}, bf16[320,2048]{1,0:T(8,128)(2,1)}, u32[]{:S(2)}, u32[]{:S(2)}) collective-permute-start(bf16[320,2048]{1,0:T(8,128)(2,1)S(1)} %constant_dynamic-update-slice_fusion.refs_8_), channel_id=1, source_target_pairs={{0,1},{1,0},{2,3},{3,2},{4,5},{5,4},{6,7},{7,6},{8,9},{9,8},{10,11... | collective-permute-start | bytes 3932168 | tf_op jit(solution)/shard_map/ppermute | solution.py:59
  42.2 7.7 %collective-permute-start.14 = (bf16[64,2048]{1,0:T(8,128)(2,1)S(1)}, bf16[64,2048]{1,0:T(8,128)(2,1)S(1)}, u32[]{:S(2)}, u32[]{:S(2)}) collective-permute-start(bf16[64,2048]{1,0:T(8,128)(2,1)S(1)} %collective-permute-done.9), channel_id=1, source_target_pairs={{0,32},{1,39},{2,34},{3,33},{4,36},{5,35},{6,38},{7,37},{8,40},{9,... | collective-permute-start | bytes 786440 | tf_op jit(solution)/shard_map/ppermute | solution.py:59
  42.3 10.4 %collective-permute-start.15 = (bf16[64,2048]{1,0:T(8,128)(2,1)S(1)}, bf16[64,2048]{1,0:T(8,128)(2,1)S(1)}, u32[]{:S(2)}, u32[]{:S(2)}) collective-permute-start(bf16[64,2048]{1,0:T(8,128)(2,1)S(1)} %collective-permute-done.10), channel_id=1, source_target_pairs={{0,32},{1,39},{2,34},{3,33},{4,36},{5,35},{6,38},{7,37},{8,40},{9,... | collective-permute-start | bytes 786440 | tf_op jit(solution)/shard_map/ppermute | solution.py:59
  42.5 11.9 %collective-permute-start.11 = (bf16[128,2048]{1,0:T(8,128)(2,1)S(1)}, bf16[128,2048]{1,0:T(8,128)(2,1)S(1)}, u32[]{:S(2)}, u32[]{:S(2)}) collective-permute-start(bf16[128,2048]{1,0:T(8,128)(2,1)S(1)} %slice.21), channel_id=1, source_target_pairs={{0,64},{1,9},{2,66},{3,11},{4,68},{5,13},{6,70},{7,15},{8,72},{9,1... | collective-permute-start | bytes 1572872 | tf_op jit(solution)/shard_map/ppermute | solution.py:59
  44.2 10.2 %collective-permute-start.12 = (bf16[128,2048]{1,0:T(8,128)(2,1)S(1)}, bf16[128,2048]{1,0:T(8,128)(2,1)}, u32[]{:S(2)}, u32[]{:S(2)}) collective-permute-start(bf16[128,2048]{1,0:T(8,128)(2,1)S(1)} %slice.22), channel_id=1, source_target_pairs={{0,192},{1,25},{2,194},{3,27},{4,196},{5,29},{6,198},{7,31},{8,200... | collective-permute-start | bytes 1572872 | tf_op jit(solution)/shard_map/ppermute | solution.py:59
  70.7 12.4 %all-to-all-start.1 = ((f32[16,2,1152]{2,1,0:T(2,128)}), f32[16,2,1152]{2,1,0:T(2,128)S(1)}, u32[]{:S(2)}, u32[]{:S(2)}) async-start(f32[16,2,1152]{2,1,0:T(2,128)} %get-tuple-element.66), calls=%async_computation.1 | async-start | bytes 294912 | tf_op jit(solution)/shard_map/all_to_all | solution.py:400
  83.1 15.6 %all-to-all-start = ((f32[16,2,1152]{2,1,0:T(2,128)}), f32[16,2,1152]{2,1,0:T(2,128)S(1)}, u32[]{:S(2)}, u32[]{:S(2)}) async-start(f32[16,2,1152]{2,1,0:T(2,128)} %get-tuple-element.65), calls=%async_computation | async-start | bytes 294912 | tf_op jit(solution)/shard_map/all_to_all | solution.py:400
  109.5 14.4 %all-to-all-start.2 = ((f32[16,8,128]{2,1,0:T(8,128)}), f32[16,8,128]{2,1,0:T(8,128)S(1)}, u32[]{:S(2)}, u32[]{:S(2)}) async-start(f32[16,8,128]{2,1,0:T(8,128)} %get-tuple-element.79), calls=%async_computation.2 | async-start | bytes 131072 | tf_op jit(solution)/shard_map/all_to_all | solution.py:400
  123.9 39.7 %all-to-all-start.3 = ((f16[16,64,1024]{2,1,0:T(8,128)(2,1)}), f16[16,64,1024]{2,1,0:T(8,128)(2,1)S(1)}, u32[]{:S(2)}, u32[]{:S(2)}) async-start(f16[16,64,1024]{2,1,0:T(8,128)(2,1)} %bitcast.65), calls=%async_computation.3 | async-start | bytes 4194304 | tf_op jit(solution)/shard_map/all_to_all | solution.py:467
  131.9 9.7 %collective-permute-start.19 = (f16[64,1024]{1,0:T(8,128)(2,1)}, f16[64,1024]{1,0:T(8,128)(2,1)S(1)}, u32[]{:S(2)}, u32[]{:S(2)}) collective-permute-start(f16[64,1024]{1,0:T(8,128)(2,1)} %fusion.30), channel_id=1, source_target_pairs={{0,38},{1,33},{2,32},{3,35},{4,34},{5,37},{6,36},{7,39},{8,46},{9,... | collective-permute-start | bytes 393224 | tf_op jit(solution)/shard_map/ppermute | solution.py:59
  133.5 8.0 %collective-permute-start.20 = (f16[64,1024]{1,0:T(8,128)(2,1)}, f16[64,1024]{1,0:T(8,128)(2,1)}, u32[]{:S(2)}, u32[]{:S(2)}) collective-permute-start(f16[64,1024]{1,0:T(8,128)(2,1)} %get-tuple-element.78), channel_id=1, source_target_pairs={{0,32},{1,39},{2,34},{3,33},{4,36},{5,35},{6,38},{7,37},{8,40},{9,... | collective-permute-start | bytes 393224 | tf_op jit(solution)/shard_map/ppermute | solution.py:59
  133.9 7.6 %collective-permute-start.21 = (f32[8,128]{1,0:T(8,128)S(1)}, f32[8,128]{1,0:T(8,128)S(1)}, u32[]{:S(2)}, u32[]{:S(2)}) collective-permute-start(f32[8,128]{1,0:T(8,128)S(1)} %reduce_sum.18), channel_id=1, source_target_pairs={{0,4},{1,5},{2,6},{3,7},{4,0},{5,1},{6,2},{7,3},{8,12},{9,13},{10,... | collective-permute-start | bytes 12296 | tf_op jit(solution)/shard_map/ppermute | solution.py:59
  153.4 8.2 %collective-permute-start.27 = (f16[64,1024]{1,0:T(8,128)(2,1)S(1)}, f16[64,1024]{1,0:T(8,128)(2,1)S(1)}, u32[]{:S(2)}, u32[]{:S(2)}) collective-permute-start(f16[64,1024]{1,0:T(8,128)(2,1)S(1)} %get-tuple-element.84), channel_id=1, source_target_pairs={{0,38},{1,33},{2,32},{3,35},{4,34},{5,37},{6,36},{7,39},{8,46},{9,... | collective-permute-start | bytes 393224 | tf_op jit(solution)/shard_map/ppermute | solution.py:59
  (20 other events, 143.1 us)
